TPU v7x, 256 devices: a whole 4x4x8 slice. The times are simulated.
256 devices in a mesh: ep: 4 (over x_hi, core), tp: 64 (over y, x_lo, z).
Axes of the slice: x: 4 (x_hi: 2, x_lo: 2; x = x_hi * 2 + x_lo), y: 4, z: 8, core: 2. Of those that a mesh axis runs over, the one named last changes fastest.
Arguments:
- tokens: bfloat16 [256, 3072], P(('ep', 'tp')), may hold values from -6 to 6
- cotangent: bfloat16 [256, 3072], P(('ep', 'tp')), may hold values from -6 to 6
- routes: int32 [256, 2], P(('ep', 'tp')), may hold values from 0 to 3, as said below
- gate_weights: bfloat16 [256, 2], P(('ep', 'tp')), may hold values from 0.099609375 to 1
- w_gate: bfloat16 [4, 3072, 8192], P('ep', None, 'tp'), may hold values from -0.109375 to 0.109375
- w_up: bfloat16 [4, 3072, 8192], P('ep', None, 'tp'), may hold values from -0.109375 to 0.109375
- w_down: bfloat16 [4, 8192, 3072], P('ep', 'tp'), may hold values from -0.0625 to 0.0625
Outputs:
- layer_out: bfloat16 [256, 3072], P(('ep', 'tp'))
- grad_tokens: bfloat16 [256, 3072], P(('ep', 'tp'))
- grad_gate: bfloat16 [4, 3072, 8192], P('ep', None, 'tp')
- grad_up: bfloat16 [4, 3072, 8192], P('ep', None, 'tp')
- grad_down: bfloat16 [4, 8192, 3072], P('ep', 'tp')
Inputs may be any that keep to these rules, and one draw needn't show every extreme that they name: `routes`: each token names two different experts. One expert is named by exactly 224 tokens; every other expert by at most 107 tokens, and one of them by exactly 107.
All inputs are finite; a program needn't handle non-finite values.
Results may differ from a plain program's by a relative error of at most 0.005.
Values may be sent and summed in bfloat16 or wider, within the bound.
No kernel may reach another device: no remote copies, remote signals or barrier semaphores. Data moves between devices by JAX's collectives and lax.ppermute only.
A program may use at most 64 MiB of HBM per device.

v0:
```python
import jax
import jax.numpy as jnp
from jax import lax
from jax.sharding import PartitionSpec as P


def side_by_side(arrays, axis, dim, along):
    both = jnp.concatenate(arrays, axis=along)
    whole, at, outs = (lax.all_gather(both, axis, axis=dim, tiled=True), 0, [])
    for a in arrays:
        outs.append(lax.slice_in_dim(whole, at, at + a.shape[along], axis=along))
        at += a.shape[along]
    return tuple(outs)


def in_blocks(value, dim, size):
    dims = value.shape
    tiles = value.reshape(*dims[:dim], size, dims[dim] // size, *dims[dim + 1 :])
    return jnp.moveaxis(tiles, dim, 0)


def one_scatter(arrays, axis, dims):
    size = lax.axis_size(axis)
    tiles = [in_blocks(a, dim, size) for a, dim in zip(arrays, dims)]
    lines = jnp.concatenate([b.reshape(size, -1) for b in tiles], axis=1)
    rows = max(16, -(-lines.shape[1] // 1024) * 8)
    lines = jnp.pad(lines, ((0, 0), (0, rows * 128 - lines.shape[1]))).reshape(-1, 128)
    vector, at, outs = (lax.psum_scatter(lines, axis, tiled=True).reshape(-1), 0, [])
    for b in tiles:
        part = b[0]
        outs.append(vector[at : at + part.size].reshape(part.shape))
        at += part.size
    return tuple(outs)


def sent_and_summed(value, axis, dim):
    size = lax.axis_size(axis)
    tiles = lax.all_to_all(in_blocks(value, dim, size), axis, 0, 0, tiled=True)
    return jnp.sum(tiles, axis=0)


def side_by_side_2(arrays, axis, dim, along):
    ends, at = ([], 0)
    for a in arrays[:-1]:
        at += a.shape[along]
        ends.append(at)
    both = jnp.concatenate(arrays, axis=along)
    return tuple(jnp.split(sent_and_summed(both, axis, dim), ends, axis=along))


def contract(left, right, left_dim, right_dim):
    return lax.dot_general(
        left, right, (((left_dim,), (right_dim,)), ((), ())), preferred_element_type=jnp.float32
    )


def expert_pass(token_rows, cotan_rows, gate_column, gate_slice, up_slice, down_slice):
    gate_pre = jnp.dot(token_rows, gate_slice, preferred_element_type=jnp.float32)
    up_pre = jnp.dot(token_rows, up_slice, preferred_element_type=jnp.float32)
    sigmoid = jax.nn.sigmoid(gate_pre)
    silu_gate = gate_pre * sigmoid
    hidden = (silu_gate * up_pre * gate_column[:, None]).astype(jnp.bfloat16)
    output = jnp.dot(hidden, down_slice, preferred_element_type=jnp.float32)
    grad_hidden = contract(cotan_rows, down_slice, 1, 1)
    grad_act = grad_hidden * gate_column[:, None]
    grad_gpre = (grad_act * up_pre * (sigmoid * (1.0 + gate_pre * (1.0 - sigmoid)))).astype(
        jnp.bfloat16
    )
    grad_upre = (grad_act * silu_gate).astype(jnp.bfloat16)
    grad_rows = contract(grad_gpre, gate_slice, 1, 1) + contract(grad_upre, up_slice, 1, 1)
    return (output, grad_rows, hidden, grad_gpre, grad_upre)


def weight_terms(token_rows, cotan_rows, hidden, grad_gpre, grad_upre):
    grad_gslice = contract(token_rows, grad_gpre, 0, 0)
    grad_uslice = contract(token_rows, grad_upre, 0, 0)
    grad_dslice = contract(hidden, cotan_rows, 0, 0)
    return (grad_gslice, grad_uslice, grad_dslice)


def pack_slots(selected, slot_of_row, n_slots):
    total_rows = selected.shape[0]
    target = jnp.where(selected == 1, slot_of_row, n_slots)
    picked = (
        jnp.zeros((n_slots + 1,), jnp.int32)
        .at[target]
        .set(jnp.arange(total_rows, dtype=jnp.int32))[:n_slots]
    )
    filled = jnp.zeros((n_slots + 1,), jnp.float32).at[target].set(1.0)[:n_slots]
    return (picked, filled)


def unpack_terms(terms, selected, slot_of_row):
    index_rows = jnp.clip(slot_of_row, 0, terms.shape[0] - 1)
    return terms[index_rows] * selected.astype(jnp.float32)[:, None]


def on_device(tokens, cotangent, routes, gate_weights, w_gate, w_up, w_down):
    n_experts = lax.axis_size("ep") * w_gate.shape[0]
    expert_ids = jnp.arange(n_experts, dtype=jnp.int32)
    chosen = (routes[:, :, None] == expert_ids[None, None, :]).astype(jnp.float32)
    gate_table = jnp.sum(gate_weights.astype(jnp.float32)[:, :, None] * chosen, axis=1).astype(
        jnp.bfloat16
    )
    group_rows = side_by_side((tokens, cotangent, gate_table), "ep", 0, 1)
    token_rows, cotan_rows, gate_rows = side_by_side(
        (group_rows[0], group_rows[1], group_rows[2]), "tp", 0, 1
    )
    group_index = lax.axis_index("ep")
    gate_float = gate_rows.astype(jnp.float32)
    own_column = (expert_ids == group_index).astype(jnp.float32)
    gate_column = jnp.sum(gate_float * own_column[None, :], axis=1)
    total_rows = gate_column.shape[0]
    most_rows = 7 * total_rows // 8
    gate_slice = w_gate[0]
    up_slice = w_up[0]
    down_slice = w_down[0]
    live_rows = (gate_column != 0.0).astype(jnp.int32)
    row_rank = jnp.cumsum(live_rows) - 1
    picked, filled = pack_slots(live_rows, row_rank, most_rows)
    slot_tokens = token_rows[picked]
    slot_cotan = cotan_rows[picked]
    output, grad_rows, hidden, grad_gpre, grad_upre = expert_pass(
        slot_tokens, slot_cotan, gate_column[picked] * filled, gate_slice, up_slice, down_slice
    )
    grad_gsum, grad_usum, grad_dsum = weight_terms(
        slot_tokens, slot_cotan, hidden, grad_gpre, grad_upre
    )
    out_terms = unpack_terms(output, live_rows, row_rank)
    grad_terms = unpack_terms(grad_rows, live_rows, row_rank)
    out_part, grad_part = one_scatter((out_terms, grad_terms), "tp", (0, 0))
    layer_out, grad_tokens = side_by_side_2((out_part, grad_part), "ep", 0, 1)
    return (
        layer_out.astype(jnp.bfloat16),
        grad_tokens.astype(jnp.bfloat16),
        grad_gsum.astype(jnp.bfloat16)[None],
        grad_usum.astype(jnp.bfloat16)[None],
        grad_dsum.astype(jnp.bfloat16)[None],
    )


def solution(mesh):
    placed = (
        P(("ep", "tp"), None),
        P(("ep", "tp"), None),
        P(("ep", "tp"), None),
        P(("ep", "tp"), None),
        P("ep", None, "tp"),
        P("ep", None, "tp"),
        P("ep", "tp", None),
    )
    return jax.shard_map(
        on_device,
        mesh=mesh,
        in_specs=placed,
        out_specs=(
            P(("ep", "tp"), None),
            P(("ep", "tp"), None),
            P("ep", None, "tp"),
            P("ep", None, "tp"),
            P("ep", "tp", None),
        ),
        check_vma=False,
    )
```

profile of v0, /device:TPU:1, one launch (start us, length us, event | category | flops | bytes accessed | tf_op | source)
XLA Modules:
  0.0 727.5 jit_solution(16204513422785563659)
XLA Ops:
  9.4 9.9 %all-gather = bf16[4,1,6148]{2,1,0:T(2,128)(2,1)S(1)} all-gather(bf16[1,1,6148]{2,1,0:T(2,128)(2,1)S(1)} %maximum_bitcast_fusion), channel_id=1, replica_groups=mesh['ep'=4,'tp'=64] {'ep'}, dimensions={0}, use_global_device_ids=true | all-gather | bytes 61480 | tf_op jit(solution)/shard_map/all_gather | solution.py:9
  20.1 260.1 %all-gather.4.cloned.1.call-done = bf16[64,4,6148]{2,1,0:T(4,128)(2,1)} async-done(((bf16[1,4,6148]{2,1,0:T(4,128)(2,1)}), bf16[64,4,6148]{2,1,0:T(4,128)(2,1)}) %all-gather.4.cloned.1.call-update) | async-done | bytes 3147792 | tf_op jit(solution)/shard_map/all_gather | solution.py:9
  280.2 5.8 reshape.291
  286.0 3.2 fusion.22
  290.9 1.4 scatter_custom_fusion
  292.3 1.9 gather_fusion.1
  294.2 5.5 gather_fusion
  299.8 2.6 gather_fusion.3
  304.5 1.8 fusion.11
  306.4 2.1 convolution_multiply_fusion
  310.8 3.4 gather_fusion.4
  314.2 4.8 gather.25
  319.0 1.7 fusion.4
  320.6 3.4 gather_fusion.2
  324.0 4.9 gather.22
  329.4 1.8 copy.13
  332.8 3.1 pad_maximum_fusion
  335.9 6.2 reshape.222
  343.5 2.4 fusion
  345.9 2.3 fusion.1
  348.2 312.5 %reduce-scatter.2.cloned.1.call-done = f32[192,128]{1,0:T(8,128)} async-done(((f32[12288,128]{1,0:T(8,128)}), f32[192,128]{1,0:T(8,128)}) %reduce-scatter.2.cloned.1.call-update) | async-done | bytes 98320 | tf_op jit(solution)/shard_map/reduce_scatter | solution.py:28
  662.3 52.7 %all-to-all-start = ((f32[4,1,6144]{2,1,0:T(1,128)}), f32[4,1,6144]{2,1,0:T(1,128)S(1)}, u32[]{:S(2)}, u32[]{:S(2)}) async-start(f32[4,1,6144]{2,1,0:T(1,128)} %reshape.225), calls=%async_computation.1 | async-start | bytes 196608 | tf_op jit(solution)/shard_map/all_to_all | solution.py:38
  715.0 2.1 fusion.2
  717.2 2.7 all-to-all-done
  (58 shorter events, 14.8 us)
Async XLA Ops:
  7.2 301.3 %copy-start = (bf16[1,3072,128]{2,1,0:T(8,128)(2,1)S(1)}, bf16[1,3072,128]{2,1,0:T(8,128)(2,1)}, u32[]{:S(2)}) copy-start(bf16[1,3072,128]{2,1,0:T(8,128)(2,1)} %param.12) | copy-start | bytes 2359300
  7.2 273.0 %all-gather.4.cloned.1.call-start = ((), (), s32[]{:S(2)}) async-start(), calls=%async_computation.3 | async-start | bytes 3261440 | tf_op jit(solution)/shard_map/all_gather | solution.py:9
  20.0 640.7 %reduce-scatter.2.cloned.1.call-start = ((), (), s32[]{:S(2)}) async-start(), calls=%async_computation.2 | async-start | bytes 6389760 | tf_op jit(solution)/shard_map/reduce_scatter | solution.py:28
  299.8 4.7 copy-start.6
  302.4 6.1 copy-start.1
  309.6 0.6 copy-start.8
  309.6 0.6 copy-start.7
  324.0 4.9 copy-start.9
  329.3 1.9 copy-start.3
  329.3 2.8 copy-start.4
  342.1 1.3 copy-start.2
  343.5 371.6 %copy-start.5 = (bf16[224,3072]{1,0:T(8,128)(2,1)S(1)}, bf16[224,3072]{1,0:T(8,128)(2,1)}, u32[]{:S(2)}) copy-start(bf16[224,3072]{1,0:T(8,128)(2,1)} %gather_fusion.3) | copy-start | bytes 4128772
  662.3 57.5 %all-to-all-start = ((f32[4,1,6144]{2,1,0:T(1,128)}), f32[4,1,6144]{2,1,0:T(1,128)S(1)}, u32[]{:S(2)}, u32[]{:S(2)}) async-start(f32[4,1,6144]{2,1,0:T(1,128)} %reshape.225), calls=%async_computation.1 | async-start | bytes 196608 | tf_op jit(solution)/shard_map/all_to_all | solution.py:38
Sparse Core Ops, SparseCore 0:
  20.2 260.0 all-gather.3
  342.3 318.4 reduce-scatter.1
where the time goes:
time: 728 us; the launch traced here: 727 us
  waiting for transfers between devices  575 us (79%)
  local copies, waits for them, and re-layouts  53 us (7%)
  starting transfers between devices  52.8 us (7%)
  matrix products  14.7 us (2%)
  between operations  14.3 us (2%)
  blocking collectives  9.92 us (1%)
  other arithmetic  7.5 us (1%)
    reduce_scatter x1, waiting for transfers between devices, one_scatter(): lax.psum_scatter(lines, axis, tiled=True).reshape(-1)  312 us
    all_gather x1, waiting for transfers between devices, side_by_side(): whole, at, outs = (lax.all_gather(both, axis, axis=dim, tiled=True), 0, [])  260 us
    all_to_all x1, starting transfers between devices, sent_and_summed(): tiles = lax.all_to_all(in_blocks(value, dim, size), axis, 0, 0, tiled=True)  52.7 us
    gather x4, local copies, waits for them, and re-layouts, unpack_terms(): return terms[index_rows] * selected.astype(jnp.float32)[:, None]  16.4 us
  transfers between devices with their start and end apart: 3, of which 3 were waited for; matrix products, arithmetic and copies ran while one was open for 1% of the time, Pallas kernels for 0%

commit v1 on v0

v1 whole, which is shorter than its diff:
```python
import jax
import jax.numpy as jnp
from jax import lax
from jax.sharding import PartitionSpec as P

NX_HI, NCORE, NY, NX_LO, NZ = 2, 2, 4, 2, 8
NX = NX_HI * NX_LO
D = 3072
F32, BF16 = jnp.float32, jnp.bfloat16


def flat(x, core, y, z):
    return ((x // 2) * NCORE + core) * (NY * NX_LO * NZ) + (y * NX_LO + x % 2) * NZ + z


def pairs(axis, d):
    out = []
    for x in range(NX):
        for core in range(NCORE):
            for y in range(NY):
                for z in range(NZ):
                    to = dict(x=x, core=core, y=y, z=z)
                    size = dict(x=NX, core=NCORE, y=NY, z=NZ)[axis]
                    to[axis] = (to[axis] + d) % size
                    out.append((flat(x, core, y, z), flat(**to)))
    return out


def give(value, axis, d):
    return lax.ppermute(value, ("ep", "tp"), pairs(axis, d))


def fetch(value, axis, d):
    return lax.ppermute(value, ("ep", "tp"), pairs(axis, -d))


def contract(left, right, left_dim, right_dim):
    return lax.dot_general(
        left, right, (((left_dim,), (right_dim,)), ((), ())), preferred_element_type=F32
    )


def gathered(row_a, row_b):
    wide = row_a.shape[1]
    both = jnp.concatenate([row_a, row_b], axis=1)
    with jax.named_scope("gather_z"):
        eight = jnp.concatenate([both] + [fetch(both, "z", d) for d in range(1, NZ)], axis=0)
    a, b = eight[:, :wide], eight[:, wide:]
    with jax.named_scope("gather_first"):
        a = jnp.concatenate([a] + [fetch(a, "x", d) for d in range(1, NX)], axis=0)
        b = jnp.concatenate([b] + [fetch(b, "y", d) for d in range(1, NY)], axis=0)
    with jax.named_scope("gather_second"):
        a = jnp.concatenate([a] + [fetch(a, "y", d) for d in range(1, NY)], axis=0)
        parts = [b] + [fetch(b, "x", d) for d in range(1, NX)]
        b = jnp.stack([p.reshape(NY, NZ, -1) for p in parts], axis=1).reshape(NX * NY * NZ, -1)
    with jax.named_scope("gather_core"):
        return fetch(a, "core", 1), a, fetch(b, "core", 1), b


def reduced(out_far, out_near, grad_far, grad_near):
    with jax.named_scope("reduce_core"):
        a = out_near + give(out_far.astype(BF16), "core", 1).astype(F32)
        b = grad_near + give(grad_far.astype(BF16), "core", 1).astype(F32)
    with jax.named_scope("reduce_first"):
        a = a.reshape(NY, NX * NZ, D)
        b = b.reshape(NY, NX, NZ, D)
        got_a = [give(a[d].astype(BF16), "y", d) for d in range(1, NY)]
        got_b = [give(b[:, d].astype(BF16).reshape(NY * NZ, D), "x", d) for d in range(1, NX)]
        a = a[0] + sum(g.astype(F32) for g in got_a)
        b = b[:, 0].reshape(NY * NZ, D) + sum(g.astype(F32) for g in got_b)
    with jax.named_scope("reduce_second"):
        a = a.reshape(NX, NZ, D)
        b = b.reshape(NY, NZ, D)
        got_a = [give(a[d].astype(BF16), "x", d) for d in range(1, NX)]
        got_b = [give(b[d].astype(BF16), "y", d) for d in range(1, NY)]
        a = a[0] + sum(g.astype(F32) for g in got_a)
        b = b[0] + sum(g.astype(F32) for g in got_b)
    with jax.named_scope("reduce_z"):
        both = jnp.concatenate([a, b], axis=1)
        sent = both.astype(BF16)
        got = [give(sent[d : d + 1], "z", d) for d in range(1, NZ)]
        total = both[:1] + sum(g.astype(F32) for g in got)
    return total[:, :D].astype(BF16), total[:, D:].astype(BF16)


def on_device(tokens, cotangent, routes, gate_weights, w_gate, w_up, w_down):
    lane = lax.broadcasted_iota(jnp.int32, (1, 128), 1)
    weights = gate_weights.astype(F32)
    gates = jnp.where(routes[:, :1] == lane, weights[:, :1], 0.0) + jnp.where(
        routes[:, 1:] == lane, weights[:, 1:], 0.0
    )
    row_a = jnp.concatenate([tokens, gates.astype(BF16)], axis=1)
    a_far, a_near, b_far, b_near = gathered(row_a, cotangent)
    a = jnp.concatenate([a_far, a_near], axis=0)
    cot = jnp.concatenate([b_far, b_near], axis=0)
    x, gate_rows = a[:, :D], a[:, D:].astype(F32)
    own = lax.broadcasted_iota(jnp.int32, (1, 128), 1) == lax.axis_index("ep")
    column = jnp.sum(jnp.where(own, gate_rows, 0.0), axis=1, keepdims=True)
    gate_slice, up_slice, down_slice = w_gate[0], w_up[0], w_down[0]
    with jax.named_scope("experts"):
        gate_pre = contract(x, gate_slice, 1, 0)
        up_pre = contract(x, up_slice, 1, 0)
        sigmoid = jax.nn.sigmoid(gate_pre)
        silu = gate_pre * sigmoid
        hidden = (silu * up_pre * column).astype(BF16)
        output = contract(hidden, down_slice, 1, 0)
        grad_act = contract(cot, down_slice, 1, 1) * column
        grad_gpre = (grad_act * up_pre * (sigmoid * (1.0 + gate_pre * (1.0 - sigmoid)))).astype(BF16)
        grad_upre = (grad_act * silu).astype(BF16)
        grad_rows = contract(grad_gpre, gate_slice, 1, 1) + contract(grad_upre, up_slice, 1, 1)
        grad_g = contract(x, grad_gpre, 0, 0).astype(BF16)[None]
        grad_u = contract(x, grad_upre, 0, 0).astype(BF16)[None]
        grad_d = contract(hidden, cot, 0, 0).astype(BF16)[None]
    half = output.shape[0] // 2
    layer_out, grad_tokens = reduced(output[:half], output[half:], grad_rows[:half], grad_rows[half:])
    return layer_out, grad_tokens, grad_g, grad_u, grad_d


def solution(mesh):
    rows, columns, units = P(("ep", "tp"), None), P("ep", None, "tp"), P("ep", "tp", None)
    return jax.shard_map(
        on_device,
        mesh=mesh,
        in_specs=(rows, rows, rows, rows, columns, columns, units),
        out_specs=(rows, rows, columns, columns, units),
        check_vma=False,
    )
```

time: 728 us -> 126 us (0.17)
  the two profiles are of different devices: /device:TPU:1 before, /device:TPU:4 now
where the time goes in v1:
time: 126 us
  starting transfers between devices  69.4 us (55%)
  waiting for transfers between devices  34.2 us (27%)
  local copies, waits for them, and re-layouts  9.5 us (8%)
  matrix products  7.74 us (6%)
  other arithmetic  4.33 us (3%)
    ppermute x21, starting transfers between devices, fetch(): return lax.ppermute(value, ('ep', 'tp'), pairs(axis, -d))  36.8 us
    ppermute x21, starting transfers between devices, give(): return lax.ppermute(value, ('ep', 'tp'), pairs(axis, d))  32.6 us
    ppermute x21, waiting for transfers between devices, fetch(): return lax.ppermute(value, ('ep', 'tp'), pairs(axis, -d))  21.6 us
    ppermute x21, waiting for transfers between devices, give(): return lax.ppermute(value, ('ep', 'tp'), pairs(axis, d))  12.6 us
    dot_general x9, matrix products, contract(): lax.dot_general(left, right, (((left_dim,), (right_dim,)), ((), ())), pre...  7.74 us
    unnamed x18, local copies, waits for them, and re-layouts  4.12 us
    convert_element_type x1, other arithmetic, on_device(): row_a = jnp.concatenate([tokens, gates.astype(BF16)], axis=1)  2.59 us
  transfers between devices with their start and end apart: 42, of which 13 were waited for; matrix products, arithmetic and copies ran while one was open for 9% of the time, Pallas kernels for 0%

profile of v1, /device:TPU:4, one launch (start us, length us, event | category | flops | bytes accessed | tf_op | source)
XLA Modules:
  0.0 126.1 jit_solution(1567637688957805658)
XLA Ops:
  3.3 2.6 %fusion.24 = bf16[1,128]{1,0:T(2,128)(2,1)S(1)} fusion(f32[]{:T(128)} %bitcast.3, s32[]{:T(128)} %bitcast.2, f32[]{:T(128)} %bitcast.1, s32[]{:T(128)} %bitcast), kind=kLoop, calls=%fused_computation.71 | loop fusion | flops 768 | bytes 272 | tf_op jit(solution)/shard_map/convert_element_type | solution.py:92
  6.6 2.0 %collective-permute-start.6 = (bf16[1,6272]{1,0:T(2,128)(2,1)S(1)}, bf16[1,6272]{1,0:T(2,128)(2,1)S(1)}, u32[]{:S(2)}, u32[]{:S(2)}) collective-permute-start(bf16[1,6272]{1,0:T(2,128)(2,1)S(1)} %pad_maximum_fusion.7), channel_id=1, source_target_pairs={{0,1},{1,2},{2,3},{3,4},{4,5},{5,6},{6,7},{7,0},{16,17},{17,18},{1... | collective-permute-start | bytes 37640 | tf_op jit(solution)/shard_map/gather_z/ppermute | solution.py:34
  8.6 3.3 %collective-permute-start.5 = (bf16[1,6272]{1,0:T(2,128)(2,1)S(1)}, bf16[1,6272]{1,0:T(2,128)(2,1)S(1)}, u32[]{:S(2)}, u32[]{:S(2)}) collective-permute-start(bf16[1,6272]{1,0:T(2,128)(2,1)S(1)} %pad_maximum_fusion.7), channel_id=1, source_target_pairs={{0,2},{1,3},{2,4},{3,5},{4,6},{5,7},{6,0},{7,1},{16,18},{17,19},{1... | collective-permute-start | bytes 37640 | tf_op jit(solution)/shard_map/gather_z/ppermute | solution.py:34
  11.9 4.0 %collective-permute-start.4 = (bf16[1,6272]{1,0:T(2,128)(2,1)S(1)}, bf16[1,6272]{1,0:T(2,128)(2,1)S(1)}, u32[]{:S(2)}, u32[]{:S(2)}) collective-permute-start(bf16[1,6272]{1,0:T(2,128)(2,1)S(1)} %pad_maximum_fusion.7), channel_id=1, source_target_pairs={{0,3},{1,4},{2,5},{3,6},{4,7},{5,0},{6,1},{7,2},{16,19},{17,20},{1... | collective-permute-start | bytes 37640 | tf_op jit(solution)/shard_map/gather_z/ppermute | solution.py:34
  16.5 4.9 %collective-permute-start.2 = (bf16[1,6272]{1,0:T(2,128)(2,1)S(1)}, bf16[1,6272]{1,0:T(2,128)(2,1)S(1)}, u32[]{:S(2)}, u32[]{:S(2)}) collective-permute-start(bf16[1,6272]{1,0:T(2,128)(2,1)S(1)} %pad_maximum_fusion.7), channel_id=1, source_target_pairs={{0,5},{1,6},{2,7},{3,0},{4,1},{5,2},{6,3},{7,4},{16,21},{17,22},{1... | collective-permute-start | bytes 37640 | tf_op jit(solution)/shard_map/gather_z/ppermute | solution.py:34
  21.4 2.7 %collective-permute-start.1 = (bf16[1,6272]{1,0:T(2,128)(2,1)S(1)}, bf16[1,6272]{1,0:T(2,128)(2,1)S(1)}, u32[]{:S(2)}, u32[]{:S(2)}) collective-permute-start(bf16[1,6272]{1,0:T(2,128)(2,1)S(1)} %pad_maximum_fusion.7), channel_id=1, source_target_pairs={{0,6},{1,7},{2,0},{3,1},{4,2},{5,3},{6,4},{7,5},{16,22},{17,23},{1... | collective-permute-start | bytes 37640 | tf_op jit(solution)/shard_map/gather_z/ppermute | solution.py:34
  33.6 2.9 %collective-permute-start.22 = (bf16[8,3072]{1,0:T(8,128)(2,1)S(1)}, bf16[8,3072]{1,0:T(8,128)(2,1)S(1)}, u32[]{:S(2)}, u32[]{:S(2)}) collective-permute-start(bf16[8,3072]{1,0:T(8,128)(2,1)S(1)} %slice.193), channel_id=1, source_target_pairs={{0,32},{1,33},{2,34},{3,35},{4,36},{5,37},{6,38},{7,39},{16,48},{1... | collective-permute-start | bytes 147464 | tf_op jit(solution)/shard_map/gather_first/ppermute | solution.py:34
  38.6 2.6 %collective-permute-start.10 = (bf16[32,3200]{1,0:T(8,128)(2,1)S(1)}, bf16[32,3200]{1,0:T(8,128)(2,1)S(1)}, u32[]{:S(2)}, u32[]{:S(2)}) collective-permute-start(bf16[32,3200]{1,0:T(8,128)(2,1)S(1)} %pad_maximum_fusion.5), channel_id=1, source_target_pairs={{0,48},{1,49},{2,50},{3,51},{4,52},{5,53},{6,54},{7,55},{16,0},{17... | collective-permute-start | bytes 614408 | tf_op jit(solution)/shard_map/gather_second/ppermute | solution.py:34
  43.1 3.6 %collective-permute-done.10 = bf16[32,3200]{1,0:T(8,128)(2,1)S(1)} collective-permute-done((bf16[32,3200]{1,0:T(8,128)(2,1)S(1)}, bf16[32,3200]{1,0:T(8,128)(2,1)S(1)}, u32[]{:S(2)}, u32[]{:S(2)}) %collective-permute-start.10) | collective-permute-done | bytes 204832 | tf_op jit(solution)/shard_map/gather_second/ppermute | solution.py:34
  48.2 5.8 %collective-permute-done.11 = bf16[32,3200]{1,0:T(8,128)(2,1)S(1)} collective-permute-done((bf16[32,3200]{1,0:T(8,128)(2,1)S(1)}, bf16[32,3200]{1,0:T(8,128)(2,1)S(1)}, u32[]{:S(2)}, u32[]{:S(2)}) %collective-permute-start.11) | collective-permute-done | bytes 204832 | tf_op jit(solution)/shard_map/gather_second/ppermute | solution.py:34
  55.4 3.1 %collective-permute-start.25 = (bf16[32,3072]{1,0:T(8,128)(2,1)S(1)}, bf16[32,3072]{1,0:T(8,128)(2,1)S(1)}, u32[]{:S(2)}, u32[]{:S(2)}) collective-permute-start(bf16[32,3072]{1,0:T(8,128)(2,1)S(1)} %get-tuple-element.27), channel_id=1, source_target_pairs={{0,128},{1,129},{2,130},{3,131},{4,132},{5,133},{6,134},{7,135},{1... | collective-permute-start | bytes 589832 | tf_op jit(solution)/shard_map/gather_second/ppermute | solution.py:34
  58.5 2.0 %collective-permute-start.26 = (bf16[32,3072]{1,0:T(8,128)(2,1)S(1)}, bf16[32,3072]{1,0:T(8,128)(2,1)S(1)}, u32[]{:S(2)}, u32[]{:S(2)}) collective-permute-start(bf16[32,3072]{1,0:T(8,128)(2,1)S(1)} %get-tuple-element.27), channel_id=1, source_target_pairs={{0,8},{1,9},{2,10},{3,11},{4,12},{5,13},{6,14},{7,15},{16,24},{17,... | collective-permute-start | bytes 589832 | tf_op jit(solution)/shard_map/gather_second/ppermute | solution.py:34
  60.5 4.2 %collective-permute-done.25 = bf16[32,3072]{1,0:T(8,128)(2,1)S(1)} collective-permute-done((bf16[32,3072]{1,0:T(8,128)(2,1)S(1)}, bf16[32,3072]{1,0:T(8,128)(2,1)S(1)}, u32[]{:S(2)}, u32[]{:S(2)}) %collective-permute-start.25) | collective-permute-done | bytes 196640 | tf_op jit(solution)/shard_map/gather_second/ppermute | solution.py:34
  64.7 4.5 %collective-permute-done.24 = bf16[32,3072]{1,0:T(8,128)(2,1)S(1)} collective-permute-done((bf16[32,3072]{1,0:T(8,128)(2,1)S(1)}, bf16[32,3072]{1,0:T(8,128)(2,1)S(1)}, u32[]{:S(2)}, u32[]{:S(2)}) %collective-permute-start.24) | collective-permute-done | bytes 196640 | tf_op jit(solution)/shard_map/gather_second/ppermute | solution.py:34
  78.4 2.8 %collective-permute-start.17 = (bf16[32,3072]{1,0:T(8,128)(2,1)S(1)}, bf16[32,3072]{1,0:T(8,128)(2,1)S(1)}, u32[]{:S(2)}, u32[]{:S(2)}) collective-permute-start(bf16[32,3072]{1,0:T(8,128)(2,1)S(1)} %get-tuple-element.12), channel_id=1, source_target_pairs={{0,48},{1,49},{2,50},{3,51},{4,52},{5,53},{6,54},{7,55},{16,0},{17... | collective-permute-start | bytes 589832 | tf_op jit(solution)/shard_map/reduce_first/ppermute | solution.py:30
  86.3 2.3 %collective-permute-start.30 = (bf16[32,3072]{1,0:T(8,128)(2,1)S(1)}, bf16[32,3072]{1,0:T(8,128)(2,1)S(1)}, u32[]{:S(2)}, u32[]{:S(2)}) collective-permute-start(bf16[32,3072]{1,0:T(8,128)(2,1)S(1)} %get-tuple-element.16), channel_id=1, source_target_pairs={{0,128},{1,129},{2,130},{3,131},{4,132},{5,133},{6,134},{7,135},{1... | collective-permute-start | bytes 589832 | tf_op jit(solution)/shard_map/reduce_first/ppermute | solution.py:30
  89.9 1.8 %collective-permute-done.16 = bf16[32,3072]{1,0:T(8,128)(2,1)S(1)} collective-permute-done((bf16[32,3072]{1,0:T(8,128)(2,1)S(1)}, bf16[32,3072]{1,0:T(8,128)(2,1)S(1)}, u32[]{:S(2)}, u32[]{:S(2)}) %collective-permute-start.16) | collective-permute-done | bytes 196640 | tf_op jit(solution)/shard_map/reduce_first/ppermute | solution.py:30
  93.9 3.5 %collective-permute-start.19 = (bf16[8,3072]{1,0:T(8,128)(2,1)S(1)}, bf16[8,3072]{1,0:T(8,128)(2,1)S(1)}, u32[]{:S(2)}, u32[]{:S(2)}) collective-permute-start(bf16[8,3072]{1,0:T(8,128)(2,1)S(1)} %get-tuple-element.22), channel_id=1, source_target_pairs={{0,128},{1,129},{2,130},{3,131},{4,132},{5,133},{6,134},{7,135},{1... | collective-permute-start | bytes 147464 | tf_op jit(solution)/shard_map/reduce_second/ppermute | solution.py:30
  98.7 2.1 %collective-permute-start.34 = (bf16[8,3072]{1,0:T(8,128)(2,1)S(1)}, bf16[8,3072]{1,0:T(8,128)(2,1)S(1)}, u32[]{:S(2)}, u32[]{:S(2)}) collective-permute-start(bf16[8,3072]{1,0:T(8,128)(2,1)S(1)} %get-tuple-element.24), channel_id=1, source_target_pairs={{0,48},{1,49},{2,50},{3,51},{4,52},{5,53},{6,54},{7,55},{16,0},{17... | collective-permute-start | bytes 147464 | tf_op jit(solution)/shard_map/reduce_second/ppermute | solution.py:30
  102.9 3.5 %collective-permute-done.33 = bf16[8,3072]{1,0:T(8,128)(2,1)S(1)} collective-permute-done((bf16[8,3072]{1,0:T(8,128)(2,1)S(1)}, bf16[8,3072]{1,0:T(8,128)(2,1)S(1)}, u32[]{:S(2)}, u32[]{:S(2)}) %collective-permute-start.33) | collective-permute-done | bytes 49184 | tf_op jit(solution)/shard_map/reduce_second/ppermute | solution.py:30
  106.7 3.2 %collective-permute-start.41 = (bf16[1,6144]{1,0:T(2,128)(2,1)S(1)}, bf16[1,6144]{1,0:T(2,128)(2,1)S(1)}, u32[]{:S(2)}, u32[]{:S(2)}) collective-permute-start(bf16[1,6144]{1,0:T(2,128)(2,1)S(1)} %get-tuple-element.31), channel_id=1, source_target_pairs={{0,7},{1,0},{2,1},{3,2},{4,3},{5,4},{6,5},{7,6},{16,23},{17,16},{1... | collective-permute-start | bytes 36872 | tf_op jit(solution)/shard_map/reduce_z/ppermute | solution.py:30
  114.1 4.3 %collective-permute-start.38 = (bf16[1,6144]{1,0:T(2,128)(2,1)S(1)}, bf16[1,6144]{1,0:T(2,128)(2,1)S(1)}, u32[]{:S(2)}, u32[]{:S(2)}) collective-permute-start(bf16[1,6144]{1,0:T(2,128)(2,1)S(1)} %get-tuple-element.34), channel_id=1, source_target_pairs={{0,4},{1,5},{2,6},{3,7},{4,0},{5,1},{6,2},{7,3},{16,20},{17,21},{1... | collective-permute-start | bytes 36872 | tf_op jit(solution)/shard_map/reduce_z/ppermute | solution.py:30
  118.4 2.2 %collective-permute-start.36 = (bf16[1,6144]{1,0:T(2,128)(2,1)S(1)}, bf16[1,6144]{1,0:T(2,128)(2,1)S(1)}, u32[]{:S(2)}, u32[]{:S(2)}) collective-permute-start(bf16[1,6144]{1,0:T(2,128)(2,1)S(1)} %get-tuple-element.36), channel_id=1, source_target_pairs={{0,2},{1,3},{2,4},{3,5},{4,6},{5,7},{6,0},{7,1},{16,18},{17,19},{1... | collective-permute-start | bytes 36872 | tf_op jit(solution)/shard_map/reduce_z/ppermute | solution.py:30
  121.9 3.5 %collective-permute-done.37 = bf16[1,6144]{1,0:T(2,128)(2,1)S(1)} collective-permute-done((bf16[1,6144]{1,0:T(2,128)(2,1)S(1)}, bf16[1,6144]{1,0:T(2,128)(2,1)S(1)}, u32[]{:S(2)}, u32[]{:S(2)}) %collective-permute-start.37) | collective-permute-done | bytes 12320 | tf_op jit(solution)/shard_map/reduce_z/ppermute | solution.py:30
  (117 shorter events, 47.8 us)
Async XLA Ops:
  6.6 14.8 %collective-permute-start.6 = (bf16[1,6272]{1,0:T(2,128)(2,1)S(1)}, bf16[1,6272]{1,0:T(2,128)(2,1)S(1)}, u32[]{:S(2)}, u32[]{:S(2)}) collective-permute-start(bf16[1,6272]{1,0:T(2,128)(2,1)S(1)} %pad_maximum_fusion.7), channel_id=1, source_target_pairs={{0,1},{1,2},{2,3},{3,4},{4,5},{5,6},{6,7},{7,0},{16,17},{17,18},{1... | collective-permute-start | bytes 37640 | tf_op jit(solution)/shard_map/gather_z/ppermute | solution.py:34
  8.6 15.5 %collective-permute-start.5 = (bf16[1,6272]{1,0:T(2,128)(2,1)S(1)}, bf16[1,6272]{1,0:T(2,128)(2,1)S(1)}, u32[]{:S(2)}, u32[]{:S(2)}) collective-permute-start(bf16[1,6272]{1,0:T(2,128)(2,1)S(1)} %pad_maximum_fusion.7), channel_id=1, source_target_pairs={{0,2},{1,3},{2,4},{3,5},{4,6},{5,7},{6,0},{7,1},{16,18},{17,19},{1... | collective-permute-start | bytes 37640 | tf_op jit(solution)/shard_map/gather_z/ppermute | solution.py:34
  11.9 13.2 %collective-permute-start.4 = (bf16[1,6272]{1,0:T(2,128)(2,1)S(1)}, bf16[1,6272]{1,0:T(2,128)(2,1)S(1)}, u32[]{:S(2)}, u32[]{:S(2)}) collective-permute-start(bf16[1,6272]{1,0:T(2,128)(2,1)S(1)} %pad_maximum_fusion.7), channel_id=1, source_target_pairs={{0,3},{1,4},{2,5},{3,6},{4,7},{5,0},{6,1},{7,2},{16,19},{17,20},{1... | collective-permute-start | bytes 37640 | tf_op jit(solution)/shard_map/gather_z/ppermute | solution.py:34
  15.9 9.2 %collective-permute-start.3 = (bf16[1,6272]{1,0:T(2,128)(2,1)S(1)}, bf16[1,6272]{1,0:T(2,128)(2,1)S(1)}, u32[]{:S(2)}, u32[]{:S(2)}) collective-permute-start(bf16[1,6272]{1,0:T(2,128)(2,1)S(1)} %pad_maximum_fusion.7), channel_id=1, source_target_pairs={{0,4},{1,5},{2,6},{3,7},{4,0},{5,1},{6,2},{7,3},{16,20},{17,21},{1... | collective-permute-start | bytes 37640 | tf_op jit(solution)/shard_map/gather_z/ppermute | solution.py:34
  32.0 23.3 %collective-permute-start.23 = (bf16[8,3072]{1,0:T(8,128)(2,1)S(1)}, bf16[8,3072]{1,0:T(8,128)(2,1)S(1)}, u32[]{:S(2)}, u32[]{:S(2)}) collective-permute-start(bf16[8,3072]{1,0:T(8,128)(2,1)S(1)} %slice.193), channel_id=1, source_target_pairs={{0,16},{1,17},{2,18},{3,19},{4,20},{5,21},{6,22},{7,23},{16,32},{1... | collective-permute-start | bytes 147464 | tf_op jit(solution)/shard_map/gather_first/ppermute | solution.py:34
  33.6 21.8 %collective-permute-start.22 = (bf16[8,3072]{1,0:T(8,128)(2,1)S(1)}, bf16[8,3072]{1,0:T(8,128)(2,1)S(1)}, u32[]{:S(2)}, u32[]{:S(2)}) collective-permute-start(bf16[8,3072]{1,0:T(8,128)(2,1)S(1)} %slice.193), channel_id=1, source_target_pairs={{0,32},{1,33},{2,34},{3,35},{4,36},{5,37},{6,38},{7,39},{16,48},{1... | collective-permute-start | bytes 147464 | tf_op jit(solution)/shard_map/gather_first/ppermute | solution.py:34
  36.5 18.9 %collective-permute-start.21 = (bf16[8,3072]{1,0:T(8,128)(2,1)S(1)}, bf16[8,3072]{1,0:T(8,128)(2,1)S(1)}, u32[]{:S(2)}, u32[]{:S(2)}) collective-permute-start(bf16[8,3072]{1,0:T(8,128)(2,1)S(1)} %slice.193), channel_id=1, source_target_pairs={{0,48},{1,49},{2,50},{3,51},{4,52},{5,53},{6,54},{7,55},{16,0},{17... | collective-permute-start | bytes 147464 | tf_op jit(solution)/shard_map/gather_first/ppermute | solution.py:34
  37.9 16.8 %collective-permute-start.12 = (bf16[32,3200]{1,0:T(8,128)(2,1)S(1)}, bf16[32,3200]{1,0:T(8,128)(2,1)S(1)}, u32[]{:S(2)}, u32[]{:S(2)}) collective-permute-start(bf16[32,3200]{1,0:T(8,128)(2,1)S(1)} %pad_maximum_fusion.5), channel_id=1, source_target_pairs={{0,16},{1,17},{2,18},{3,19},{4,20},{5,21},{6,22},{7,23},{16,32},{1... | collective-permute-start | bytes 614408 | tf_op jit(solution)/shard_map/gather_second/ppermute | solution.py:34
  55.3 14.1 %collective-permute-start.13 = (bf16[128,3200]{1,0:T(8,128)(2,1)}, bf16[128,3200]{1,0:T(8,128)(2,1)S(1)}, u32[]{:S(2)}, u32[]{:S(2)}) collective-permute-start(bf16[128,3200]{1,0:T(8,128)(2,1)} %constant_dynamic-update-slice_fusion), channel_id=1, source_target_pairs={{0,64},{1,65},{2,66},{3,67},{4,68},{5,69},{6,70},{7,71},{16,80},{1... | collective-permute-start | bytes 2457608 | tf_op jit(solution)/shard_map/gather_core/ppermute | solution.py:34
  55.4 9.3 %collective-permute-start.25 = (bf16[32,3072]{1,0:T(8,128)(2,1)S(1)}, bf16[32,3072]{1,0:T(8,128)(2,1)S(1)}, u32[]{:S(2)}, u32[]{:S(2)}) collective-permute-start(bf16[32,3072]{1,0:T(8,128)(2,1)S(1)} %get-tuple-element.27), channel_id=1, source_target_pairs={{0,128},{1,129},{2,130},{3,131},{4,132},{5,133},{6,134},{7,135},{1... | collective-permute-start | bytes 589832 | tf_op jit(solution)/shard_map/gather_second/ppermute | solution.py:34
  58.5 10.7 %collective-permute-start.24 = (bf16[32,3072]{1,0:T(8,128)(2,1)S(1)}, bf16[32,3072]{1,0:T(8,128)(2,1)S(1)}, u32[]{:S(2)}, u32[]{:S(2)}) collective-permute-start(bf16[32,3072]{1,0:T(8,128)(2,1)S(1)} %get-tuple-element.27), channel_id=1, source_target_pairs={{0,136},{1,137},{2,138},{3,139},{4,140},{5,141},{6,142},{7,143},{1... | collective-permute-start | bytes 589832 | tf_op jit(solution)/shard_map/gather_second/ppermute | solution.py:34
  58.5 10.7 %collective-permute-start.26 = (bf16[32,3072]{1,0:T(8,128)(2,1)S(1)}, bf16[32,3072]{1,0:T(8,128)(2,1)S(1)}, u32[]{:S(2)}, u32[]{:S(2)}) collective-permute-start(bf16[32,3072]{1,0:T(8,128)(2,1)S(1)} %get-tuple-element.27), channel_id=1, source_target_pairs={{0,8},{1,9},{2,10},{3,11},{4,12},{5,13},{6,14},{7,15},{16,24},{17,... | collective-permute-start | bytes 589832 | tf_op jit(solution)/shard_map/gather_second/ppermute | solution.py:34
  77.4 8.9 %collective-permute-start.15 = (bf16[32,3072]{1,0:T(8,128)(2,1)S(1)}, bf16[32,3072]{1,0:T(8,128)(2,1)S(1)}, u32[]{:S(2)}, u32[]{:S(2)}) collective-permute-start(bf16[32,3072]{1,0:T(8,128)(2,1)S(1)} %get-tuple-element.11), channel_id=1, source_target_pairs={{0,16},{1,17},{2,18},{3,19},{4,20},{5,21},{6,22},{7,23},{16,32},{1... | collective-permute-start | bytes 589832 | tf_op jit(solution)/shard_map/reduce_first/ppermute | solution.py:30
  78.4 11.4 %collective-permute-start.17 = (bf16[32,3072]{1,0:T(8,128)(2,1)S(1)}, bf16[32,3072]{1,0:T(8,128)(2,1)S(1)}, u32[]{:S(2)}, u32[]{:S(2)}) collective-permute-start(bf16[32,3072]{1,0:T(8,128)(2,1)S(1)} %get-tuple-element.12), channel_id=1, source_target_pairs={{0,48},{1,49},{2,50},{3,51},{4,52},{5,53},{6,54},{7,55},{16,0},{17... | collective-permute-start | bytes 589832 | tf_op jit(solution)/shard_map/reduce_first/ppermute | solution.py:30
  81.2 10.5 %collective-permute-start.16 = (bf16[32,3072]{1,0:T(8,128)(2,1)S(1)}, bf16[32,3072]{1,0:T(8,128)(2,1)S(1)}, u32[]{:S(2)}, u32[]{:S(2)}) collective-permute-start(bf16[32,3072]{1,0:T(8,128)(2,1)S(1)} %get-tuple-element.13), channel_id=1, source_target_pairs={{0,32},{1,33},{2,34},{3,35},{4,36},{5,37},{6,38},{7,39},{16,48},{1... | collective-permute-start | bytes 589832 | tf_op jit(solution)/shard_map/reduce_first/ppermute | solution.py:30
  82.8 11.1 %collective-permute-start.29 = (bf16[32,3072]{1,0:T(8,128)(2,1)S(1)}, bf16[32,3072]{1,0:T(8,128)(2,1)S(1)}, u32[]{:S(2)}, u32[]{:S(2)}) collective-permute-start(bf16[32,3072]{1,0:T(8,128)(2,1)S(1)} %get-tuple-element.14), channel_id=1, source_target_pairs={{0,8},{1,9},{2,10},{3,11},{4,12},{5,13},{6,14},{7,15},{16,24},{17,... | collective-permute-start | bytes 589832 | tf_op jit(solution)/shard_map/reduce_first/ppermute | solution.py:30
  83.6 13.8 %collective-permute-start.31 = (bf16[32,3072]{1,0:T(8,128)(2,1)S(1)}, bf16[32,3072]{1,0:T(8,128)(2,1)S(1)}, u32[]{:S(2)}, u32[]{:S(2)}) collective-permute-start(bf16[32,3072]{1,0:T(8,128)(2,1)S(1)} %get-tuple-element.15), channel_id=1, source_target_pairs={{0,136},{1,137},{2,138},{3,139},{4,140},{5,141},{6,142},{7,143},{1... | collective-permute-start | bytes 589832 | tf_op jit(solution)/shard_map/reduce_first/ppermute | solution.py:30
  86.3 11.1 %collective-permute-start.30 = (bf16[32,3072]{1,0:T(8,128)(2,1)S(1)}, bf16[32,3072]{1,0:T(8,128)(2,1)S(1)}, u32[]{:S(2)}, u32[]{:S(2)}) collective-permute-start(bf16[32,3072]{1,0:T(8,128)(2,1)S(1)} %get-tuple-element.16), channel_id=1, source_target_pairs={{0,128},{1,129},{2,130},{3,131},{4,132},{5,133},{6,134},{7,135},{1... | collective-permute-start | bytes 589832 | tf_op jit(solution)/shard_map/reduce_first/ppermute | solution.py:30
  91.8 9.0 %collective-permute-start.18 = (bf16[8,3072]{1,0:T(8,128)(2,1)S(1)}, bf16[8,3072]{1,0:T(8,128)(2,1)S(1)}, u32[]{:S(2)}, u32[]{:S(2)}) collective-permute-start(bf16[8,3072]{1,0:T(8,128)(2,1)S(1)} %get-tuple-element.20), channel_id=1, source_target_pairs={{0,8},{1,9},{2,10},{3,11},{4,12},{5,13},{6,14},{7,15},{16,24},{17,... | collective-permute-start | bytes 147464 | tf_op jit(solution)/shard_map/reduce_second/ppermute | solution.py:30
  92.6 9.2 %collective-permute-start.20 = (bf16[8,3072]{1,0:T(8,128)(2,1)S(1)}, bf16[8,3072]{1,0:T(8,128)(2,1)S(1)}, u32[]{:S(2)}, u32[]{:S(2)}) collective-permute-start(bf16[8,3072]{1,0:T(8,128)(2,1)S(1)} %get-tuple-element.21), channel_id=1, source_target_pairs={{0,136},{1,137},{2,138},{3,139},{4,140},{5,141},{6,142},{7,143},{1... | collective-permute-start | bytes 147464 | tf_op jit(solution)/shard_map/reduce_second/ppermute | solution.py:30
  106.6 11.8 %collective-permute-start.35 = (bf16[1,6144]{1,0:T(2,128)(2,1)S(1)}, bf16[1,6144]{1,0:T(2,128)(2,1)S(1)}, u32[]{:S(2)}, u32[]{:S(2)}) collective-permute-start(bf16[1,6144]{1,0:T(2,128)(2,1)S(1)} %get-tuple-element.30), channel_id=1, source_target_pairs={{0,1},{1,2},{2,3},{3,4},{4,5},{5,6},{6,7},{7,0},{16,17},{17,18},{1... | collective-permute-start | bytes 36872 | tf_op jit(solution)/shard_map/reduce_z/ppermute | solution.py:30
  106.7 11.7 %collective-permute-start.41 = (bf16[1,6144]{1,0:T(2,128)(2,1)S(1)}, bf16[1,6144]{1,0:T(2,128)(2,1)S(1)}, u32[]{:S(2)}, u32[]{:S(2)}) collective-permute-start(bf16[1,6144]{1,0:T(2,128)(2,1)S(1)} %get-tuple-element.31), channel_id=1, source_target_pairs={{0,7},{1,0},{2,1},{3,2},{4,3},{5,4},{6,5},{7,6},{16,23},{17,16},{1... | collective-permute-start | bytes 36872 | tf_op jit(solution)/shard_map/reduce_z/ppermute | solution.py:30
  111.5 10.4 %collective-permute-start.40 = (bf16[1,6144]{1,0:T(2,128)(2,1)S(1)}, bf16[1,6144]{1,0:T(2,128)(2,1)S(1)}, u32[]{:S(2)}, u32[]{:S(2)}) collective-permute-start(bf16[1,6144]{1,0:T(2,128)(2,1)S(1)} %get-tuple-element.32), channel_id=1, source_target_pairs={{0,6},{1,7},{2,0},{3,1},{4,2},{5,3},{6,4},{7,5},{16,22},{17,23},{1... | collective-permute-start | bytes 36872 | tf_op jit(solution)/shard_map/reduce_z/ppermute | solution.py:30
  112.4 9.5 %collective-permute-start.39 = (bf16[1,6144]{1,0:T(2,128)(2,1)S(1)}, bf16[1,6144]{1,0:T(2,128)(2,1)S(1)}, u32[]{:S(2)}, u32[]{:S(2)}) collective-permute-start(bf16[1,6144]{1,0:T(2,128)(2,1)S(1)} %get-tuple-element.33), channel_id=1, source_target_pairs={{0,5},{1,6},{2,7},{3,0},{4,1},{5,2},{6,3},{7,4},{16,21},{17,22},{1... | collective-permute-start | bytes 36872 | tf_op jit(solution)/shard_map/reduce_z/ppermute | solution.py:30
  (21 other events, 188.0 us)

commit v2 on v1

v2 whole, which is shorter than its diff:
```python
import jax
import jax.numpy as jnp
from jax import lax
from jax.experimental import pallas as pl
from jax.experimental.pallas import tpu as pltpu
from jax.sharding import Mesh, PartitionSpec as P

NX_HI, NCORE, NY, NX_LO, NZ = 2, 2, 4, 2, 8
NXY = NX_HI * NX_LO * NY
AXES = ("x_hi", "core", "y", "x_lo", "z")
EP, TP, XY = ("x_hi", "core"), ("y", "x_lo", "z"), ("x_hi", "x_lo", "y")
D, PAD = 3072, 128
F32, BF16 = jnp.float32, jnp.bfloat16


def swapped(value):
    return lax.ppermute(value, "core", [(0, 1), (1, 0)])


def exchanged(value, axis):
    return lax.all_to_all(value, axis, 0, 0, tiled=True)


def contract(left, right, left_dim, right_dim):
    return lax.dot_general(
        left, right, (((left_dim,), (right_dim,)), ((), ())), preferred_element_type=F32
    )


def row_kernel(tokens, cotangent, routes, weights, out):
    lane = lax.broadcasted_iota(jnp.int32, (1, PAD), 1)
    r, w = routes[...], weights[...].astype(F32)
    gates = jnp.where(r[:, :1] == lane, w[:, :1], 0.0) + jnp.where(r[:, 1:] == lane, w[:, 1:], 0.0)
    first = jnp.concatenate([tokens[...].astype(F32), gates], axis=1)
    second = jnp.concatenate([cotangent[...].astype(F32), jnp.zeros((1, PAD), F32)], axis=1)
    both = jnp.concatenate([first, second], axis=0).astype(BF16)
    for i in range(NZ):
        out[i] = both


def copies_of_row(tokens, cotangent, routes, gate_weights):
    return pl.pallas_call(
        row_kernel,
        out_shape=jax.ShapeDtypeStruct((NZ, 2, D + PAD), BF16),
        name="copies_of_row",
    )(tokens, cotangent, routes, gate_weights)


def summed(parts):
    return sum(parts[i].astype(F32) for i in range(parts.shape[0]))


def on_device(tokens, cotangent, routes, gate_weights, w_gate, w_up, w_down):
    gate_slice, up_slice, down_slice = w_gate[0], w_up[0], w_down[0]
    half = NXY * NZ
    with jax.named_scope("gather_z"):
        eight = exchanged(copies_of_row(tokens, cotangent, routes, gate_weights), "z")
        eight = jnp.concatenate([eight[:, 0], eight[:, 1, :D]], axis=1)
    with jax.named_scope("gather_xy"):
        near = exchanged(jnp.broadcast_to(eight[None], (NXY,) + eight.shape), XY).reshape(half, -1)
    with jax.named_scope("gather_core"):
        rows = jnp.concatenate([swapped(near), near], axis=0)
    x, gate_rows, cot = rows[:, :D], rows[:, D : D + PAD].astype(F32), rows[:, D + PAD :]
    own = lax.broadcasted_iota(jnp.int32, (1, PAD), 1) == lax.axis_index(EP)
    column = jnp.sum(jnp.where(own, gate_rows, 0.0), axis=1, keepdims=True)
    with jax.named_scope("experts"):
        gate_pre = contract(x, gate_slice, 1, 0)
        up_pre = contract(x, up_slice, 1, 0)
        sigmoid = jax.nn.sigmoid(gate_pre)
        silu = gate_pre * sigmoid
        hidden = (silu * up_pre * column).astype(BF16)
        output = contract(hidden, down_slice, 1, 0)
        grad_act = contract(cot, down_slice, 1, 1) * column
        grad_gpre = (grad_act * up_pre * (sigmoid * (1.0 + gate_pre * (1.0 - sigmoid)))).astype(BF16)
        grad_upre = (grad_act * silu).astype(BF16)
        grad_rows = contract(grad_gpre, gate_slice, 1, 1) + contract(grad_upre, up_slice, 1, 1)
    with jax.named_scope("reduce_core"):
        out = output[half:] + swapped(output[:half].astype(BF16)).astype(F32)
        grad = grad_rows[half:] + swapped(grad_rows[:half].astype(BF16)).astype(F32)
    with jax.named_scope("reduce_xy"):
        both = jnp.concatenate([out.astype(BF16), grad.astype(BF16)], axis=1)
        both = summed(exchanged(both.reshape(NXY, NZ, 2 * D), XY)).astype(BF16)
    with jax.named_scope("weights"):
        grad_g = contract(x, grad_gpre, 0, 0).astype(BF16)[None]
        grad_u = contract(x, grad_upre, 0, 0).astype(BF16)[None]
        grad_d = contract(hidden, cot, 0, 0).astype(BF16)[None]
    with jax.named_scope("reduce_z"):
        total = summed(exchanged(both.reshape(NZ, 2, D), "z")).astype(BF16)
    return total[:1], total[1:], grad_g, grad_u, grad_d


def solution(mesh):
    fine = Mesh(mesh.devices.reshape(NX_HI, NCORE, NY, NX_LO, NZ), AXES)
    rows, columns, units = P(EP + TP, None), P(EP, None, TP), P(EP, TP, None)
    return jax.shard_map(
        on_device,
        mesh=fine,
        in_specs=(rows, rows, rows, rows, columns, columns, units),
        out_specs=(rows, rows, columns, columns, units),
        check_vma=False,
    )
```

time: 126 us -> 109 us (0.87)
  the two profiles are of different devices: /device:TPU:4 before, /device:TPU:1 now
where the time goes in v2:
time: 109 us; the launch traced here: 108 us
  blocking collectives  44 us (40%)
  waiting for transfers between devices  28.1 us (26%)
  matrix products  12.8 us (12%)
  starting transfers between devices  11.9 us (11%)
  other arithmetic  7.19 us (7%)
  local copies, waits for them, and re-layouts  1.62 us (1%)
  Pallas kernels  1.52 us (1%)
    all_to_all x2, blocking collectives, exchanged(): return lax.all_to_all(value, axis, 0, 0, tiled=True)  44 us
    all_to_all x2, waiting for transfers between devices, exchanged(): return lax.all_to_all(value, axis, 0, 0, tiled=True)  23 us
    dot_general x9, matrix products, contract(): lax.dot_general(left, right, (((left_dim,), (right_dim,)), ((), ())), pre...  12.8 us
    all_to_all x2, starting transfers between devices, exchanged(): return lax.all_to_all(value, axis, 0, 0, tiled=True)  7.76 us
    ppermute x3, waiting for transfers between devices, swapped(): return lax.ppermute(value, 'core', [(0, 1), (1, 0)])  5.16 us
    ppermute x3, starting transfers between devices, swapped(): return lax.ppermute(value, 'core', [(0, 1), (1, 0)])  4.17 us
  transfers between devices with their start and end apart: 5, of which 5 were waited for; matrix products, arithmetic and copies ran while one was open for 9% of the time, Pallas kernels for 0%

profile of v2, /device:TPU:1, one launch (start us, length us, event | category | flops | bytes accessed | tf_op | source)
XLA Modules:
  0.0 108.1 jit_solution(10219729841290948840)
XLA Ops:
  0.6 1.5 %copies_of_row.1 = bf16[8,2,3200]{2,1,0:T(2,128)(2,1)} custom-call(bf16[1,3072]{1,0:T(2,128)(2,1)} %tokens.1, bf16[1,3072]{1,0:T(2,128)(2,1)} %cotangent.1, s32[1,2]{1,0:T(1,128)} %routes.1, bf16[1,2]{1,0:T(2,128)(2,1)} %weights.1), custom_call_target="tpu_custom_call" | custom-call | tf_op jit(solution)/shard_map/gather_z/copies_of_row/pallas_call | solution.py:42
  2.2 16.6 %all_to_all.20 = bf16[8,2,3200]{2,1,0:T(2,128)(2,1)S(1)} all-to-all(bf16[8,2,3200]{2,1,0:T(2,128)(2,1)} %copies_of_row.1), channel_id=1, replica_groups=mesh['x_hi'=2,'core'=2,'y'=4,'x_lo'=2,'z'=8] {'z'}, dimensions={0} | all-to-all | bytes 204800 | tf_op jit(solution)/shard_map/gather_z/all_to_all | solution.py:21
  19.1 27.4 %all_to_all.21 = bf16[16,8,6272]{2,1,0:T(8,128)(2,1)S(1)} all-to-all(bf16[16,8,6272]{2,1,0:T(8,128)(2,1)S(1)} %broadcast_in_dim.28), channel_id=1, replica_groups=mesh['x_hi'=2,'core'=2,'y'=4,'x_lo'=2,'z'=8] {'x_hi','x_lo','y'}, dimensions={0} | all-to-all | bytes 3211264 | tf_op jit(solution)/shard_map/gather_xy/all_to_all | solution.py:21
  46.5 3.5 %collective-permute-start = (bf16[128,6272]{1,0:T(8,128)(2,1)S(1)}, bf16[128,6272]{1,0:T(8,128)(2,1)}, u32[]{:S(2)}, u32[]{:S(2)}) collective-permute-start(bf16[128,6272]{1,0:T(8,128)(2,1)S(1)} %bitcast.47), channel_id=1, source_target_pairs={{0,64},{64,0},{1,65},{65,1},{2,66},{66,2},{3,67},{67,3},{4,68},{68... | collective-permute-start | bytes 4816904 | tf_op jit(solution)/shard_map/gather_core/ppermute | solution.py:17
  50.0 3.2 %collective-permute-done = bf16[128,6272]{1,0:T(8,128)(2,1)} collective-permute-done((bf16[128,6272]{1,0:T(8,128)(2,1)S(1)}, bf16[128,6272]{1,0:T(8,128)(2,1)}, u32[]{:S(2)}, u32[]{:S(2)}) %collective-permute-start) | collective-permute-done | bytes 1605664 | tf_op jit(solution)/shard_map/gather_core/ppermute | solution.py:17
  53.2 1.3 %fusion.3 = bf16[256,3072]{1,0:T(8,128)(2,1)S(1)} fusion(bf16[128,6272]{1,0:T(8,128)(2,1)} %collective-permute-done, bf16[128,6272]{1,0:T(8,128)(2,1)S(1)} %bitcast.48), kind=kLoop, calls=%fused_computation.11 | loop fusion | flops 3145728 | bytes 4784128 | tf_op jit(solution)/shard_map/gather_core/concatenate | solution.py:62
  55.1 0.9 select_reduce_fusion
  56.2 1.7 %convolution_multiply_fusion = f32[256,128]{1,0:T(8,128)S(1)} fusion(bf16[1,128,3072]{2,1,0:T(8,128)(2,1)S(1)} %copy-done.2, bf16[128,6272]{1,0:T(8,128)(2,1)S(1)} %bitcast.50, bf16[128,6272]{1,0:T(8,128)(2,1)} %collective-permute-done, f32[256]{0:T(256)S(1)} %select_reduce_fusion), kind=kOutput, calls=%fused_computation.20 | convolution fusion | flops 204505088 | bytes 4129792 | tf_op jit(solution)/shard_map/experts/dot_general | solution.py:25
  58.0 0.6 multiply_convert_fusion.2
  59.7 0.6 fusion.12
  60.2 0.6 convolution_add_fusion
  61.8 1.5 %collective-permute-done.2 = bf16[128,3072]{1,0:T(8,128)(2,1)S(1)} collective-permute-done((bf16[128,3072]{1,0:T(8,128)(2,1)S(1)}, bf16[128,3072]{1,0:T(8,128)(2,1)S(1)}, u32[]{:S(2)}, u32[]{:S(2)}) %collective-permute-start.2) | collective-permute-done | bytes 786464 | tf_op jit(solution)/shard_map/reduce_core/ppermute | solution.py:17
  63.5 1.3 %maximum_bitcast_fusion = bf16[16,8,6144]{2,1,0:T(8,128)(2,1)} fusion(bf16[128,3072]{1,0:T(8,128)(2,1)S(1)} %fusion.4, bf16[128,3072]{1,0:T(8,128)(2,1)S(1)} %fusion.5), kind=kLoop, calls=%fused_computation.19 | loop fusion | flops 3145728 | bytes 3145728 | tf_op jit(solution)/shard_map/reduce_xy/reshape | solution.py:82
  64.8 4.4 %all-to-all-start.2 = ((bf16[16,8,6144]{2,1,0:T(8,128)(2,1)}), bf16[16,8,6144]{2,1,0:T(8,128)(2,1)}, u32[]{:S(2)}, u32[]{:S(2)}) async-start(bf16[16,8,6144]{2,1,0:T(8,128)(2,1)} %maximum_bitcast_fusion), calls=%async_computation.2 | async-start | bytes 3145728 | tf_op jit(solution)/shard_map/reduce_xy/all_to_all | solution.py:21
  69.2 2.9 %fusion = bf16[1,3072,128]{2,1,0:T(8,128)(2,1)} fusion(bf16[256,3072]{1,0:T(8,128)(2,1)} %copy-done.1, bf16[256,128]{1,0:T(8,128)(2,1)S(1)} %get-tuple-element.6), kind=kOutput, calls=%fused_computation.8 | convolution fusion | flops 201719808 | bytes 2424832 | tf_op jit(solution)/shard_map/weights/dot_general | solution.py:25
  72.1 20.8 %all-to-all-done.2 = bf16[16,8,6144]{2,1,0:T(8,128)(2,1)} async-done(((bf16[16,8,6144]{2,1,0:T(8,128)(2,1)}), bf16[16,8,6144]{2,1,0:T(8,128)(2,1)}, u32[]{:S(2)}, u32[]{:S(2)}) %all-to-all-start.2) | async-done | bytes 1572896 | tf_op jit(solution)/shard_map/reduce_xy/all_to_all | solution.py:21
  92.9 1.6 %add_add_fusion = f32[1,8,6144]{2,1,0:T(8,128)S(1)} fusion(bf16[16,8,6144]{2,1,0:T(8,128)(2,1)} %all-to-all-done.2), kind=kLoop, calls=%fused_computation.31 | loop fusion | flops 1425408 | bytes 1671168 | tf_op jit(solution)/shard_map/reduce_xy/add | solution.py:50
  94.7 0.9 slice_convert_fusion.2
  95.8 0.7 add_convert_fusion
  96.6 3.4 %all-to-all-start.3 = ((bf16[8,2,3072]{2,1,0:T(2,128)(2,1)}), bf16[8,2,3072]{2,1,0:T(2,128)(2,1)S(1)}, u32[]{:S(2)}, u32[]{:S(2)}) async-start(bf16[8,2,3072]{2,1,0:T(2,128)(2,1)} %add_convert_fusion), calls=%async_computation.3 | async-start | bytes 196608 | tf_op jit(solution)/shard_map/reduce_z/all_to_all | solution.py:21
  99.9 2.9 %fusion.1 = bf16[1,3072,128]{2,1,0:T(8,128)(2,1)} fusion(bf16[256,3072]{1,0:T(8,128)(2,1)} %copy-done.1, bf16[256,128]{1,0:T(8,128)(2,1)S(1)} %get-tuple-element.7), kind=kOutput, calls=%fused_computation.9 | convolution fusion | flops 201719808 | bytes 2424832 | tf_op jit(solution)/shard_map/weights/dot_general | solution.py:25
  102.8 2.4 %fusion.2 = bf16[1,128,3072]{2,1,0:T(8,128)(2,1)} fusion(bf16[256,128]{1,0:T(8,128)(2,1)S(1)} %get-tuple-element.5, bf16[128,6272]{1,0:T(8,128)(2,1)S(1)} %bitcast.51, bf16[128,6272]{1,0:T(8,128)(2,1)} %collective-permute-done), kind=kOutput, calls=%fused_computation.10 | convolution fusion | flops 204865536 | bytes 4063232 | tf_op jit(solution)/shard_map/weights/dot_general | solution.py:25
  105.3 2.2 %all-to-all-done.3 = bf16[8,2,3072]{2,1,0:T(2,128)(2,1)S(1)} async-done(((bf16[8,2,3072]{2,1,0:T(2,128)(2,1)}), bf16[8,2,3072]{2,1,0:T(2,128)(2,1)S(1)}, u32[]{:S(2)}, u32[]{:S(2)}) %all-to-all-start.3) | async-done | bytes 98336 | tf_op jit(solution)/shard_map/reduce_z/all_to_all | solution.py:21
  107.5 0.6 slice_bitcast_fusion
  (26 shorter events, 3.7 us)
Async XLA Ops:
  0.6 57.3 %copy-start = (bf16[1,3072,128]{2,1,0:T(8,128)(2,1)S(1)}, bf16[1,3072,128]{2,1,0:T(8,128)(2,1)}, u32[]{:S(2)}) copy-start(bf16[1,3072,128]{2,1,0:T(8,128)(2,1)} %param.12) | copy-start | bytes 2359300
  46.5 6.7 %collective-permute-start = (bf16[128,6272]{1,0:T(8,128)(2,1)S(1)}, bf16[128,6272]{1,0:T(8,128)(2,1)}, u32[]{:S(2)}, u32[]{:S(2)}) collective-permute-start(bf16[128,6272]{1,0:T(8,128)(2,1)S(1)} %bitcast.47), channel_id=1, source_target_pairs={{0,64},{64,0},{1,65},{65,1},{2,66},{66,2},{3,67},{67,3},{4,68},{68... | collective-permute-start | bytes 4816904 | tf_op jit(solution)/shard_map/gather_core/ppermute | solution.py:17
  50.0 4.5 %copy-start.3 = (bf16[1,3072,128]{2,1,0:T(8,128)(2,1)S(1)}, bf16[1,3072,128]{2,1,0:T(8,128)(2,1)}, u32[]{:S(2)}) copy-start(bf16[1,3072,128]{2,1,0:T(8,128)(2,1)} %param.11) | copy-start | bytes 2359300
  54.5 3.5 %copy-start.1 = (bf16[256,3072]{1,0:T(8,128)(2,1)}, bf16[256,3072]{1,0:T(8,128)(2,1)S(1)}, u32[]{:S(2)}) copy-start(bf16[256,3072]{1,0:T(8,128)(2,1)S(1)} %fusion.3) | copy-start | bytes 4718596
  55.1 1.2 %copy-start.2 = (bf16[1,128,3072]{2,1,0:T(8,128)(2,1)S(1)}, bf16[1,128,3072]{2,1,0:T(8,128)(2,1)}, u32[]{:S(2)}) copy-start(bf16[1,128,3072]{2,1,0:T(8,128)(2,1)} %param.13) | copy-start | bytes 2359300
  59.2 2.4 %collective-permute-start.1 = (bf16[128,3072]{1,0:T(8,128)(2,1)S(1)}, bf16[128,3072]{1,0:T(8,128)(2,1)S(1)}, u32[]{:S(2)}, u32[]{:S(2)}) collective-permute-start(bf16[128,3072]{1,0:T(8,128)(2,1)S(1)} %slice.231), channel_id=1, source_target_pairs={{0,64},{64,0},{1,65},{65,1},{2,66},{66,2},{3,67},{67,3},{4,68},{68... | collective-permute-start | bytes 2359304 | tf_op jit(solution)/shard_map/reduce_core/ppermute | solution.py:17
  60.9 2.4 %collective-permute-start.2 = (bf16[128,3072]{1,0:T(8,128)(2,1)S(1)}, bf16[128,3072]{1,0:T(8,128)(2,1)S(1)}, u32[]{:S(2)}, u32[]{:S(2)}) collective-permute-start(bf16[128,3072]{1,0:T(8,128)(2,1)S(1)} %slice.230), channel_id=1, source_target_pairs={{0,64},{64,0},{1,65},{65,1},{2,66},{66,2},{3,67},{67,3},{4,68},{68... | collective-permute-start | bytes 2359304 | tf_op jit(solution)/shard_map/reduce_core/ppermute | solution.py:17
  64.8 28.2 %all-to-all-start.2 = ((bf16[16,8,6144]{2,1,0:T(8,128)(2,1)}), bf16[16,8,6144]{2,1,0:T(8,128)(2,1)}, u32[]{:S(2)}, u32[]{:S(2)}) async-start(bf16[16,8,6144]{2,1,0:T(8,128)(2,1)} %maximum_bitcast_fusion), calls=%async_computation.2 | async-start | bytes 3145728 | tf_op jit(solution)/shard_map/reduce_xy/all_to_all | solution.py:21
  96.6 10.9 %all-to-all-start.3 = ((bf16[8,2,3072]{2,1,0:T(2,128)(2,1)}), bf16[8,2,3072]{2,1,0:T(2,128)(2,1)S(1)}, u32[]{:S(2)}, u32[]{:S(2)}) async-start(bf16[8,2,3072]{2,1,0:T(2,128)(2,1)} %add_convert_fusion), calls=%async_computation.3 | async-start | bytes 196608 | tf_op jit(solution)/shard_map/reduce_z/all_to_all | solution.py:21

commit v3 on v2

v3 whole, which is shorter than its diff:
```python
import jax
import jax.numpy as jnp
from jax import lax
from jax.experimental import pallas as pl
from jax.experimental.pallas import tpu as pltpu
from jax.sharding import Mesh, PartitionSpec as P

NX_HI, NCORE, NY, NX_LO, NZ, RING = 2, 2, 4, 2, 8, 4
AXES = ("x_hi", "core", "y", "x_lo", "z")
EP, TP = ("x_hi", "core"), ("y", "x_lo", "z")
D, PAD, UNITS = 3072, 128, 128
F32, BF16 = jnp.float32, jnp.bfloat16
VMEM = pl.BlockSpec(memory_space=pltpu.VMEM)
SMEM = pl.BlockSpec(memory_space=pltpu.SMEM)
PARAMS = pltpu.CompilerParams(vmem_limit_bytes=48 << 20)


def flat(x, core, y, z):
    return (((x // 2) * NCORE + core) * NY + y) * NX_LO * NZ + (x % 2) * NZ + z


def pairs(stage, d):
    out = []
    for x in range(RING):
        for core in range(NCORE):
            for y in range(RING):
                along_x = (stage == "light") == (core == 0)
                tx, ty = ((x + d) % RING, y) if along_x else (x, (y + d) % RING)
                out += [(flat(x, core, y, z), flat(tx, core, ty, z)) for z in range(NZ)]
    return out


def give(value, stage, d):
    return lax.ppermute(value, AXES, pairs(stage, d))


def fetch(value, stage, d):
    return lax.ppermute(value, AXES, pairs(stage, -d))


def swapped(value):
    return lax.ppermute(value, "core", [(0, 1), (1, 0)])


def exchanged(value, axis):
    return lax.all_to_all(value, axis, 0, 0, tiled=True)


def dot(left, right, left_dim, right_dim):
    return lax.dot_general(
        left, right, (((left_dim,), (right_dim,)), ((), ())), preferred_element_type=F32
    )


def row_kernel(tokens, cotangent, routes, weights, out):
    lane = lax.broadcasted_iota(jnp.int32, (1, PAD), 1)
    r, w = routes[...], weights[...].astype(F32)
    gates = jnp.where(r[:, :1] == lane, w[:, :1], 0.0) + jnp.where(r[:, 1:] == lane, w[:, 1:], 0.0)
    first = jnp.concatenate([tokens[...].astype(F32), gates], axis=1)
    second = jnp.concatenate([cotangent[...].astype(F32), jnp.zeros((1, PAD), F32)], axis=1)
    both = jnp.concatenate([first, second], axis=0).astype(BF16)
    for i in range(NZ):
        out[i] = both


def copies_of_row(tokens, cotangent, routes, gate_weights):
    return pl.pallas_call(
        row_kernel,
        out_shape=jax.ShapeDtypeStruct((NZ, 2, D + PAD), BF16),
        out_specs=VMEM,
        name="copies_of_row",
    )(tokens, cotangent, routes, gate_weights)


def expert_kernel(group, rows, gate_slice, up_slice, down_slice, terms, acts):
    lane = lax.broadcasted_iota(jnp.int32, (rows.shape[0], PAD), 1)
    gates = jnp.where(lane == group[0], rows[:, 2 * D :].astype(F32), 0.0)
    column = jnp.sum(gates, axis=1, keepdims=True)
    x, cot = rows[:, :D], rows[:, D : 2 * D]
    gate_pre = dot(x, gate_slice[...], 1, 0)
    up_pre = dot(x, up_slice[...], 1, 0)
    grad_act = dot(cot, down_slice[...], 1, 1) * column
    sigmoid = jax.nn.sigmoid(gate_pre)
    silu = gate_pre * sigmoid
    hidden = (silu * up_pre * column).astype(BF16)
    grad_gpre = (grad_act * up_pre * (sigmoid * (1.0 + gate_pre * (1.0 - sigmoid)))).astype(BF16)
    grad_upre = (grad_act * silu).astype(BF16)
    acts[:, :UNITS] = hidden
    acts[:, UNITS : 2 * UNITS] = grad_gpre
    acts[:, 2 * UNITS :] = grad_upre
    terms[:, :D] = dot(hidden, down_slice[...], 1, 0).astype(terms.dtype)
    grad_rows = dot(grad_gpre, gate_slice[...], 1, 1) + dot(grad_upre, up_slice[...], 1, 1)
    terms[:, D:] = grad_rows.astype(terms.dtype)


def expert_terms(group, rows, gate_slice, up_slice, down_slice, kind):
    n = rows.shape[0]
    return pl.pallas_call(
        expert_kernel,
        out_shape=(
            jax.ShapeDtypeStruct((n, 2 * D), kind),
            jax.ShapeDtypeStruct((n, 3 * UNITS), BF16),
        ),
        in_specs=[SMEM] + [VMEM] * 4,
        out_specs=(VMEM, VMEM),
        compiler_params=PARAMS,
        cost_estimate=pl.CostEstimate(
            flops=12 * n * D * UNITS, transcendentals=n * UNITS, bytes_accessed=4 * n * D + 6 * D * UNITS
        ),
        name="expert_terms",
    )(group, rows, gate_slice, up_slice, down_slice)


def weight_kernel(far, near, acts_far, acts_near, grad_g, grad_u, grad_d):
    u = UNITS

    def both(left_at, left_rows, right_at):
        def part(rows, acts):
            left = rows[:, left_at : left_at + D] if left_rows else acts[:, :u]
            right = acts[:, right_at : right_at + u] if left_rows else rows[:, D : 2 * D]
            return dot(left, right, 0, 0)

        return (part(far, acts_far) + part(near, acts_near)).astype(BF16)

    grad_g[0] = both(0, True, u)
    grad_u[0] = both(0, True, 2 * u)
    grad_d[0] = both(0, False, 0)


def weight_grads(far, near, acts_far, acts_near):
    n = 2 * far.shape[0]
    return pl.pallas_call(
        weight_kernel,
        out_shape=(
            jax.ShapeDtypeStruct((1, D, UNITS), BF16),
            jax.ShapeDtypeStruct((1, D, UNITS), BF16),
            jax.ShapeDtypeStruct((1, UNITS, D), BF16),
        ),
        in_specs=[VMEM] * 4,
        out_specs=(VMEM,) * 3,
        compiler_params=PARAMS,
        cost_estimate=pl.CostEstimate(
            flops=6 * n * D * UNITS, transcendentals=0, bytes_accessed=4 * n * D + 6 * D * UNITS
        ),
        name="weight_grads",
    )(far, near, acts_far, acts_near)


def last_kernel(own, one, two, three, out):
    total = own[...] + one[...].astype(F32) + two[...].astype(F32) + three[...].astype(F32)
    for i in range(NZ):
        row = total[i : i + 1]
        out[i] = jnp.concatenate([row[:, :D], row[:, D:]], axis=0).astype(BF16)


def summed_pairs(own, parts):
    return pl.pallas_call(
        last_kernel,
        out_shape=jax.ShapeDtypeStruct((NZ, 2, D), BF16),
        in_specs=[VMEM] * 4,
        out_specs=VMEM,
        name="summed_pairs",
    )(own, *parts)


def on_device(tokens, cotangent, routes, gate_weights, w_gate, w_up, w_down):
    slices = (w_gate[0], w_up[0], w_down[0])
    group = lax.axis_index(EP).astype(jnp.int32).reshape(1)
    with jax.named_scope("gather_z"):
        rows = exchanged(copies_of_row(tokens, cotangent, routes, gate_weights), "z")
        rows = jnp.concatenate([rows[:, 0, :D], rows[:, 1, :D], rows[:, 0, D:]], axis=1)
    with jax.named_scope("gather_light"):
        rows = jnp.concatenate([rows] + [fetch(rows, "light", d) for d in range(1, RING)], axis=0)
    with jax.named_scope("gather_heavy"):
        near = [rows] + [fetch(rows, "heavy", d) for d in range(1, RING)]
    with jax.named_scope("gather_core"):
        far = jnp.concatenate([swapped(chunk) for chunk in near], axis=0)
        near = jnp.concatenate(near, axis=0)
    with jax.named_scope("experts"):
        far_terms, far_acts = expert_terms(group, far, *slices, BF16)
        other = swapped(far_terms)
        near_terms, near_acts = expert_terms(group, near, *slices, F32)
    with jax.named_scope("weights"):
        grad_g, grad_u, grad_d = weight_grads(far, near, far_acts, near_acts)
    with jax.named_scope("reduce_heavy"):
        total = (near_terms + other.astype(F32)).reshape(RING, RING * NZ, 2 * D)
        got = [give(total[d].astype(BF16), "heavy", d) for d in range(1, RING)]
        total = total[0] + sum(g.astype(F32) for g in got)
    with jax.named_scope("reduce_light"):
        total = total.reshape(RING, NZ, 2 * D)
        got = [give(total[d].astype(BF16), "light", d) for d in range(1, RING)]
    with jax.named_scope("reduce_z"):
        got = exchanged(summed_pairs(total[0], got), "z")
        total = sum(got[i].astype(F32) for i in range(NZ)).astype(BF16)
    return total[:1], total[1:], grad_g, grad_u, grad_d


def solution(mesh):
    fine = Mesh(mesh.devices.reshape(NX_HI, NCORE, NY, NX_LO, NZ), AXES)
    rows, columns, units = P(EP + TP, None), P(EP, None, TP), P(EP, TP, None)
    return jax.shard_map(
        on_device,
        mesh=fine,
        in_specs=(rows, rows, rows, rows, columns, columns, units),
        out_specs=(rows, rows, columns, columns, units),
        check_vma=False,
    )
```

time: 109 us -> 91.5 us (0.84)
  blocking collectives: 44 us -> 16.6 us
  matrix products: 12.8 us -> 0 us
  starting transfers between devices: 11.9 us -> 22.5 us
  Pallas kernels: 1.52 us -> 10.3 us
  waiting for transfers between devices: 28.1 us -> 34.3 us
  other arithmetic: 7.19 us -> 2.64 us
    all_to_all x2 -> x1, blocking collectives: 44 us -> 16.6 us  [exchanged(): return lax.all_to_all(value, axis, 0, 0, tiled=True)]
    ppermute x0 -> x12, waiting for transfers between devices: none -> 27.3 us  [the longest x6 13.8 us: fetch(): return lax.ppermute(value, AXES, pairs(stage, -d))]
    all_to_all x2 -> x1, waiting for transfers between devices: 23 us -> 5.17 us  [exchanged(): return lax.all_to_all(value, axis, 0, 0, tiled=True)]
    dot_general x9 -> x0, matrix products: 12.8 us -> none  [contract(): lax.dot_general(left, right, (((left_dim,), (right_dim,)), ((), ())), pre...]
    ppermute x0 -> x12, starting transfers between devices: none -> 12.6 us  [the longest x6 7.15 us: fetch(): return lax.ppermute(value, AXES, pairs(stage, -d))]
    pallas_call x0 -> x4, Pallas kernels: none -> 8.86 us  [the longest x2 4.57 us: expert_terms(): pl.pallas_call(expert_kernel, out_shape=(jax.ShapeDtypeStruct((n, 2 * D),...]
    all_to_all x2 -> x1, starting transfers between devices: 7.76 us -> 3.36 us  [exchanged(): return lax.all_to_all(value, axis, 0, 0, tiled=True)]
    ppermute x3 -> x5, waiting for transfers between devices: 5.16 us -> 1.82 us  [swapped(): return lax.ppermute(value, 'core', [(0, 1), (1, 0)])]
  transfers between devices with their start and end apart: 5 -> 18, of which waited for: 5 -> 10; matrix products, arithmetic and copies ran while one was open for 9% -> 1% of each run, Pallas kernels for 0% -> 6%
where the time goes in v3:
time: 91.5 us; the launch traced here: 89.7 us
  waiting for transfers between devices  34.3 us (37%)
  starting transfers between devices  22.5 us (25%)
  blocking collectives  16.6 us (18%)
  Pallas kernels  10.3 us (11%)
  other arithmetic  2.64 us (3%)
  local copies, waits for them, and re-layouts  2.54 us (3%)
    all_to_all x1, blocking collectives, exchanged(): return lax.all_to_all(value, axis, 0, 0, tiled=True)  16.6 us
    ppermute x6, waiting for transfers between devices, fetch(): return lax.ppermute(value, AXES, pairs(stage, -d))  13.8 us
    ppermute x6, waiting for transfers between devices, give(): return lax.ppermute(value, AXES, pairs(stage, d))  13.5 us
    ppermute x6, starting transfers between devices, fetch(): return lax.ppermute(value, AXES, pairs(stage, -d))  7.15 us
    ppermute x5, starting transfers between devices, swapped(): return lax.ppermute(value, 'core', [(0, 1), (1, 0)])  6.46 us
    ppermute x6, starting transfers between devices, give(): return lax.ppermute(value, AXES, pairs(stage, d))  5.49 us
    all_to_all x1, waiting for transfers between devices, exchanged(): return lax.all_to_all(value, axis, 0, 0, tiled=True)  5.17 us
    pallas_call x2, Pallas kernels, expert_terms(): pl.pallas_call(expert_kernel, out_shape=(jax.ShapeDtypeStruct((n, 2 * D),...  4.57 us
  transfers between devices with their start and end apart: 18, of which 10 were waited for; matrix products, arithmetic and copies ran while one was open for 1% of the time, Pallas kernels for 6%

profile of v3, /device:TPU:1, one launch (start us, length us, event | category | flops | bytes accessed | tf_op | source)
XLA Modules:
  0.0 89.7 jit_solution(13044975150514939928)
XLA Ops:
  0.6 1.5 %copies_of_row.1 = bf16[8,2,3200]{2,1,0:T(2,128)(2,1)} custom-call(bf16[1,3072]{1,0:T(2,128)(2,1)} %tokens.1, bf16[1,3072]{1,0:T(2,128)(2,1)} %cotangent.1, s32[1,2]{1,0:T(1,128)} %routes.1, bf16[1,2]{1,0:T(2,128)(2,1)} %weights.1), custom_call_target="tpu_custom_call" | custom-call | tf_op jit(solution)/shard_map/gather_z/copies_of_row/pallas_call | solution.py:67
  2.1 16.6 %all_to_all.10 = bf16[8,2,3200]{2,1,0:T(2,128)(2,1)S(1)} all-to-all(bf16[8,2,3200]{2,1,0:T(2,128)(2,1)} %copies_of_row.1), channel_id=1, replica_groups=mesh['x_hi'=2,'core'=2,'y'=4,'x_lo'=2,'z'=8] {'z'}, dimensions={0} | all-to-all | bytes 204800 | tf_op jit(solution)/shard_map/gather_z/all_to_all | solution.py:46
  18.9 3.0 %collective-permute-start.1 = (bf16[8,6272]{1,0:T(8,128)(2,1)S(1)}, bf16[8,6272]{1,0:T(8,128)(2,1)S(1)}, u32[]{:S(2)}, u32[]{:S(2)}) collective-permute-start(bf16[8,6272]{1,0:T(8,128)(2,1)S(1)} %get-tuple-element.31), channel_id=1, source_target_pairs={{0,128},{1,129},{2,130},{3,131},{4,132},{5,133},{6,134},{7,135},{1... | collective-permute-start | bytes 301064 | tf_op jit(solution)/shard_map/gather_light/ppermute | solution.py:38
  21.9 0.8 collective-permute-start
  24.0 1.4 %collective-permute-done = bf16[8,6272]{1,0:T(8,128)(2,1)S(1)} collective-permute-done((bf16[8,6272]{1,0:T(8,128)(2,1)S(1)}, bf16[8,6272]{1,0:T(8,128)(2,1)S(1)}, u32[]{:S(2)}, u32[]{:S(2)}) %collective-permute-start) | collective-permute-done | bytes 100384 | tf_op jit(solution)/shard_map/gather_light/ppermute | solution.py:38
  25.4 2.0 %collective-permute-done.2 = bf16[8,6272]{1,0:T(8,128)(2,1)S(1)} collective-permute-done((bf16[8,6272]{1,0:T(8,128)(2,1)S(1)}, bf16[8,6272]{1,0:T(8,128)(2,1)S(1)}, u32[]{:S(2)}, u32[]{:S(2)}) %collective-permute-start.2) | collective-permute-done | bytes 100384 | tf_op jit(solution)/shard_map/gather_light/ppermute | solution.py:38
  27.5 3.8 %collective-permute-start.6 = (bf16[32,6272]{1,0:T(8,128)(2,1)S(1)}, bf16[32,6272]{1,0:T(8,128)(2,1)S(1)}, u32[]{:S(2)}, u32[]{:S(2)}) collective-permute-start(bf16[32,6272]{1,0:T(8,128)(2,1)S(1)} %pad_maximum_fusion), channel_id=1, source_target_pairs={{0,64},{64,0},{1,65},{65,1},{2,66},{66,2},{3,67},{67,3},{4,68},{68... | collective-permute-start | bytes 1204232 | tf_op jit(solution)/shard_map/gather_core/ppermute | solution.py:42
  31.3 0.9 %collective-permute-start.4 = (bf16[32,6272]{1,0:T(8,128)(2,1)S(1)}, bf16[32,6272]{1,0:T(8,128)(2,1)S(1)}, u32[]{:S(2)}, u32[]{:S(2)}) collective-permute-start(bf16[32,6272]{1,0:T(8,128)(2,1)S(1)} %pad_maximum_fusion), channel_id=1, source_target_pairs={{0,32},{1,33},{2,34},{3,35},{4,36},{5,37},{6,38},{7,39},{16,48},{1... | collective-permute-start | bytes 1204232 | tf_op jit(solution)/shard_map/gather_heavy/ppermute | solution.py:38
  32.2 1.8 %collective-permute-start.3 = (bf16[32,6272]{1,0:T(8,128)(2,1)S(1)}, bf16[32,6272]{1,0:T(8,128)(2,1)S(1)}, u32[]{:S(2)}, u32[]{:S(2)}) collective-permute-start(bf16[32,6272]{1,0:T(8,128)(2,1)S(1)} %pad_maximum_fusion), channel_id=1, source_target_pairs={{0,48},{1,49},{2,50},{3,51},{4,52},{5,53},{6,54},{7,55},{16,0},{17... | collective-permute-start | bytes 1204232 | tf_op jit(solution)/shard_map/gather_heavy/ppermute | solution.py:38
  34.0 9.8 %collective-permute-done.5 = bf16[32,6272]{1,0:T(8,128)(2,1)S(1)} collective-permute-done((bf16[32,6272]{1,0:T(8,128)(2,1)S(1)}, bf16[32,6272]{1,0:T(8,128)(2,1)S(1)}, u32[]{:S(2)}, u32[]{:S(2)}) %collective-permute-start.5) | collective-permute-done | bytes 401440 | tf_op jit(solution)/shard_map/gather_heavy/ppermute | solution.py:38
  43.8 2.2 %collective-permute-start.8 = (bf16[32,6272]{1,0:T(8,128)(2,1)S(1)}, bf16[32,6272]{1,0:T(8,128)(2,1)S(1)}, u32[]{:S(2)}, u32[]{:S(2)}) collective-permute-start(bf16[32,6272]{1,0:T(8,128)(2,1)S(1)} %collective-permute-done.4), channel_id=1, source_target_pairs={{0,64},{64,0},{1,65},{65,1},{2,66},{66,2},{3,67},{67,3},{4,68},{68... | collective-permute-start | bytes 1204232 | tf_op jit(solution)/shard_map/gather_core/ppermute | solution.py:42
  46.1 1.8 %collective-permute-done.7 = bf16[32,6272]{1,0:T(8,128)(2,1)S(1)} collective-permute-done((bf16[32,6272]{1,0:T(8,128)(2,1)S(1)}, bf16[32,6272]{1,0:T(8,128)(2,1)S(1)}, u32[]{:S(2)}, u32[]{:S(2)}) %collective-permute-start.7) | collective-permute-done | bytes 401440 | tf_op jit(solution)/shard_map/gather_core/ppermute | solution.py:42
  48.1 1.5 %expert_terms.3 = (bf16[128,6144]{1,0:T(8,128)(2,1)S(1)}, bf16[128,384]{1,0:T(8,128)(2,1)S(1)}) custom-call(s32[1]{0:T(128)} %bitcast.group, bf16[128,6272]{1,0:T(8,128)(2,1)S(1)} %constant_dynamic-update-slice_fusion.7.rows.far, bf16[3072,128]{1,0:T(8,128)(2,1)S(1)} %bitcast.15, bf16[3072,128]{1,0:T(8,128)(2,1)S(1)} %bitcast.17, bf16[128,3072]{1,0:T(8,128)(2,1)S(1)} %bitcast.19), custom_call_target="tpu_custom_call" | custom-call | flops 603979776 | bytes 3932160 | tf_op jit(solution)/shard_map/experts/expert_terms/pallas_call | solution.py:98
  50.1 3.1 %expert_terms.2 = (f32[128,6144]{1,0:T(8,128)}, bf16[128,384]{1,0:T(8,128)(2,1)S(1)}) custom-call(s32[1]{0:T(128)} %bitcast.group, bf16[128,6272]{1,0:T(8,128)(2,1)S(1)} %constant_dynamic-update-slice_fusion.rows.near, bf16[3072,128]{1,0:T(8,128)(2,1)S(1)} %bitcast.16, bf16[3072,128]{1,0:T(8,128)(2,1)S(1)} %bitcast.18, bf16[128,3072]{1,0:T(8,128)(2,1)S(1)} %bitcast.20), custom_call_target="tpu_custom_call" | custom-call | flops 603979776 | bytes 3932160 | tf_op jit(solution)/shard_map/experts/expert_terms/pallas_call | solution.py:98
  53.2 2.4 %fusion.1 = (bf16[128,6144]{1,0:T(8,128)(2,1)S(1)}, f32[128,6144]{1,0:T(8,128)S(1)}) fusion(f32[128,6144]{1,0:T(8,128)} %get-tuple-element.12, bf16[128,6144]{1,0:T(8,128)(2,1)S(1)} %collective-permute-done.10), kind=kLoop, calls=%fused_computation.22 | loop fusion | flops 2359296 | bytes 9437184 | tf_op jit(solution)/shard_map/convert.9
  55.7 2.7 %collective-permute-start.13 = (bf16[32,6144]{1,0:T(8,128)(2,1)S(1)}, bf16[32,6144]{1,0:T(8,128)(2,1)S(1)}, u32[]{:S(2)}, u32[]{:S(2)}) collective-permute-start(bf16[32,6144]{1,0:T(8,128)(2,1)S(1)} %get-tuple-element.24), channel_id=1, source_target_pairs={{0,48},{1,49},{2,50},{3,51},{4,52},{5,53},{6,54},{7,55},{16,0},{17... | collective-permute-start | bytes 1179656 | tf_op jit(solution)/shard_map/reduce_heavy/ppermute | solution.py:34
  58.4 9.7 %collective-permute-done.11 = bf16[32,6144]{1,0:T(8,128)(2,1)S(1)} collective-permute-done((bf16[32,6144]{1,0:T(8,128)(2,1)S(1)}, bf16[32,6144]{1,0:T(8,128)(2,1)S(1)}, u32[]{:S(2)}, u32[]{:S(2)}) %collective-permute-start.11) | collective-permute-done | bytes 393248 | tf_op jit(solution)/shard_map/reduce_heavy/ppermute | solution.py:34
  68.3 1.5 %collective-permute-start.16 = (bf16[8,6144]{1,0:T(8,128)(2,1)S(1)}, bf16[8,6144]{1,0:T(8,128)(2,1)S(1)}, u32[]{:S(2)}, u32[]{:S(2)}) collective-permute-start(bf16[8,6144]{1,0:T(8,128)(2,1)S(1)} %get-tuple-element.26), channel_id=1, source_target_pairs={{0,136},{1,137},{2,138},{3,139},{4,140},{5,141},{6,142},{7,143},{1... | collective-permute-start | bytes 294920 | tf_op jit(solution)/shard_map/reduce_light/ppermute | solution.py:34
  69.8 1.0 %collective-permute-start.15 = (bf16[8,6144]{1,0:T(8,128)(2,1)S(1)}, bf16[8,6144]{1,0:T(8,128)(2,1)S(1)}, u32[]{:S(2)}, u32[]{:S(2)}) collective-permute-start(bf16[8,6144]{1,0:T(8,128)(2,1)S(1)} %get-tuple-element.27), channel_id=1, source_target_pairs={{0,128},{1,129},{2,130},{3,131},{4,132},{5,133},{6,134},{7,135},{1... | collective-permute-start | bytes 294920 | tf_op jit(solution)/shard_map/reduce_light/ppermute | solution.py:34
  71.8 3.0 %collective-permute-done.15.two = bf16[8,6144]{1,0:T(8,128)(2,1)S(1)} collective-permute-done((bf16[8,6144]{1,0:T(8,128)(2,1)S(1)}, bf16[8,6144]{1,0:T(8,128)(2,1)S(1)}, u32[]{:S(2)}, u32[]{:S(2)}) %collective-permute-start.15) | collective-permute-done | bytes 98336 | tf_op jit(solution)/shard_map/reduce_light/ppermute | solution.py:34
  76.2 1.9 %summed_pairs.1 = bf16[8,2,3072]{2,1,0:T(2,128)(2,1)} custom-call(f32[8,6144]{1,0:T(8,128)} %slice.107.own, bf16[8,6144]{1,0:T(8,128)(2,1)} %collective-permute-done.14.one, bf16[8,6144]{1,0:T(8,128)(2,1)} %copy-done.4, bf16[8,6144]{1,0:T(8,128)(2,1)} %copy-done.3), custom_call_target="tpu_custom_call" | custom-call | tf_op jit(solution)/shard_map/reduce_z/summed_pairs/pallas_call | solution.py:157
  78.1 3.4 %all-to-all-start.1 = ((bf16[8,2,3072]{2,1,0:T(2,128)(2,1)}), bf16[8,2,3072]{2,1,0:T(2,128)(2,1)S(1)}, u32[]{:S(2)}, u32[]{:S(2)}) async-start(bf16[8,2,3072]{2,1,0:T(2,128)(2,1)} %summed_pairs.1), calls=%async_computation.1 | async-start | bytes 196608 | tf_op jit(solution)/shard_map/reduce_z/all_to_all | solution.py:46
  81.5 2.4 %weight_grads.1 = (bf16[1,3072,128]{2,1,0:T(8,128)(2,1)}, bf16[1,3072,128]{2,1,0:T(8,128)(2,1)}, bf16[1,128,3072]{2,1,0:T(8,128)(2,1)}) custom-call(bf16[128,6272]{1,0:T(8,128)(2,1)S(1)} %constant_dynamic-update-slice_fusion.7.rows.far, bf16[128,6272]{1,0:T(8,128)(2,1)S(1)} %constant_dynamic-update-slice_fusion.rows.near, ...), custom_call_target="tpu_custom_call" | custom-call | flops 603979776 | bytes 5505024 | tf_op jit(solution)/shard_map/weights/weight_grads/pallas_call | solution.py:132
  83.9 5.2 %all-to-all-done.1 = bf16[8,2,3072]{2,1,0:T(2,128)(2,1)S(1)} async-done(((bf16[8,2,3072]{2,1,0:T(2,128)(2,1)}), bf16[8,2,3072]{2,1,0:T(2,128)(2,1)S(1)}, u32[]{:S(2)}, u32[]{:S(2)}) %all-to-all-start.1) | async-done | bytes 98336 | tf_op jit(solution)/shard_map/reduce_z/all_to_all | solution.py:46
  (51 shorter events, 5.8 us)
Async XLA Ops:
  18.9 5.1 %collective-permute-start.1 = (bf16[8,6272]{1,0:T(8,128)(2,1)S(1)}, bf16[8,6272]{1,0:T(8,128)(2,1)S(1)}, u32[]{:S(2)}, u32[]{:S(2)}) collective-permute-start(bf16[8,6272]{1,0:T(8,128)(2,1)S(1)} %get-tuple-element.31), channel_id=1, source_target_pairs={{0,128},{1,129},{2,130},{3,131},{4,132},{5,133},{6,134},{7,135},{1... | collective-permute-start | bytes 301064 | tf_op jit(solution)/shard_map/gather_light/ppermute | solution.py:38
  21.9 3.5 %collective-permute-start = (bf16[8,6272]{1,0:T(8,128)(2,1)S(1)}, bf16[8,6272]{1,0:T(8,128)(2,1)S(1)}, u32[]{:S(2)}, u32[]{:S(2)}) collective-permute-start(bf16[8,6272]{1,0:T(8,128)(2,1)S(1)} %get-tuple-element.31), channel_id=1, source_target_pairs={{0,136},{1,137},{2,138},{3,139},{4,140},{5,141},{6,142},{7,143},{1... | collective-permute-start | bytes 301064 | tf_op jit(solution)/shard_map/gather_light/ppermute | solution.py:38
  22.7 4.7 %collective-permute-start.2 = (bf16[8,6272]{1,0:T(8,128)(2,1)S(1)}, bf16[8,6272]{1,0:T(8,128)(2,1)S(1)}, u32[]{:S(2)}, u32[]{:S(2)}) collective-permute-start(bf16[8,6272]{1,0:T(8,128)(2,1)S(1)} %get-tuple-element.31), channel_id=1, source_target_pairs={{0,8},{1,9},{2,10},{3,11},{4,12},{5,13},{6,14},{7,15},{16,24},{17,... | collective-permute-start | bytes 301064 | tf_op jit(solution)/shard_map/gather_light/ppermute | solution.py:38
  27.5 18.6 %collective-permute-start.6 = (bf16[32,6272]{1,0:T(8,128)(2,1)S(1)}, bf16[32,6272]{1,0:T(8,128)(2,1)S(1)}, u32[]{:S(2)}, u32[]{:S(2)}) collective-permute-start(bf16[32,6272]{1,0:T(8,128)(2,1)S(1)} %pad_maximum_fusion), channel_id=1, source_target_pairs={{0,64},{64,0},{1,65},{65,1},{2,66},{66,2},{3,67},{67,3},{4,68},{68... | collective-permute-start | bytes 1204232 | tf_op jit(solution)/shard_map/gather_core/ppermute | solution.py:42
  31.3 12.5 %collective-permute-start.5 = (bf16[32,6272]{1,0:T(8,128)(2,1)S(1)}, bf16[32,6272]{1,0:T(8,128)(2,1)S(1)}, u32[]{:S(2)}, u32[]{:S(2)}) collective-permute-start(bf16[32,6272]{1,0:T(8,128)(2,1)S(1)} %pad_maximum_fusion), channel_id=1, source_target_pairs={{0,16},{1,17},{2,18},{3,19},{4,20},{5,21},{6,22},{7,23},{16,32},{1... | collective-permute-start | bytes 1204232 | tf_op jit(solution)/shard_map/gather_heavy/ppermute | solution.py:38
  31.3 12.5 %collective-permute-start.4 = (bf16[32,6272]{1,0:T(8,128)(2,1)S(1)}, bf16[32,6272]{1,0:T(8,128)(2,1)S(1)}, u32[]{:S(2)}, u32[]{:S(2)}) collective-permute-start(bf16[32,6272]{1,0:T(8,128)(2,1)S(1)} %pad_maximum_fusion), channel_id=1, source_target_pairs={{0,32},{1,33},{2,34},{3,35},{4,36},{5,37},{6,38},{7,39},{16,48},{1... | collective-permute-start | bytes 1204232 | tf_op jit(solution)/shard_map/gather_heavy/ppermute | solution.py:38
  32.2 13.8 %collective-permute-start.3 = (bf16[32,6272]{1,0:T(8,128)(2,1)S(1)}, bf16[32,6272]{1,0:T(8,128)(2,1)S(1)}, u32[]{:S(2)}, u32[]{:S(2)}) collective-permute-start(bf16[32,6272]{1,0:T(8,128)(2,1)S(1)} %pad_maximum_fusion), channel_id=1, source_target_pairs={{0,48},{1,49},{2,50},{3,51},{4,52},{5,53},{6,54},{7,55},{16,0},{17... | collective-permute-start | bytes 1204232 | tf_op jit(solution)/shard_map/gather_heavy/ppermute | solution.py:38
  43.8 4.2 %collective-permute-start.9 = (bf16[32,6272]{1,0:T(8,128)(2,1)S(1)}, bf16[32,6272]{1,0:T(8,128)(2,1)S(1)}, u32[]{:S(2)}, u32[]{:S(2)}) collective-permute-start(bf16[32,6272]{1,0:T(8,128)(2,1)S(1)} %collective-permute-done.5), channel_id=1, source_target_pairs={{0,64},{64,0},{1,65},{65,1},{2,66},{66,2},{3,67},{67,3},{4,68},{68... | collective-permute-start | bytes 1204232 | tf_op jit(solution)/shard_map/gather_core/ppermute | solution.py:42
  43.8 4.2 %collective-permute-start.8 = (bf16[32,6272]{1,0:T(8,128)(2,1)S(1)}, bf16[32,6272]{1,0:T(8,128)(2,1)S(1)}, u32[]{:S(2)}, u32[]{:S(2)}) collective-permute-start(bf16[32,6272]{1,0:T(8,128)(2,1)S(1)} %collective-permute-done.4), channel_id=1, source_target_pairs={{0,64},{64,0},{1,65},{65,1},{2,66},{66,2},{3,67},{67,3},{4,68},{68... | collective-permute-start | bytes 1204232 | tf_op jit(solution)/shard_map/gather_core/ppermute | solution.py:42
  46.0 1.9 %collective-permute-start.7 = (bf16[32,6272]{1,0:T(8,128)(2,1)S(1)}, bf16[32,6272]{1,0:T(8,128)(2,1)S(1)}, u32[]{:S(2)}, u32[]{:S(2)}) collective-permute-start(bf16[32,6272]{1,0:T(8,128)(2,1)S(1)} %collective-permute-done.3), channel_id=1, source_target_pairs={{0,64},{64,0},{1,65},{65,1},{2,66},{66,2},{3,67},{67,3},{4,68},{68... | collective-permute-start | bytes 1204232 | tf_op jit(solution)/shard_map/gather_core/ppermute | solution.py:42
  46.0 2.0 %copy-start = (bf16[1,3072,128]{2,1,0:T(8,128)(2,1)S(1)}, bf16[1,3072,128]{2,1,0:T(8,128)(2,1)}, u32[]{:S(2)}) copy-start(bf16[1,3072,128]{2,1,0:T(8,128)(2,1)} %param.11) | copy-start | bytes 2359300
  46.0 2.0 %copy-start.1 = (bf16[1,3072,128]{2,1,0:T(8,128)(2,1)S(1)}, bf16[1,3072,128]{2,1,0:T(8,128)(2,1)}, u32[]{:S(2)}) copy-start(bf16[1,3072,128]{2,1,0:T(8,128)(2,1)} %param.12) | copy-start | bytes 2359300
  46.0 2.0 %copy-start.2 = (bf16[1,128,3072]{2,1,0:T(8,128)(2,1)S(1)}, bf16[1,128,3072]{2,1,0:T(8,128)(2,1)}, u32[]{:S(2)}) copy-start(bf16[1,128,3072]{2,1,0:T(8,128)(2,1)} %param.13) | copy-start | bytes 2359300
  49.6 3.6 %collective-permute-start.10 = (bf16[128,6144]{1,0:T(8,128)(2,1)S(1)}, bf16[128,6144]{1,0:T(8,128)(2,1)S(1)}, u32[]{:S(2)}, u32[]{:S(2)}) collective-permute-start(bf16[128,6144]{1,0:T(8,128)(2,1)S(1)} %get-tuple-element.13), channel_id=1, source_target_pairs={{0,64},{64,0},{1,65},{65,1},{2,66},{66,2},{3,67},{67,3},{4,68},{68... | collective-permute-start | bytes 4718600 | tf_op jit(solution)/shard_map/experts/ppermute | solution.py:42
  55.7 12.4 %collective-permute-start.11 = (bf16[32,6144]{1,0:T(8,128)(2,1)S(1)}, bf16[32,6144]{1,0:T(8,128)(2,1)S(1)}, u32[]{:S(2)}, u32[]{:S(2)}) collective-permute-start(bf16[32,6144]{1,0:T(8,128)(2,1)S(1)} %get-tuple-element.23), channel_id=1, source_target_pairs={{0,16},{1,17},{2,18},{3,19},{4,20},{5,21},{6,22},{7,23},{16,32},{1... | collective-permute-start | bytes 1179656 | tf_op jit(solution)/shard_map/reduce_heavy/ppermute | solution.py:34
  55.7 12.3 %collective-permute-start.13 = (bf16[32,6144]{1,0:T(8,128)(2,1)S(1)}, bf16[32,6144]{1,0:T(8,128)(2,1)S(1)}, u32[]{:S(2)}, u32[]{:S(2)}) collective-permute-start(bf16[32,6144]{1,0:T(8,128)(2,1)S(1)} %get-tuple-element.24), channel_id=1, source_target_pairs={{0,48},{1,49},{2,50},{3,51},{4,52},{5,53},{6,54},{7,55},{16,0},{17... | collective-permute-start | bytes 1179656 | tf_op jit(solution)/shard_map/reduce_heavy/ppermute | solution.py:34
  58.4 9.7 %collective-permute-start.12 = (bf16[32,6144]{1,0:T(8,128)(2,1)S(1)}, bf16[32,6144]{1,0:T(8,128)(2,1)S(1)}, u32[]{:S(2)}, u32[]{:S(2)}) collective-permute-start(bf16[32,6144]{1,0:T(8,128)(2,1)S(1)} %get-tuple-element.25), channel_id=1, source_target_pairs={{0,32},{1,33},{2,34},{3,35},{4,36},{5,37},{6,38},{7,39},{16,48},{1... | collective-permute-start | bytes 1179656 | tf_op jit(solution)/shard_map/reduce_heavy/ppermute | solution.py:34
  68.3 3.5 %collective-permute-start.16 = (bf16[8,6144]{1,0:T(8,128)(2,1)S(1)}, bf16[8,6144]{1,0:T(8,128)(2,1)S(1)}, u32[]{:S(2)}, u32[]{:S(2)}) collective-permute-start(bf16[8,6144]{1,0:T(8,128)(2,1)S(1)} %get-tuple-element.26), channel_id=1, source_target_pairs={{0,136},{1,137},{2,138},{3,139},{4,140},{5,141},{6,142},{7,143},{1... | collective-permute-start | bytes 294920 | tf_op jit(solution)/shard_map/reduce_light/ppermute | solution.py:34
  69.8 5.0 %collective-permute-start.15 = (bf16[8,6144]{1,0:T(8,128)(2,1)S(1)}, bf16[8,6144]{1,0:T(8,128)(2,1)S(1)}, u32[]{:S(2)}, u32[]{:S(2)}) collective-permute-start(bf16[8,6144]{1,0:T(8,128)(2,1)S(1)} %get-tuple-element.27), channel_id=1, source_target_pairs={{0,128},{1,129},{2,130},{3,131},{4,132},{5,133},{6,134},{7,135},{1... | collective-permute-start | bytes 294920 | tf_op jit(solution)/shard_map/reduce_light/ppermute | solution.py:34
  70.8 5.4 %collective-permute-start.14 = (bf16[8,6144]{1,0:T(8,128)(2,1)S(1)}, bf16[8,6144]{1,0:T(8,128)(2,1)}, u32[]{:S(2)}, u32[]{:S(2)}) collective-permute-start(bf16[8,6144]{1,0:T(8,128)(2,1)S(1)} %get-tuple-element.28), channel_id=1, source_target_pairs={{0,8},{1,9},{2,10},{3,11},{4,12},{5,13},{6,14},{7,15},{16,24},{17,... | collective-permute-start | bytes 294920 | tf_op jit(solution)/shard_map/reduce_light/ppermute | solution.py:34
  71.8 4.4 %copy-start.3 = (bf16[8,6144]{1,0:T(8,128)(2,1)}, bf16[8,6144]{1,0:T(8,128)(2,1)S(1)}, u32[]{:S(2)}) copy-start(bf16[8,6144]{1,0:T(8,128)(2,1)S(1)} %collective-permute-done.16.three) | copy-start | bytes 294916
  74.8 0.6 copy-start.4
  78.1 11.0 %all-to-all-start.1 = ((bf16[8,2,3072]{2,1,0:T(2,128)(2,1)}), bf16[8,2,3072]{2,1,0:T(2,128)(2,1)S(1)}, u32[]{:S(2)}, u32[]{:S(2)}) async-start(bf16[8,2,3072]{2,1,0:T(2,128)(2,1)} %summed_pairs.1), calls=%async_computation.1 | async-start | bytes 196608 | tf_op jit(solution)/shard_map/reduce_z/all_to_all | solution.py:46

commit v4 on v3

v4 whole, which is shorter than its diff:
```python
import jax
import jax.numpy as jnp
from jax import lax
from jax.experimental import pallas as pl
from jax.experimental.pallas import tpu as pltpu
from jax.sharding import Mesh, PartitionSpec as P

NX_HI, NCORE, NY, NX_LO, NZ, RING = 2, 2, 4, 2, 8, 4
AXES = ("x_hi", "core", "y", "x_lo", "z")
EP, TP = ("x_hi", "core"), ("y", "x_lo", "z")
D, PAD, UNITS = 3072, 128, 128
F32, BF16 = jnp.float32, jnp.bfloat16
VMEM = pl.BlockSpec(memory_space=pltpu.VMEM)
SMEM = pl.BlockSpec(memory_space=pltpu.SMEM)


def grant(mebibytes):
    return pltpu.CompilerParams(vmem_limit_bytes=mebibytes << 20)


def flat(x, core, y, z):
    return (((x // 2) * NCORE + core) * NY + y) * NX_LO * NZ + (x % 2) * NZ + z


def pairs(stage, kind):
    mate = (lambda p: p ^ 1) if kind == "low" else (lambda p: 3 - p)
    out = []
    for x in range(RING):
        for core in range(NCORE):
            for y in range(RING):
                along_x = (stage == "light") == (core == 0)
                tx, ty = (mate(x), y) if along_x else (x, mate(y))
                out += [(flat(x, core, y, z), flat(tx, core, ty, z)) for z in range(NZ)]
    return out


def mated(value, stage, kind):
    return lax.ppermute(value, AXES, pairs(stage, kind))


def swapped(value):
    return lax.ppermute(value, "core", [(0, 1), (1, 0)])


def exchanged(value, axis):
    return lax.all_to_all(value, axis, 0, 0, tiled=True)


def dot(left, right, left_dim, right_dim):
    return lax.dot_general(
        left, right, (((left_dim,), (right_dim,)), ((), ())), preferred_element_type=F32
    )


def row_kernel(tokens, cotangent, routes, weights, out):
    lane = lax.broadcasted_iota(jnp.int32, (1, PAD), 1)
    r, w = routes[...], weights[...].astype(F32)
    gates = jnp.where(r[:, :1] == lane, w[:, :1], 0.0) + jnp.where(r[:, 1:] == lane, w[:, 1:], 0.0)
    first = jnp.concatenate([tokens[...].astype(F32), gates], axis=1)
    second = jnp.concatenate([cotangent[...].astype(F32), jnp.zeros((1, PAD), F32)], axis=1)
    both = jnp.concatenate([first, second], axis=0).astype(BF16)
    for i in range(NZ):
        out[i] = both


def copies_of_row(tokens, cotangent, routes, gate_weights):
    return pl.pallas_call(
        row_kernel,
        out_shape=jax.ShapeDtypeStruct((NZ, 2, D + PAD), BF16),
        out_specs=VMEM,
        name="copies_of_row",
    )(tokens, cotangent, routes, gate_weights)


def other_order(value):
    blocks = []
    for k in range(RING * RING):
        h1, h0, l1, l0 = (k >> 3) & 1, (k >> 2) & 1, (k >> 1) & 1, k & 1
        at = (h0 * 8 + h1 * 4 + l0 * 2 + l1) * NZ
        blocks.append(value[at : at + NZ])
    return jnp.concatenate(blocks, axis=0)


def expert_kernel(group, rows, cot, gate_slice, up_slice, down_slice, out, grad, acts):
    lane = lax.broadcasted_iota(jnp.int32, (rows.shape[0], PAD), 1)
    gates = jnp.where(lane == group[0], rows[:, D:].astype(F32), 0.0)
    column = jnp.sum(gates, axis=1, keepdims=True)
    x = rows[:, :D]
    gate_pre = dot(x, gate_slice[...], 1, 0)
    up_pre = dot(x, up_slice[...], 1, 0)
    grad_act = other_order(dot(cot[...], down_slice[...], 1, 1)) * column
    sigmoid = jax.nn.sigmoid(gate_pre)
    silu = gate_pre * sigmoid
    hidden = silu * up_pre * column
    grad_gpre = grad_act * up_pre * (sigmoid * (1.0 + gate_pre * (1.0 - sigmoid)))
    grad_upre = grad_act * silu
    acts[:, :UNITS] = other_order(hidden).astype(BF16)
    acts[:, UNITS : 2 * UNITS] = grad_gpre.astype(BF16)
    acts[:, 2 * UNITS :] = grad_upre.astype(BF16)
    out[...] = dot(hidden.astype(BF16), down_slice[...], 1, 0).astype(out.dtype)
    grad_rows = dot(other_order(grad_gpre).astype(BF16), gate_slice[...], 1, 1)
    grad_rows += dot(other_order(grad_upre).astype(BF16), up_slice[...], 1, 1)
    grad[...] = grad_rows.astype(grad.dtype)


def expert_terms(group, rows, cot, gate_slice, up_slice, down_slice, kind):
    n = rows.shape[0]
    return pl.pallas_call(
        expert_kernel,
        out_shape=(
            jax.ShapeDtypeStruct((n, D), kind),
            jax.ShapeDtypeStruct((n, D), kind),
            jax.ShapeDtypeStruct((n, 3 * UNITS), BF16),
        ),
        in_specs=[SMEM] + [VMEM] * 5,
        out_specs=(VMEM,) * 3,
        compiler_params=grant(16),
        cost_estimate=pl.CostEstimate(
            flops=12 * n * D * UNITS, transcendentals=n * UNITS, bytes_accessed=4 * n * D + 6 * D * UNITS
        ),
        name="expert_terms",
    )(group, rows, cot, gate_slice, up_slice, down_slice)


def weight_kernel(far, near, cot_far, cot_near, acts_far, acts_near, grad_g, grad_u, grad_d):
    u = UNITS
    for grad, at in ((grad_g, u), (grad_u, 2 * u)):
        total = dot(far[:, :D], acts_far[:, at : at + u], 0, 0)
        total += dot(near[:, :D], acts_near[:, at : at + u], 0, 0)
        grad[0] = total.astype(BF16)
    total = dot(acts_far[:, :u], cot_far[...], 0, 0) + dot(acts_near[:, :u], cot_near[...], 0, 0)
    grad_d[0] = total.astype(BF16)


def weight_grads(*operands):
    n = 2 * operands[0].shape[0]
    return pl.pallas_call(
        weight_kernel,
        out_shape=(
            jax.ShapeDtypeStruct((1, D, UNITS), BF16),
            jax.ShapeDtypeStruct((1, D, UNITS), BF16),
            jax.ShapeDtypeStruct((1, UNITS, D), BF16),
        ),
        in_specs=[VMEM] * 6,
        out_specs=(VMEM,) * 3,
        compiler_params=grant(16),
        cost_estimate=pl.CostEstimate(
            flops=6 * n * D * UNITS, transcendentals=0, bytes_accessed=4 * n * D + 6 * D * UNITS
        ),
        name="weight_grads",
    )(*operands)


def last_kernel(own_a, got_a, own_b, got_b, out):
    a = own_a[...] + got_a[...].astype(F32)
    b = own_b[...] + got_b[...].astype(F32)
    for i in range(NZ):
        out[i] = jnp.concatenate([a[i : i + 1], b[i : i + 1]], axis=0).astype(BF16)


def summed_pairs(*operands):
    return pl.pallas_call(
        last_kernel,
        out_shape=jax.ShapeDtypeStruct((NZ, 2, D), BF16),
        in_specs=[VMEM] * 4,
        out_specs=VMEM,
        compiler_params=grant(1),
        name="summed_pairs",
    )(*operands)


def doubled(a, b, stage):
    for kind_a, kind_b in (("low", "high"), ("high", "low")):
        got_a, got_b = mated(a, stage, kind_a), mated(b, stage, kind_b)
        a, b = jnp.concatenate([a, got_a], axis=0), jnp.concatenate([b, got_b], axis=0)
    return a, b


def halves(value):
    n = value.shape[0] // 2
    return value[:n], value[n:].astype(BF16)


def on_device(tokens, cotangent, routes, gate_weights, w_gate, w_up, w_down):
    slices = (w_gate[0], w_up[0], w_down[0])
    group = lax.axis_index(EP).astype(jnp.int32).reshape(1)
    with jax.named_scope("gather_z"):
        rows = exchanged(copies_of_row(tokens, cotangent, routes, gate_weights), "z")
        a, b = rows[:, 0], rows[:, 1, :D]
    with jax.named_scope("gather_light"):
        a, b = doubled(a, b, "light")
    with jax.named_scope("gather_heavy"):
        a, b = doubled(a, b, "heavy")
    with jax.named_scope("gather_core"):
        n = a.shape[0] // 2
        far_a = jnp.concatenate([swapped(a[:n]), swapped(a[n:])], axis=0)
        far_b = jnp.concatenate([swapped(b[:n]), swapped(b[n:])], axis=0)
    with jax.named_scope("experts"):
        far_out, far_grad, far_acts = expert_terms(group, far_a, far_b, *slices, BF16)
        other_out, other_grad = swapped(far_out), swapped(far_grad)
        near_out, near_grad, near_acts = expert_terms(group, a, b, *slices, F32)
    with jax.named_scope("weights"):
        grad_g, grad_u, grad_d = weight_grads(far_a, a, far_b, b, far_acts, near_acts)
    out, grad = near_out + other_out.astype(F32), near_grad + other_grad.astype(F32)
    steps = [(stage, kind) for stage in ("heavy", "light") for kind in ("high", "low")]
    for stage, kind in steps:
        with jax.named_scope("reduce_" + stage):
            (out, send_out), (grad, send_grad) = halves(out), halves(grad)
            got_out = mated(send_out, stage, kind)
            got_grad = mated(send_grad, stage, "low" if kind == "high" else "high")
            if (stage, kind) != steps[-1]:
                out, grad = out + got_out.astype(F32), grad + got_grad.astype(F32)
    with jax.named_scope("reduce_z"):
        got = exchanged(summed_pairs(out, got_out, grad, got_grad), "z")
        total = sum(got[i].astype(F32) for i in range(NZ)).astype(BF16)
    return total[:1], total[1:], grad_g, grad_u, grad_d


def solution(mesh):
    fine = Mesh(mesh.devices.reshape(NX_HI, NCORE, NY, NX_LO, NZ), AXES)
    rows, columns, units = P(EP + TP, None), P(EP, None, TP), P(EP, TP, None)
    return jax.shard_map(
        on_device,
        mesh=fine,
        in_specs=(rows, rows, rows, rows, columns, columns, units),
        out_specs=(rows, rows, columns, columns, units),
        check_vma=False,
    )
```

time: 91.5 us -> 95.8 us (1.047)
  the two profiles are of different devices: /device:TPU:1 before, /device:TPU:32 now
where the time goes in v4:
time: 95.8 us; the launch traced here: 95.4 us
  waiting for transfers between devices  50.5 us (53%)
  starting transfers between devices  34.4 us (36%)
  Pallas kernels  7.57 us (8%)
  local copies, waits for them, and re-layouts  1.22 us (1%)
    ppermute x16, waiting for transfers between devices, mated(): return lax.ppermute(value, AXES, pairs(stage, kind))  36.6 us
    ppermute x16, starting transfers between devices, mated(): return lax.ppermute(value, AXES, pairs(stage, kind))  20.7 us
    all_to_all x2, starting transfers between devices, exchanged(): return lax.all_to_all(value, axis, 0, 0, tiled=True)  13 us
    all_to_all x2, waiting for transfers between devices, exchanged(): return lax.all_to_all(value, axis, 0, 0, tiled=True)  12.1 us
    pallas_call x2, Pallas kernels, expert_terms(): pl.pallas_call(expert_kernel, out_shape=(jax.ShapeDtypeStruct((n, D), kin...  2.93 us
    pallas_call x1, Pallas kernels, weight_grads(): pl.pallas_call(weight_kernel, out_shape=(jax.ShapeDtypeStruct((1, D, UNIT...  2.42 us
  transfers between devices with their start and end apart: 24, of which 20 were waited for; matrix products, arithmetic and copies ran while one was open for 1% of the time, Pallas kernels for 4%

profile of v4, /device:TPU:32, one launch (start us, length us, event | category | flops | bytes accessed | tf_op | source)
XLA Modules:
  0.0 95.4 jit_solution(7975475059459015389)
XLA Ops:
  2.1 8.6 %all-to-all-start = ((bf16[8,2,3200]{2,1,0:T(2,128)(2,1)}), bf16[8,2,3200]{2,1,0:T(2,128)(2,1)S(1)}, u32[]{:S(2)}, u32[]{:S(2)}) async-start(bf16[8,2,3200]{2,1,0:T(2,128)(2,1)} %copies_of_row.1), calls=%async_computation | async-start | bytes 204800 | tf_op jit(solution)/shard_map/gather_z/all_to_all | solution.py:46
  10.7 7.2 %all-to-all-done = bf16[8,2,3200]{2,1,0:T(2,128)(2,1)S(1)} async-done(((bf16[8,2,3200]{2,1,0:T(2,128)(2,1)}), bf16[8,2,3200]{2,1,0:T(2,128)(2,1)S(1)}, u32[]{:S(2)}, u32[]{:S(2)}) %all-to-all-start) | async-done | bytes 102432 | tf_op jit(solution)/shard_map/gather_z/all_to_all | solution.py:46
  18.0 2.8 %collective-permute-start.4 = (bf16[8,3072]{1,0:T(8,128)(2,1)S(1)}, bf16[8,3072]{1,0:T(8,128)(2,1)S(1)}, u32[]{:S(2)}, u32[]{:S(2)}) collective-permute-start(bf16[8,3072]{1,0:T(8,128)(2,1)S(1)} %get-tuple-element.24), channel_id=1, source_target_pairs={{0,136},{1,137},{2,138},{3,139},{4,140},{5,141},{6,142},{7,143},{1... | collective-permute-start | bytes 147464 | tf_op jit(solution)/shard_map/gather_light/ppermute | solution.py:38
  21.1 2.2 %collective-permute-done.4 = bf16[8,3072]{1,0:T(8,128)(2,1)S(1)} collective-permute-done((bf16[8,3072]{1,0:T(8,128)(2,1)S(1)}, bf16[8,3072]{1,0:T(8,128)(2,1)S(1)}, u32[]{:S(2)}, u32[]{:S(2)}) %collective-permute-start.4) | collective-permute-done | bytes 49184 | tf_op jit(solution)/shard_map/gather_light/ppermute | solution.py:38
  26.4 1.7 %collective-permute-done.5 = bf16[16,3072]{1,0:T(8,128)(2,1)S(1)} collective-permute-done((bf16[16,3072]{1,0:T(8,128)(2,1)S(1)}, bf16[16,3072]{1,0:T(8,128)(2,1)S(1)}, u32[]{:S(2)}, u32[]{:S(2)}) %collective-permute-start.5) | collective-permute-done | bytes 98336 | tf_op jit(solution)/shard_map/gather_light/ppermute | solution.py:38
  28.1 3.1 %collective-permute-start.6 = (bf16[32,3072]{1,0:T(8,128)(2,1)S(1)}, bf16[32,3072]{1,0:T(8,128)(2,1)S(1)}, u32[]{:S(2)}, u32[]{:S(2)}) collective-permute-start(bf16[32,3072]{1,0:T(8,128)(2,1)S(1)} %pad_maximum_fusion.3), channel_id=1, source_target_pairs={{0,48},{1,49},{2,50},{3,51},{4,52},{5,53},{6,54},{7,55},{16,32},{1... | collective-permute-start | bytes 589832 | tf_op jit(solution)/shard_map/gather_heavy/ppermute | solution.py:38
  32.7 2.4 %collective-permute-done.6 = bf16[32,3072]{1,0:T(8,128)(2,1)S(1)} collective-permute-done((bf16[32,3072]{1,0:T(8,128)(2,1)S(1)}, bf16[32,3072]{1,0:T(8,128)(2,1)S(1)}, u32[]{:S(2)}, u32[]{:S(2)}) %collective-permute-start.6) | collective-permute-done | bytes 196640 | tf_op jit(solution)/shard_map/gather_heavy/ppermute | solution.py:38
  35.6 2.1 %collective-permute-done.2 = bf16[32,3200]{1,0:T(8,128)(2,1)S(1)} collective-permute-done((bf16[32,3200]{1,0:T(8,128)(2,1)S(1)}, bf16[32,3200]{1,0:T(8,128)(2,1)S(1)}, u32[]{:S(2)}, u32[]{:S(2)}) %collective-permute-start.2) | collective-permute-done | bytes 204832 | tf_op jit(solution)/shard_map/gather_heavy/ppermute | solution.py:38
  37.7 3.0 %collective-permute-start.3 = (bf16[64,3200]{1,0:T(8,128)(2,1)S(1)}, bf16[64,3200]{1,0:T(8,128)(2,1)S(1)}, u32[]{:S(2)}, u32[]{:S(2)}) collective-permute-start(bf16[64,3200]{1,0:T(8,128)(2,1)S(1)} %pad_maximum_fusion), channel_id=1, source_target_pairs={{0,48},{1,49},{2,50},{3,51},{4,52},{5,53},{6,54},{7,55},{16,32},{1... | collective-permute-start | bytes 1228808 | tf_op jit(solution)/shard_map/gather_heavy/ppermute | solution.py:38
  40.8 2.2 %collective-permute-done.7 = bf16[64,3072]{1,0:T(8,128)(2,1)S(1)} collective-permute-done((bf16[64,3072]{1,0:T(8,128)(2,1)S(1)}, bf16[64,3072]{1,0:T(8,128)(2,1)S(1)}, u32[]{:S(2)}, u32[]{:S(2)}) %collective-permute-start.7) | collective-permute-done | bytes 393248 | tf_op jit(solution)/shard_map/gather_heavy/ppermute | solution.py:38
  43.0 3.9 %collective-permute-done.3 = bf16[64,3200]{1,0:T(8,128)(2,1)S(1)} collective-permute-done((bf16[64,3200]{1,0:T(8,128)(2,1)S(1)}, bf16[64,3200]{1,0:T(8,128)(2,1)S(1)}, u32[]{:S(2)}, u32[]{:S(2)}) %collective-permute-start.3) | collective-permute-done | bytes 409632 | tf_op jit(solution)/shard_map/gather_heavy/ppermute | solution.py:38
  47.0 1.7 %collective-permute-done.9 = bf16[64,3200]{1,0:T(8,128)(2,1)S(1)} collective-permute-done((bf16[64,3200]{1,0:T(8,128)(2,1)S(1)}, bf16[64,3200]{1,0:T(8,128)(2,1)S(1)}, u32[]{:S(2)}, u32[]{:S(2)}) %collective-permute-start.9) | collective-permute-done | bytes 409632 | tf_op jit(solution)/shard_map/gather_core/ppermute | solution.py:42
  52.8 3.2 %collective-permute-start.13 = (bf16[64,3072]{1,0:T(8,128)(2,1)S(1)}, bf16[64,3072]{1,0:T(8,128)(2,1)S(1)}, u32[]{:S(2)}, u32[]{:S(2)}) collective-permute-start(bf16[64,3072]{1,0:T(8,128)(2,1)S(1)} %slice.175), channel_id=1, source_target_pairs={{0,48},{1,49},{2,50},{3,51},{4,52},{5,53},{6,54},{7,55},{16,32},{1... | collective-permute-start | bytes 1179656 | tf_op jit(solution)/shard_map/reduce_heavy/ppermute | solution.py:38
  56.3 5.7 %collective-permute-done.13 = bf16[64,3072]{1,0:T(8,128)(2,1)S(1)} collective-permute-done((bf16[64,3072]{1,0:T(8,128)(2,1)S(1)}, bf16[64,3072]{1,0:T(8,128)(2,1)S(1)}, u32[]{:S(2)}, u32[]{:S(2)}) %collective-permute-start.13) | collective-permute-done | bytes 393248 | tf_op jit(solution)/shard_map/reduce_heavy/ppermute | solution.py:38
  62.3 1.8 %collective-permute-done.18 = bf16[64,3072]{1,0:T(8,128)(2,1)S(1)} collective-permute-done((bf16[64,3072]{1,0:T(8,128)(2,1)S(1)}, bf16[64,3072]{1,0:T(8,128)(2,1)S(1)}, u32[]{:S(2)}, u32[]{:S(2)}) %collective-permute-start.18) | collective-permute-done | bytes 393248 | tf_op jit(solution)/shard_map/reduce_heavy/ppermute | solution.py:38
  65.4 2.5 %collective-permute-done.14 = bf16[32,3072]{1,0:T(8,128)(2,1)S(1)} collective-permute-done((bf16[32,3072]{1,0:T(8,128)(2,1)S(1)}, bf16[32,3072]{1,0:T(8,128)(2,1)S(1)}, u32[]{:S(2)}, u32[]{:S(2)}) %collective-permute-start.14) | collective-permute-done | bytes 196640 | tf_op jit(solution)/shard_map/reduce_heavy/ppermute | solution.py:38
  68.0 2.3 %collective-permute-start.15 = (bf16[16,3072]{1,0:T(8,128)(2,1)S(1)}, bf16[16,3072]{1,0:T(8,128)(2,1)S(1)}, u32[]{:S(2)}, u32[]{:S(2)}) collective-permute-start(bf16[16,3072]{1,0:T(8,128)(2,1)S(1)} %slice.179), channel_id=1, source_target_pairs={{0,136},{1,137},{2,138},{3,139},{4,140},{5,141},{6,142},{7,143},{1... | collective-permute-start | bytes 294920 | tf_op jit(solution)/shard_map/reduce_light/ppermute | solution.py:38
  70.3 1.7 %collective-permute-done.19 = bf16[32,3072]{1,0:T(8,128)(2,1)S(1)} collective-permute-done((bf16[32,3072]{1,0:T(8,128)(2,1)S(1)}, bf16[32,3072]{1,0:T(8,128)(2,1)S(1)}, u32[]{:S(2)}, u32[]{:S(2)}) %collective-permute-start.19) | collective-permute-done | bytes 196640 | tf_op jit(solution)/shard_map/reduce_heavy/ppermute | solution.py:38
  72.2 1.8 %collective-permute-done.15 = bf16[16,3072]{1,0:T(8,128)(2,1)S(1)} collective-permute-done((bf16[16,3072]{1,0:T(8,128)(2,1)S(1)}, bf16[16,3072]{1,0:T(8,128)(2,1)S(1)}, u32[]{:S(2)}, u32[]{:S(2)}) %collective-permute-start.15) | collective-permute-done | bytes 98336 | tf_op jit(solution)/shard_map/reduce_light/ppermute | solution.py:38
  74.3 2.5 %collective-permute-done.20 = bf16[16,3072]{1,0:T(8,128)(2,1)S(1)} collective-permute-done((bf16[16,3072]{1,0:T(8,128)(2,1)S(1)}, bf16[16,3072]{1,0:T(8,128)(2,1)S(1)}, u32[]{:S(2)}, u32[]{:S(2)}) %collective-permute-start.20) | collective-permute-done | bytes 98336 | tf_op jit(solution)/shard_map/reduce_light/ppermute | solution.py:38
  78.1 4.1 %collective-permute-done.21.got_b = bf16[8,3072]{1,0:T(8,128)(2,1)S(1)} collective-permute-done((bf16[8,3072]{1,0:T(8,128)(2,1)S(1)}, bf16[8,3072]{1,0:T(8,128)(2,1)S(1)}, u32[]{:S(2)}, u32[]{:S(2)}) %collective-permute-start.21) | collective-permute-done | bytes 49184 | tf_op jit(solution)/shard_map/reduce_light/ppermute | solution.py:38
  83.0 4.4 %all-to-all-start.1 = ((bf16[8,2,3072]{2,1,0:T(2,128)(2,1)}), bf16[8,2,3072]{2,1,0:T(2,128)(2,1)S(1)}, u32[]{:S(2)}, u32[]{:S(2)}) async-start(bf16[8,2,3072]{2,1,0:T(2,128)(2,1)} %summed_pairs.1), calls=%async_computation.1 | async-start | bytes 196608 | tf_op jit(solution)/shard_map/reduce_z/all_to_all | solution.py:46
  87.4 2.4 %weight_grads.1 = (bf16[1,3072,128]{2,1,0:T(8,128)(2,1)}, bf16[1,3072,128]{2,1,0:T(8,128)(2,1)}, bf16[1,128,3072]{2,1,0:T(8,128)(2,1)}) custom-call(bf16[128,3200]{1,0:T(8,128)(2,1)S(1)} %constant_dynamic-update-slice_fusion.10.rows.far, bf16[128,3200]{1,0:T(8,128)(2,1)S(1)} %constant_dynamic-update-slice_fusion.rows.near, ...), custom_call_target="tpu_custom_call" | custom-call | flops 603979776 | bytes 5505024 | tf_op jit(solution)/shard_map/weights/weight_grads/pallas_call | solution.py:137
  89.8 4.9 %all-to-all-done.1 = bf16[8,2,3072]{2,1,0:T(2,128)(2,1)S(1)} async-done(((bf16[8,2,3072]{2,1,0:T(2,128)(2,1)}), bf16[8,2,3072]{2,1,0:T(2,128)(2,1)S(1)}, u32[]{:S(2)}, u32[]{:S(2)}) %all-to-all-start.1) | async-done | bytes 98336 | tf_op jit(solution)/shard_map/reduce_z/all_to_all | solution.py:46
  (76 shorter events, 16.3 us)
Async XLA Ops:
  2.1 15.7 %all-to-all-start = ((bf16[8,2,3200]{2,1,0:T(2,128)(2,1)}), bf16[8,2,3200]{2,1,0:T(2,128)(2,1)S(1)}, u32[]{:S(2)}, u32[]{:S(2)}) async-start(bf16[8,2,3200]{2,1,0:T(2,128)(2,1)} %copies_of_row.1), calls=%async_computation | async-start | bytes 204800 | tf_op jit(solution)/shard_map/gather_z/all_to_all | solution.py:46
  18.0 5.4 %collective-permute-start.4 = (bf16[8,3072]{1,0:T(8,128)(2,1)S(1)}, bf16[8,3072]{1,0:T(8,128)(2,1)S(1)}, u32[]{:S(2)}, u32[]{:S(2)}) collective-permute-start(bf16[8,3072]{1,0:T(8,128)(2,1)S(1)} %get-tuple-element.24), channel_id=1, source_target_pairs={{0,136},{1,137},{2,138},{3,139},{4,140},{5,141},{6,142},{7,143},{1... | collective-permute-start | bytes 147464 | tf_op jit(solution)/shard_map/gather_light/ppermute | solution.py:38
  20.8 4.2 %collective-permute-start = (bf16[8,3200]{1,0:T(8,128)(2,1)S(1)}, bf16[8,3200]{1,0:T(8,128)(2,1)S(1)}, u32[]{:S(2)}, u32[]{:S(2)}) collective-permute-start(bf16[8,3200]{1,0:T(8,128)(2,1)S(1)} %get-tuple-element.26), channel_id=1, source_target_pairs={{0,8},{1,9},{2,10},{3,11},{4,12},{5,13},{6,14},{7,15},{16,24},{17,... | collective-permute-start | bytes 153608 | tf_op jit(solution)/shard_map/gather_light/ppermute | solution.py:38
  23.4 4.7 %collective-permute-start.5 = (bf16[16,3072]{1,0:T(8,128)(2,1)S(1)}, bf16[16,3072]{1,0:T(8,128)(2,1)S(1)}, u32[]{:S(2)}, u32[]{:S(2)}) collective-permute-start(bf16[16,3072]{1,0:T(8,128)(2,1)S(1)} %pad_maximum_fusion.5), channel_id=1, source_target_pairs={{0,8},{1,9},{2,10},{3,11},{4,12},{5,13},{6,14},{7,15},{16,24},{17,... | collective-permute-start | bytes 294920 | tf_op jit(solution)/shard_map/gather_light/ppermute | solution.py:38
  25.0 6.7 %collective-permute-start.1 = (bf16[16,3200]{1,0:T(8,128)(2,1)S(1)}, bf16[16,3200]{1,0:T(8,128)(2,1)S(1)}, u32[]{:S(2)}, u32[]{:S(2)}) collective-permute-start(bf16[16,3200]{1,0:T(8,128)(2,1)S(1)} %pad_maximum_fusion.4), channel_id=1, source_target_pairs={{0,136},{1,137},{2,138},{3,139},{4,140},{5,141},{6,142},{7,143},{1... | collective-permute-start | bytes 307208 | tf_op jit(solution)/shard_map/gather_light/ppermute | solution.py:38
  28.1 7.0 %collective-permute-start.6 = (bf16[32,3072]{1,0:T(8,128)(2,1)S(1)}, bf16[32,3072]{1,0:T(8,128)(2,1)S(1)}, u32[]{:S(2)}, u32[]{:S(2)}) collective-permute-start(bf16[32,3072]{1,0:T(8,128)(2,1)S(1)} %pad_maximum_fusion.3), channel_id=1, source_target_pairs={{0,48},{1,49},{2,50},{3,51},{4,52},{5,53},{6,54},{7,55},{16,32},{1... | collective-permute-start | bytes 589832 | tf_op jit(solution)/shard_map/gather_heavy/ppermute | solution.py:38
  31.8 5.8 %collective-permute-start.2 = (bf16[32,3200]{1,0:T(8,128)(2,1)S(1)}, bf16[32,3200]{1,0:T(8,128)(2,1)S(1)}, u32[]{:S(2)}, u32[]{:S(2)}) collective-permute-start(bf16[32,3200]{1,0:T(8,128)(2,1)S(1)} %pad_maximum_fusion.2), channel_id=1, source_target_pairs={{0,16},{1,17},{2,18},{3,19},{4,20},{5,21},{6,22},{7,23},{16,0},{17... | collective-permute-start | bytes 614408 | tf_op jit(solution)/shard_map/gather_heavy/ppermute | solution.py:38
  35.1 7.9 %collective-permute-start.7 = (bf16[64,3072]{1,0:T(8,128)(2,1)S(1)}, bf16[64,3072]{1,0:T(8,128)(2,1)S(1)}, u32[]{:S(2)}, u32[]{:S(2)}) collective-permute-start(bf16[64,3072]{1,0:T(8,128)(2,1)S(1)} %pad_maximum_fusion.1), channel_id=1, source_target_pairs={{0,16},{1,17},{2,18},{3,19},{4,20},{5,21},{6,22},{7,23},{16,0},{17... | collective-permute-start | bytes 1179656 | tf_op jit(solution)/shard_map/gather_heavy/ppermute | solution.py:38
  35.5 7.4 %collective-permute-start.10 = (bf16[64,3072]{1,0:T(8,128)(2,1)S(1)}, bf16[64,3072]{1,0:T(8,128)(2,1)S(1)}, u32[]{:S(2)}, u32[]{:S(2)}) collective-permute-start(bf16[64,3072]{1,0:T(8,128)(2,1)S(1)} %pad_maximum_fusion.1), channel_id=1, source_target_pairs={{0,64},{64,0},{1,65},{65,1},{2,66},{66,2},{3,67},{67,3},{4,68},{68... | collective-permute-start | bytes 1179656 | tf_op jit(solution)/shard_map/gather_core/ppermute | solution.py:42
  37.7 9.2 %collective-permute-start.3 = (bf16[64,3200]{1,0:T(8,128)(2,1)S(1)}, bf16[64,3200]{1,0:T(8,128)(2,1)S(1)}, u32[]{:S(2)}, u32[]{:S(2)}) collective-permute-start(bf16[64,3200]{1,0:T(8,128)(2,1)S(1)} %pad_maximum_fusion), channel_id=1, source_target_pairs={{0,48},{1,49},{2,50},{3,51},{4,52},{5,53},{6,54},{7,55},{16,32},{1... | collective-permute-start | bytes 1228808 | tf_op jit(solution)/shard_map/gather_heavy/ppermute | solution.py:38
  40.7 6.2 %collective-permute-start.8 = (bf16[64,3200]{1,0:T(8,128)(2,1)S(1)}, bf16[64,3200]{1,0:T(8,128)(2,1)S(1)}, u32[]{:S(2)}, u32[]{:S(2)}) collective-permute-start(bf16[64,3200]{1,0:T(8,128)(2,1)S(1)} %pad_maximum_fusion), channel_id=1, source_target_pairs={{0,64},{64,0},{1,65},{65,1},{2,66},{66,2},{3,67},{67,3},{4,68},{68... | collective-permute-start | bytes 1228808 | tf_op jit(solution)/shard_map/gather_core/ppermute | solution.py:42
  43.0 4.0 %collective-permute-start.11 = (bf16[64,3072]{1,0:T(8,128)(2,1)S(1)}, bf16[64,3072]{1,0:T(8,128)(2,1)S(1)}, u32[]{:S(2)}, u32[]{:S(2)}) collective-permute-start(bf16[64,3072]{1,0:T(8,128)(2,1)S(1)} %collective-permute-done.7), channel_id=1, source_target_pairs={{0,64},{64,0},{1,65},{65,1},{2,66},{66,2},{3,67},{67,3},{4,68},{68... | collective-permute-start | bytes 1179656 | tf_op jit(solution)/shard_map/gather_core/ppermute | solution.py:42
  46.9 1.7 %collective-permute-start.9 = (bf16[64,3200]{1,0:T(8,128)(2,1)S(1)}, bf16[64,3200]{1,0:T(8,128)(2,1)S(1)}, u32[]{:S(2)}, u32[]{:S(2)}) collective-permute-start(bf16[64,3200]{1,0:T(8,128)(2,1)S(1)} %collective-permute-done.3), channel_id=1, source_target_pairs={{0,64},{64,0},{1,65},{65,1},{2,66},{66,2},{3,67},{67,3},{4,68},{68... | collective-permute-start | bytes 1228808 | tf_op jit(solution)/shard_map/gather_core/ppermute | solution.py:42
  50.2 2.4 %collective-permute-start.12 = (bf16[128,3072]{1,0:T(8,128)(2,1)S(1)}, bf16[128,3072]{1,0:T(8,128)(2,1)S(1)}, u32[]{:S(2)}, u32[]{:S(2)}) collective-permute-start(bf16[128,3072]{1,0:T(8,128)(2,1)S(1)} %get-tuple-element.15), channel_id=1, source_target_pairs={{0,64},{64,0},{1,65},{65,1},{2,66},{66,2},{3,67},{67,3},{4,68},{68... | collective-permute-start | bytes 2359304 | tf_op jit(solution)/shard_map/experts/ppermute | solution.py:42
  50.5 5.5 %collective-permute-start.17 = (bf16[128,3072]{1,0:T(8,128)(2,1)S(1)}, bf16[128,3072]{1,0:T(8,128)(2,1)S(1)}, u32[]{:S(2)}, u32[]{:S(2)}) collective-permute-start(bf16[128,3072]{1,0:T(8,128)(2,1)S(1)} %get-tuple-element.17), channel_id=1, source_target_pairs={{0,64},{64,0},{1,65},{65,1},{2,66},{66,2},{3,67},{67,3},{4,68},{68... | collective-permute-start | bytes 2359304 | tf_op jit(solution)/shard_map/experts/ppermute | solution.py:42
  52.8 9.3 %collective-permute-start.13 = (bf16[64,3072]{1,0:T(8,128)(2,1)S(1)}, bf16[64,3072]{1,0:T(8,128)(2,1)S(1)}, u32[]{:S(2)}, u32[]{:S(2)}) collective-permute-start(bf16[64,3072]{1,0:T(8,128)(2,1)S(1)} %slice.175), channel_id=1, source_target_pairs={{0,48},{1,49},{2,50},{3,51},{4,52},{5,53},{6,54},{7,55},{16,32},{1... | collective-permute-start | bytes 1179656 | tf_op jit(solution)/shard_map/reduce_heavy/ppermute | solution.py:38
  56.2 7.9 %collective-permute-start.18 = (bf16[64,3072]{1,0:T(8,128)(2,1)S(1)}, bf16[64,3072]{1,0:T(8,128)(2,1)S(1)}, u32[]{:S(2)}, u32[]{:S(2)}) collective-permute-start(bf16[64,3072]{1,0:T(8,128)(2,1)S(1)} %slice.174), channel_id=1, source_target_pairs={{0,16},{1,17},{2,18},{3,19},{4,20},{5,21},{6,22},{7,23},{16,0},{17... | collective-permute-start | bytes 1179656 | tf_op jit(solution)/shard_map/reduce_heavy/ppermute | solution.py:38
  62.2 5.8 %collective-permute-start.14 = (bf16[32,3072]{1,0:T(8,128)(2,1)S(1)}, bf16[32,3072]{1,0:T(8,128)(2,1)S(1)}, u32[]{:S(2)}, u32[]{:S(2)}) collective-permute-start(bf16[32,3072]{1,0:T(8,128)(2,1)S(1)} %slice.177), channel_id=1, source_target_pairs={{0,16},{1,17},{2,18},{3,19},{4,20},{5,21},{6,22},{7,23},{16,0},{17... | collective-permute-start | bytes 589832 | tf_op jit(solution)/shard_map/reduce_heavy/ppermute | solution.py:38
  64.2 7.8 %collective-permute-start.19 = (bf16[32,3072]{1,0:T(8,128)(2,1)S(1)}, bf16[32,3072]{1,0:T(8,128)(2,1)S(1)}, u32[]{:S(2)}, u32[]{:S(2)}) collective-permute-start(bf16[32,3072]{1,0:T(8,128)(2,1)S(1)} %slice.176), channel_id=1, source_target_pairs={{0,48},{1,49},{2,50},{3,51},{4,52},{5,53},{6,54},{7,55},{16,32},{1... | collective-permute-start | bytes 589832 | tf_op jit(solution)/shard_map/reduce_heavy/ppermute | solution.py:38
  68.0 5.9 %collective-permute-start.15 = (bf16[16,3072]{1,0:T(8,128)(2,1)S(1)}, bf16[16,3072]{1,0:T(8,128)(2,1)S(1)}, u32[]{:S(2)}, u32[]{:S(2)}) collective-permute-start(bf16[16,3072]{1,0:T(8,128)(2,1)S(1)} %slice.179), channel_id=1, source_target_pairs={{0,136},{1,137},{2,138},{3,139},{4,140},{5,141},{6,142},{7,143},{1... | collective-permute-start | bytes 294920 | tf_op jit(solution)/shard_map/reduce_light/ppermute | solution.py:38
  72.1 4.7 %collective-permute-start.20 = (bf16[16,3072]{1,0:T(8,128)(2,1)S(1)}, bf16[16,3072]{1,0:T(8,128)(2,1)S(1)}, u32[]{:S(2)}, u32[]{:S(2)}) collective-permute-start(bf16[16,3072]{1,0:T(8,128)(2,1)S(1)} %slice.178), channel_id=1, source_target_pairs={{0,8},{1,9},{2,10},{3,11},{4,12},{5,13},{6,14},{7,15},{16,24},{17,... | collective-permute-start | bytes 294920 | tf_op jit(solution)/shard_map/reduce_light/ppermute | solution.py:38
  74.0 4.2 %collective-permute-start.16 = (bf16[8,3072]{1,0:T(8,128)(2,1)S(1)}, bf16[8,3072]{1,0:T(8,128)(2,1)S(1)}, u32[]{:S(2)}, u32[]{:S(2)}) collective-permute-start(bf16[8,3072]{1,0:T(8,128)(2,1)S(1)} %slice.181), channel_id=1, source_target_pairs={{0,8},{1,9},{2,10},{3,11},{4,12},{5,13},{6,14},{7,15},{16,24},{17,... | collective-permute-start | bytes 147464 | tf_op jit(solution)/shard_map/reduce_light/ppermute | solution.py:38
  76.8 5.4 %collective-permute-start.21 = (bf16[8,3072]{1,0:T(8,128)(2,1)S(1)}, bf16[8,3072]{1,0:T(8,128)(2,1)S(1)}, u32[]{:S(2)}, u32[]{:S(2)}) collective-permute-start(bf16[8,3072]{1,0:T(8,128)(2,1)S(1)} %slice.180), channel_id=1, source_target_pairs={{0,136},{1,137},{2,138},{3,139},{4,140},{5,141},{6,142},{7,143},{1... | collective-permute-start | bytes 147464 | tf_op jit(solution)/shard_map/reduce_light/ppermute | solution.py:38
  83.0 11.7 %all-to-all-start.1 = ((bf16[8,2,3072]{2,1,0:T(2,128)(2,1)}), bf16[8,2,3072]{2,1,0:T(2,128)(2,1)S(1)}, u32[]{:S(2)}, u32[]{:S(2)}) async-start(bf16[8,2,3072]{2,1,0:T(2,128)(2,1)} %summed_pairs.1), calls=%async_computation.1 | async-start | bytes 196608 | tf_op jit(solution)/shard_map/reduce_z/all_to_all | solution.py:46
  (3 other events, 23.9 us)

commit v5 on v3

--- a/solution.py
+++ b/solution.py
@@ -12,7 +12,11 @@
 F32, BF16 = jnp.float32, jnp.bfloat16
 VMEM = pl.BlockSpec(memory_space=pltpu.VMEM)
 SMEM = pl.BlockSpec(memory_space=pltpu.SMEM)
-PARAMS = pltpu.CompilerParams(vmem_limit_bytes=48 << 20)
+ORDER = (2, 1, 3)
+
+
+def grant(mebibytes):
+    return pltpu.CompilerParams(vmem_limit_bytes=mebibytes << 20)
 
 
 def flat(x, core, y, z):
@@ -103,7 +107,7 @@
         ),
         in_specs=[SMEM] + [VMEM] * 4,
         out_specs=(VMEM, VMEM),
-        compiler_params=PARAMS,
+        compiler_params=grant(16),
         cost_estimate=pl.CostEstimate(
             flops=12 * n * D * UNITS, transcendentals=n * UNITS, bytes_accessed=4 * n * D + 6 * D * UNITS
         ),
@@ -138,7 +142,7 @@
         ),
         in_specs=[VMEM] * 4,
         out_specs=(VMEM,) * 3,
-        compiler_params=PARAMS,
+        compiler_params=grant(16),
         cost_estimate=pl.CostEstimate(
             flops=6 * n * D * UNITS, transcendentals=0, bytes_accessed=4 * n * D + 6 * D * UNITS
         ),
@@ -159,6 +163,7 @@
         out_shape=jax.ShapeDtypeStruct((NZ, 2, D), BF16),
         in_specs=[VMEM] * 4,
         out_specs=VMEM,
+        compiler_params=grant(1),
         name="summed_pairs",
     )(own, *parts)
 
@@ -170,9 +175,9 @@
         rows = exchanged(copies_of_row(tokens, cotangent, routes, gate_weights), "z")
         rows = jnp.concatenate([rows[:, 0, :D], rows[:, 1, :D], rows[:, 0, D:]], axis=1)
     with jax.named_scope("gather_light"):
-        rows = jnp.concatenate([rows] + [fetch(rows, "light", d) for d in range(1, RING)], axis=0)
+        rows = jnp.concatenate([rows] + [fetch(rows, "light", d) for d in ORDER], axis=0)
     with jax.named_scope("gather_heavy"):
-        near = [rows] + [fetch(rows, "heavy", d) for d in range(1, RING)]
+        near = [rows] + [fetch(rows, "heavy", d) for d in ORDER]
     with jax.named_scope("gather_core"):
         far = jnp.concatenate([swapped(chunk) for chunk in near], axis=0)
         near = jnp.concatenate(near, axis=0)
@@ -184,11 +189,11 @@
         grad_g, grad_u, grad_d = weight_grads(far, near, far_acts, near_acts)
     with jax.named_scope("reduce_heavy"):
         total = (near_terms + other.astype(F32)).reshape(RING, RING * NZ, 2 * D)
-        got = [give(total[d].astype(BF16), "heavy", d) for d in range(1, RING)]
+        got = [give(total[1 + i].astype(BF16), "heavy", d) for i, d in enumerate(ORDER)]
         total = total[0] + sum(g.astype(F32) for g in got)
     with jax.named_scope("reduce_light"):
         total = total.reshape(RING, NZ, 2 * D)
-        got = [give(total[d].astype(BF16), "light", d) for d in range(1, RING)]
+        got = [give(total[1 + i].astype(BF16), "light", d) for i, d in enumerate(ORDER)]
     with jax.named_scope("reduce_z"):
         got = exchanged(summed_pairs(total[0], got), "z")
         total = sum(got[i].astype(F32) for i in range(NZ)).astype(BF16)

time: 91.5 us -> 87.9 us (0.961)
  waiting for transfers between devices: 34.3 us -> 38 us
  Pallas kernels: 10.3 us -> 7.6 us
  other arithmetic: 2.64 us -> 0.75 us
  local copies, waits for them, and re-layouts: 2.54 us -> 1.36 us
  starting transfers between devices: 22.5 us -> 21.5 us
    another operation x2, other arithmetic: 2.53 us -> 0.65 us
    ppermute x6, waiting for transfers between devices: 13.5 us -> 15.2 us  [give(): return lax.ppermute(value, AXES, pairs(stage, d))]
    pallas_call x2, Pallas kernels: 4.57 us -> 2.93 us  [expert_terms(): pl.pallas_call(expert_kernel, out_shape=(jax.ShapeDtypeStruct((n, 2 * D),...]
    pallas_call x1, Pallas kernels: 1.87 us -> 0.79 us  [summed_pairs(): pl.pallas_call(last_kernel, out_shape=jax.ShapeDtypeStruct((NZ, 2, D), BF...]
    ppermute x5, waiting for transfers between devices: 1.82 us -> 2.86 us  [swapped(): return lax.ppermute(value, 'core', [(0, 1), (1, 0)])]
    ppermute x6, waiting for transfers between devices: 13.8 us -> 14.8 us  [fetch(): return lax.ppermute(value, AXES, pairs(stage, -d))]
  transfers between devices with their start and end apart: 18 -> 18, of which waited for: 10 -> 12; matrix products, arithmetic and copies ran while one was open for 1% -> 0% of each run, Pallas kernels for 6% -> 4%
where the time goes in v5:
time: 87.9 us; the launch traced here: 86.7 us
  waiting for transfers between devices  38 us (43%)
  starting transfers between devices  21.5 us (24%)
  blocking collectives  16.6 us (19%)
  Pallas kernels  7.6 us (9%)
  local copies, waits for them, and re-layouts  1.36 us (2%)
    all_to_all x1, blocking collectives, exchanged(): return lax.all_to_all(value, axis, 0, 0, tiled=True)  16.6 us
    ppermute x6, waiting for transfers between devices, give(): return lax.ppermute(value, AXES, pairs(stage, d))  15.2 us
    ppermute x6, waiting for transfers between devices, fetch(): return lax.ppermute(value, AXES, pairs(stage, -d))  14.8 us
    ppermute x6, starting transfers between devices, fetch(): return lax.ppermute(value, AXES, pairs(stage, -d))  6.53 us
    ppermute x5, starting transfers between devices, swapped(): return lax.ppermute(value, 'core', [(0, 1), (1, 0)])  5.88 us
    ppermute x6, starting transfers between devices, give(): return lax.ppermute(value, AXES, pairs(stage, d))  5.74 us
    all_to_all x1, waiting for transfers between devices, exchanged(): return lax.all_to_all(value, axis, 0, 0, tiled=True)  5.07 us
    all_to_all x1, starting transfers between devices, exchanged(): return lax.all_to_all(value, axis, 0, 0, tiled=True)  3.36 us
  transfers between devices with their start and end apart: 18, of which 12 were waited for; matrix products, arithmetic and copies ran while one was open for 0% of the time, Pallas kernels for 4%

profile of v5, /device:TPU:1, one launch (start us, length us, event | category | flops | bytes accessed | tf_op | source)
XLA Modules:
  0.0 86.7 jit_solution(11555951069318752574)
XLA Ops:
  0.6 1.5 %copies_of_row.1 = bf16[8,2,3200]{2,1,0:T(2,128)(2,1)} custom-call(bf16[1,3072]{1,0:T(2,128)(2,1)} %tokens.1, bf16[1,3072]{1,0:T(2,128)(2,1)} %cotangent.1, s32[1,2]{1,0:T(1,128)} %routes.1, bf16[1,2]{1,0:T(2,128)(2,1)} %weights.1), custom_call_target="tpu_custom_call" | custom-call | tf_op jit(solution)/shard_map/gather_z/copies_of_row/pallas_call | solution.py:71
  2.1 16.6 %all_to_all.10 = bf16[8,2,3200]{2,1,0:T(2,128)(2,1)S(1)} all-to-all(bf16[8,2,3200]{2,1,0:T(2,128)(2,1)} %copies_of_row.1), channel_id=1, replica_groups=mesh['x_hi'=2,'core'=2,'y'=4,'x_lo'=2,'z'=8] {'z'}, dimensions={0} | all-to-all | bytes 204800 | tf_op jit(solution)/shard_map/gather_z/all_to_all | solution.py:50
  18.9 2.8 %collective-permute-start.1 = (bf16[8,6272]{1,0:T(8,128)(2,1)S(1)}, bf16[8,6272]{1,0:T(8,128)(2,1)S(1)}, u32[]{:S(2)}, u32[]{:S(2)}) collective-permute-start(bf16[8,6272]{1,0:T(8,128)(2,1)S(1)} %get-tuple-element.31), channel_id=1, source_target_pairs={{0,136},{1,137},{2,138},{3,139},{4,140},{5,141},{6,142},{7,143},{1... | collective-permute-start | bytes 301064 | tf_op jit(solution)/shard_map/gather_light/ppermute | solution.py:42
  22.8 1.6 %collective-permute-done.1 = bf16[8,6272]{1,0:T(8,128)(2,1)S(1)} collective-permute-done((bf16[8,6272]{1,0:T(8,128)(2,1)S(1)}, bf16[8,6272]{1,0:T(8,128)(2,1)S(1)}, u32[]{:S(2)}, u32[]{:S(2)}) %collective-permute-start.1) | collective-permute-done | bytes 100384 | tf_op jit(solution)/shard_map/gather_light/ppermute | solution.py:42
  24.4 2.4 %collective-permute-done = bf16[8,6272]{1,0:T(8,128)(2,1)S(1)} collective-permute-done((bf16[8,6272]{1,0:T(8,128)(2,1)S(1)}, bf16[8,6272]{1,0:T(8,128)(2,1)S(1)}, u32[]{:S(2)}, u32[]{:S(2)}) %collective-permute-start) | collective-permute-done | bytes 100384 | tf_op jit(solution)/shard_map/gather_light/ppermute | solution.py:42
  26.9 1.0 %collective-permute-done.2 = bf16[8,6272]{1,0:T(8,128)(2,1)S(1)} collective-permute-done((bf16[8,6272]{1,0:T(8,128)(2,1)S(1)}, bf16[8,6272]{1,0:T(8,128)(2,1)S(1)}, u32[]{:S(2)}, u32[]{:S(2)}) %collective-permute-start.2) | collective-permute-done | bytes 100384 | tf_op jit(solution)/shard_map/gather_light/ppermute | solution.py:42
  27.9 3.4 %collective-permute-start.6 = (bf16[32,6272]{1,0:T(8,128)(2,1)S(1)}, bf16[32,6272]{1,0:T(8,128)(2,1)S(1)}, u32[]{:S(2)}, u32[]{:S(2)}) collective-permute-start(bf16[32,6272]{1,0:T(8,128)(2,1)S(1)} %pad_maximum_fusion), channel_id=1, source_target_pairs={{0,64},{64,0},{1,65},{65,1},{2,66},{66,2},{3,67},{67,3},{4,68},{68... | collective-permute-start | bytes 1204232 | tf_op jit(solution)/shard_map/gather_core/ppermute | solution.py:46
  31.2 2.7 %collective-permute-start.4 = (bf16[32,6272]{1,0:T(8,128)(2,1)S(1)}, bf16[32,6272]{1,0:T(8,128)(2,1)S(1)}, u32[]{:S(2)}, u32[]{:S(2)}) collective-permute-start(bf16[32,6272]{1,0:T(8,128)(2,1)S(1)} %pad_maximum_fusion), channel_id=1, source_target_pairs={{0,48},{1,49},{2,50},{3,51},{4,52},{5,53},{6,54},{7,55},{16,0},{17... | collective-permute-start | bytes 1204232 | tf_op jit(solution)/shard_map/gather_heavy/ppermute | solution.py:42
  34.0 9.8 %collective-permute-done.5 = bf16[32,6272]{1,0:T(8,128)(2,1)S(1)} collective-permute-done((bf16[32,6272]{1,0:T(8,128)(2,1)S(1)}, bf16[32,6272]{1,0:T(8,128)(2,1)S(1)}, u32[]{:S(2)}, u32[]{:S(2)}) %collective-permute-start.5) | collective-permute-done | bytes 401440 | tf_op jit(solution)/shard_map/gather_heavy/ppermute | solution.py:42
  44.3 1.7 %collective-permute-start.7 = (bf16[32,6272]{1,0:T(8,128)(2,1)S(1)}, bf16[32,6272]{1,0:T(8,128)(2,1)S(1)}, u32[]{:S(2)}, u32[]{:S(2)}) collective-permute-start(bf16[32,6272]{1,0:T(8,128)(2,1)S(1)} %collective-permute-done.3), channel_id=1, source_target_pairs={{0,64},{64,0},{1,65},{65,1},{2,66},{66,2},{3,67},{67,3},{4,68},{68... | collective-permute-start | bytes 1204232 | tf_op jit(solution)/shard_map/gather_core/ppermute | solution.py:46
  46.0 1.2 %collective-permute-done.7 = bf16[32,6272]{1,0:T(8,128)(2,1)S(1)} collective-permute-done((bf16[32,6272]{1,0:T(8,128)(2,1)S(1)}, bf16[32,6272]{1,0:T(8,128)(2,1)S(1)}, u32[]{:S(2)}, u32[]{:S(2)}) %collective-permute-start.7) | collective-permute-done | bytes 401440 | tf_op jit(solution)/shard_map/gather_core/ppermute | solution.py:46
  47.6 1.5 %expert_terms.3 = (bf16[128,6144]{1,0:T(8,128)(2,1)S(1)}, bf16[128,384]{1,0:T(8,128)(2,1)S(1)}) custom-call(s32[1]{0:T(128)} %bitcast.group, bf16[128,6272]{1,0:T(8,128)(2,1)S(1)} %constant_dynamic-update-slice_fusion.7.rows.far, bf16[3072,128]{1,0:T(8,128)(2,1)S(1)} %bitcast.15, bf16[3072,128]{1,0:T(8,128)(2,1)S(1)} %bitcast.17, bf16[128,3072]{1,0:T(8,128)(2,1)S(1)} %bitcast.19), custom_call_target="tpu_custom_call" | custom-call | flops 603979776 | bytes 3932160 | tf_op jit(solution)/shard_map/experts/expert_terms/pallas_call | solution.py:102
  49.5 1.5 %expert_terms.2 = (f32[128,6144]{1,0:T(8,128)S(1)}, bf16[128,384]{1,0:T(8,128)(2,1)S(1)}) custom-call(s32[1]{0:T(128)} %bitcast.group, bf16[128,6272]{1,0:T(8,128)(2,1)S(1)} %constant_dynamic-update-slice_fusion.rows.near, bf16[3072,128]{1,0:T(8,128)(2,1)S(1)} %bitcast.16, bf16[3072,128]{1,0:T(8,128)(2,1)S(1)} %bitcast.18, bf16[128,3072]{1,0:T(8,128)(2,1)S(1)} %bitcast.20), custom_call_target="tpu_custom_call" | custom-call | flops 603979776 | bytes 3932160 | tf_op jit(solution)/shard_map/experts/expert_terms/pallas_call | solution.py:102
  50.9 1.6 %collective-permute-done.10 = bf16[128,6144]{1,0:T(8,128)(2,1)S(1)} collective-permute-done((bf16[128,6144]{1,0:T(8,128)(2,1)S(1)}, bf16[128,6144]{1,0:T(8,128)(2,1)S(1)}, u32[]{:S(2)}, u32[]{:S(2)}) %collective-permute-start.10) | collective-permute-done | bytes 1572896 | tf_op jit(solution)/shard_map/experts/ppermute | solution.py:46
  55.4 6.3 %collective-permute-done.11 = bf16[32,6144]{1,0:T(8,128)(2,1)S(1)} collective-permute-done((bf16[32,6144]{1,0:T(8,128)(2,1)S(1)}, bf16[32,6144]{1,0:T(8,128)(2,1)S(1)}, u32[]{:S(2)}, u32[]{:S(2)}) %collective-permute-start.11) | collective-permute-done | bytes 393248 | tf_op jit(solution)/shard_map/reduce_heavy/ppermute | solution.py:38
  61.7 2.8 %collective-permute-done.13 = bf16[32,6144]{1,0:T(8,128)(2,1)S(1)} collective-permute-done((bf16[32,6144]{1,0:T(8,128)(2,1)S(1)}, bf16[32,6144]{1,0:T(8,128)(2,1)S(1)}, u32[]{:S(2)}, u32[]{:S(2)}) %collective-permute-start.13) | collective-permute-done | bytes 393248 | tf_op jit(solution)/shard_map/reduce_heavy/ppermute | solution.py:38
  64.5 1.3 %collective-permute-done.12 = bf16[32,6144]{1,0:T(8,128)(2,1)S(1)} collective-permute-done((bf16[32,6144]{1,0:T(8,128)(2,1)S(1)}, bf16[32,6144]{1,0:T(8,128)(2,1)S(1)}, u32[]{:S(2)}, u32[]{:S(2)}) %collective-permute-start.12) | collective-permute-done | bytes 393248 | tf_op jit(solution)/shard_map/reduce_heavy/ppermute | solution.py:38
  66.1 2.2 %collective-permute-start.16 = (bf16[8,6144]{1,0:T(8,128)(2,1)S(1)}, bf16[8,6144]{1,0:T(8,128)(2,1)S(1)}, u32[]{:S(2)}, u32[]{:S(2)}) collective-permute-start(bf16[8,6144]{1,0:T(8,128)(2,1)S(1)} %get-tuple-element.26), channel_id=1, source_target_pairs={{0,136},{1,137},{2,138},{3,139},{4,140},{5,141},{6,142},{7,143},{1... | collective-permute-start | bytes 294920 | tf_op jit(solution)/shard_map/reduce_light/ppermute | solution.py:38
  68.3 1.3 %collective-permute-start.14 = (bf16[8,6144]{1,0:T(8,128)(2,1)S(1)}, bf16[8,6144]{1,0:T(8,128)(2,1)S(1)}, u32[]{:S(2)}, u32[]{:S(2)}) collective-permute-start(bf16[8,6144]{1,0:T(8,128)(2,1)S(1)} %get-tuple-element.28), channel_id=1, source_target_pairs={{0,128},{1,129},{2,130},{3,131},{4,132},{5,133},{6,134},{7,135},{1... | collective-permute-start | bytes 294920 | tf_op jit(solution)/shard_map/reduce_light/ppermute | solution.py:38
  69.9 4.4 %collective-permute-done.15.two = bf16[8,6144]{1,0:T(8,128)(2,1)S(1)} collective-permute-done((bf16[8,6144]{1,0:T(8,128)(2,1)S(1)}, bf16[8,6144]{1,0:T(8,128)(2,1)S(1)}, u32[]{:S(2)}, u32[]{:S(2)}) %collective-permute-start.15) | collective-permute-done | bytes 98336 | tf_op jit(solution)/shard_map/reduce_light/ppermute | solution.py:38
  74.3 0.8 summed_pairs.1
  75.1 3.4 %all-to-all-start.1 = ((bf16[8,2,3072]{2,1,0:T(2,128)(2,1)}), bf16[8,2,3072]{2,1,0:T(2,128)(2,1)S(1)}, u32[]{:S(2)}, u32[]{:S(2)}) async-start(bf16[8,2,3072]{2,1,0:T(2,128)(2,1)} %summed_pairs.1), calls=%async_computation.1 | async-start | bytes 196608 | tf_op jit(solution)/shard_map/reduce_z/all_to_all | solution.py:50
  78.5 2.4 %weight_grads.1 = (bf16[1,3072,128]{2,1,0:T(8,128)(2,1)}, bf16[1,3072,128]{2,1,0:T(8,128)(2,1)}, bf16[1,128,3072]{2,1,0:T(8,128)(2,1)}) custom-call(bf16[128,6272]{1,0:T(8,128)(2,1)S(1)} %constant_dynamic-update-slice_fusion.7.rows.far, bf16[128,6272]{1,0:T(8,128)(2,1)S(1)} %constant_dynamic-update-slice_fusion.rows.near, ...), custom_call_target="tpu_custom_call" | custom-call | flops 603979776 | bytes 5505024 | tf_op jit(solution)/shard_map/weights/weight_grads/pallas_call | solution.py:136
  80.9 5.1 %all-to-all-done.1 = bf16[8,2,3072]{2,1,0:T(2,128)(2,1)S(1)} async-done(((bf16[8,2,3072]{2,1,0:T(2,128)(2,1)}), bf16[8,2,3072]{2,1,0:T(2,128)(2,1)S(1)}, u32[]{:S(2)}, u32[]{:S(2)}) %all-to-all-start.1) | async-done | bytes 98336 | tf_op jit(solution)/shard_map/reduce_z/all_to_all | solution.py:50
  (47 shorter events, 6.6 us)
Async XLA Ops:
  18.9 5.5 %collective-permute-start.1 = (bf16[8,6272]{1,0:T(8,128)(2,1)S(1)}, bf16[8,6272]{1,0:T(8,128)(2,1)S(1)}, u32[]{:S(2)}, u32[]{:S(2)}) collective-permute-start(bf16[8,6272]{1,0:T(8,128)(2,1)S(1)} %get-tuple-element.31), channel_id=1, source_target_pairs={{0,136},{1,137},{2,138},{3,139},{4,140},{5,141},{6,142},{7,143},{1... | collective-permute-start | bytes 301064 | tf_op jit(solution)/shard_map/gather_light/ppermute | solution.py:42
  21.8 5.1 %collective-permute-start = (bf16[8,6272]{1,0:T(8,128)(2,1)S(1)}, bf16[8,6272]{1,0:T(8,128)(2,1)S(1)}, u32[]{:S(2)}, u32[]{:S(2)}) collective-permute-start(bf16[8,6272]{1,0:T(8,128)(2,1)S(1)} %get-tuple-element.31), channel_id=1, source_target_pairs={{0,128},{1,129},{2,130},{3,131},{4,132},{5,133},{6,134},{7,135},{1... | collective-permute-start | bytes 301064 | tf_op jit(solution)/shard_map/gather_light/ppermute | solution.py:42
  22.1 5.7 %collective-permute-start.2 = (bf16[8,6272]{1,0:T(8,128)(2,1)S(1)}, bf16[8,6272]{1,0:T(8,128)(2,1)S(1)}, u32[]{:S(2)}, u32[]{:S(2)}) collective-permute-start(bf16[8,6272]{1,0:T(8,128)(2,1)S(1)} %get-tuple-element.31), channel_id=1, source_target_pairs={{0,8},{1,9},{2,10},{3,11},{4,12},{5,13},{6,14},{7,15},{16,24},{17,... | collective-permute-start | bytes 301064 | tf_op jit(solution)/shard_map/gather_light/ppermute | solution.py:42
  27.9 18.1 %collective-permute-start.6 = (bf16[32,6272]{1,0:T(8,128)(2,1)S(1)}, bf16[32,6272]{1,0:T(8,128)(2,1)S(1)}, u32[]{:S(2)}, u32[]{:S(2)}) collective-permute-start(bf16[32,6272]{1,0:T(8,128)(2,1)S(1)} %pad_maximum_fusion), channel_id=1, source_target_pairs={{0,64},{64,0},{1,65},{65,1},{2,66},{66,2},{3,67},{67,3},{4,68},{68... | collective-permute-start | bytes 1204232 | tf_op jit(solution)/shard_map/gather_core/ppermute | solution.py:46
  31.2 12.5 %collective-permute-start.5 = (bf16[32,6272]{1,0:T(8,128)(2,1)S(1)}, bf16[32,6272]{1,0:T(8,128)(2,1)S(1)}, u32[]{:S(2)}, u32[]{:S(2)}) collective-permute-start(bf16[32,6272]{1,0:T(8,128)(2,1)S(1)} %pad_maximum_fusion), channel_id=1, source_target_pairs={{0,16},{1,17},{2,18},{3,19},{4,20},{5,21},{6,22},{7,23},{16,32},{1... | collective-permute-start | bytes 1204232 | tf_op jit(solution)/shard_map/gather_heavy/ppermute | solution.py:42
  31.2 12.5 %collective-permute-start.4 = (bf16[32,6272]{1,0:T(8,128)(2,1)S(1)}, bf16[32,6272]{1,0:T(8,128)(2,1)S(1)}, u32[]{:S(2)}, u32[]{:S(2)}) collective-permute-start(bf16[32,6272]{1,0:T(8,128)(2,1)S(1)} %pad_maximum_fusion), channel_id=1, source_target_pairs={{0,48},{1,49},{2,50},{3,51},{4,52},{5,53},{6,54},{7,55},{16,0},{17... | collective-permute-start | bytes 1204232 | tf_op jit(solution)/shard_map/gather_heavy/ppermute | solution.py:42
  33.9 10.4 %collective-permute-start.3 = (bf16[32,6272]{1,0:T(8,128)(2,1)S(1)}, bf16[32,6272]{1,0:T(8,128)(2,1)S(1)}, u32[]{:S(2)}, u32[]{:S(2)}) collective-permute-start(bf16[32,6272]{1,0:T(8,128)(2,1)S(1)} %pad_maximum_fusion), channel_id=1, source_target_pairs={{0,32},{1,33},{2,34},{3,35},{4,36},{5,37},{6,38},{7,39},{16,48},{1... | collective-permute-start | bytes 1204232 | tf_op jit(solution)/shard_map/gather_heavy/ppermute | solution.py:42
  43.7 3.6 %collective-permute-start.9 = (bf16[32,6272]{1,0:T(8,128)(2,1)S(1)}, bf16[32,6272]{1,0:T(8,128)(2,1)S(1)}, u32[]{:S(2)}, u32[]{:S(2)}) collective-permute-start(bf16[32,6272]{1,0:T(8,128)(2,1)S(1)} %collective-permute-done.5), channel_id=1, source_target_pairs={{0,64},{64,0},{1,65},{65,1},{2,66},{66,2},{3,67},{67,3},{4,68},{68... | collective-permute-start | bytes 1204232 | tf_op jit(solution)/shard_map/gather_core/ppermute | solution.py:46
  43.8 3.6 %collective-permute-start.8 = (bf16[32,6272]{1,0:T(8,128)(2,1)S(1)}, bf16[32,6272]{1,0:T(8,128)(2,1)S(1)}, u32[]{:S(2)}, u32[]{:S(2)}) collective-permute-start(bf16[32,6272]{1,0:T(8,128)(2,1)S(1)} %collective-permute-done.4), channel_id=1, source_target_pairs={{0,64},{64,0},{1,65},{65,1},{2,66},{66,2},{3,67},{67,3},{4,68},{68... | collective-permute-start | bytes 1204232 | tf_op jit(solution)/shard_map/gather_core/ppermute | solution.py:46
  44.3 3.0 %collective-permute-start.7 = (bf16[32,6272]{1,0:T(8,128)(2,1)S(1)}, bf16[32,6272]{1,0:T(8,128)(2,1)S(1)}, u32[]{:S(2)}, u32[]{:S(2)}) collective-permute-start(bf16[32,6272]{1,0:T(8,128)(2,1)S(1)} %collective-permute-done.3), channel_id=1, source_target_pairs={{0,64},{64,0},{1,65},{65,1},{2,66},{66,2},{3,67},{67,3},{4,68},{68... | collective-permute-start | bytes 1204232 | tf_op jit(solution)/shard_map/gather_core/ppermute | solution.py:46
  46.0 1.5 %copy-start = (bf16[1,3072,128]{2,1,0:T(8,128)(2,1)S(1)}, bf16[1,3072,128]{2,1,0:T(8,128)(2,1)}, u32[]{:S(2)}) copy-start(bf16[1,3072,128]{2,1,0:T(8,128)(2,1)} %param.11) | copy-start | bytes 2359300
  46.0 1.5 %copy-start.1 = (bf16[1,3072,128]{2,1,0:T(8,128)(2,1)S(1)}, bf16[1,3072,128]{2,1,0:T(8,128)(2,1)}, u32[]{:S(2)}) copy-start(bf16[1,3072,128]{2,1,0:T(8,128)(2,1)} %param.12) | copy-start | bytes 2359300
  46.0 1.6 %copy-start.2 = (bf16[1,128,3072]{2,1,0:T(8,128)(2,1)S(1)}, bf16[1,128,3072]{2,1,0:T(8,128)(2,1)}, u32[]{:S(2)}) copy-start(bf16[1,128,3072]{2,1,0:T(8,128)(2,1)} %param.13) | copy-start | bytes 2359300
  49.1 3.5 %collective-permute-start.10 = (bf16[128,6144]{1,0:T(8,128)(2,1)S(1)}, bf16[128,6144]{1,0:T(8,128)(2,1)S(1)}, u32[]{:S(2)}, u32[]{:S(2)}) collective-permute-start(bf16[128,6144]{1,0:T(8,128)(2,1)S(1)} %get-tuple-element.13), channel_id=1, source_target_pairs={{0,64},{64,0},{1,65},{65,1},{2,66},{66,2},{3,67},{67,3},{4,68},{68... | collective-permute-start | bytes 4718600 | tf_op jit(solution)/shard_map/experts/ppermute | solution.py:46
  53.1 8.6 %collective-permute-start.11 = (bf16[32,6144]{1,0:T(8,128)(2,1)S(1)}, bf16[32,6144]{1,0:T(8,128)(2,1)S(1)}, u32[]{:S(2)}, u32[]{:S(2)}) collective-permute-start(bf16[32,6144]{1,0:T(8,128)(2,1)S(1)} %get-tuple-element.23), channel_id=1, source_target_pairs={{0,32},{1,33},{2,34},{3,35},{4,36},{5,37},{6,38},{7,39},{16,48},{1... | collective-permute-start | bytes 1179656 | tf_op jit(solution)/shard_map/reduce_heavy/ppermute | solution.py:38
  53.9 10.6 %collective-permute-start.13 = (bf16[32,6144]{1,0:T(8,128)(2,1)S(1)}, bf16[32,6144]{1,0:T(8,128)(2,1)S(1)}, u32[]{:S(2)}, u32[]{:S(2)}) collective-permute-start(bf16[32,6144]{1,0:T(8,128)(2,1)S(1)} %get-tuple-element.24), channel_id=1, source_target_pairs={{0,48},{1,49},{2,50},{3,51},{4,52},{5,53},{6,54},{7,55},{16,0},{17... | collective-permute-start | bytes 1179656 | tf_op jit(solution)/shard_map/reduce_heavy/ppermute | solution.py:38
  54.6 11.2 %collective-permute-start.12 = (bf16[32,6144]{1,0:T(8,128)(2,1)S(1)}, bf16[32,6144]{1,0:T(8,128)(2,1)S(1)}, u32[]{:S(2)}, u32[]{:S(2)}) collective-permute-start(bf16[32,6144]{1,0:T(8,128)(2,1)S(1)} %get-tuple-element.25), channel_id=1, source_target_pairs={{0,16},{1,17},{2,18},{3,19},{4,20},{5,21},{6,22},{7,23},{16,32},{1... | collective-permute-start | bytes 1179656 | tf_op jit(solution)/shard_map/reduce_heavy/ppermute | solution.py:38
  66.1 3.9 %collective-permute-start.16 = (bf16[8,6144]{1,0:T(8,128)(2,1)S(1)}, bf16[8,6144]{1,0:T(8,128)(2,1)S(1)}, u32[]{:S(2)}, u32[]{:S(2)}) collective-permute-start(bf16[8,6144]{1,0:T(8,128)(2,1)S(1)} %get-tuple-element.26), channel_id=1, source_target_pairs={{0,136},{1,137},{2,138},{3,139},{4,140},{5,141},{6,142},{7,143},{1... | collective-permute-start | bytes 294920 | tf_op jit(solution)/shard_map/reduce_light/ppermute | solution.py:38
  68.3 6.0 %collective-permute-start.15 = (bf16[8,6144]{1,0:T(8,128)(2,1)S(1)}, bf16[8,6144]{1,0:T(8,128)(2,1)S(1)}, u32[]{:S(2)}, u32[]{:S(2)}) collective-permute-start(bf16[8,6144]{1,0:T(8,128)(2,1)S(1)} %get-tuple-element.27), channel_id=1, source_target_pairs={{0,8},{1,9},{2,10},{3,11},{4,12},{5,13},{6,14},{7,15},{16,24},{17,... | collective-permute-start | bytes 294920 | tf_op jit(solution)/shard_map/reduce_light/ppermute | solution.py:38
  68.3 6.0 %collective-permute-start.14 = (bf16[8,6144]{1,0:T(8,128)(2,1)S(1)}, bf16[8,6144]{1,0:T(8,128)(2,1)S(1)}, u32[]{:S(2)}, u32[]{:S(2)}) collective-permute-start(bf16[8,6144]{1,0:T(8,128)(2,1)S(1)} %get-tuple-element.28), channel_id=1, source_target_pairs={{0,128},{1,129},{2,130},{3,131},{4,132},{5,133},{6,134},{7,135},{1... | collective-permute-start | bytes 294920 | tf_op jit(solution)/shard_map/reduce_light/ppermute | solution.py:38
  75.1 10.9 %all-to-all-start.1 = ((bf16[8,2,3072]{2,1,0:T(2,128)(2,1)}), bf16[8,2,3072]{2,1,0:T(2,128)(2,1)S(1)}, u32[]{:S(2)}, u32[]{:S(2)}) async-start(bf16[8,2,3072]{2,1,0:T(2,128)(2,1)} %summed_pairs.1), calls=%async_computation.1 | async-start | bytes 196608 | tf_op jit(solution)/shard_map/reduce_z/all_to_all | solution.py:50

commit v6 on v5

--- a/solution.py
+++ b/solution.py
@@ -5,7 +5,7 @@
 from jax.experimental.pallas import tpu as pltpu
 from jax.sharding import Mesh, PartitionSpec as P
 
-NX_HI, NCORE, NY, NX_LO, NZ, RING = 2, 2, 4, 2, 8, 4
+NX_HI, NCORE, NY, NX_LO, NZ, RING, PLANE = 2, 2, 4, 2, 8, 4, 32
 AXES = ("x_hi", "core", "y", "x_lo", "z")
 EP, TP = ("x_hi", "core"), ("y", "x_lo", "z")
 D, PAD, UNITS = 3072, 128, 128
@@ -23,31 +23,36 @@
     return (((x // 2) * NCORE + core) * NY + y) * NX_LO * NZ + (x % 2) * NZ + z
 
 
-def pairs(stage, d):
+def pairs(d):
     out = []
     for x in range(RING):
         for core in range(NCORE):
             for y in range(RING):
-                along_x = (stage == "light") == (core == 0)
-                tx, ty = ((x + d) % RING, y) if along_x else (x, (y + d) % RING)
+                tx, ty = (x, (y + d) % RING) if core == 0 else ((x + d) % RING, y)
                 out += [(flat(x, core, y, z), flat(tx, core, ty, z)) for z in range(NZ)]
     return out
 
 
-def give(value, stage, d):
-    return lax.ppermute(value, AXES, pairs(stage, d))
-
-
-def fetch(value, stage, d):
-    return lax.ppermute(value, AXES, pairs(stage, -d))
+def give(value, d):
+    return lax.ppermute(value, AXES, pairs(d))
+
+
+def fetch(value, d):
+    return lax.ppermute(value, AXES, pairs(-d))
 
 
 def swapped(value):
     return lax.ppermute(value, "core", [(0, 1), (1, 0)])
 
 
-def exchanged(value, axis):
-    return lax.all_to_all(value, axis, 0, 0, tiled=True)
+def planes():
+    along_x = [[flat(x, 0, y, z) for x in range(RING) for z in range(NZ)] for y in range(RING)]
+    along_y = [[flat(x, 1, y, z) for y in range(RING) for z in range(NZ)] for x in range(RING)]
+    return along_x + along_y
+
+
+def exchanged(value):
+    return lax.all_to_all(value, AXES, 0, 0, axis_index_groups=planes(), tiled=True)
 
 
 def dot(left, right, left_dim, right_dim):
@@ -63,14 +68,14 @@
     first = jnp.concatenate([tokens[...].astype(F32), gates], axis=1)
     second = jnp.concatenate([cotangent[...].astype(F32), jnp.zeros((1, PAD), F32)], axis=1)
     both = jnp.concatenate([first, second], axis=0).astype(BF16)
-    for i in range(NZ):
+    for i in range(PLANE):
         out[i] = both
 
 
 def copies_of_row(tokens, cotangent, routes, gate_weights):
     return pl.pallas_call(
         row_kernel,
-        out_shape=jax.ShapeDtypeStruct((NZ, 2, D + PAD), BF16),
+        out_shape=jax.ShapeDtypeStruct((PLANE, 2, D + PAD), BF16),
         out_specs=VMEM,
         name="copies_of_row",
     )(tokens, cotangent, routes, gate_weights)
@@ -152,7 +157,7 @@
 
 def last_kernel(own, one, two, three, out):
     total = own[...] + one[...].astype(F32) + two[...].astype(F32) + three[...].astype(F32)
-    for i in range(NZ):
+    for i in range(PLANE):
         row = total[i : i + 1]
         out[i] = jnp.concatenate([row[:, :D], row[:, D:]], axis=0).astype(BF16)
 
@@ -160,10 +165,10 @@
 def summed_pairs(own, parts):
     return pl.pallas_call(
         last_kernel,
-        out_shape=jax.ShapeDtypeStruct((NZ, 2, D), BF16),
+        out_shape=jax.ShapeDtypeStruct((PLANE, 2, D), BF16),
         in_specs=[VMEM] * 4,
         out_specs=VMEM,
-        compiler_params=grant(1),
+        compiler_params=grant(4),
         name="summed_pairs",
     )(own, *parts)
 
@@ -171,16 +176,14 @@
 def on_device(tokens, cotangent, routes, gate_weights, w_gate, w_up, w_down):
     slices = (w_gate[0], w_up[0], w_down[0])
     group = lax.axis_index(EP).astype(jnp.int32).reshape(1)
-    with jax.named_scope("gather_z"):
-        rows = exchanged(copies_of_row(tokens, cotangent, routes, gate_weights), "z")
+    with jax.named_scope("gather_plane"):
+        rows = exchanged(copies_of_row(tokens, cotangent, routes, gate_weights))
         rows = jnp.concatenate([rows[:, 0, :D], rows[:, 1, :D], rows[:, 0, D:]], axis=1)
-    with jax.named_scope("gather_light"):
-        rows = jnp.concatenate([rows] + [fetch(rows, "light", d) for d in ORDER], axis=0)
     with jax.named_scope("gather_heavy"):
-        near = [rows] + [fetch(rows, "heavy", d) for d in ORDER]
+        near = [rows] + [fetch(rows, d) for d in ORDER]
     with jax.named_scope("gather_core"):
         far = jnp.concatenate([swapped(chunk) for chunk in near], axis=0)
-        near = jnp.concatenate(near, axis=0)
+        far, near = lax.optimization_barrier((far, jnp.concatenate(near, axis=0)))
     with jax.named_scope("experts"):
         far_terms, far_acts = expert_terms(group, far, *slices, BF16)
         other = swapped(far_terms)
@@ -188,15 +191,11 @@
     with jax.named_scope("weights"):
         grad_g, grad_u, grad_d = weight_grads(far, near, far_acts, near_acts)
     with jax.named_scope("reduce_heavy"):
-        total = (near_terms + other.astype(F32)).reshape(RING, RING * NZ, 2 * D)
-        got = [give(total[1 + i].astype(BF16), "heavy", d) for i, d in enumerate(ORDER)]
-        total = total[0] + sum(g.astype(F32) for g in got)
-    with jax.named_scope("reduce_light"):
-        total = total.reshape(RING, NZ, 2 * D)
-        got = [give(total[1 + i].astype(BF16), "light", d) for i, d in enumerate(ORDER)]
-    with jax.named_scope("reduce_z"):
-        got = exchanged(summed_pairs(total[0], got), "z")
-        total = sum(got[i].astype(F32) for i in range(NZ)).astype(BF16)
+        total = (near_terms + other.astype(F32)).reshape(RING, PLANE, 2 * D)
+        got = [give(total[1 + i].astype(BF16), d) for i, d in enumerate(ORDER)]
+    with jax.named_scope("reduce_plane"):
+        got = exchanged(summed_pairs(total[0], got))
+        total = sum(got[i].astype(F32) for i in range(PLANE)).astype(BF16)
     return total[:1], total[1:], grad_g, grad_u, grad_d
 
 

time: 87.9 us -> 90.9 us (1.034)
  waiting for transfers between devices: 38 us -> 25.3 us
  blocking collectives: 16.6 us -> 24 us
  starting transfers between devices: 21.5 us -> 28 us
  other arithmetic: 0.75 us -> 2.67 us
    ppermute x12 -> x6, waiting for transfers between devices: 30.1 us -> 10.4 us  [the longest x3 10.4 us: give(): return lax.ppermute(value, AXES, pairs(d))]
    ppermute x5, starting transfers between devices: 5.88 us -> 14.4 us  [swapped(): return lax.ppermute(value, 'core', [(0, 1), (1, 0)])]
    all_to_all x1, blocking collectives: 16.6 us -> 24 us  [exchanged(): lax.all_to_all(value, AXES, 0, 0, axis_index_groups=planes(), tiled=True)]
    all_to_all x1, waiting for transfers between devices: 5.07 us -> 12.1 us  [exchanged(): lax.all_to_all(value, AXES, 0, 0, axis_index_groups=planes(), tiled=True)]
    ppermute x12 -> x6, starting transfers between devices: 12.3 us -> 7.45 us  [the longest x3 4.47 us: fetch(): return lax.ppermute(value, AXES, pairs(-d))]
    all_to_all x1, starting transfers between devices: 3.36 us -> 6.21 us  [exchanged(): lax.all_to_all(value, AXES, 0, 0, axis_index_groups=planes(), tiled=True)]
    convert_element_type x1, other arithmetic: 0.06 us -> 1.19 us  [on_device(): total = sum((got[i].astype(F32) for i in range(PLANE))).astype(BF16)]
  transfers between devices with their start and end apart: 18 -> 12, of which waited for: 12 -> 5; matrix products, arithmetic and copies ran while one was open for 0% -> 0% of each run, Pallas kernels for 4% -> 4%
where the time goes in v6:
time: 90.9 us; the launch traced here: 90.5 us
  starting transfers between devices  28 us (31%)
  waiting for transfers between devices  25.3 us (28%)
  blocking collectives  24 us (26%)
  Pallas kernels  7.59 us (8%)
  other arithmetic  2.67 us (3%)
  local copies, waits for them, and re-layouts  2.2 us (2%)
    all_to_all x1, blocking collectives, exchanged(): lax.all_to_all(value, AXES, 0, 0, axis_index_groups=planes(), tiled=True)  24 us
    ppermute x5, starting transfers between devices, swapped(): return lax.ppermute(value, 'core', [(0, 1), (1, 0)])  14.4 us
    all_to_all x1, waiting for transfers between devices, exchanged(): lax.all_to_all(value, AXES, 0, 0, axis_index_groups=planes(), tiled=True)  12.1 us
    ppermute x3, waiting for transfers between devices, give(): return lax.ppermute(value, AXES, pairs(d))  10.4 us
    all_to_all x1, starting transfers between devices, exchanged(): lax.all_to_all(value, AXES, 0, 0, axis_index_groups=planes(), tiled=True)  6.21 us
    ppermute x3, starting transfers between devices, fetch(): return lax.ppermute(value, AXES, pairs(-d))  4.47 us
    pallas_call x2, Pallas kernels, expert_terms(): pl.pallas_call(expert_kernel, out_shape=(jax.ShapeDtypeStruct((n, 2 * D),...  3 us
    ppermute x3, starting transfers between devices, give(): return lax.ppermute(value, AXES, pairs(d))  2.97 us
  transfers between devices with their start and end apart: 12, of which 5 were waited for; matrix products, arithmetic and copies ran while one was open for 0% of the time, Pallas kernels for 4%

profile of v6, /device:TPU:1, one launch (start us, length us, event | category | flops | bytes accessed | tf_op | source)
XLA Modules:
  0.0 90.5 jit_solution(5018630518551903214)
XLA Ops:
  0.6 1.6 %copies_of_row.1 = bf16[32,2,3200]{2,1,0:T(2,128)(2,1)} custom-call(bf16[1,3072]{1,0:T(2,128)(2,1)} %tokens.1, bf16[1,3072]{1,0:T(2,128)(2,1)} %cotangent.1, s32[1,2]{1,0:T(1,128)} %routes.1, bf16[1,2]{1,0:T(2,128)(2,1)} %weights.1), custom_call_target="tpu_custom_call" | custom-call | tf_op jit(solution)/shard_map/gather_plane/copies_of_row/pallas_call | solution.py:76
  2.2 24.0 %all_to_all.10 = bf16[32,2,3200]{2,1,0:T(2,128)(2,1)S(1)} all-to-all(bf16[32,2,3200]{2,1,0:T(2,128)(2,1)} %copies_of_row.1), channel_id=1, replica_groups={{0,1,2,3,4,5,6,7,8,9,10,11,12,13,14,15,128,129,130,131,132,133,134,135,..., dimensions={0} | all-to-all | bytes 819200 | tf_op jit(solution)/shard_map/gather_plane/all_to_all | solution.py:55
  26.9 0.8 pad_maximum_fusion.2
  27.7 1.2 %collective-permute-start.5 = (bf16[32,6272]{1,0:T(8,128)(2,1)}, bf16[32,6272]{1,0:T(8,128)(2,1)S(1)}, u32[]{:S(2)}, u32[]{:S(2)}) collective-permute-start(bf16[32,6272]{1,0:T(8,128)(2,1)} %pad_maximum_fusion.2), channel_id=1, source_target_pairs={{0,16},{1,17},{2,18},{3,19},{4,20},{5,21},{6,22},{7,23},{16,32},{1... | collective-permute-start | bytes 1204232 | tf_op jit(solution)/shard_map/gather_heavy/ppermute | solution.py:41
  28.9 1.5 %collective-permute-start.3 = (bf16[32,6272]{1,0:T(8,128)(2,1)}, bf16[32,6272]{1,0:T(8,128)(2,1)S(1)}, u32[]{:S(2)}, u32[]{:S(2)}) collective-permute-start(bf16[32,6272]{1,0:T(8,128)(2,1)} %pad_maximum_fusion.2), channel_id=1, source_target_pairs={{0,48},{1,49},{2,50},{3,51},{4,52},{5,53},{6,54},{7,55},{16,0},{17... | collective-permute-start | bytes 1204232 | tf_op jit(solution)/shard_map/gather_heavy/ppermute | solution.py:41
  30.3 1.8 %collective-permute-start.1 = (bf16[32,6272]{1,0:T(8,128)(2,1)}, bf16[32,6272]{1,0:T(8,128)(2,1)S(1)}, u32[]{:S(2)}, u32[]{:S(2)}) collective-permute-start(bf16[32,6272]{1,0:T(8,128)(2,1)} %pad_maximum_fusion.2), channel_id=1, source_target_pairs={{0,32},{1,33},{2,34},{3,35},{4,36},{5,37},{6,38},{7,39},{16,48},{1... | collective-permute-start | bytes 1204232 | tf_op jit(solution)/shard_map/gather_heavy/ppermute | solution.py:41
  32.1 4.4 %collective-permute-start = (bf16[32,6272]{1,0:T(8,128)(2,1)}, bf16[32,6272]{1,0:T(8,128)(2,1)S(1)}, u32[]{:S(2)}, u32[]{:S(2)}) collective-permute-start(bf16[32,6272]{1,0:T(8,128)(2,1)} %pad_maximum_fusion.2), channel_id=1, source_target_pairs={{0,64},{64,0},{1,65},{65,1},{2,66},{66,2},{3,67},{67,3},{4,68},{68... | collective-permute-start | bytes 1204232 | tf_op jit(solution)/shard_map/gather_core/ppermute | solution.py:45
  36.5 4.2 %collective-permute-start.6 = (bf16[32,6272]{1,0:T(8,128)(2,1)S(1)}, bf16[32,6272]{1,0:T(8,128)(2,1)S(1)}, u32[]{:S(2)}, u32[]{:S(2)}) collective-permute-start(bf16[32,6272]{1,0:T(8,128)(2,1)S(1)} %collective-permute-done.5), channel_id=1, source_target_pairs={{0,64},{64,0},{1,65},{65,1},{2,66},{66,2},{3,67},{67,3},{4,68},{68... | collective-permute-start | bytes 1204232 | tf_op jit(solution)/shard_map/gather_core/ppermute | solution.py:45
  40.7 4.0 %collective-permute-start.4 = (bf16[32,6272]{1,0:T(8,128)(2,1)S(1)}, bf16[32,6272]{1,0:T(8,128)(2,1)S(1)}, u32[]{:S(2)}, u32[]{:S(2)}) collective-permute-start(bf16[32,6272]{1,0:T(8,128)(2,1)S(1)} %collective-permute-done.3), channel_id=1, source_target_pairs={{0,64},{64,0},{1,65},{65,1},{2,66},{66,2},{3,67},{67,3},{4,68},{68... | collective-permute-start | bytes 1204232 | tf_op jit(solution)/shard_map/gather_core/ppermute | solution.py:45
  44.7 1.4 %collective-permute-start.2 = (bf16[32,6272]{1,0:T(8,128)(2,1)S(1)}, bf16[32,6272]{1,0:T(8,128)(2,1)S(1)}, u32[]{:S(2)}, u32[]{:S(2)}) collective-permute-start(bf16[32,6272]{1,0:T(8,128)(2,1)S(1)} %collective-permute-done.1), channel_id=1, source_target_pairs={{0,64},{64,0},{1,65},{65,1},{2,66},{66,2},{3,67},{67,3},{4,68},{68... | collective-permute-start | bytes 1204232 | tf_op jit(solution)/shard_map/gather_core/ppermute | solution.py:45
  46.2 1.2 %collective-permute-done.2 = bf16[32,6272]{1,0:T(8,128)(2,1)S(1)} collective-permute-done((bf16[32,6272]{1,0:T(8,128)(2,1)S(1)}, bf16[32,6272]{1,0:T(8,128)(2,1)S(1)}, u32[]{:S(2)}, u32[]{:S(2)}) %collective-permute-start.2) | collective-permute-done | bytes 401440 | tf_op jit(solution)/shard_map/gather_core/ppermute | solution.py:45
  47.6 1.5 %expert_terms.3 = (bf16[128,6144]{1,0:T(8,128)(2,1)S(1)}, bf16[128,384]{1,0:T(8,128)(2,1)S(1)}) custom-call(s32[1]{0:T(128)} %bitcast.group, bf16[128,6272]{1,0:T(8,128)(2,1)S(1)} %pad_maximum_fusion.rows.far, bf16[3072,128]{1,0:T(8,128)(2,1)S(1)} %bitcast.98, bf16[3072,128]{1,0:T(8,128)(2,1)S(1)} %bitcast.100, bf16[128,3072]{1,0:T(8,128)(2,1)S(1)} %bitcast.102), custom_call_target="tpu_custom_call" | custom-call | flops 603979776 | bytes 3932160 | tf_op jit(solution)/shard_map/experts/expert_terms/pallas_call | solution.py:107
  49.6 1.5 %expert_terms.2 = (f32[128,6144]{1,0:T(8,128)S(1)}, bf16[128,384]{1,0:T(8,128)(2,1)S(1)}) custom-call(s32[1]{0:T(128)} %bitcast.group, bf16[128,6272]{1,0:T(8,128)(2,1)S(1)} %pad_maximum_fusion.1.rows.near, bf16[3072,128]{1,0:T(8,128)(2,1)S(1)} %bitcast.99, bf16[3072,128]{1,0:T(8,128)(2,1)S(1)} %bitcast.101, bf16[128,3072]{1,0:T(8,128)(2,1)S(1)} %bitcast.103), custom_call_target="tpu_custom_call" | custom-call | flops 603979776 | bytes 3932160 | tf_op jit(solution)/shard_map/experts/expert_terms/pallas_call | solution.py:107
  51.1 1.5 %collective-permute-done.7 = bf16[128,6144]{1,0:T(8,128)(2,1)S(1)} collective-permute-done((bf16[128,6144]{1,0:T(8,128)(2,1)S(1)}, bf16[128,6144]{1,0:T(8,128)(2,1)S(1)}, u32[]{:S(2)}, u32[]{:S(2)}) %collective-permute-start.7) | collective-permute-done | bytes 1572896 | tf_op jit(solution)/shard_map/experts/ppermute | solution.py:45
  53.2 1.1 %collective-permute-start.10 = (bf16[32,6144]{1,0:T(8,128)(2,1)S(1)}, bf16[32,6144]{1,0:T(8,128)(2,1)S(1)}, u32[]{:S(2)}, u32[]{:S(2)}) collective-permute-start(bf16[32,6144]{1,0:T(8,128)(2,1)S(1)} %get-tuple-element.25), channel_id=1, source_target_pairs={{0,48},{1,49},{2,50},{3,51},{4,52},{5,53},{6,54},{7,55},{16,0},{17... | collective-permute-start | bytes 1179656 | tf_op jit(solution)/shard_map/reduce_heavy/ppermute | solution.py:37
  54.7 1.4 %collective-permute-start.8 = (bf16[32,6144]{1,0:T(8,128)(2,1)S(1)}, bf16[32,6144]{1,0:T(8,128)(2,1)S(1)}, u32[]{:S(2)}, u32[]{:S(2)}) collective-permute-start(bf16[32,6144]{1,0:T(8,128)(2,1)S(1)} %get-tuple-element.27), channel_id=1, source_target_pairs={{0,32},{1,33},{2,34},{3,35},{4,36},{5,37},{6,38},{7,39},{16,48},{1... | collective-permute-start | bytes 1179656 | tf_op jit(solution)/shard_map/reduce_heavy/ppermute | solution.py:37
  56.2 4.0 %collective-permute-done.10.three = bf16[32,6144]{1,0:T(8,128)(2,1)S(1)} collective-permute-done((bf16[32,6144]{1,0:T(8,128)(2,1)S(1)}, bf16[32,6144]{1,0:T(8,128)(2,1)S(1)}, u32[]{:S(2)}, u32[]{:S(2)}) %collective-permute-start.10) | collective-permute-done | bytes 393248 | tf_op jit(solution)/shard_map/reduce_heavy/ppermute | solution.py:37
  60.2 6.5 %collective-permute-done.9.two = bf16[32,6144]{1,0:T(8,128)(2,1)S(1)} collective-permute-done((bf16[32,6144]{1,0:T(8,128)(2,1)S(1)}, bf16[32,6144]{1,0:T(8,128)(2,1)S(1)}, u32[]{:S(2)}, u32[]{:S(2)}) %collective-permute-start.9) | collective-permute-done | bytes 393248 | tf_op jit(solution)/shard_map/reduce_heavy/ppermute | solution.py:37
  67.2 0.7 copy-done.3
  68.0 6.2 %all-to-all-start.1 = ((bf16[32,2,3072]{2,1,0:T(2,128)(2,1)}), bf16[32,2,3072]{2,1,0:T(2,128)(2,1)}, u32[]{:S(2)}, u32[]{:S(2)}) async-start(bf16[32,2,3072]{2,1,0:T(2,128)(2,1)} %copy-done.3), calls=%async_computation.1 | async-start | bytes 786432 | tf_op jit(solution)/shard_map/reduce_plane/all_to_all | solution.py:55
  74.2 2.4 %weight_grads.1 = (bf16[1,3072,128]{2,1,0:T(8,128)(2,1)}, bf16[1,3072,128]{2,1,0:T(8,128)(2,1)}, bf16[1,128,3072]{2,1,0:T(8,128)(2,1)}) custom-call(bf16[128,6272]{1,0:T(8,128)(2,1)S(1)} %pad_maximum_fusion.rows.far, bf16[128,6272]{1,0:T(8,128)(2,1)S(1)} %pad_maximum_fusion.1.rows.near, bf16[128,384]{1,0:T(8,128)(2,1)S(1)} %get-tuple-element.18.acts_far, ...), custom_call_target="tpu_custom_call" | custom-call | flops 603979776 | bytes 5505024 | tf_op jit(solution)/shard_map/weights/weight_grads/pallas_call | solution.py:141
  76.6 12.1 %all-to-all-done.1 = bf16[32,2,3072]{2,1,0:T(2,128)(2,1)} async-done(((bf16[32,2,3072]{2,1,0:T(2,128)(2,1)}), bf16[32,2,3072]{2,1,0:T(2,128)(2,1)}, u32[]{:S(2)}, u32[]{:S(2)}) %all-to-all-start.1) | async-done | bytes 393248 | tf_op jit(solution)/shard_map/reduce_plane/all_to_all | solution.py:55
  88.7 1.2 %fusion = bf16[2,3072]{1,0:T(2,128)(2,1)S(1)} fusion(bf16[32,2,3072]{2,1,0:T(2,128)(2,1)} %all-to-all-done.1), kind=kLoop, calls=%fused_computation.7 | loop fusion | flops 393216 | bytes 405504 | tf_op jit(solution)/shard_map/reduce_plane/convert_element_type | solution.py:198
  89.9 0.6 fusion.4
  (26 shorter events, 3.1 us)
Async XLA Ops:
  27.7 8.8 %collective-permute-start.5 = (bf16[32,6272]{1,0:T(8,128)(2,1)}, bf16[32,6272]{1,0:T(8,128)(2,1)S(1)}, u32[]{:S(2)}, u32[]{:S(2)}) collective-permute-start(bf16[32,6272]{1,0:T(8,128)(2,1)} %pad_maximum_fusion.2), channel_id=1, source_target_pairs={{0,16},{1,17},{2,18},{3,19},{4,20},{5,21},{6,22},{7,23},{16,32},{1... | collective-permute-start | bytes 1204232 | tf_op jit(solution)/shard_map/gather_heavy/ppermute | solution.py:41
  28.9 11.9 %collective-permute-start.3 = (bf16[32,6272]{1,0:T(8,128)(2,1)}, bf16[32,6272]{1,0:T(8,128)(2,1)S(1)}, u32[]{:S(2)}, u32[]{:S(2)}) collective-permute-start(bf16[32,6272]{1,0:T(8,128)(2,1)} %pad_maximum_fusion.2), channel_id=1, source_target_pairs={{0,48},{1,49},{2,50},{3,51},{4,52},{5,53},{6,54},{7,55},{16,0},{17... | collective-permute-start | bytes 1204232 | tf_op jit(solution)/shard_map/gather_heavy/ppermute | solution.py:41
  30.3 14.4 %collective-permute-start.1 = (bf16[32,6272]{1,0:T(8,128)(2,1)}, bf16[32,6272]{1,0:T(8,128)(2,1)S(1)}, u32[]{:S(2)}, u32[]{:S(2)}) collective-permute-start(bf16[32,6272]{1,0:T(8,128)(2,1)} %pad_maximum_fusion.2), channel_id=1, source_target_pairs={{0,32},{1,33},{2,34},{3,35},{4,36},{5,37},{6,38},{7,39},{16,48},{1... | collective-permute-start | bytes 1204232 | tf_op jit(solution)/shard_map/gather_heavy/ppermute | solution.py:41
  32.1 15.4 %copy-start = (bf16[1,3072,128]{2,1,0:T(8,128)(2,1)S(1)}, bf16[1,3072,128]{2,1,0:T(8,128)(2,1)}, u32[]{:S(2)}) copy-start(bf16[1,3072,128]{2,1,0:T(8,128)(2,1)} %param.11) | copy-start | bytes 2359300
  32.1 15.4 %copy-start.1 = (bf16[1,3072,128]{2,1,0:T(8,128)(2,1)S(1)}, bf16[1,3072,128]{2,1,0:T(8,128)(2,1)}, u32[]{:S(2)}) copy-start(bf16[1,3072,128]{2,1,0:T(8,128)(2,1)} %param.12) | copy-start | bytes 2359300
  32.1 15.4 %copy-start.2 = (bf16[1,128,3072]{2,1,0:T(8,128)(2,1)S(1)}, bf16[1,128,3072]{2,1,0:T(8,128)(2,1)}, u32[]{:S(2)}) copy-start(bf16[1,128,3072]{2,1,0:T(8,128)(2,1)} %param.13) | copy-start | bytes 2359300
  32.1 14.1 %collective-permute-start = (bf16[32,6272]{1,0:T(8,128)(2,1)}, bf16[32,6272]{1,0:T(8,128)(2,1)S(1)}, u32[]{:S(2)}, u32[]{:S(2)}) collective-permute-start(bf16[32,6272]{1,0:T(8,128)(2,1)} %pad_maximum_fusion.2), channel_id=1, source_target_pairs={{0,64},{64,0},{1,65},{65,1},{2,66},{66,2},{3,67},{67,3},{4,68},{68... | collective-permute-start | bytes 1204232 | tf_op jit(solution)/shard_map/gather_core/ppermute | solution.py:45
  36.5 9.7 %collective-permute-start.6 = (bf16[32,6272]{1,0:T(8,128)(2,1)S(1)}, bf16[32,6272]{1,0:T(8,128)(2,1)S(1)}, u32[]{:S(2)}, u32[]{:S(2)}) collective-permute-start(bf16[32,6272]{1,0:T(8,128)(2,1)S(1)} %collective-permute-done.5), channel_id=1, source_target_pairs={{0,64},{64,0},{1,65},{65,1},{2,66},{66,2},{3,67},{67,3},{4,68},{68... | collective-permute-start | bytes 1204232 | tf_op jit(solution)/shard_map/gather_core/ppermute | solution.py:45
  40.7 5.5 %collective-permute-start.4 = (bf16[32,6272]{1,0:T(8,128)(2,1)S(1)}, bf16[32,6272]{1,0:T(8,128)(2,1)S(1)}, u32[]{:S(2)}, u32[]{:S(2)}) collective-permute-start(bf16[32,6272]{1,0:T(8,128)(2,1)S(1)} %collective-permute-done.3), channel_id=1, source_target_pairs={{0,64},{64,0},{1,65},{65,1},{2,66},{66,2},{3,67},{67,3},{4,68},{68... | collective-permute-start | bytes 1204232 | tf_op jit(solution)/shard_map/gather_core/ppermute | solution.py:45
  44.7 2.7 %collective-permute-start.2 = (bf16[32,6272]{1,0:T(8,128)(2,1)S(1)}, bf16[32,6272]{1,0:T(8,128)(2,1)S(1)}, u32[]{:S(2)}, u32[]{:S(2)}) collective-permute-start(bf16[32,6272]{1,0:T(8,128)(2,1)S(1)} %collective-permute-done.1), channel_id=1, source_target_pairs={{0,64},{64,0},{1,65},{65,1},{2,66},{66,2},{3,67},{67,3},{4,68},{68... | collective-permute-start | bytes 1204232 | tf_op jit(solution)/shard_map/gather_core/ppermute | solution.py:45
  49.1 3.5 %collective-permute-start.7 = (bf16[128,6144]{1,0:T(8,128)(2,1)S(1)}, bf16[128,6144]{1,0:T(8,128)(2,1)S(1)}, u32[]{:S(2)}, u32[]{:S(2)}) collective-permute-start(bf16[128,6144]{1,0:T(8,128)(2,1)S(1)} %get-tuple-element.17), channel_id=1, source_target_pairs={{0,64},{64,0},{1,65},{65,1},{2,66},{66,2},{3,67},{67,3},{4,68},{68... | collective-permute-start | bytes 4718600 | tf_op jit(solution)/shard_map/experts/ppermute | solution.py:45
  53.2 7.0 %collective-permute-start.10 = (bf16[32,6144]{1,0:T(8,128)(2,1)S(1)}, bf16[32,6144]{1,0:T(8,128)(2,1)S(1)}, u32[]{:S(2)}, u32[]{:S(2)}) collective-permute-start(bf16[32,6144]{1,0:T(8,128)(2,1)S(1)} %get-tuple-element.25), channel_id=1, source_target_pairs={{0,48},{1,49},{2,50},{3,51},{4,52},{5,53},{6,54},{7,55},{16,0},{17... | collective-permute-start | bytes 1179656 | tf_op jit(solution)/shard_map/reduce_heavy/ppermute | solution.py:37
  54.3 12.3 %collective-permute-start.9 = (bf16[32,6144]{1,0:T(8,128)(2,1)S(1)}, bf16[32,6144]{1,0:T(8,128)(2,1)S(1)}, u32[]{:S(2)}, u32[]{:S(2)}) collective-permute-start(bf16[32,6144]{1,0:T(8,128)(2,1)S(1)} %get-tuple-element.26), channel_id=1, source_target_pairs={{0,16},{1,17},{2,18},{3,19},{4,20},{5,21},{6,22},{7,23},{16,32},{1... | collective-permute-start | bytes 1179656 | tf_op jit(solution)/shard_map/reduce_heavy/ppermute | solution.py:37
  54.7 11.9 %collective-permute-start.8 = (bf16[32,6144]{1,0:T(8,128)(2,1)S(1)}, bf16[32,6144]{1,0:T(8,128)(2,1)S(1)}, u32[]{:S(2)}, u32[]{:S(2)}) collective-permute-start(bf16[32,6144]{1,0:T(8,128)(2,1)S(1)} %get-tuple-element.27), channel_id=1, source_target_pairs={{0,32},{1,33},{2,34},{3,35},{4,36},{5,37},{6,38},{7,39},{16,48},{1... | collective-permute-start | bytes 1179656 | tf_op jit(solution)/shard_map/reduce_heavy/ppermute | solution.py:37
  67.2 0.7 copy-start.3
  68.0 20.7 %all-to-all-start.1 = ((bf16[32,2,3072]{2,1,0:T(2,128)(2,1)}), bf16[32,2,3072]{2,1,0:T(2,128)(2,1)}, u32[]{:S(2)}, u32[]{:S(2)}) async-start(bf16[32,2,3072]{2,1,0:T(2,128)(2,1)} %copy-done.3), calls=%async_computation.1 | async-start | bytes 786432 | tf_op jit(solution)/shard_map/reduce_plane/all_to_all | solution.py:55

commit v7 on v5

--- a/solution.py
+++ b/solution.py
@@ -5,7 +5,7 @@
 from jax.experimental.pallas import tpu as pltpu
 from jax.sharding import Mesh, PartitionSpec as P
 
-NX_HI, NCORE, NY, NX_LO, NZ, RING = 2, 2, 4, 2, 8, 4
+NX_HI, NCORE, NY, NX_LO, NZ, RING, PLANE = 2, 2, 4, 2, 8, 4, 32
 AXES = ("x_hi", "core", "y", "x_lo", "z")
 EP, TP = ("x_hi", "core"), ("y", "x_lo", "z")
 D, PAD, UNITS = 3072, 128, 128
@@ -48,6 +48,16 @@
 
 def exchanged(value, axis):
     return lax.all_to_all(value, axis, 0, 0, tiled=True)
+
+
+def planes():
+    along_x = [[flat(x, 0, y, z) for x in range(RING) for z in range(NZ)] for y in range(RING)]
+    along_y = [[flat(x, 1, y, z) for y in range(RING) for z in range(NZ)] for x in range(RING)]
+    return along_x + along_y
+
+
+def scattered(value):
+    return lax.all_to_all(value, AXES, 0, 0, axis_index_groups=planes(), tiled=True)
 
 
 def dot(left, right, left_dim, right_dim):
@@ -142,7 +152,7 @@
         ),
         in_specs=[VMEM] * 4,
         out_specs=(VMEM,) * 3,
-        compiler_params=grant(16),
+        compiler_params=grant(8),
         cost_estimate=pl.CostEstimate(
             flops=6 * n * D * UNITS, transcendentals=0, bytes_accessed=4 * n * D + 6 * D * UNITS
         ),
@@ -151,19 +161,24 @@
 
 
 def last_kernel(own, one, two, three, out):
-    total = own[...] + one[...].astype(F32) + two[...].astype(F32) + three[...].astype(F32)
-    for i in range(NZ):
-        row = total[i : i + 1]
-        out[i] = jnp.concatenate([row[:, :D], row[:, D:]], axis=0).astype(BF16)
+    x, y = lax.axis_index(("x_hi", "x_lo")), lax.axis_index("y")
+    place = jnp.where(lax.axis_index("core") == 0, x, y).astype(jnp.int32)
+    for k, d in enumerate((0,) + ORDER):
+        at = slice(k * NZ, (k + 1) * NZ)
+        total = own[at] + one[at].astype(F32) + two[at].astype(F32) + three[at].astype(F32)
+        first = lax.rem(place + d, RING) * NZ
+        for i in range(NZ):
+            row = total[i : i + 1]
+            out[first + i] = jnp.concatenate([row[:, :D], row[:, D:]], axis=0).astype(BF16)
 
 
 def summed_pairs(own, parts):
     return pl.pallas_call(
         last_kernel,
-        out_shape=jax.ShapeDtypeStruct((NZ, 2, D), BF16),
+        out_shape=jax.ShapeDtypeStruct((PLANE, 2, D), BF16),
         in_specs=[VMEM] * 4,
         out_specs=VMEM,
-        compiler_params=grant(1),
+        compiler_params=grant(2),
         name="summed_pairs",
     )(own, *parts)
 
@@ -188,15 +203,12 @@
     with jax.named_scope("weights"):
         grad_g, grad_u, grad_d = weight_grads(far, near, far_acts, near_acts)
     with jax.named_scope("reduce_heavy"):
-        total = (near_terms + other.astype(F32)).reshape(RING, RING * NZ, 2 * D)
+        total = (near_terms + other.astype(F32)).reshape(RING, PLANE, 2 * D)
         got = [give(total[1 + i].astype(BF16), "heavy", d) for i, d in enumerate(ORDER)]
-        total = total[0] + sum(g.astype(F32) for g in got)
-    with jax.named_scope("reduce_light"):
-        total = total.reshape(RING, NZ, 2 * D)
-        got = [give(total[1 + i].astype(BF16), "light", d) for i, d in enumerate(ORDER)]
-    with jax.named_scope("reduce_z"):
-        got = exchanged(summed_pairs(total[0], got), "z")
-        total = sum(got[i].astype(F32) for i in range(NZ)).astype(BF16)
+        *got, grad_g, grad_u, grad_d = lax.optimization_barrier((*got, grad_g, grad_u, grad_d))
+    with jax.named_scope("reduce_plane"):
+        got = scattered(summed_pairs(total[0], got))
+        total = sum(got[i].astype(F32) for i in range(PLANE)).astype(BF16)
     return total[:1], total[1:], grad_g, grad_u, grad_d
 
 

time: 87.9 us -> 86.6 us (0.985); the launches traced: 86.7 us -> 86.3 us
  blocking collectives: 16.6 us -> 34.9 us
  waiting for transfers between devices: 38 us -> 26.1 us
  starting transfers between devices: 21.5 us -> 15 us
    all_to_all x0 -> x1, blocking collectives: none -> 18.3 us  [scattered(): lax.all_to_all(value, AXES, 0, 0, axis_index_groups=planes(), tiled=True)]
    ppermute x6 -> x3, waiting for transfers between devices: 15.2 us -> 8.43 us  [give(): return lax.ppermute(value, AXES, pairs(stage, d))]
    all_to_all x1 -> x0, waiting for transfers between devices: 5.07 us -> none  [exchanged(): return lax.all_to_all(value, axis, 0, 0, tiled=True)]
    all_to_all x1 -> x0, starting transfers between devices: 3.36 us -> none  [exchanged(): return lax.all_to_all(value, axis, 0, 0, tiled=True)]
    ppermute x6 -> x3, starting transfers between devices: 5.74 us -> 2.55 us  [give(): return lax.ppermute(value, AXES, pairs(stage, d))]
  transfers between devices with their start and end apart: 18 -> 14, of which waited for: 12 -> 8; matrix products, arithmetic and copies ran while one was open for 0% -> 0% of each run, Pallas kernels for 4% -> 4%
where the time goes in v7:
time: 86.6 us; the launch traced here: 86.3 us
  blocking collectives  34.9 us (40%)
  waiting for transfers between devices  26.1 us (30%)
  starting transfers between devices  15 us (17%)
  Pallas kernels  7.41 us (9%)
  local copies, waits for them, and re-layouts  1.37 us (2%)
    all_to_all x1, blocking collectives, scattered(): lax.all_to_all(value, AXES, 0, 0, axis_index_groups=planes(), tiled=True)  18.3 us
    all_to_all x1, blocking collectives, exchanged(): return lax.all_to_all(value, axis, 0, 0, tiled=True)  16.6 us
    ppermute x6, waiting for transfers between devices, fetch(): return lax.ppermute(value, AXES, pairs(stage, -d))  14.8 us
    ppermute x3, waiting for transfers between devices, give(): return lax.ppermute(value, AXES, pairs(stage, d))  8.43 us
    ppermute x6, starting transfers between devices, fetch(): return lax.ppermute(value, AXES, pairs(stage, -d))  6.53 us
    ppermute x5, starting transfers between devices, swapped(): return lax.ppermute(value, 'core', [(0, 1), (1, 0)])  5.88 us
    pallas_call x2, Pallas kernels, expert_terms(): pl.pallas_call(expert_kernel, out_shape=(jax.ShapeDtypeStruct((n, 2 * D),...  2.93 us
    ppermute x5, waiting for transfers between devices, swapped(): return lax.ppermute(value, 'core', [(0, 1), (1, 0)])  2.86 us
  transfers between devices with their start and end apart: 14, of which 8 were waited for; matrix products, arithmetic and copies ran while one was open for 0% of the time, Pallas kernels for 4%

profile of v7, /device:TPU:1, one launch (start us, length us, event | category | flops | bytes accessed | tf_op | source)
XLA Modules:
  0.0 86.3 jit_solution(3573242176002482317)
XLA Ops:
  0.6 1.5 %copies_of_row.1 = bf16[8,2,3200]{2,1,0:T(2,128)(2,1)} custom-call(bf16[1,3072]{1,0:T(2,128)(2,1)} %tokens.1, bf16[1,3072]{1,0:T(2,128)(2,1)} %cotangent.1, s32[1,2]{1,0:T(1,128)} %routes.1, bf16[1,2]{1,0:T(2,128)(2,1)} %weights.1), custom_call_target="tpu_custom_call" | custom-call | tf_op jit(solution)/shard_map/gather_z/copies_of_row/pallas_call | solution.py:81
  2.1 16.6 %all_to_all.10 = bf16[8,2,3200]{2,1,0:T(2,128)(2,1)S(1)} all-to-all(bf16[8,2,3200]{2,1,0:T(2,128)(2,1)} %copies_of_row.1), channel_id=1, replica_groups=mesh['x_hi'=2,'core'=2,'y'=4,'x_lo'=2,'z'=8] {'z'}, dimensions={0} | all-to-all | bytes 204800 | tf_op jit(solution)/shard_map/gather_z/all_to_all | solution.py:50
  18.9 2.8 %collective-permute-start.1 = (bf16[8,6272]{1,0:T(8,128)(2,1)S(1)}, bf16[8,6272]{1,0:T(8,128)(2,1)S(1)}, u32[]{:S(2)}, u32[]{:S(2)}) collective-permute-start(bf16[8,6272]{1,0:T(8,128)(2,1)S(1)} %get-tuple-element.38), channel_id=1, source_target_pairs={{0,136},{1,137},{2,138},{3,139},{4,140},{5,141},{6,142},{7,143},{1... | collective-permute-start | bytes 301064 | tf_op jit(solution)/shard_map/gather_light/ppermute | solution.py:42
  22.1 0.7 collective-permute-start.2
  22.8 1.6 %collective-permute-done.1 = bf16[8,6272]{1,0:T(8,128)(2,1)S(1)} collective-permute-done((bf16[8,6272]{1,0:T(8,128)(2,1)S(1)}, bf16[8,6272]{1,0:T(8,128)(2,1)S(1)}, u32[]{:S(2)}, u32[]{:S(2)}) %collective-permute-start.1) | collective-permute-done | bytes 100384 | tf_op jit(solution)/shard_map/gather_light/ppermute | solution.py:42
  24.4 2.4 %collective-permute-done = bf16[8,6272]{1,0:T(8,128)(2,1)S(1)} collective-permute-done((bf16[8,6272]{1,0:T(8,128)(2,1)S(1)}, bf16[8,6272]{1,0:T(8,128)(2,1)S(1)}, u32[]{:S(2)}, u32[]{:S(2)}) %collective-permute-start) | collective-permute-done | bytes 100384 | tf_op jit(solution)/shard_map/gather_light/ppermute | solution.py:42
  26.9 1.0 %collective-permute-done.2 = bf16[8,6272]{1,0:T(8,128)(2,1)S(1)} collective-permute-done((bf16[8,6272]{1,0:T(8,128)(2,1)S(1)}, bf16[8,6272]{1,0:T(8,128)(2,1)S(1)}, u32[]{:S(2)}, u32[]{:S(2)}) %collective-permute-start.2) | collective-permute-done | bytes 100384 | tf_op jit(solution)/shard_map/gather_light/ppermute | solution.py:42
  27.9 3.4 %collective-permute-start.6 = (bf16[32,6272]{1,0:T(8,128)(2,1)S(1)}, bf16[32,6272]{1,0:T(8,128)(2,1)S(1)}, u32[]{:S(2)}, u32[]{:S(2)}) collective-permute-start(bf16[32,6272]{1,0:T(8,128)(2,1)S(1)} %pad_maximum_fusion), channel_id=1, source_target_pairs={{0,64},{64,0},{1,65},{65,1},{2,66},{66,2},{3,67},{67,3},{4,68},{68... | collective-permute-start | bytes 1204232 | tf_op jit(solution)/shard_map/gather_core/ppermute | solution.py:46
  31.2 2.7 %collective-permute-start.4 = (bf16[32,6272]{1,0:T(8,128)(2,1)S(1)}, bf16[32,6272]{1,0:T(8,128)(2,1)S(1)}, u32[]{:S(2)}, u32[]{:S(2)}) collective-permute-start(bf16[32,6272]{1,0:T(8,128)(2,1)S(1)} %pad_maximum_fusion), channel_id=1, source_target_pairs={{0,48},{1,49},{2,50},{3,51},{4,52},{5,53},{6,54},{7,55},{16,0},{17... | collective-permute-start | bytes 1204232 | tf_op jit(solution)/shard_map/gather_heavy/ppermute | solution.py:42
  34.0 9.8 %collective-permute-done.5 = bf16[32,6272]{1,0:T(8,128)(2,1)S(1)} collective-permute-done((bf16[32,6272]{1,0:T(8,128)(2,1)S(1)}, bf16[32,6272]{1,0:T(8,128)(2,1)S(1)}, u32[]{:S(2)}, u32[]{:S(2)}) %collective-permute-start.5) | collective-permute-done | bytes 401440 | tf_op jit(solution)/shard_map/gather_heavy/ppermute | solution.py:42
  43.8 0.5 collective-permute-start.8
  44.3 1.7 %collective-permute-start.7 = (bf16[32,6272]{1,0:T(8,128)(2,1)S(1)}, bf16[32,6272]{1,0:T(8,128)(2,1)S(1)}, u32[]{:S(2)}, u32[]{:S(2)}) collective-permute-start(bf16[32,6272]{1,0:T(8,128)(2,1)S(1)} %collective-permute-done.3), channel_id=1, source_target_pairs={{0,64},{64,0},{1,65},{65,1},{2,66},{66,2},{3,67},{67,3},{4,68},{68... | collective-permute-start | bytes 1204232 | tf_op jit(solution)/shard_map/gather_core/ppermute | solution.py:46
  46.0 1.2 %collective-permute-done.7 = bf16[32,6272]{1,0:T(8,128)(2,1)S(1)} collective-permute-done((bf16[32,6272]{1,0:T(8,128)(2,1)S(1)}, bf16[32,6272]{1,0:T(8,128)(2,1)S(1)}, u32[]{:S(2)}, u32[]{:S(2)}) %collective-permute-start.7) | collective-permute-done | bytes 401440 | tf_op jit(solution)/shard_map/gather_core/ppermute | solution.py:46
  47.6 1.5 %expert_terms.3 = (bf16[128,6144]{1,0:T(8,128)(2,1)S(1)}, bf16[128,384]{1,0:T(8,128)(2,1)S(1)}) custom-call(s32[1]{0:T(128)} %bitcast.group, bf16[128,6272]{1,0:T(8,128)(2,1)S(1)} %constant_dynamic-update-slice_fusion.7.rows.far, bf16[3072,128]{1,0:T(8,128)(2,1)S(1)} %bitcast.98, bf16[3072,128]{1,0:T(8,128)(2,1)S(1)} %bitcast.100, ...), custom_call_target="tpu_custom_call" | custom-call | flops 603979776 | bytes 3932160 | tf_op jit(solution)/shard_map/experts/expert_terms/pallas_call | solution.py:112
  49.5 1.5 %expert_terms.2 = (f32[128,6144]{1,0:T(8,128)S(1)}, bf16[128,384]{1,0:T(8,128)(2,1)S(1)}) custom-call(s32[1]{0:T(128)} %bitcast.group, bf16[128,6272]{1,0:T(8,128)(2,1)S(1)} %constant_dynamic-update-slice_fusion.rows.near, bf16[3072,128]{1,0:T(8,128)(2,1)S(1)} %bitcast.99, bf16[3072,128]{1,0:T(8,128)(2,1)S(1)} %bitcast.101, bf16[128,3072]{1,0:T(8,128)(2,1)S(1)} %bitcast.103), custom_call_target="tpu_custom_call" | custom-call | flops 603979776 | bytes 3932160 | tf_op jit(solution)/shard_map/experts/expert_terms/pallas_call | solution.py:112
  50.9 1.6 %collective-permute-done.10 = bf16[128,6144]{1,0:T(8,128)(2,1)S(1)} collective-permute-done((bf16[128,6144]{1,0:T(8,128)(2,1)S(1)}, bf16[128,6144]{1,0:T(8,128)(2,1)S(1)}, u32[]{:S(2)}, u32[]{:S(2)}) %collective-permute-start.10) | collective-permute-done | bytes 1572896 | tf_op jit(solution)/shard_map/experts/ppermute | solution.py:46
  53.1 1.1 %collective-permute-start.13 = (bf16[32,6144]{1,0:T(8,128)(2,1)S(1)}, bf16[32,6144]{1,0:T(8,128)(2,1)S(1)}, u32[]{:S(2)}, u32[]{:S(2)}) collective-permute-start(bf16[32,6144]{1,0:T(8,128)(2,1)S(1)} %get-tuple-element.33), channel_id=1, source_target_pairs={{0,48},{1,49},{2,50},{3,51},{4,52},{5,53},{6,54},{7,55},{16,0},{17... | collective-permute-start | bytes 1179656 | tf_op jit(solution)/shard_map/reduce_heavy/ppermute | solution.py:38
  54.7 1.0 %collective-permute-start.11 = (bf16[32,6144]{1,0:T(8,128)(2,1)S(1)}, bf16[32,6144]{1,0:T(8,128)(2,1)S(1)}, u32[]{:S(2)}, u32[]{:S(2)}) collective-permute-start(bf16[32,6144]{1,0:T(8,128)(2,1)S(1)} %get-tuple-element.35), channel_id=1, source_target_pairs={{0,32},{1,33},{2,34},{3,35},{4,36},{5,37},{6,38},{7,39},{16,48},{1... | collective-permute-start | bytes 1179656 | tf_op jit(solution)/shard_map/reduce_heavy/ppermute | solution.py:38
  55.7 2.4 %weight_grads.1 = (bf16[1,3072,128]{2,1,0:T(8,128)(2,1)}, bf16[1,3072,128]{2,1,0:T(8,128)(2,1)}, bf16[1,128,3072]{2,1,0:T(8,128)(2,1)}) custom-call(bf16[128,6272]{1,0:T(8,128)(2,1)S(1)} %constant_dynamic-update-slice_fusion.7.rows.far, bf16[128,6272]{1,0:T(8,128)(2,1)S(1)} %constant_dynamic-update-slice_fusion.rows.near, ...), custom_call_target="tpu_custom_call" | custom-call | flops 603979776 | bytes 5505024 | tf_op jit(solution)/shard_map/weights/weight_grads/pallas_call | solution.py:146
  58.2 2.0 %collective-permute-done.13.three = bf16[32,6144]{1,0:T(8,128)(2,1)S(1)} collective-permute-done((bf16[32,6144]{1,0:T(8,128)(2,1)S(1)}, bf16[32,6144]{1,0:T(8,128)(2,1)S(1)}, u32[]{:S(2)}, u32[]{:S(2)}) %collective-permute-start.13) | collective-permute-done | bytes 393248 | tf_op jit(solution)/shard_map/reduce_heavy/ppermute | solution.py:38
  60.1 6.4 %collective-permute-done.12.two = bf16[32,6144]{1,0:T(8,128)(2,1)S(1)} collective-permute-done((bf16[32,6144]{1,0:T(8,128)(2,1)S(1)}, bf16[32,6144]{1,0:T(8,128)(2,1)S(1)}, u32[]{:S(2)}, u32[]{:S(2)}) %collective-permute-start.12) | collective-permute-done | bytes 393248 | tf_op jit(solution)/shard_map/reduce_heavy/ppermute | solution.py:38
  66.6 0.6 summed_pairs.1
  67.2 18.3 %all_to_all.11 = bf16[32,2,3072]{2,1,0:T(2,128)(2,1)S(1)} all-to-all(bf16[32,2,3072]{2,1,0:T(2,128)(2,1)S(1)} %summed_pairs.1), channel_id=1, replica_groups={{0,1,2,3,4,5,6,7,8,9,10,11,12,13,14,15,128,129,130,131,132,133,134,135,..., dimensions={0} | all-to-all | bytes 786432 | tf_op jit(solution)/shard_map/reduce_plane/all_to_all | solution.py:60
  85.7 0.6 fusion.4
  (38 shorter events, 2.7 us)
Async XLA Ops:
  18.9 5.5 %collective-permute-start.1 = (bf16[8,6272]{1,0:T(8,128)(2,1)S(1)}, bf16[8,6272]{1,0:T(8,128)(2,1)S(1)}, u32[]{:S(2)}, u32[]{:S(2)}) collective-permute-start(bf16[8,6272]{1,0:T(8,128)(2,1)S(1)} %get-tuple-element.38), channel_id=1, source_target_pairs={{0,136},{1,137},{2,138},{3,139},{4,140},{5,141},{6,142},{7,143},{1... | collective-permute-start | bytes 301064 | tf_op jit(solution)/shard_map/gather_light/ppermute | solution.py:42
  21.8 5.1 %collective-permute-start = (bf16[8,6272]{1,0:T(8,128)(2,1)S(1)}, bf16[8,6272]{1,0:T(8,128)(2,1)S(1)}, u32[]{:S(2)}, u32[]{:S(2)}) collective-permute-start(bf16[8,6272]{1,0:T(8,128)(2,1)S(1)} %get-tuple-element.38), channel_id=1, source_target_pairs={{0,128},{1,129},{2,130},{3,131},{4,132},{5,133},{6,134},{7,135},{1... | collective-permute-start | bytes 301064 | tf_op jit(solution)/shard_map/gather_light/ppermute | solution.py:42
  22.1 5.7 %collective-permute-start.2 = (bf16[8,6272]{1,0:T(8,128)(2,1)S(1)}, bf16[8,6272]{1,0:T(8,128)(2,1)S(1)}, u32[]{:S(2)}, u32[]{:S(2)}) collective-permute-start(bf16[8,6272]{1,0:T(8,128)(2,1)S(1)} %get-tuple-element.38), channel_id=1, source_target_pairs={{0,8},{1,9},{2,10},{3,11},{4,12},{5,13},{6,14},{7,15},{16,24},{17,... | collective-permute-start | bytes 301064 | tf_op jit(solution)/shard_map/gather_light/ppermute | solution.py:42
  27.9 18.1 %collective-permute-start.6 = (bf16[32,6272]{1,0:T(8,128)(2,1)S(1)}, bf16[32,6272]{1,0:T(8,128)(2,1)S(1)}, u32[]{:S(2)}, u32[]{:S(2)}) collective-permute-start(bf16[32,6272]{1,0:T(8,128)(2,1)S(1)} %pad_maximum_fusion), channel_id=1, source_target_pairs={{0,64},{64,0},{1,65},{65,1},{2,66},{66,2},{3,67},{67,3},{4,68},{68... | collective-permute-start | bytes 1204232 | tf_op jit(solution)/shard_map/gather_core/ppermute | solution.py:46
  31.2 12.5 %collective-permute-start.5 = (bf16[32,6272]{1,0:T(8,128)(2,1)S(1)}, bf16[32,6272]{1,0:T(8,128)(2,1)S(1)}, u32[]{:S(2)}, u32[]{:S(2)}) collective-permute-start(bf16[32,6272]{1,0:T(8,128)(2,1)S(1)} %pad_maximum_fusion), channel_id=1, source_target_pairs={{0,16},{1,17},{2,18},{3,19},{4,20},{5,21},{6,22},{7,23},{16,32},{1... | collective-permute-start | bytes 1204232 | tf_op jit(solution)/shard_map/gather_heavy/ppermute | solution.py:42
  31.2 12.5 %collective-permute-start.4 = (bf16[32,6272]{1,0:T(8,128)(2,1)S(1)}, bf16[32,6272]{1,0:T(8,128)(2,1)S(1)}, u32[]{:S(2)}, u32[]{:S(2)}) collective-permute-start(bf16[32,6272]{1,0:T(8,128)(2,1)S(1)} %pad_maximum_fusion), channel_id=1, source_target_pairs={{0,48},{1,49},{2,50},{3,51},{4,52},{5,53},{6,54},{7,55},{16,0},{17... | collective-permute-start | bytes 1204232 | tf_op jit(solution)/shard_map/gather_heavy/ppermute | solution.py:42
  33.9 10.4 %collective-permute-start.3 = (bf16[32,6272]{1,0:T(8,128)(2,1)S(1)}, bf16[32,6272]{1,0:T(8,128)(2,1)S(1)}, u32[]{:S(2)}, u32[]{:S(2)}) collective-permute-start(bf16[32,6272]{1,0:T(8,128)(2,1)S(1)} %pad_maximum_fusion), channel_id=1, source_target_pairs={{0,32},{1,33},{2,34},{3,35},{4,36},{5,37},{6,38},{7,39},{16,48},{1... | collective-permute-start | bytes 1204232 | tf_op jit(solution)/shard_map/gather_heavy/ppermute | solution.py:42
  43.7 3.6 %collective-permute-start.9 = (bf16[32,6272]{1,0:T(8,128)(2,1)S(1)}, bf16[32,6272]{1,0:T(8,128)(2,1)S(1)}, u32[]{:S(2)}, u32[]{:S(2)}) collective-permute-start(bf16[32,6272]{1,0:T(8,128)(2,1)S(1)} %collective-permute-done.5), channel_id=1, source_target_pairs={{0,64},{64,0},{1,65},{65,1},{2,66},{66,2},{3,67},{67,3},{4,68},{68... | collective-permute-start | bytes 1204232 | tf_op jit(solution)/shard_map/gather_core/ppermute | solution.py:46
  43.8 3.6 %collective-permute-start.8 = (bf16[32,6272]{1,0:T(8,128)(2,1)S(1)}, bf16[32,6272]{1,0:T(8,128)(2,1)S(1)}, u32[]{:S(2)}, u32[]{:S(2)}) collective-permute-start(bf16[32,6272]{1,0:T(8,128)(2,1)S(1)} %collective-permute-done.4), channel_id=1, source_target_pairs={{0,64},{64,0},{1,65},{65,1},{2,66},{66,2},{3,67},{67,3},{4,68},{68... | collective-permute-start | bytes 1204232 | tf_op jit(solution)/shard_map/gather_core/ppermute | solution.py:46
  44.3 3.0 %collective-permute-start.7 = (bf16[32,6272]{1,0:T(8,128)(2,1)S(1)}, bf16[32,6272]{1,0:T(8,128)(2,1)S(1)}, u32[]{:S(2)}, u32[]{:S(2)}) collective-permute-start(bf16[32,6272]{1,0:T(8,128)(2,1)S(1)} %collective-permute-done.3), channel_id=1, source_target_pairs={{0,64},{64,0},{1,65},{65,1},{2,66},{66,2},{3,67},{67,3},{4,68},{68... | collective-permute-start | bytes 1204232 | tf_op jit(solution)/shard_map/gather_core/ppermute | solution.py:46
  46.0 1.5 %copy-start = (bf16[1,3072,128]{2,1,0:T(8,128)(2,1)S(1)}, bf16[1,3072,128]{2,1,0:T(8,128)(2,1)}, u32[]{:S(2)}) copy-start(bf16[1,3072,128]{2,1,0:T(8,128)(2,1)} %param.11) | copy-start | bytes 2359300
  46.0 1.5 %copy-start.1 = (bf16[1,3072,128]{2,1,0:T(8,128)(2,1)S(1)}, bf16[1,3072,128]{2,1,0:T(8,128)(2,1)}, u32[]{:S(2)}) copy-start(bf16[1,3072,128]{2,1,0:T(8,128)(2,1)} %param.12) | copy-start | bytes 2359300
  46.0 1.6 %copy-start.2 = (bf16[1,128,3072]{2,1,0:T(8,128)(2,1)S(1)}, bf16[1,128,3072]{2,1,0:T(8,128)(2,1)}, u32[]{:S(2)}) copy-start(bf16[1,128,3072]{2,1,0:T(8,128)(2,1)} %param.13) | copy-start | bytes 2359300
  49.1 3.5 %collective-permute-start.10 = (bf16[128,6144]{1,0:T(8,128)(2,1)S(1)}, bf16[128,6144]{1,0:T(8,128)(2,1)S(1)}, u32[]{:S(2)}, u32[]{:S(2)}) collective-permute-start(bf16[128,6144]{1,0:T(8,128)(2,1)S(1)} %get-tuple-element.19), channel_id=1, source_target_pairs={{0,64},{64,0},{1,65},{65,1},{2,66},{66,2},{3,67},{67,3},{4,68},{68... | collective-permute-start | bytes 4718600 | tf_op jit(solution)/shard_map/experts/ppermute | solution.py:46
  53.1 7.0 %collective-permute-start.13 = (bf16[32,6144]{1,0:T(8,128)(2,1)S(1)}, bf16[32,6144]{1,0:T(8,128)(2,1)S(1)}, u32[]{:S(2)}, u32[]{:S(2)}) collective-permute-start(bf16[32,6144]{1,0:T(8,128)(2,1)S(1)} %get-tuple-element.33), channel_id=1, source_target_pairs={{0,48},{1,49},{2,50},{3,51},{4,52},{5,53},{6,54},{7,55},{16,0},{17... | collective-permute-start | bytes 1179656 | tf_op jit(solution)/shard_map/reduce_heavy/ppermute | solution.py:38
  54.2 12.3 %collective-permute-start.12 = (bf16[32,6144]{1,0:T(8,128)(2,1)S(1)}, bf16[32,6144]{1,0:T(8,128)(2,1)S(1)}, u32[]{:S(2)}, u32[]{:S(2)}) collective-permute-start(bf16[32,6144]{1,0:T(8,128)(2,1)S(1)} %get-tuple-element.34), channel_id=1, source_target_pairs={{0,16},{1,17},{2,18},{3,19},{4,20},{5,21},{6,22},{7,23},{16,32},{1... | collective-permute-start | bytes 1179656 | tf_op jit(solution)/shard_map/reduce_heavy/ppermute | solution.py:38
  54.7 11.9 %collective-permute-start.11 = (bf16[32,6144]{1,0:T(8,128)(2,1)S(1)}, bf16[32,6144]{1,0:T(8,128)(2,1)S(1)}, u32[]{:S(2)}, u32[]{:S(2)}) collective-permute-start(bf16[32,6144]{1,0:T(8,128)(2,1)S(1)} %get-tuple-element.35), channel_id=1, source_target_pairs={{0,32},{1,33},{2,34},{3,35},{4,36},{5,37},{6,38},{7,39},{16,48},{1... | collective-permute-start | bytes 1179656 | tf_op jit(solution)/shard_map/reduce_heavy/ppermute | solution.py:38

commit v8 on v7

--- a/solution.py
+++ b/solution.py
@@ -12,7 +12,7 @@
 F32, BF16 = jnp.float32, jnp.bfloat16
 VMEM = pl.BlockSpec(memory_space=pltpu.VMEM)
 SMEM = pl.BlockSpec(memory_space=pltpu.SMEM)
-ORDER = (2, 1, 3)
+ORDER, ISSUE = (2, 1, 3), (3, 1, 2)
 
 
 def grant(mebibytes):
@@ -125,24 +125,19 @@
     )(group, rows, gate_slice, up_slice, down_slice)
 
 
-def weight_kernel(far, near, acts_far, acts_near, grad_g, grad_u, grad_d):
-    u = UNITS
-
-    def both(left_at, left_rows, right_at):
-        def part(rows, acts):
-            left = rows[:, left_at : left_at + D] if left_rows else acts[:, :u]
-            right = acts[:, right_at : right_at + u] if left_rows else rows[:, D : 2 * D]
-            return dot(left, right, 0, 0)
-
-        return (part(far, acts_far) + part(near, acts_near)).astype(BF16)
-
-    grad_g[0] = both(0, True, u)
-    grad_u[0] = both(0, True, 2 * u)
-    grad_d[0] = both(0, False, 0)
-
-
-def weight_grads(far, near, acts_far, acts_near):
-    n = 2 * far.shape[0]
+def weight_kernel(*refs):
+    u, parts = UNITS, len(refs) // 2
+    grad_g, grad_u, grad_d = refs[-3:]
+    pairs_of = list(zip(refs[: parts - 1], refs[parts - 1 : -3]))
+    for grad, at in ((grad_g, u), (grad_u, 2 * u)):
+        total = sum(dot(rows[:, :D], acts[:, at : at + u], 0, 0) for rows, acts in pairs_of)
+        grad[0] = total.astype(BF16)
+    total = sum(dot(acts[:, :u], rows[:, D : 2 * D], 0, 0) for rows, acts in pairs_of)
+    grad_d[0] = total.astype(BF16)
+
+
+def weight_grads(rows, acts):
+    n = sum(r.shape[0] for r in rows)
     return pl.pallas_call(
         weight_kernel,
         out_shape=(
@@ -150,14 +145,14 @@
             jax.ShapeDtypeStruct((1, D, UNITS), BF16),
             jax.ShapeDtypeStruct((1, UNITS, D), BF16),
         ),
-        in_specs=[VMEM] * 4,
+        in_specs=[VMEM] * (len(rows) + len(acts)),
         out_specs=(VMEM,) * 3,
         compiler_params=grant(8),
         cost_estimate=pl.CostEstimate(
             flops=6 * n * D * UNITS, transcendentals=0, bytes_accessed=4 * n * D + 6 * D * UNITS
         ),
         name="weight_grads",
-    )(far, near, acts_far, acts_near)
+    )(*rows, *acts)
 
 
 def last_kernel(own, one, two, three, out):
@@ -190,24 +185,34 @@
         rows = exchanged(copies_of_row(tokens, cotangent, routes, gate_weights), "z")
         rows = jnp.concatenate([rows[:, 0, :D], rows[:, 1, :D], rows[:, 0, D:]], axis=1)
     with jax.named_scope("gather_light"):
-        rows = jnp.concatenate([rows] + [fetch(rows, "light", d) for d in ORDER], axis=0)
+        got = {d: fetch(rows, "light", d) for d in (2, 3, 1)}
+        rows = jnp.concatenate([rows] + [got[d] for d in ORDER], axis=0)
     with jax.named_scope("gather_heavy"):
-        near = [rows] + [fetch(rows, "heavy", d) for d in ORDER]
+        got = {d: fetch(rows, "heavy", d) for d in ISSUE}
     with jax.named_scope("gather_core"):
-        far = jnp.concatenate([swapped(chunk) for chunk in near], axis=0)
-        near = jnp.concatenate(near, axis=0)
+        own, got[2] = lax.optimization_barrier((rows, got[2]))
+        far = {d: swapped(got[d]) for d in ORDER}
+        far_one = jnp.concatenate([swapped(own), far[2]], axis=0)
+        far_two = jnp.concatenate([far[1], far[3]], axis=0)
+        near = jnp.concatenate([own] + [got[d] for d in ORDER], axis=0)
     with jax.named_scope("experts"):
-        far_terms, far_acts = expert_terms(group, far, *slices, BF16)
-        other = swapped(far_terms)
+        terms_one, acts_one = expert_terms(group, far_one, *slices, BF16)
+        other_one = swapped(terms_one)
+        terms_two, acts_two = expert_terms(group, far_two, *slices, BF16)
+        other_two = swapped(terms_two)
         near_terms, near_acts = expert_terms(group, near, *slices, F32)
     with jax.named_scope("weights"):
-        grad_g, grad_u, grad_d = weight_grads(far, near, far_acts, near_acts)
+        grads = weight_grads((far_one, far_two, near), (acts_one, acts_two, near_acts))
     with jax.named_scope("reduce_heavy"):
-        total = (near_terms + other.astype(F32)).reshape(RING, PLANE, 2 * D)
-        got = [give(total[1 + i].astype(BF16), "heavy", d) for i, d in enumerate(ORDER)]
-        *got, grad_g, grad_u, grad_d = lax.optimization_barrier((*got, grad_g, grad_u, grad_d))
+        half = 2 * PLANE
+        one = near_terms[:half] + other_one.astype(F32)
+        two = near_terms[half:] + other_two.astype(F32)
+        send = {1: two[:PLANE], 2: one[PLANE:], 3: two[PLANE:]}
+        got = {d: give(send[d].astype(BF16), "heavy", d) for d in ISSUE}
+        got = [got[d] for d in ORDER]
+        *got, grad_g, grad_u, grad_d = lax.optimization_barrier((*got, *grads))
     with jax.named_scope("reduce_plane"):
-        got = scattered(summed_pairs(total[0], got))
+        got = scattered(summed_pairs(one[:PLANE], got))
         total = sum(got[i].astype(F32) for i in range(PLANE)).astype(BF16)
     return total[:1], total[1:], grad_g, grad_u, grad_d
 

time: 86.6 us -> 83.4 us (0.963)
  waiting for transfers between devices: 26.1 us -> 13.7 us
  starting transfers between devices: 15 us -> 23 us
  Pallas kernels: 7.41 us -> 9.72 us
  blocking collectives: 34.9 us -> 33.9 us
    ppermute x6, waiting for transfers between devices: 14.8 us -> 6.57 us  [fetch(): return lax.ppermute(value, AXES, pairs(stage, -d))]
    ppermute x5 -> x6, starting transfers between devices: 5.88 us -> 9.97 us  [swapped(): return lax.ppermute(value, 'core', [(0, 1), (1, 0)])]
    ppermute x6, starting transfers between devices: 6.53 us -> 9.96 us  [fetch(): return lax.ppermute(value, AXES, pairs(stage, -d))]
    ppermute x5 -> x6, waiting for transfers between devices: 2.86 us -> 0.38 us  [swapped(): return lax.ppermute(value, 'core', [(0, 1), (1, 0)])]
    pallas_call x2 -> x3, Pallas kernels: 2.93 us -> 4.64 us  [expert_terms(): pl.pallas_call(expert_kernel, out_shape=(jax.ShapeDtypeStruct((n, 2 * D),...]
    ppermute x3, waiting for transfers between devices: 8.43 us -> 6.72 us  [give(): return lax.ppermute(value, AXES, pairs(stage, d))]
    all_to_all x1, blocking collectives: 18.3 us -> 17.3 us  [scattered(): lax.all_to_all(value, AXES, 0, 0, axis_index_groups=planes(), tiled=True)]
  transfers between devices with their start and end apart: 14 -> 15, of which waited for: 8 -> 7; matrix products, arithmetic and copies ran while one was open for 0% -> 0% of each run, Pallas kernels for 4% -> 9%
where the time goes in v8:
time: 83.4 us; the launch traced here: 83 us
  blocking collectives  33.9 us (41%)
  starting transfers between devices  23 us (28%)
  waiting for transfers between devices  13.7 us (16%)
  Pallas kernels  9.72 us (12%)
  local copies, waits for them, and re-layouts  1.23 us (1%)
  between operations  0.86 us (1%)
    all_to_all x1, blocking collectives, scattered(): lax.all_to_all(value, AXES, 0, 0, axis_index_groups=planes(), tiled=True)  17.3 us
    all_to_all x1, blocking collectives, exchanged(): return lax.all_to_all(value, axis, 0, 0, tiled=True)  16.6 us
    ppermute x6, starting transfers between devices, swapped(): return lax.ppermute(value, 'core', [(0, 1), (1, 0)])  9.97 us
    ppermute x6, starting transfers between devices, fetch(): return lax.ppermute(value, AXES, pairs(stage, -d))  9.96 us
    ppermute x3, waiting for transfers between devices, give(): return lax.ppermute(value, AXES, pairs(stage, d))  6.72 us
    ppermute x6, waiting for transfers between devices, fetch(): return lax.ppermute(value, AXES, pairs(stage, -d))  6.57 us
    pallas_call x3, Pallas kernels, expert_terms(): pl.pallas_call(expert_kernel, out_shape=(jax.ShapeDtypeStruct((n, 2 * D),...  4.64 us
    ppermute x3, starting transfers between devices, give(): return lax.ppermute(value, AXES, pairs(stage, d))  3.1 us
  transfers between devices with their start and end apart: 15, of which 7 were waited for; matrix products, arithmetic and copies ran while one was open for 0% of the time, Pallas kernels for 9%

profile of v8, /device:TPU:1, one launch (start us, length us, event | category | flops | bytes accessed | tf_op | source)
XLA Modules:
  0.0 83.0 jit_solution(16078382020165583388)
XLA Ops:
  0.6 1.5 %copies_of_row.1 = bf16[8,2,3200]{2,1,0:T(2,128)(2,1)} custom-call(bf16[1,3072]{1,0:T(2,128)(2,1)} %tokens.1, bf16[1,3072]{1,0:T(2,128)(2,1)} %cotangent.1, s32[1,2]{1,0:T(1,128)} %routes.1, bf16[1,2]{1,0:T(2,128)(2,1)} %weights.1), custom_call_target="tpu_custom_call" | custom-call | tf_op jit(solution)/shard_map/gather_z/copies_of_row/pallas_call | solution.py:81
  2.1 16.6 %all_to_all.10 = bf16[8,2,3200]{2,1,0:T(2,128)(2,1)S(1)} all-to-all(bf16[8,2,3200]{2,1,0:T(2,128)(2,1)} %copies_of_row.1), channel_id=1, replica_groups=mesh['x_hi'=2,'core'=2,'y'=4,'x_lo'=2,'z'=8] {'z'}, dimensions={0} | all-to-all | bytes 204800 | tf_op jit(solution)/shard_map/gather_z/all_to_all | solution.py:50
  18.9 1.4 %collective-permute-start.2 = (bf16[8,6272]{1,0:T(8,128)(2,1)S(1)}, bf16[8,6272]{1,0:T(8,128)(2,1)S(1)}, u32[]{:S(2)}, u32[]{:S(2)}) collective-permute-start(bf16[8,6272]{1,0:T(8,128)(2,1)S(1)} %pad_maximum_fusion.1), channel_id=1, source_target_pairs={{0,8},{1,9},{2,10},{3,11},{4,12},{5,13},{6,14},{7,15},{16,24},{17,... | collective-permute-start | bytes 301064 | tf_op jit(solution)/shard_map/gather_light/ppermute | solution.py:42
  20.3 1.5 %collective-permute-start.1 = (bf16[8,6272]{1,0:T(8,128)(2,1)S(1)}, bf16[8,6272]{1,0:T(8,128)(2,1)S(1)}, u32[]{:S(2)}, u32[]{:S(2)}) collective-permute-start(bf16[8,6272]{1,0:T(8,128)(2,1)S(1)} %pad_maximum_fusion.1), channel_id=1, source_target_pairs={{0,136},{1,137},{2,138},{3,139},{4,140},{5,141},{6,142},{7,143},{1... | collective-permute-start | bytes 301064 | tf_op jit(solution)/shard_map/gather_light/ppermute | solution.py:42
  21.8 1.6 %collective-permute-start = (bf16[8,6272]{1,0:T(8,128)(2,1)S(1)}, bf16[8,6272]{1,0:T(8,128)(2,1)S(1)}, u32[]{:S(2)}, u32[]{:S(2)}) collective-permute-start(bf16[8,6272]{1,0:T(8,128)(2,1)S(1)} %pad_maximum_fusion.1), channel_id=1, source_target_pairs={{0,128},{1,129},{2,130},{3,131},{4,132},{5,133},{6,134},{7,135},{1... | collective-permute-start | bytes 301064 | tf_op jit(solution)/shard_map/gather_light/ppermute | solution.py:42
  23.8 3.0 %collective-permute-done = bf16[8,6272]{1,0:T(8,128)(2,1)S(1)} collective-permute-done((bf16[8,6272]{1,0:T(8,128)(2,1)S(1)}, bf16[8,6272]{1,0:T(8,128)(2,1)S(1)}, u32[]{:S(2)}, u32[]{:S(2)}) %collective-permute-start) | collective-permute-done | bytes 100384 | tf_op jit(solution)/shard_map/gather_light/ppermute | solution.py:42
  26.9 2.8 %collective-permute-start.3 = (bf16[32,6272]{1,0:T(8,128)(2,1)S(1)}, bf16[32,6272]{1,0:T(8,128)(2,1)S(1)}, u32[]{:S(2)}, u32[]{:S(2)}) collective-permute-start(bf16[32,6272]{1,0:T(8,128)(2,1)S(1)} %pad_maximum_fusion), channel_id=1, source_target_pairs={{0,32},{1,33},{2,34},{3,35},{4,36},{5,37},{6,38},{7,39},{16,48},{1... | collective-permute-start | bytes 1204232 | tf_op jit(solution)/shard_map/gather_heavy/ppermute | solution.py:42
  30.0 2.4 %collective-permute-start.4 = (bf16[32,6272]{1,0:T(8,128)(2,1)S(1)}, bf16[32,6272]{1,0:T(8,128)(2,1)S(1)}, u32[]{:S(2)}, u32[]{:S(2)}) collective-permute-start(bf16[32,6272]{1,0:T(8,128)(2,1)S(1)} %pad_maximum_fusion), channel_id=1, source_target_pairs={{0,48},{1,49},{2,50},{3,51},{4,52},{5,53},{6,54},{7,55},{16,0},{17... | collective-permute-start | bytes 1204232 | tf_op jit(solution)/shard_map/gather_heavy/ppermute | solution.py:42
  32.4 3.1 %collective-permute-done.3 = bf16[32,6272]{1,0:T(8,128)(2,1)S(1)} collective-permute-done((bf16[32,6272]{1,0:T(8,128)(2,1)S(1)}, bf16[32,6272]{1,0:T(8,128)(2,1)S(1)}, u32[]{:S(2)}, u32[]{:S(2)}) %collective-permute-start.3) | collective-permute-done | bytes 401440 | tf_op jit(solution)/shard_map/gather_heavy/ppermute | solution.py:42
  35.5 4.6 %collective-permute-start.6 = (bf16[32,6272]{1,0:T(8,128)(2,1)S(1)}, bf16[32,6272]{1,0:T(8,128)(2,1)S(1)}, u32[]{:S(2)}, u32[]{:S(2)}) collective-permute-start(bf16[32,6272]{1,0:T(8,128)(2,1)S(1)} %pad_maximum_fusion), channel_id=1, source_target_pairs={{0,64},{64,0},{1,65},{65,1},{2,66},{66,2},{3,67},{67,3},{4,68},{68... | collective-permute-start | bytes 1204232 | tf_op jit(solution)/shard_map/gather_core/ppermute | solution.py:46
  40.2 4.1 %collective-permute-start.11 = (bf16[32,6272]{1,0:T(8,128)(2,1)S(1)}, bf16[32,6272]{1,0:T(8,128)(2,1)S(1)}, u32[]{:S(2)}, u32[]{:S(2)}) collective-permute-start(bf16[32,6272]{1,0:T(8,128)(2,1)S(1)} %collective-permute-done.5), channel_id=1, source_target_pairs={{0,64},{64,0},{1,65},{65,1},{2,66},{66,2},{3,67},{67,3},{4,68},{68... | collective-permute-start | bytes 1204232 | tf_op jit(solution)/shard_map/gather_core/ppermute | solution.py:46
  44.3 0.6 collective-permute-start.10
  45.1 1.6 %expert_terms.4 = (bf16[64,6144]{1,0:T(8,128)(2,1)S(1)}, bf16[64,384]{1,0:T(8,128)(2,1)S(1)}) custom-call(s32[1]{0:T(128)} %bitcast.group, bf16[64,6272]{1,0:T(8,128)(2,1)S(1)} %constant_dynamic-update-slice_fusion.4.rows.refs_0_, bf16[3072,128]{1,0:T(8,128)(2,1)S(1)} %bitcast.98, bf16[3072,128]{1,0:T(8,128)(2,1)S(1)} %bitcast.101, ...), custom_call_target="tpu_custom_call" | custom-call | flops 301989888 | bytes 3145728 | tf_op jit(solution)/shard_map/experts/expert_terms/pallas_call | solution.py:112
  46.9 1.6 %expert_terms.5 = (bf16[64,6144]{1,0:T(8,128)(2,1)S(1)}, bf16[64,384]{1,0:T(8,128)(2,1)S(1)}) custom-call(s32[1]{0:T(128)} %bitcast.group, bf16[64,6272]{1,0:T(8,128)(2,1)S(1)} %constant_dynamic-update-slice_fusion.6.rows.refs_1_, bf16[3072,128]{1,0:T(8,128)(2,1)S(1)} %bitcast.99, bf16[3072,128]{1,0:T(8,128)(2,1)S(1)} %bitcast.102, ...), custom_call_target="tpu_custom_call" | custom-call | flops 301989888 | bytes 3145728 | tf_op jit(solution)/shard_map/experts/expert_terms/pallas_call | solution.py:112
  49.1 1.5 %expert_terms.3 = (f32[128,6144]{1,0:T(8,128)S(1)}, bf16[128,384]{1,0:T(8,128)(2,1)S(1)}) custom-call(s32[1]{0:T(128)} %bitcast.group, bf16[128,6272]{1,0:T(8,128)(2,1)S(1)} %constant_dynamic-update-slice_fusion.rows.refs_2_, bf16[3072,128]{1,0:T(8,128)(2,1)S(1)} %bitcast.100, bf16[3072,128]{1,0:T(8,128)(2,1)S(1)} %bitcast.103, bf16[128,3072]{1,0:T(8,128)(2,1)S(1)} %bitcast.106), custom_call_target="tpu_custom_call" | custom-call | flops 603979776 | bytes 3932160 | tf_op jit(solution)/shard_map/experts/expert_terms/pallas_call | solution.py:112
  51.3 1.6 %collective-permute-start.9 = (bf16[32,6144]{1,0:T(8,128)(2,1)S(1)}, bf16[32,6144]{1,0:T(8,128)(2,1)S(1)}, u32[]{:S(2)}, u32[]{:S(2)}) collective-permute-start(bf16[32,6144]{1,0:T(8,128)(2,1)S(1)} %slice.285), channel_id=1, source_target_pairs={{0,32},{1,33},{2,34},{3,35},{4,36},{5,37},{6,38},{7,39},{16,48},{1... | collective-permute-start | bytes 1179656 | tf_op jit(solution)/shard_map/reduce_heavy/ppermute | solution.py:38
  53.0 0.9 %collective-permute-start.14 = (bf16[32,6144]{1,0:T(8,128)(2,1)S(1)}, bf16[32,6144]{1,0:T(8,128)(2,1)S(1)}, u32[]{:S(2)}, u32[]{:S(2)}) collective-permute-start(bf16[32,6144]{1,0:T(8,128)(2,1)S(1)} %get-tuple-element.41), channel_id=1, source_target_pairs={{0,48},{1,49},{2,50},{3,51},{4,52},{5,53},{6,54},{7,55},{16,0},{17... | collective-permute-start | bytes 1179656 | tf_op jit(solution)/shard_map/reduce_heavy/ppermute | solution.py:38
  54.4 3.0 %weight_grads.1 = (bf16[1,3072,128]{2,1,0:T(8,128)(2,1)}, bf16[1,3072,128]{2,1,0:T(8,128)(2,1)}, bf16[1,128,3072]{2,1,0:T(8,128)(2,1)}) custom-call(bf16[64,6272]{1,0:T(8,128)(2,1)S(1)} %constant_dynamic-update-slice_fusion.4.rows.refs_0_, bf16[64,6272]{1,0:T(8,128)(2,1)S(1)} %constant_dynamic-update-slice_fusion.6.rows.refs_1_, ...), custom_call_target="tpu_custom_call" | custom-call | flops 603979776 | bytes 5505024 | tf_op jit(solution)/shard_map/weights/weight_grads/pallas_call | solution.py:141
  57.5 2.6 %collective-permute-done.9.one = bf16[32,6144]{1,0:T(8,128)(2,1)S(1)} collective-permute-done((bf16[32,6144]{1,0:T(8,128)(2,1)S(1)}, bf16[32,6144]{1,0:T(8,128)(2,1)S(1)}, u32[]{:S(2)}, u32[]{:S(2)}) %collective-permute-start.9) | collective-permute-done | bytes 393248 | tf_op jit(solution)/shard_map/reduce_heavy/ppermute | solution.py:38
  60.1 2.9 %collective-permute-done.14.three = bf16[32,6144]{1,0:T(8,128)(2,1)S(1)} collective-permute-done((bf16[32,6144]{1,0:T(8,128)(2,1)S(1)}, bf16[32,6144]{1,0:T(8,128)(2,1)S(1)}, u32[]{:S(2)}, u32[]{:S(2)}) %collective-permute-start.14) | collective-permute-done | bytes 393248 | tf_op jit(solution)/shard_map/reduce_heavy/ppermute | solution.py:38
  63.0 1.2 %collective-permute-done.13.two = bf16[32,6144]{1,0:T(8,128)(2,1)S(1)} collective-permute-done((bf16[32,6144]{1,0:T(8,128)(2,1)S(1)}, bf16[32,6144]{1,0:T(8,128)(2,1)S(1)}, u32[]{:S(2)}, u32[]{:S(2)}) %collective-permute-start.13) | collective-permute-done | bytes 393248 | tf_op jit(solution)/shard_map/reduce_heavy/ppermute | solution.py:38
  64.2 0.6 summed_pairs.1
  64.8 17.3 %all_to_all.11 = bf16[32,2,3072]{2,1,0:T(2,128)(2,1)S(1)} all-to-all(bf16[32,2,3072]{2,1,0:T(2,128)(2,1)S(1)} %summed_pairs.1), channel_id=1, replica_groups={{0,1,2,3,4,5,6,7,8,9,10,11,12,13,14,15,128,129,130,131,132,133,134,135,..., dimensions={0} | all-to-all | bytes 786432 | tf_op jit(solution)/shard_map/reduce_plane/all_to_all | solution.py:60
  82.4 0.6 fusion.3
  (40 shorter events, 3.5 us)
Async XLA Ops:
  18.9 4.8 %collective-permute-start.2 = (bf16[8,6272]{1,0:T(8,128)(2,1)S(1)}, bf16[8,6272]{1,0:T(8,128)(2,1)S(1)}, u32[]{:S(2)}, u32[]{:S(2)}) collective-permute-start(bf16[8,6272]{1,0:T(8,128)(2,1)S(1)} %pad_maximum_fusion.1), channel_id=1, source_target_pairs={{0,8},{1,9},{2,10},{3,11},{4,12},{5,13},{6,14},{7,15},{16,24},{17,... | collective-permute-start | bytes 301064 | tf_op jit(solution)/shard_map/gather_light/ppermute | solution.py:42
  20.3 3.5 %collective-permute-start.1 = (bf16[8,6272]{1,0:T(8,128)(2,1)S(1)}, bf16[8,6272]{1,0:T(8,128)(2,1)S(1)}, u32[]{:S(2)}, u32[]{:S(2)}) collective-permute-start(bf16[8,6272]{1,0:T(8,128)(2,1)S(1)} %pad_maximum_fusion.1), channel_id=1, source_target_pairs={{0,136},{1,137},{2,138},{3,139},{4,140},{5,141},{6,142},{7,143},{1... | collective-permute-start | bytes 301064 | tf_op jit(solution)/shard_map/gather_light/ppermute | solution.py:42
  21.8 5.0 %collective-permute-start = (bf16[8,6272]{1,0:T(8,128)(2,1)S(1)}, bf16[8,6272]{1,0:T(8,128)(2,1)S(1)}, u32[]{:S(2)}, u32[]{:S(2)}) collective-permute-start(bf16[8,6272]{1,0:T(8,128)(2,1)S(1)} %pad_maximum_fusion.1), channel_id=1, source_target_pairs={{0,128},{1,129},{2,130},{3,131},{4,132},{5,133},{6,134},{7,135},{1... | collective-permute-start | bytes 301064 | tf_op jit(solution)/shard_map/gather_light/ppermute | solution.py:42
  26.9 8.6 %collective-permute-start.3 = (bf16[32,6272]{1,0:T(8,128)(2,1)S(1)}, bf16[32,6272]{1,0:T(8,128)(2,1)S(1)}, u32[]{:S(2)}, u32[]{:S(2)}) collective-permute-start(bf16[32,6272]{1,0:T(8,128)(2,1)S(1)} %pad_maximum_fusion), channel_id=1, source_target_pairs={{0,32},{1,33},{2,34},{3,35},{4,36},{5,37},{6,38},{7,39},{16,48},{1... | collective-permute-start | bytes 1204232 | tf_op jit(solution)/shard_map/gather_heavy/ppermute | solution.py:42
  29.7 10.5 %collective-permute-start.5 = (bf16[32,6272]{1,0:T(8,128)(2,1)S(1)}, bf16[32,6272]{1,0:T(8,128)(2,1)S(1)}, u32[]{:S(2)}, u32[]{:S(2)}) collective-permute-start(bf16[32,6272]{1,0:T(8,128)(2,1)S(1)} %pad_maximum_fusion), channel_id=1, source_target_pairs={{0,16},{1,17},{2,18},{3,19},{4,20},{5,21},{6,22},{7,23},{16,32},{1... | collective-permute-start | bytes 1204232 | tf_op jit(solution)/shard_map/gather_heavy/ppermute | solution.py:42
  30.0 14.3 %collective-permute-start.4 = (bf16[32,6272]{1,0:T(8,128)(2,1)S(1)}, bf16[32,6272]{1,0:T(8,128)(2,1)S(1)}, u32[]{:S(2)}, u32[]{:S(2)}) collective-permute-start(bf16[32,6272]{1,0:T(8,128)(2,1)S(1)} %pad_maximum_fusion), channel_id=1, source_target_pairs={{0,48},{1,49},{2,50},{3,51},{4,52},{5,53},{6,54},{7,55},{16,0},{17... | collective-permute-start | bytes 1204232 | tf_op jit(solution)/shard_map/gather_heavy/ppermute | solution.py:42
  35.5 9.5 %collective-permute-start.6 = (bf16[32,6272]{1,0:T(8,128)(2,1)S(1)}, bf16[32,6272]{1,0:T(8,128)(2,1)S(1)}, u32[]{:S(2)}, u32[]{:S(2)}) collective-permute-start(bf16[32,6272]{1,0:T(8,128)(2,1)S(1)} %pad_maximum_fusion), channel_id=1, source_target_pairs={{0,64},{64,0},{1,65},{65,1},{2,66},{66,2},{3,67},{67,3},{4,68},{68... | collective-permute-start | bytes 1204232 | tf_op jit(solution)/shard_map/gather_core/ppermute | solution.py:46
  40.1 4.9 %collective-permute-start.7 = (bf16[32,6272]{1,0:T(8,128)(2,1)S(1)}, bf16[32,6272]{1,0:T(8,128)(2,1)S(1)}, u32[]{:S(2)}, u32[]{:S(2)}) collective-permute-start(bf16[32,6272]{1,0:T(8,128)(2,1)S(1)} %collective-permute-done.3), channel_id=1, source_target_pairs={{0,64},{64,0},{1,65},{65,1},{2,66},{66,2},{3,67},{67,3},{4,68},{68... | collective-permute-start | bytes 1204232 | tf_op jit(solution)/shard_map/gather_core/ppermute | solution.py:46
  40.1 5.0 %copy-start = (bf16[1,3072,128]{2,1,0:T(8,128)(2,1)S(1)}, bf16[1,3072,128]{2,1,0:T(8,128)(2,1)}, u32[]{:S(2)}) copy-start(bf16[1,3072,128]{2,1,0:T(8,128)(2,1)} %param.11) | copy-start | bytes 2359300
  40.1 5.0 %copy-start.1 = (bf16[1,3072,128]{2,1,0:T(8,128)(2,1)S(1)}, bf16[1,3072,128]{2,1,0:T(8,128)(2,1)}, u32[]{:S(2)}) copy-start(bf16[1,3072,128]{2,1,0:T(8,128)(2,1)} %param.12) | copy-start | bytes 2359300
  40.2 5.0 %copy-start.2 = (bf16[1,128,3072]{2,1,0:T(8,128)(2,1)S(1)}, bf16[1,128,3072]{2,1,0:T(8,128)(2,1)}, u32[]{:S(2)}) copy-start(bf16[1,128,3072]{2,1,0:T(8,128)(2,1)} %param.13) | copy-start | bytes 2359300
  40.2 6.7 %collective-permute-start.11 = (bf16[32,6272]{1,0:T(8,128)(2,1)S(1)}, bf16[32,6272]{1,0:T(8,128)(2,1)S(1)}, u32[]{:S(2)}, u32[]{:S(2)}) collective-permute-start(bf16[32,6272]{1,0:T(8,128)(2,1)S(1)} %collective-permute-done.5), channel_id=1, source_target_pairs={{0,64},{64,0},{1,65},{65,1},{2,66},{66,2},{3,67},{67,3},{4,68},{68... | collective-permute-start | bytes 1204232 | tf_op jit(solution)/shard_map/gather_core/ppermute | solution.py:46
  44.3 2.5 %collective-permute-start.10 = (bf16[32,6272]{1,0:T(8,128)(2,1)S(1)}, bf16[32,6272]{1,0:T(8,128)(2,1)S(1)}, u32[]{:S(2)}, u32[]{:S(2)}) collective-permute-start(bf16[32,6272]{1,0:T(8,128)(2,1)S(1)} %collective-permute-done.4), channel_id=1, source_target_pairs={{0,64},{64,0},{1,65},{65,1},{2,66},{66,2},{3,67},{67,3},{4,68},{68... | collective-permute-start | bytes 1204232 | tf_op jit(solution)/shard_map/gather_core/ppermute | solution.py:46
  46.7 3.9 %collective-permute-start.8 = (bf16[64,6144]{1,0:T(8,128)(2,1)S(1)}, bf16[64,6144]{1,0:T(8,128)(2,1)S(1)}, u32[]{:S(2)}, u32[]{:S(2)}) collective-permute-start(bf16[64,6144]{1,0:T(8,128)(2,1)S(1)} %get-tuple-element.25), channel_id=1, source_target_pairs={{0,64},{64,0},{1,65},{65,1},{2,66},{66,2},{3,67},{67,3},{4,68},{68... | collective-permute-start | bytes 2359304 | tf_op jit(solution)/shard_map/experts/ppermute | solution.py:46
  48.5 2.5 %collective-permute-start.12 = (bf16[64,6144]{1,0:T(8,128)(2,1)S(1)}, bf16[64,6144]{1,0:T(8,128)(2,1)S(1)}, u32[]{:S(2)}, u32[]{:S(2)}) collective-permute-start(bf16[64,6144]{1,0:T(8,128)(2,1)S(1)} %get-tuple-element.26), channel_id=1, source_target_pairs={{0,64},{64,0},{1,65},{65,1},{2,66},{66,2},{3,67},{67,3},{4,68},{68... | collective-permute-start | bytes 2359304 | tf_op jit(solution)/shard_map/experts/ppermute | solution.py:46
  51.3 8.7 %collective-permute-start.9 = (bf16[32,6144]{1,0:T(8,128)(2,1)S(1)}, bf16[32,6144]{1,0:T(8,128)(2,1)S(1)}, u32[]{:S(2)}, u32[]{:S(2)}) collective-permute-start(bf16[32,6144]{1,0:T(8,128)(2,1)S(1)} %slice.285), channel_id=1, source_target_pairs={{0,32},{1,33},{2,34},{3,35},{4,36},{5,37},{6,38},{7,39},{16,48},{1... | collective-permute-start | bytes 1179656 | tf_op jit(solution)/shard_map/reduce_heavy/ppermute | solution.py:38
  53.0 10.0 %collective-permute-start.14 = (bf16[32,6144]{1,0:T(8,128)(2,1)S(1)}, bf16[32,6144]{1,0:T(8,128)(2,1)S(1)}, u32[]{:S(2)}, u32[]{:S(2)}) collective-permute-start(bf16[32,6144]{1,0:T(8,128)(2,1)S(1)} %get-tuple-element.41), channel_id=1, source_target_pairs={{0,48},{1,49},{2,50},{3,51},{4,52},{5,53},{6,54},{7,55},{16,0},{17... | collective-permute-start | bytes 1179656 | tf_op jit(solution)/shard_map/reduce_heavy/ppermute | solution.py:38
  53.9 10.4 %collective-permute-start.13 = (bf16[32,6144]{1,0:T(8,128)(2,1)S(1)}, bf16[32,6144]{1,0:T(8,128)(2,1)S(1)}, u32[]{:S(2)}, u32[]{:S(2)}) collective-permute-start(bf16[32,6144]{1,0:T(8,128)(2,1)S(1)} %get-tuple-element.42), channel_id=1, source_target_pairs={{0,16},{1,17},{2,18},{3,19},{4,20},{5,21},{6,22},{7,23},{16,32},{1... | collective-permute-start | bytes 1179656 | tf_op jit(solution)/shard_map/reduce_heavy/ppermute | solution.py:38

commit v9 on v8

--- a/solution.py
+++ b/solution.py
@@ -86,13 +86,13 @@
     )(tokens, cotangent, routes, gate_weights)
 
 
-def expert_kernel(group, rows, gate_slice, up_slice, down_slice, terms, acts):
+def expert_kernel(group, rows, pair_slice, down_slice, terms, acts):
     lane = lax.broadcasted_iota(jnp.int32, (rows.shape[0], PAD), 1)
     gates = jnp.where(lane == group[0], rows[:, 2 * D :].astype(F32), 0.0)
     column = jnp.sum(gates, axis=1, keepdims=True)
     x, cot = rows[:, :D], rows[:, D : 2 * D]
-    gate_pre = dot(x, gate_slice[...], 1, 0)
-    up_pre = dot(x, up_slice[...], 1, 0)
+    pre = dot(x, pair_slice[...], 1, 0)
+    gate_pre, up_pre = pre[:, :UNITS], pre[:, UNITS:]
     grad_act = dot(cot, down_slice[...], 1, 1) * column
     sigmoid = jax.nn.sigmoid(gate_pre)
     silu = gate_pre * sigmoid
@@ -103,11 +103,11 @@
     acts[:, UNITS : 2 * UNITS] = grad_gpre
     acts[:, 2 * UNITS :] = grad_upre
     terms[:, :D] = dot(hidden, down_slice[...], 1, 0).astype(terms.dtype)
-    grad_rows = dot(grad_gpre, gate_slice[...], 1, 1) + dot(grad_upre, up_slice[...], 1, 1)
+    grad_rows = dot(acts[:, UNITS:], pair_slice[...], 1, 1)
     terms[:, D:] = grad_rows.astype(terms.dtype)
 
 
-def expert_terms(group, rows, gate_slice, up_slice, down_slice, kind):
+def expert_terms(group, rows, pair_slice, down_slice, kind):
     n = rows.shape[0]
     return pl.pallas_call(
         expert_kernel,
@@ -115,14 +115,14 @@
             jax.ShapeDtypeStruct((n, 2 * D), kind),
             jax.ShapeDtypeStruct((n, 3 * UNITS), BF16),
         ),
-        in_specs=[SMEM] + [VMEM] * 4,
+        in_specs=[SMEM] + [VMEM] * 3,
         out_specs=(VMEM, VMEM),
         compiler_params=grant(16),
         cost_estimate=pl.CostEstimate(
             flops=12 * n * D * UNITS, transcendentals=n * UNITS, bytes_accessed=4 * n * D + 6 * D * UNITS
         ),
         name="expert_terms",
-    )(group, rows, gate_slice, up_slice, down_slice)
+    )(group, rows, pair_slice, down_slice)
 
 
 def weight_kernel(*refs):
@@ -179,18 +179,19 @@
 
 
 def on_device(tokens, cotangent, routes, gate_weights, w_gate, w_up, w_down):
-    slices = (w_gate[0], w_up[0], w_down[0])
     group = lax.axis_index(EP).astype(jnp.int32).reshape(1)
     with jax.named_scope("gather_z"):
         rows = exchanged(copies_of_row(tokens, cotangent, routes, gate_weights), "z")
         rows = jnp.concatenate([rows[:, 0, :D], rows[:, 1, :D], rows[:, 0, D:]], axis=1)
     with jax.named_scope("gather_light"):
-        got = {d: fetch(rows, "light", d) for d in (2, 3, 1)}
-        rows = jnp.concatenate([rows] + [got[d] for d in ORDER], axis=0)
+        got = {d: fetch(rows, "light", d) for d in ISSUE}
+        first = lax.optimization_barrier(jnp.concatenate([rows, got[2]], axis=0))
+        rows = jnp.concatenate([first, got[1], got[3]], axis=0)
     with jax.named_scope("gather_heavy"):
         got = {d: fetch(rows, "heavy", d) for d in ISSUE}
     with jax.named_scope("gather_core"):
-        own, got[2] = lax.optimization_barrier((rows, got[2]))
+        own, got[2], gate_slice = lax.optimization_barrier((rows, got[2], w_gate[0]))
+        slices = (jnp.concatenate([gate_slice, w_up[0]], axis=1), w_down[0])
         far = {d: swapped(got[d]) for d in ORDER}
         far_one = jnp.concatenate([swapped(own), far[2]], axis=0)
         far_two = jnp.concatenate([far[1], far[3]], axis=0)
@@ -198,6 +199,7 @@
     with jax.named_scope("experts"):
         terms_one, acts_one = expert_terms(group, far_one, *slices, BF16)
         other_one = swapped(terms_one)
+        _, far_two = lax.optimization_barrier((terms_one, far_two))
         terms_two, acts_two = expert_terms(group, far_two, *slices, BF16)
         other_two = swapped(terms_two)
         near_terms, near_acts = expert_terms(group, near, *slices, F32)

time: 83.4 us -> 89.2 us (1.070)
  starting transfers between devices: 23 us -> 26.8 us
  waiting for transfers between devices: 13.7 us -> 15.1 us
    ppermute x6, starting transfers between devices: 9.97 us -> 15 us  [swapped(): return lax.ppermute(value, 'core', [(0, 1), (1, 0)])]
    ppermute x3, starting transfers between devices: 3.1 us -> 1.81 us  [give(): return lax.ppermute(value, AXES, pairs(stage, d))]
    ppermute x3, waiting for transfers between devices: 6.72 us -> 7.82 us  [give(): return lax.ppermute(value, AXES, pairs(stage, d))]
  transfers between devices with their start and end apart: 15 -> 15, of which waited for: 7 -> 8; matrix products, arithmetic and copies ran while one was open for 0% -> 1% of each run, Pallas kernels for 9% -> 8%
where the time goes in v9:
time: 89.2 us; the launch traced here: 88.8 us
  blocking collectives  33.9 us (38%)
  starting transfers between devices  26.8 us (30%)
  waiting for transfers between devices  15.1 us (17%)
  Pallas kernels  9.27 us (10%)
  local copies, waits for them, and re-layouts  2.01 us (2%)
    all_to_all x1, blocking collectives, scattered(): lax.all_to_all(value, AXES, 0, 0, axis_index_groups=planes(), tiled=True)  17.3 us
    all_to_all x1, blocking collectives, exchanged(): return lax.all_to_all(value, axis, 0, 0, tiled=True)  16.6 us
    ppermute x6, starting transfers between devices, swapped(): return lax.ppermute(value, 'core', [(0, 1), (1, 0)])  15 us
    ppermute x6, starting transfers between devices, fetch(): return lax.ppermute(value, AXES, pairs(stage, -d))  9.97 us
    ppermute x3, waiting for transfers between devices, give(): return lax.ppermute(value, AXES, pairs(stage, d))  7.82 us
    ppermute x6, waiting for transfers between devices, fetch(): return lax.ppermute(value, AXES, pairs(stage, -d))  6.87 us
    pallas_call x3, Pallas kernels, expert_terms(): pl.pallas_call(expert_kernel, out_shape=(jax.ShapeDtypeStruct((n, 2 * D),...  4.2 us
    pallas_call x1, Pallas kernels, weight_grads(): pl.pallas_call(weight_kernel, out_shape=(jax.ShapeDtypeStruct((1, D, UNIT...  3.02 us
  transfers between devices with their start and end apart: 15, of which 8 were waited for; matrix products, arithmetic and copies ran while one was open for 1% of the time, Pallas kernels for 8%

profile of v9, /device:TPU:1, one launch (start us, length us, event | category | flops | bytes accessed | tf_op | source)
XLA Modules:
  0.0 88.8 jit_solution(14062729307304936244)
XLA Ops:
  0.6 1.5 %copies_of_row.1 = bf16[8,2,3200]{2,1,0:T(2,128)(2,1)} custom-call(bf16[1,3072]{1,0:T(2,128)(2,1)} %tokens.1, bf16[1,3072]{1,0:T(2,128)(2,1)} %cotangent.1, s32[1,2]{1,0:T(1,128)} %routes.1, bf16[1,2]{1,0:T(2,128)(2,1)} %weights.1), custom_call_target="tpu_custom_call" | custom-call | tf_op jit(solution)/shard_map/gather_z/copies_of_row/pallas_call | solution.py:81
  2.1 16.6 %all_to_all.10 = bf16[8,2,3200]{2,1,0:T(2,128)(2,1)S(1)} all-to-all(bf16[8,2,3200]{2,1,0:T(2,128)(2,1)} %copies_of_row.1), channel_id=1, replica_groups=mesh['x_hi'=2,'core'=2,'y'=4,'x_lo'=2,'z'=8] {'z'}, dimensions={0} | all-to-all | bytes 204800 | tf_op jit(solution)/shard_map/gather_z/all_to_all | solution.py:50
  18.9 3.0 %collective-permute-start = (bf16[8,6272]{1,0:T(8,128)(2,1)S(1)}, bf16[8,6272]{1,0:T(8,128)(2,1)S(1)}, u32[]{:S(2)}, u32[]{:S(2)}) collective-permute-start(bf16[8,6272]{1,0:T(8,128)(2,1)S(1)} %pad_maximum_fusion.4), channel_id=1, source_target_pairs={{0,128},{1,129},{2,130},{3,131},{4,132},{5,133},{6,134},{7,135},{1... | collective-permute-start | bytes 301064 | tf_op jit(solution)/shard_map/gather_light/ppermute | solution.py:42
  21.9 0.8 collective-permute-start.1
  22.7 0.7 collective-permute-start.2
  24.1 1.4 %collective-permute-done.1 = bf16[8,6272]{1,0:T(8,128)(2,1)S(1)} collective-permute-done((bf16[8,6272]{1,0:T(8,128)(2,1)S(1)}, bf16[8,6272]{1,0:T(8,128)(2,1)S(1)}, u32[]{:S(2)}, u32[]{:S(2)}) %collective-permute-start.1) | collective-permute-done | bytes 100384 | tf_op jit(solution)/shard_map/gather_light/ppermute | solution.py:42
  25.4 2.0 %collective-permute-done.2 = bf16[8,6272]{1,0:T(8,128)(2,1)S(1)} collective-permute-done((bf16[8,6272]{1,0:T(8,128)(2,1)S(1)}, bf16[8,6272]{1,0:T(8,128)(2,1)S(1)}, u32[]{:S(2)}, u32[]{:S(2)}) %collective-permute-start.2) | collective-permute-done | bytes 100384 | tf_op jit(solution)/shard_map/gather_light/ppermute | solution.py:42
  27.5 2.8 %collective-permute-start.3 = (bf16[32,6272]{1,0:T(8,128)(2,1)S(1)}, bf16[32,6272]{1,0:T(8,128)(2,1)S(1)}, u32[]{:S(2)}, u32[]{:S(2)}) collective-permute-start(bf16[32,6272]{1,0:T(8,128)(2,1)S(1)} %pad_maximum_fusion.2), channel_id=1, source_target_pairs={{0,32},{1,33},{2,34},{3,35},{4,36},{5,37},{6,38},{7,39},{16,48},{1... | collective-permute-start | bytes 1204232 | tf_op jit(solution)/shard_map/gather_heavy/ppermute | solution.py:42
  30.9 2.1 %collective-permute-start.4 = (bf16[32,6272]{1,0:T(8,128)(2,1)S(1)}, bf16[32,6272]{1,0:T(8,128)(2,1)S(1)}, u32[]{:S(2)}, u32[]{:S(2)}) collective-permute-start(bf16[32,6272]{1,0:T(8,128)(2,1)S(1)} %pad_maximum_fusion.2), channel_id=1, source_target_pairs={{0,48},{1,49},{2,50},{3,51},{4,52},{5,53},{6,54},{7,55},{16,0},{17... | collective-permute-start | bytes 1204232 | tf_op jit(solution)/shard_map/gather_heavy/ppermute | solution.py:42
  33.0 2.9 %collective-permute-done.3 = bf16[32,6272]{1,0:T(8,128)(2,1)S(1)} collective-permute-done((bf16[32,6272]{1,0:T(8,128)(2,1)S(1)}, bf16[32,6272]{1,0:T(8,128)(2,1)S(1)}, u32[]{:S(2)}, u32[]{:S(2)}) %collective-permute-start.3) | collective-permute-done | bytes 401440 | tf_op jit(solution)/shard_map/gather_heavy/ppermute | solution.py:42
  35.9 9.6 %collective-permute-start.6 = (bf16[32,6272]{1,0:T(8,128)(2,1)S(1)}, bf16[32,6272]{1,0:T(8,128)(2,1)S(1)}, u32[]{:S(2)}, u32[]{:S(2)}) collective-permute-start(bf16[32,6272]{1,0:T(8,128)(2,1)S(1)} %pad_maximum_fusion.2), channel_id=1, source_target_pairs={{0,64},{64,0},{1,65},{65,1},{2,66},{66,2},{3,67},{67,3},{4,68},{68... | collective-permute-start | bytes 1204232 | tf_op jit(solution)/shard_map/gather_core/ppermute | solution.py:46
  45.5 4.2 %collective-permute-start.11 = (bf16[32,6272]{1,0:T(8,128)(2,1)S(1)}, bf16[32,6272]{1,0:T(8,128)(2,1)S(1)}, u32[]{:S(2)}, u32[]{:S(2)}) collective-permute-start(bf16[32,6272]{1,0:T(8,128)(2,1)S(1)} %collective-permute-done.5), channel_id=1, source_target_pairs={{0,64},{64,0},{1,65},{65,1},{2,66},{66,2},{3,67},{67,3},{4,68},{68... | collective-permute-start | bytes 1204232 | tf_op jit(solution)/shard_map/gather_core/ppermute | solution.py:46
  49.7 0.6 collective-permute-start.10
  50.7 0.8 copy-done
  51.5 1.4 %expert_terms.4 = (bf16[64,6144]{1,0:T(8,128)(2,1)S(1)}, bf16[64,384]{1,0:T(8,128)(2,1)S(1)}) custom-call(s32[1]{0:T(128)} %bitcast.group, bf16[64,6272]{1,0:T(8,128)(2,1)S(1)} %constant_dynamic-update-slice_fusion.4.rows.refs_0_, bf16[3072,256]{1,0:T(8,128)(2,1)S(1)} %pad_maximum_fusion.pair_slice, bf16[128,3072]{1,0:T(8,128)(2,1)S(1)} %bitcast.98), custom_call_target="tpu_custom_call" | custom-call | flops 301989888 | bytes 3145728 | tf_op jit(solution)/shard_map/experts/expert_terms/pallas_call | solution.py:112
  53.1 1.4 %expert_terms.5 = (bf16[64,6144]{1,0:T(8,128)(2,1)S(1)}, bf16[64,384]{1,0:T(8,128)(2,1)S(1)}) custom-call(s32[1]{0:T(128)} %bitcast.group, bf16[64,6272]{1,0:T(8,128)(2,1)S(1)} %pad_maximum_fusion.1.rows.refs_1_, bf16[3072,256]{1,0:T(8,128)(2,1)S(1)} %pad_maximum_fusion.pair_slice, bf16[128,3072]{1,0:T(8,128)(2,1)S(1)} %bitcast.99), custom_call_target="tpu_custom_call" | custom-call | flops 301989888 | bytes 3145728 | tf_op jit(solution)/shard_map/experts/expert_terms/pallas_call | solution.py:112
  55.1 1.4 %expert_terms.3 = (f32[128,6144]{1,0:T(8,128)S(1)}, bf16[128,384]{1,0:T(8,128)(2,1)S(1)}) custom-call(s32[1]{0:T(128)} %bitcast.group, bf16[128,6272]{1,0:T(8,128)(2,1)S(1)} %constant_dynamic-update-slice_fusion.rows.refs_2_, bf16[3072,256]{1,0:T(8,128)(2,1)S(1)} %pad_maximum_fusion.pair_slice, bf16[128,3072]{1,0:T(8,128)(2,1)S(1)} %bitcast.100), custom_call_target="tpu_custom_call" | custom-call | flops 603979776 | bytes 3932160 | tf_op jit(solution)/shard_map/experts/expert_terms/pallas_call | solution.py:112
  57.7 1.5 %collective-permute-start.13 = (bf16[32,6144]{1,0:T(8,128)(2,1)S(1)}, bf16[32,6144]{1,0:T(8,128)(2,1)S(1)}, u32[]{:S(2)}, u32[]{:S(2)}) collective-permute-start(bf16[32,6144]{1,0:T(8,128)(2,1)S(1)} %get-tuple-element.46), channel_id=1, source_target_pairs={{0,16},{1,17},{2,18},{3,19},{4,20},{5,21},{6,22},{7,23},{16,32},{1... | collective-permute-start | bytes 1179656 | tf_op jit(solution)/shard_map/reduce_heavy/ppermute | solution.py:38
  59.2 3.0 %weight_grads.1 = (bf16[1,3072,128]{2,1,0:T(8,128)(2,1)}, bf16[1,3072,128]{2,1,0:T(8,128)(2,1)}, bf16[1,128,3072]{2,1,0:T(8,128)(2,1)}) custom-call(bf16[64,6272]{1,0:T(8,128)(2,1)S(1)} %constant_dynamic-update-slice_fusion.4.rows.refs_0_, bf16[64,6272]{1,0:T(8,128)(2,1)S(1)} %pad_maximum_fusion.1.rows.refs_1_, ...), custom_call_target="tpu_custom_call" | custom-call | flops 603979776 | bytes 5505024 | tf_op jit(solution)/shard_map/weights/weight_grads/pallas_call | solution.py:141
  62.2 3.7 %collective-permute-done.9.one = bf16[32,6144]{1,0:T(8,128)(2,1)S(1)} collective-permute-done((bf16[32,6144]{1,0:T(8,128)(2,1)S(1)}, bf16[32,6144]{1,0:T(8,128)(2,1)S(1)}, u32[]{:S(2)}, u32[]{:S(2)}) %collective-permute-start.9) | collective-permute-done | bytes 393248 | tf_op jit(solution)/shard_map/reduce_heavy/ppermute | solution.py:38
  65.9 1.1 %collective-permute-done.14.three = bf16[32,6144]{1,0:T(8,128)(2,1)S(1)} collective-permute-done((bf16[32,6144]{1,0:T(8,128)(2,1)S(1)}, bf16[32,6144]{1,0:T(8,128)(2,1)S(1)}, u32[]{:S(2)}, u32[]{:S(2)}) %collective-permute-start.14) | collective-permute-done | bytes 393248 | tf_op jit(solution)/shard_map/reduce_heavy/ppermute | solution.py:38
  67.0 3.1 %collective-permute-done.13.two = bf16[32,6144]{1,0:T(8,128)(2,1)S(1)} collective-permute-done((bf16[32,6144]{1,0:T(8,128)(2,1)S(1)}, bf16[32,6144]{1,0:T(8,128)(2,1)S(1)}, u32[]{:S(2)}, u32[]{:S(2)}) %collective-permute-start.13) | collective-permute-done | bytes 393248 | tf_op jit(solution)/shard_map/reduce_heavy/ppermute | solution.py:38
  70.7 17.3 %all_to_all.11 = bf16[32,2,3072]{2,1,0:T(2,128)(2,1)S(1)} all-to-all(bf16[32,2,3072]{2,1,0:T(2,128)(2,1)S(1)} %summed_pairs.1), channel_id=1, replica_groups={{0,1,2,3,4,5,6,7,8,9,10,11,12,13,14,15,128,129,130,131,132,133,134,135,..., dimensions={0} | all-to-all | bytes 786432 | tf_op jit(solution)/shard_map/reduce_plane/all_to_all | solution.py:60
  88.2 0.6 fusion.3
  (41 shorter events, 4.6 us)
Async XLA Ops:
  18.9 5.1 %collective-permute-start = (bf16[8,6272]{1,0:T(8,128)(2,1)S(1)}, bf16[8,6272]{1,0:T(8,128)(2,1)S(1)}, u32[]{:S(2)}, u32[]{:S(2)}) collective-permute-start(bf16[8,6272]{1,0:T(8,128)(2,1)S(1)} %pad_maximum_fusion.4), channel_id=1, source_target_pairs={{0,128},{1,129},{2,130},{3,131},{4,132},{5,133},{6,134},{7,135},{1... | collective-permute-start | bytes 301064 | tf_op jit(solution)/shard_map/gather_light/ppermute | solution.py:42
  21.9 3.5 %collective-permute-start.1 = (bf16[8,6272]{1,0:T(8,128)(2,1)S(1)}, bf16[8,6272]{1,0:T(8,128)(2,1)S(1)}, u32[]{:S(2)}, u32[]{:S(2)}) collective-permute-start(bf16[8,6272]{1,0:T(8,128)(2,1)S(1)} %pad_maximum_fusion.4), channel_id=1, source_target_pairs={{0,136},{1,137},{2,138},{3,139},{4,140},{5,141},{6,142},{7,143},{1... | collective-permute-start | bytes 301064 | tf_op jit(solution)/shard_map/gather_light/ppermute | solution.py:42
  22.7 4.7 %collective-permute-start.2 = (bf16[8,6272]{1,0:T(8,128)(2,1)S(1)}, bf16[8,6272]{1,0:T(8,128)(2,1)S(1)}, u32[]{:S(2)}, u32[]{:S(2)}) collective-permute-start(bf16[8,6272]{1,0:T(8,128)(2,1)S(1)} %pad_maximum_fusion.4), channel_id=1, source_target_pairs={{0,8},{1,9},{2,10},{3,11},{4,12},{5,13},{6,14},{7,15},{16,24},{17,... | collective-permute-start | bytes 301064 | tf_op jit(solution)/shard_map/gather_light/ppermute | solution.py:42
  24.0 26.3 %copy-start.1 = (bf16[1,3072,128]{2,1,0:T(8,128)(2,1)S(1)}, bf16[1,3072,128]{2,1,0:T(8,128)(2,1)}, u32[]{:S(2)}) copy-start(bf16[1,3072,128]{2,1,0:T(8,128)(2,1)} %param.12) | copy-start | bytes 2359300
  24.1 26.3 %copy-start.2 = (bf16[1,3072,128]{2,1,0:T(8,128)(2,1)S(1)}, bf16[1,3072,128]{2,1,0:T(8,128)(2,1)}, u32[]{:S(2)}) copy-start(bf16[1,3072,128]{2,1,0:T(8,128)(2,1)} %param.11) | copy-start | bytes 2359300
  27.5 8.4 %collective-permute-start.3 = (bf16[32,6272]{1,0:T(8,128)(2,1)S(1)}, bf16[32,6272]{1,0:T(8,128)(2,1)S(1)}, u32[]{:S(2)}, u32[]{:S(2)}) collective-permute-start(bf16[32,6272]{1,0:T(8,128)(2,1)S(1)} %pad_maximum_fusion.2), channel_id=1, source_target_pairs={{0,32},{1,33},{2,34},{3,35},{4,36},{5,37},{6,38},{7,39},{16,48},{1... | collective-permute-start | bytes 1204232 | tf_op jit(solution)/shard_map/gather_heavy/ppermute | solution.py:42
  30.3 15.2 %collective-permute-start.5 = (bf16[32,6272]{1,0:T(8,128)(2,1)S(1)}, bf16[32,6272]{1,0:T(8,128)(2,1)S(1)}, u32[]{:S(2)}, u32[]{:S(2)}) collective-permute-start(bf16[32,6272]{1,0:T(8,128)(2,1)S(1)} %pad_maximum_fusion.2), channel_id=1, source_target_pairs={{0,16},{1,17},{2,18},{3,19},{4,20},{5,21},{6,22},{7,23},{16,32},{1... | collective-permute-start | bytes 1204232 | tf_op jit(solution)/shard_map/gather_heavy/ppermute | solution.py:42
  30.9 18.8 %collective-permute-start.4 = (bf16[32,6272]{1,0:T(8,128)(2,1)S(1)}, bf16[32,6272]{1,0:T(8,128)(2,1)S(1)}, u32[]{:S(2)}, u32[]{:S(2)}) collective-permute-start(bf16[32,6272]{1,0:T(8,128)(2,1)S(1)} %pad_maximum_fusion.2), channel_id=1, source_target_pairs={{0,48},{1,49},{2,50},{3,51},{4,52},{5,53},{6,54},{7,55},{16,0},{17... | collective-permute-start | bytes 1204232 | tf_op jit(solution)/shard_map/gather_heavy/ppermute | solution.py:42
  35.9 14.7 %collective-permute-start.6 = (bf16[32,6272]{1,0:T(8,128)(2,1)S(1)}, bf16[32,6272]{1,0:T(8,128)(2,1)S(1)}, u32[]{:S(2)}, u32[]{:S(2)}) collective-permute-start(bf16[32,6272]{1,0:T(8,128)(2,1)S(1)} %pad_maximum_fusion.2), channel_id=1, source_target_pairs={{0,64},{64,0},{1,65},{65,1},{2,66},{66,2},{3,67},{67,3},{4,68},{68... | collective-permute-start | bytes 1204232 | tf_op jit(solution)/shard_map/gather_core/ppermute | solution.py:46
  45.5 5.2 %collective-permute-start.7 = (bf16[32,6272]{1,0:T(8,128)(2,1)S(1)}, bf16[32,6272]{1,0:T(8,128)(2,1)S(1)}, u32[]{:S(2)}, u32[]{:S(2)}) collective-permute-start(bf16[32,6272]{1,0:T(8,128)(2,1)S(1)} %collective-permute-done.3), channel_id=1, source_target_pairs={{0,64},{64,0},{1,65},{65,1},{2,66},{66,2},{3,67},{67,3},{4,68},{68... | collective-permute-start | bytes 1204232 | tf_op jit(solution)/shard_map/gather_core/ppermute | solution.py:46
  45.5 7.5 %collective-permute-start.11 = (bf16[32,6272]{1,0:T(8,128)(2,1)S(1)}, bf16[32,6272]{1,0:T(8,128)(2,1)S(1)}, u32[]{:S(2)}, u32[]{:S(2)}) collective-permute-start(bf16[32,6272]{1,0:T(8,128)(2,1)S(1)} %collective-permute-done.5), channel_id=1, source_target_pairs={{0,64},{64,0},{1,65},{65,1},{2,66},{66,2},{3,67},{67,3},{4,68},{68... | collective-permute-start | bytes 1204232 | tf_op jit(solution)/shard_map/gather_core/ppermute | solution.py:46
  49.7 3.3 %collective-permute-start.10 = (bf16[32,6272]{1,0:T(8,128)(2,1)S(1)}, bf16[32,6272]{1,0:T(8,128)(2,1)S(1)}, u32[]{:S(2)}, u32[]{:S(2)}) collective-permute-start(bf16[32,6272]{1,0:T(8,128)(2,1)S(1)} %collective-permute-done.4), channel_id=1, source_target_pairs={{0,64},{64,0},{1,65},{65,1},{2,66},{66,2},{3,67},{67,3},{4,68},{68... | collective-permute-start | bytes 1204232 | tf_op jit(solution)/shard_map/gather_core/ppermute | solution.py:46
  50.4 1.1 %copy-start = (bf16[1,128,3072]{2,1,0:T(8,128)(2,1)S(1)}, bf16[1,128,3072]{2,1,0:T(8,128)(2,1)}, u32[]{:S(2)}) copy-start(bf16[1,128,3072]{2,1,0:T(8,128)(2,1)} %param.13) | copy-start | bytes 2359300
  52.9 3.6 %collective-permute-start.8 = (bf16[64,6144]{1,0:T(8,128)(2,1)S(1)}, bf16[64,6144]{1,0:T(8,128)(2,1)S(1)}, u32[]{:S(2)}, u32[]{:S(2)}) collective-permute-start(bf16[64,6144]{1,0:T(8,128)(2,1)S(1)} %get-tuple-element.28), channel_id=1, source_target_pairs={{0,64},{64,0},{1,65},{65,1},{2,66},{66,2},{3,67},{67,3},{4,68},{68... | collective-permute-start | bytes 2359304 | tf_op jit(solution)/shard_map/experts/ppermute | solution.py:46
  54.5 2.5 %collective-permute-start.12 = (bf16[64,6144]{1,0:T(8,128)(2,1)S(1)}, bf16[64,6144]{1,0:T(8,128)(2,1)S(1)}, u32[]{:S(2)}, u32[]{:S(2)}) collective-permute-start(bf16[64,6144]{1,0:T(8,128)(2,1)S(1)} %get-tuple-element.30), channel_id=1, source_target_pairs={{0,64},{64,0},{1,65},{65,1},{2,66},{66,2},{3,67},{67,3},{4,68},{68... | collective-permute-start | bytes 2359304 | tf_op jit(solution)/shard_map/experts/ppermute | solution.py:46
  57.3 8.6 %collective-permute-start.9 = (bf16[32,6144]{1,0:T(8,128)(2,1)S(1)}, bf16[32,6144]{1,0:T(8,128)(2,1)S(1)}, u32[]{:S(2)}, u32[]{:S(2)}) collective-permute-start(bf16[32,6144]{1,0:T(8,128)(2,1)S(1)} %slice.285), channel_id=1, source_target_pairs={{0,32},{1,33},{2,34},{3,35},{4,36},{5,37},{6,38},{7,39},{16,48},{1... | collective-permute-start | bytes 1179656 | tf_op jit(solution)/shard_map/reduce_heavy/ppermute | solution.py:38
  57.4 9.5 %collective-permute-start.14 = (bf16[32,6144]{1,0:T(8,128)(2,1)S(1)}, bf16[32,6144]{1,0:T(8,128)(2,1)S(1)}, u32[]{:S(2)}, u32[]{:S(2)}) collective-permute-start(bf16[32,6144]{1,0:T(8,128)(2,1)S(1)} %get-tuple-element.45), channel_id=1, source_target_pairs={{0,48},{1,49},{2,50},{3,51},{4,52},{5,53},{6,54},{7,55},{16,0},{17... | collective-permute-start | bytes 1179656 | tf_op jit(solution)/shard_map/reduce_heavy/ppermute | solution.py:38
  57.7 12.4 %collective-permute-start.13 = (bf16[32,6144]{1,0:T(8,128)(2,1)S(1)}, bf16[32,6144]{1,0:T(8,128)(2,1)S(1)}, u32[]{:S(2)}, u32[]{:S(2)}) collective-permute-start(bf16[32,6144]{1,0:T(8,128)(2,1)S(1)} %get-tuple-element.46), channel_id=1, source_target_pairs={{0,16},{1,17},{2,18},{3,19},{4,20},{5,21},{6,22},{7,23},{16,32},{1... | collective-permute-start | bytes 1179656 | tf_op jit(solution)/shard_map/reduce_heavy/ppermute | solution.py:38

commit v10 on v9

--- a/solution.py
+++ b/solution.py
@@ -185,30 +185,32 @@
         rows = jnp.concatenate([rows[:, 0, :D], rows[:, 1, :D], rows[:, 0, D:]], axis=1)
     with jax.named_scope("gather_light"):
         got = {d: fetch(rows, "light", d) for d in ISSUE}
-        first = lax.optimization_barrier(jnp.concatenate([rows, got[2]], axis=0))
-        rows = jnp.concatenate([first, got[1], got[3]], axis=0)
+        rows = jnp.concatenate([rows] + [got[d] for d in ORDER], axis=0)
     with jax.named_scope("gather_heavy"):
         got = {d: fetch(rows, "heavy", d) for d in ISSUE}
     with jax.named_scope("gather_core"):
         own, got[2], gate_slice = lax.optimization_barrier((rows, got[2], w_gate[0]))
         slices = (jnp.concatenate([gate_slice, w_up[0]], axis=1), w_down[0])
-        far = {d: swapped(got[d]) for d in ORDER}
-        far_one = jnp.concatenate([swapped(own), far[2]], axis=0)
-        far_two = jnp.concatenate([far[1], far[3]], axis=0)
-        near = jnp.concatenate([own] + [got[d] for d in ORDER], axis=0)
+        near_one = jnp.concatenate([own, got[2]], axis=0)
+        far_one = jnp.concatenate([swapped(own), swapped(got[2])], axis=0)
     with jax.named_scope("experts"):
+        near_terms_one, near_acts_one = expert_terms(group, near_one, *slices, F32)
+        near_terms_one, got[1], got[3] = lax.optimization_barrier((near_terms_one, got[1], got[3]))
+        near_two = jnp.concatenate([got[1], got[3]], axis=0)
+        far_two = jnp.concatenate([swapped(got[1]), swapped(got[3])], axis=0)
         terms_one, acts_one = expert_terms(group, far_one, *slices, BF16)
         other_one = swapped(terms_one)
         _, far_two = lax.optimization_barrier((terms_one, far_two))
         terms_two, acts_two = expert_terms(group, far_two, *slices, BF16)
         other_two = swapped(terms_two)
-        near_terms, near_acts = expert_terms(group, near, *slices, F32)
+        _, near_two = lax.optimization_barrier((terms_two, near_two))
+        near_terms_two, near_acts_two = expert_terms(group, near_two, *slices, F32)
     with jax.named_scope("weights"):
-        grads = weight_grads((far_one, far_two, near), (acts_one, acts_two, near_acts))
+        rows = (far_one, far_two, near_one, near_two)
+        grads = weight_grads(rows, (acts_one, acts_two, near_acts_one, near_acts_two))
     with jax.named_scope("reduce_heavy"):
-        half = 2 * PLANE
-        one = near_terms[:half] + other_one.astype(F32)
-        two = near_terms[half:] + other_two.astype(F32)
+        one = near_terms_one + other_one.astype(F32)
+        two = near_terms_two + other_two.astype(F32)
         send = {1: two[:PLANE], 2: one[PLANE:], 3: two[PLANE:]}
         got = {d: give(send[d].astype(BF16), "heavy", d) for d in ISSUE}
         got = [got[d] for d in ORDER]

time: 89.2 us -> 82.6 us (0.926)
  starting transfers between devices: 26.8 us -> 20.7 us
  waiting for transfers between devices: 15.1 us -> 12.5 us
  Pallas kernels: 9.27 us -> 11.2 us
    ppermute x6, starting transfers between devices: 15 us -> 7.75 us  [swapped(): return lax.ppermute(value, 'core', [(0, 1), (1, 0)])]
    ppermute x3, waiting for transfers between devices: 7.82 us -> 4.78 us  [give(): return lax.ppermute(value, AXES, pairs(stage, d))]
    ppermute x3, starting transfers between devices: 1.81 us -> 4.24 us  [give(): return lax.ppermute(value, AXES, pairs(stage, d))]
    pallas_call x3 -> x4, Pallas kernels: 4.2 us -> 5.49 us  [expert_terms(): pl.pallas_call(expert_kernel, out_shape=(jax.ShapeDtypeStruct((n, 2 * D),...]
    ppermute x6, starting transfers between devices: 9.97 us -> 8.75 us  [fetch(): return lax.ppermute(value, AXES, pairs(stage, -d))]
  transfers between devices with their start and end apart: 15 -> 15, of which waited for: 8 -> 5; matrix products, arithmetic and copies ran while one was open for 1% -> 1% of each run, Pallas kernels for 8% -> 11%
where the time goes in v10:
time: 82.6 us; the launch traced here: 82.3 us
  blocking collectives  34.1 us (41%)
  starting transfers between devices  20.7 us (25%)
  waiting for transfers between devices  12.5 us (15%)
  Pallas kernels  11.2 us (14%)
  local copies, waits for them, and re-layouts  2.04 us (2%)
  between operations  0.84 us (1%)
  other arithmetic  0.83 us (1%)
    all_to_all x1, blocking collectives, scattered(): lax.all_to_all(value, AXES, 0, 0, axis_index_groups=planes(), tiled=True)  17.5 us
    all_to_all x1, blocking collectives, exchanged(): return lax.all_to_all(value, axis, 0, 0, tiled=True)  16.6 us
    ppermute x6, starting transfers between devices, fetch(): return lax.ppermute(value, AXES, pairs(stage, -d))  8.75 us
    ppermute x6, starting transfers between devices, swapped(): return lax.ppermute(value, 'core', [(0, 1), (1, 0)])  7.75 us
    ppermute x6, waiting for transfers between devices, fetch(): return lax.ppermute(value, AXES, pairs(stage, -d))  7.74 us
    pallas_call x4, Pallas kernels, expert_terms(): pl.pallas_call(expert_kernel, out_shape=(jax.ShapeDtypeStruct((n, 2 * D),...  5.49 us
    ppermute x3, waiting for transfers between devices, give(): return lax.ppermute(value, AXES, pairs(stage, d))  4.78 us
    ppermute x3, starting transfers between devices, give(): return lax.ppermute(value, AXES, pairs(stage, d))  4.24 us
  transfers between devices with their start and end apart: 15, of which 5 were waited for; matrix products, arithmetic and copies ran while one was open for 1% of the time, Pallas kernels for 11%

profile of v10, /device:TPU:1, one launch (start us, length us, event | category | flops | bytes accessed | tf_op | source)
XLA Modules:
  0.0 82.3 jit_solution(16668193392885323456)
XLA Ops:
  0.6 1.5 %copies_of_row.1 = bf16[8,2,3200]{2,1,0:T(2,128)(2,1)} custom-call(bf16[1,3072]{1,0:T(2,128)(2,1)} %tokens.1, bf16[1,3072]{1,0:T(2,128)(2,1)} %cotangent.1, s32[1,2]{1,0:T(1,128)} %routes.1, bf16[1,2]{1,0:T(2,128)(2,1)} %weights.1), custom_call_target="tpu_custom_call" | custom-call | tf_op jit(solution)/shard_map/gather_z/copies_of_row/pallas_call | solution.py:81
  2.1 16.6 %all_to_all.10 = bf16[8,2,3200]{2,1,0:T(2,128)(2,1)S(1)} all-to-all(bf16[8,2,3200]{2,1,0:T(2,128)(2,1)} %copies_of_row.1), channel_id=1, replica_groups=mesh['x_hi'=2,'core'=2,'y'=4,'x_lo'=2,'z'=8] {'z'}, dimensions={0} | all-to-all | bytes 204800 | tf_op jit(solution)/shard_map/gather_z/all_to_all | solution.py:50
  19.0 1.4 %collective-permute-start.2 = (bf16[8,6272]{1,0:T(8,128)(2,1)S(1)}, bf16[8,6272]{1,0:T(8,128)(2,1)S(1)}, u32[]{:S(2)}, u32[]{:S(2)}) collective-permute-start(bf16[8,6272]{1,0:T(8,128)(2,1)S(1)} %pad_maximum_fusion.4), channel_id=1, source_target_pairs={{0,8},{1,9},{2,10},{3,11},{4,12},{5,13},{6,14},{7,15},{16,24},{17,... | collective-permute-start | bytes 301064 | tf_op jit(solution)/shard_map/gather_light/ppermute | solution.py:42
  20.3 1.5 %collective-permute-start.1 = (bf16[8,6272]{1,0:T(8,128)(2,1)S(1)}, bf16[8,6272]{1,0:T(8,128)(2,1)S(1)}, u32[]{:S(2)}, u32[]{:S(2)}) collective-permute-start(bf16[8,6272]{1,0:T(8,128)(2,1)S(1)} %pad_maximum_fusion.4), channel_id=1, source_target_pairs={{0,136},{1,137},{2,138},{3,139},{4,140},{5,141},{6,142},{7,143},{1... | collective-permute-start | bytes 301064 | tf_op jit(solution)/shard_map/gather_light/ppermute | solution.py:42
  21.9 1.6 %collective-permute-start = (bf16[8,6272]{1,0:T(8,128)(2,1)S(1)}, bf16[8,6272]{1,0:T(8,128)(2,1)S(1)}, u32[]{:S(2)}, u32[]{:S(2)}) collective-permute-start(bf16[8,6272]{1,0:T(8,128)(2,1)S(1)} %pad_maximum_fusion.4), channel_id=1, source_target_pairs={{0,128},{1,129},{2,130},{3,131},{4,132},{5,133},{6,134},{7,135},{1... | collective-permute-start | bytes 301064 | tf_op jit(solution)/shard_map/gather_light/ppermute | solution.py:42
  23.8 3.0 %collective-permute-done = bf16[8,6272]{1,0:T(8,128)(2,1)S(1)} collective-permute-done((bf16[8,6272]{1,0:T(8,128)(2,1)S(1)}, bf16[8,6272]{1,0:T(8,128)(2,1)S(1)}, u32[]{:S(2)}, u32[]{:S(2)}) %collective-permute-start) | collective-permute-done | bytes 100384 | tf_op jit(solution)/shard_map/gather_light/ppermute | solution.py:42
  26.9 2.8 %collective-permute-start.3 = (bf16[32,6272]{1,0:T(8,128)(2,1)S(1)}, bf16[32,6272]{1,0:T(8,128)(2,1)S(1)}, u32[]{:S(2)}, u32[]{:S(2)}) collective-permute-start(bf16[32,6272]{1,0:T(8,128)(2,1)S(1)} %pad_maximum_fusion.3), channel_id=1, source_target_pairs={{0,32},{1,33},{2,34},{3,35},{4,36},{5,37},{6,38},{7,39},{16,48},{1... | collective-permute-start | bytes 1204232 | tf_op jit(solution)/shard_map/gather_heavy/ppermute | solution.py:42
  29.7 0.9 %collective-permute-start.4 = (bf16[32,6272]{1,0:T(8,128)(2,1)S(1)}, bf16[32,6272]{1,0:T(8,128)(2,1)S(1)}, u32[]{:S(2)}, u32[]{:S(2)}) collective-permute-start(bf16[32,6272]{1,0:T(8,128)(2,1)S(1)} %pad_maximum_fusion.3), channel_id=1, source_target_pairs={{0,48},{1,49},{2,50},{3,51},{4,52},{5,53},{6,54},{7,55},{16,0},{17... | collective-permute-start | bytes 1204232 | tf_op jit(solution)/shard_map/gather_heavy/ppermute | solution.py:42
  30.6 0.6 collective-permute-start.5
  31.2 4.3 %collective-permute-done.3 = bf16[32,6272]{1,0:T(8,128)(2,1)S(1)} collective-permute-done((bf16[32,6272]{1,0:T(8,128)(2,1)S(1)}, bf16[32,6272]{1,0:T(8,128)(2,1)S(1)}, u32[]{:S(2)}, u32[]{:S(2)}) %collective-permute-start.3) | collective-permute-done | bytes 401440 | tf_op jit(solution)/shard_map/gather_heavy/ppermute | solution.py:42
  35.5 4.6 %collective-permute-start.6 = (bf16[32,6272]{1,0:T(8,128)(2,1)S(1)}, bf16[32,6272]{1,0:T(8,128)(2,1)S(1)}, u32[]{:S(2)}, u32[]{:S(2)}) collective-permute-start(bf16[32,6272]{1,0:T(8,128)(2,1)S(1)} %pad_maximum_fusion.3), channel_id=1, source_target_pairs={{0,64},{64,0},{1,65},{65,1},{2,66},{66,2},{3,67},{67,3},{4,68},{68... | collective-permute-start | bytes 1204232 | tf_op jit(solution)/shard_map/gather_core/ppermute | solution.py:46
  40.5 0.9 %copy-done = bf16[1,128,3072]{2,1,0:T(8,128)(2,1)S(1)} copy-done((bf16[1,128,3072]{2,1,0:T(8,128)(2,1)S(1)}, bf16[1,128,3072]{2,1,0:T(8,128)(2,1)}, u32[]{:S(2)}) %copy-start) | copy-done | bytes 786456
  41.5 1.4 %expert_terms.4 = (f32[64,6144]{1,0:T(8,128)S(1)}, bf16[64,384]{1,0:T(8,128)(2,1)S(1)}) custom-call(s32[1]{0:T(128)} %bitcast.group, bf16[64,6272]{1,0:T(8,128)(2,1)S(1)} %constant_dynamic-update-slice_fusion.rows.refs_2_, bf16[3072,256]{1,0:T(8,128)(2,1)S(1)} %pad_maximum_fusion.pair_slice, bf16[128,3072]{1,0:T(8,128)(2,1)S(1)} %bitcast.98), custom_call_target="tpu_custom_call" | custom-call | flops 301989888 | bytes 3145728 | tf_op jit(solution)/shard_map/experts/expert_terms/pallas_call | solution.py:112
  42.9 2.2 %collective-permute-start.11 = (bf16[32,6272]{1,0:T(8,128)(2,1)S(1)}, bf16[32,6272]{1,0:T(8,128)(2,1)S(1)}, u32[]{:S(2)}, u32[]{:S(2)}) collective-permute-start(bf16[32,6272]{1,0:T(8,128)(2,1)S(1)} %collective-permute-done.5), channel_id=1, source_target_pairs={{0,64},{64,0},{1,65},{65,1},{2,66},{66,2},{3,67},{67,3},{4,68},{68... | collective-permute-start | bytes 1204232 | tf_op jit(solution)/shard_map/experts/ppermute | solution.py:46
  45.2 1.4 %expert_terms.5 = (bf16[64,6144]{1,0:T(8,128)(2,1)S(1)}, bf16[64,384]{1,0:T(8,128)(2,1)S(1)}) custom-call(s32[1]{0:T(128)} %bitcast.group, bf16[64,6272]{1,0:T(8,128)(2,1)S(1)} %constant_dynamic-update-slice_fusion.2.rows.refs_0_, bf16[3072,256]{1,0:T(8,128)(2,1)S(1)} %pad_maximum_fusion.pair_slice, bf16[128,3072]{1,0:T(8,128)(2,1)S(1)} %bitcast.99), custom_call_target="tpu_custom_call" | custom-call | flops 301989888 | bytes 3145728 | tf_op jit(solution)/shard_map/experts/expert_terms/pallas_call | solution.py:112
  47.2 1.4 %expert_terms.6 = (bf16[64,6144]{1,0:T(8,128)(2,1)S(1)}, bf16[64,384]{1,0:T(8,128)(2,1)S(1)}) custom-call(s32[1]{0:T(128)} %bitcast.group, bf16[64,6272]{1,0:T(8,128)(2,1)S(1)} %pad_maximum_fusion.1.rows.refs_1_, bf16[3072,256]{1,0:T(8,128)(2,1)S(1)} %pad_maximum_fusion.pair_slice, bf16[128,3072]{1,0:T(8,128)(2,1)S(1)} %bitcast.100), custom_call_target="tpu_custom_call" | custom-call | flops 301989888 | bytes 3145728 | tf_op jit(solution)/shard_map/experts/expert_terms/pallas_call | solution.py:112
  48.9 1.4 %expert_terms.7 = (f32[64,6144]{1,0:T(8,128)S(1)}, bf16[64,384]{1,0:T(8,128)(2,1)S(1)}) custom-call(s32[1]{0:T(128)} %bitcast.group, bf16[64,6272]{1,0:T(8,128)(2,1)S(1)} %pad_maximum_fusion.2.rows.refs_3_, bf16[3072,256]{1,0:T(8,128)(2,1)S(1)} %pad_maximum_fusion.pair_slice, bf16[128,3072]{1,0:T(8,128)(2,1)S(1)} %bitcast.101), custom_call_target="tpu_custom_call" | custom-call | flops 301989888 | bytes 3145728 | tf_op jit(solution)/shard_map/experts/expert_terms/pallas_call | solution.py:112
  50.4 1.5 %collective-permute-start.9 = (bf16[32,6144]{1,0:T(8,128)(2,1)S(1)}, bf16[32,6144]{1,0:T(8,128)(2,1)S(1)}, u32[]{:S(2)}, u32[]{:S(2)}) collective-permute-start(bf16[32,6144]{1,0:T(8,128)(2,1)S(1)} %slice.275), channel_id=1, source_target_pairs={{0,32},{1,33},{2,34},{3,35},{4,36},{5,37},{6,38},{7,39},{16,48},{1... | collective-permute-start | bytes 1179656 | tf_op jit(solution)/shard_map/reduce_heavy/ppermute | solution.py:38
  52.5 2.4 %collective-permute-start.14 = (bf16[32,6144]{1,0:T(8,128)(2,1)S(1)}, bf16[32,6144]{1,0:T(8,128)(2,1)S(1)}, u32[]{:S(2)}, u32[]{:S(2)}) collective-permute-start(bf16[32,6144]{1,0:T(8,128)(2,1)S(1)} %get-tuple-element.55), channel_id=1, source_target_pairs={{0,48},{1,49},{2,50},{3,51},{4,52},{5,53},{6,54},{7,55},{16,0},{17... | collective-permute-start | bytes 1179656 | tf_op jit(solution)/shard_map/reduce_heavy/ppermute | solution.py:38
  54.9 3.6 %weight_grads.1 = (bf16[1,3072,128]{2,1,0:T(8,128)(2,1)}, bf16[1,3072,128]{2,1,0:T(8,128)(2,1)}, bf16[1,128,3072]{2,1,0:T(8,128)(2,1)}) custom-call(bf16[64,6272]{1,0:T(8,128)(2,1)S(1)} %constant_dynamic-update-slice_fusion.2.rows.refs_0_, bf16[64,6272]{1,0:T(8,128)(2,1)S(1)} %pad_maximum_fusion.1.rows.refs_1_, ...), custom_call_target="tpu_custom_call" | custom-call | flops 603979776 | bytes 5505024 | tf_op jit(solution)/shard_map/weights/weight_grads/pallas_call | solution.py:141
  58.6 0.6 collective-permute-done.9.one
  59.2 4.2 %collective-permute-done.13.two = bf16[32,6144]{1,0:T(8,128)(2,1)S(1)} collective-permute-done((bf16[32,6144]{1,0:T(8,128)(2,1)S(1)}, bf16[32,6144]{1,0:T(8,128)(2,1)S(1)}, u32[]{:S(2)}, u32[]{:S(2)}) %collective-permute-start.13) | collective-permute-done | bytes 393248 | tf_op jit(solution)/shard_map/reduce_heavy/ppermute | solution.py:38
  64.0 17.5 %all_to_all.11 = bf16[32,2,3072]{2,1,0:T(2,128)(2,1)S(1)} all-to-all(bf16[32,2,3072]{2,1,0:T(2,128)(2,1)S(1)} %summed_pairs.1), channel_id=1, replica_groups={{0,1,2,3,4,5,6,7,8,9,10,11,12,13,14,15,128,129,130,131,132,133,134,135,..., dimensions={0} | all-to-all | bytes 786432 | tf_op jit(solution)/shard_map/reduce_plane/all_to_all | solution.py:60
  81.6 0.6 fusion.3
  (41 shorter events, 3.7 us)
Async XLA Ops:
  18.7 21.6 %copy-start.1 = (bf16[1,3072,128]{2,1,0:T(8,128)(2,1)S(1)}, bf16[1,3072,128]{2,1,0:T(8,128)(2,1)}, u32[]{:S(2)}) copy-start(bf16[1,3072,128]{2,1,0:T(8,128)(2,1)} %param.12) | copy-start | bytes 2359300
  18.7 21.6 %copy-start.2 = (bf16[1,3072,128]{2,1,0:T(8,128)(2,1)S(1)}, bf16[1,3072,128]{2,1,0:T(8,128)(2,1)}, u32[]{:S(2)}) copy-start(bf16[1,3072,128]{2,1,0:T(8,128)(2,1)} %param.11) | copy-start | bytes 2359300
  19.0 4.8 %collective-permute-start.2 = (bf16[8,6272]{1,0:T(8,128)(2,1)S(1)}, bf16[8,6272]{1,0:T(8,128)(2,1)S(1)}, u32[]{:S(2)}, u32[]{:S(2)}) collective-permute-start(bf16[8,6272]{1,0:T(8,128)(2,1)S(1)} %pad_maximum_fusion.4), channel_id=1, source_target_pairs={{0,8},{1,9},{2,10},{3,11},{4,12},{5,13},{6,14},{7,15},{16,24},{17,... | collective-permute-start | bytes 301064 | tf_op jit(solution)/shard_map/gather_light/ppermute | solution.py:42
  20.3 3.5 %collective-permute-start.1 = (bf16[8,6272]{1,0:T(8,128)(2,1)S(1)}, bf16[8,6272]{1,0:T(8,128)(2,1)S(1)}, u32[]{:S(2)}, u32[]{:S(2)}) collective-permute-start(bf16[8,6272]{1,0:T(8,128)(2,1)S(1)} %pad_maximum_fusion.4), channel_id=1, source_target_pairs={{0,136},{1,137},{2,138},{3,139},{4,140},{5,141},{6,142},{7,143},{1... | collective-permute-start | bytes 301064 | tf_op jit(solution)/shard_map/gather_light/ppermute | solution.py:42
  21.9 5.0 %collective-permute-start = (bf16[8,6272]{1,0:T(8,128)(2,1)S(1)}, bf16[8,6272]{1,0:T(8,128)(2,1)S(1)}, u32[]{:S(2)}, u32[]{:S(2)}) collective-permute-start(bf16[8,6272]{1,0:T(8,128)(2,1)S(1)} %pad_maximum_fusion.4), channel_id=1, source_target_pairs={{0,128},{1,129},{2,130},{3,131},{4,132},{5,133},{6,134},{7,135},{1... | collective-permute-start | bytes 301064 | tf_op jit(solution)/shard_map/gather_light/ppermute | solution.py:42
  26.9 8.6 %collective-permute-start.3 = (bf16[32,6272]{1,0:T(8,128)(2,1)S(1)}, bf16[32,6272]{1,0:T(8,128)(2,1)S(1)}, u32[]{:S(2)}, u32[]{:S(2)}) collective-permute-start(bf16[32,6272]{1,0:T(8,128)(2,1)S(1)} %pad_maximum_fusion.3), channel_id=1, source_target_pairs={{0,32},{1,33},{2,34},{3,35},{4,36},{5,37},{6,38},{7,39},{16,48},{1... | collective-permute-start | bytes 1204232 | tf_op jit(solution)/shard_map/gather_heavy/ppermute | solution.py:42
  29.7 13.1 %collective-permute-start.4 = (bf16[32,6272]{1,0:T(8,128)(2,1)S(1)}, bf16[32,6272]{1,0:T(8,128)(2,1)S(1)}, u32[]{:S(2)}, u32[]{:S(2)}) collective-permute-start(bf16[32,6272]{1,0:T(8,128)(2,1)S(1)} %pad_maximum_fusion.3), channel_id=1, source_target_pairs={{0,48},{1,49},{2,50},{3,51},{4,52},{5,53},{6,54},{7,55},{16,0},{17... | collective-permute-start | bytes 1204232 | tf_op jit(solution)/shard_map/gather_heavy/ppermute | solution.py:42
  30.6 12.3 %collective-permute-start.5 = (bf16[32,6272]{1,0:T(8,128)(2,1)S(1)}, bf16[32,6272]{1,0:T(8,128)(2,1)S(1)}, u32[]{:S(2)}, u32[]{:S(2)}) collective-permute-start(bf16[32,6272]{1,0:T(8,128)(2,1)S(1)} %pad_maximum_fusion.3), channel_id=1, source_target_pairs={{0,16},{1,17},{2,18},{3,19},{4,20},{5,21},{6,22},{7,23},{16,32},{1... | collective-permute-start | bytes 1204232 | tf_op jit(solution)/shard_map/gather_heavy/ppermute | solution.py:42
  35.5 9.6 %collective-permute-start.6 = (bf16[32,6272]{1,0:T(8,128)(2,1)S(1)}, bf16[32,6272]{1,0:T(8,128)(2,1)S(1)}, u32[]{:S(2)}, u32[]{:S(2)}) collective-permute-start(bf16[32,6272]{1,0:T(8,128)(2,1)S(1)} %pad_maximum_fusion.3), channel_id=1, source_target_pairs={{0,64},{64,0},{1,65},{65,1},{2,66},{66,2},{3,67},{67,3},{4,68},{68... | collective-permute-start | bytes 1204232 | tf_op jit(solution)/shard_map/gather_core/ppermute | solution.py:46
  40.2 5.0 %collective-permute-start.7 = (bf16[32,6272]{1,0:T(8,128)(2,1)S(1)}, bf16[32,6272]{1,0:T(8,128)(2,1)S(1)}, u32[]{:S(2)}, u32[]{:S(2)}) collective-permute-start(bf16[32,6272]{1,0:T(8,128)(2,1)S(1)} %collective-permute-done.3), channel_id=1, source_target_pairs={{0,64},{64,0},{1,65},{65,1},{2,66},{66,2},{3,67},{67,3},{4,68},{68... | collective-permute-start | bytes 1204232 | tf_op jit(solution)/shard_map/gather_core/ppermute | solution.py:46
  40.3 1.1 %copy-start = (bf16[1,128,3072]{2,1,0:T(8,128)(2,1)S(1)}, bf16[1,128,3072]{2,1,0:T(8,128)(2,1)}, u32[]{:S(2)}) copy-start(bf16[1,128,3072]{2,1,0:T(8,128)(2,1)} %param.13) | copy-start | bytes 2359300
  42.9 4.3 %collective-permute-start.11 = (bf16[32,6272]{1,0:T(8,128)(2,1)S(1)}, bf16[32,6272]{1,0:T(8,128)(2,1)S(1)}, u32[]{:S(2)}, u32[]{:S(2)}) collective-permute-start(bf16[32,6272]{1,0:T(8,128)(2,1)S(1)} %collective-permute-done.5), channel_id=1, source_target_pairs={{0,64},{64,0},{1,65},{65,1},{2,66},{66,2},{3,67},{67,3},{4,68},{68... | collective-permute-start | bytes 1204232 | tf_op jit(solution)/shard_map/experts/ppermute | solution.py:46
  45.0 2.1 %collective-permute-start.10 = (bf16[32,6272]{1,0:T(8,128)(2,1)S(1)}, bf16[32,6272]{1,0:T(8,128)(2,1)S(1)}, u32[]{:S(2)}, u32[]{:S(2)}) collective-permute-start(bf16[32,6272]{1,0:T(8,128)(2,1)S(1)} %collective-permute-done.4), channel_id=1, source_target_pairs={{0,64},{64,0},{1,65},{65,1},{2,66},{66,2},{3,67},{67,3},{4,68},{68... | collective-permute-start | bytes 1204232 | tf_op jit(solution)/shard_map/experts/ppermute | solution.py:46
  46.6 3.7 %collective-permute-start.8 = (bf16[64,6144]{1,0:T(8,128)(2,1)S(1)}, bf16[64,6144]{1,0:T(8,128)(2,1)S(1)}, u32[]{:S(2)}, u32[]{:S(2)}) collective-permute-start(bf16[64,6144]{1,0:T(8,128)(2,1)S(1)} %get-tuple-element.35), channel_id=1, source_target_pairs={{0,64},{64,0},{1,65},{65,1},{2,66},{66,2},{3,67},{67,3},{4,68},{68... | collective-permute-start | bytes 2359304 | tf_op jit(solution)/shard_map/experts/ppermute | solution.py:46
  48.6 3.3 %collective-permute-start.12 = (bf16[64,6144]{1,0:T(8,128)(2,1)S(1)}, bf16[64,6144]{1,0:T(8,128)(2,1)S(1)}, u32[]{:S(2)}, u32[]{:S(2)}) collective-permute-start(bf16[64,6144]{1,0:T(8,128)(2,1)S(1)} %get-tuple-element.39), channel_id=1, source_target_pairs={{0,64},{64,0},{1,65},{65,1},{2,66},{66,2},{3,67},{67,3},{4,68},{68... | collective-permute-start | bytes 2359304 | tf_op jit(solution)/shard_map/experts/ppermute | solution.py:46
  50.4 8.7 %collective-permute-start.9 = (bf16[32,6144]{1,0:T(8,128)(2,1)S(1)}, bf16[32,6144]{1,0:T(8,128)(2,1)S(1)}, u32[]{:S(2)}, u32[]{:S(2)}) collective-permute-start(bf16[32,6144]{1,0:T(8,128)(2,1)S(1)} %slice.275), channel_id=1, source_target_pairs={{0,32},{1,33},{2,34},{3,35},{4,36},{5,37},{6,38},{7,39},{16,48},{1... | collective-permute-start | bytes 1179656 | tf_op jit(solution)/shard_map/reduce_heavy/ppermute | solution.py:38
  52.1 11.2 %collective-permute-start.13 = (bf16[32,6144]{1,0:T(8,128)(2,1)S(1)}, bf16[32,6144]{1,0:T(8,128)(2,1)S(1)}, u32[]{:S(2)}, u32[]{:S(2)}) collective-permute-start(bf16[32,6144]{1,0:T(8,128)(2,1)S(1)} %get-tuple-element.56), channel_id=1, source_target_pairs={{0,16},{1,17},{2,18},{3,19},{4,20},{5,21},{6,22},{7,23},{16,32},{1... | collective-permute-start | bytes 1179656 | tf_op jit(solution)/shard_map/reduce_heavy/ppermute | solution.py:38
  52.5 10.8 %collective-permute-start.14 = (bf16[32,6144]{1,0:T(8,128)(2,1)S(1)}, bf16[32,6144]{1,0:T(8,128)(2,1)S(1)}, u32[]{:S(2)}, u32[]{:S(2)}) collective-permute-start(bf16[32,6144]{1,0:T(8,128)(2,1)S(1)} %get-tuple-element.55), channel_id=1, source_target_pairs={{0,48},{1,49},{2,50},{3,51},{4,52},{5,53},{6,54},{7,55},{16,0},{17... | collective-permute-start | bytes 1179656 | tf_op jit(solution)/shard_map/reduce_heavy/ppermute | solution.py:38

commit v11 on v10

--- a/solution.py
+++ b/solution.py
@@ -195,15 +195,15 @@
         far_one = jnp.concatenate([swapped(own), swapped(got[2])], axis=0)
     with jax.named_scope("experts"):
         near_terms_one, near_acts_one = expert_terms(group, near_one, *slices, F32)
-        near_terms_one, got[1], got[3] = lax.optimization_barrier((near_terms_one, got[1], got[3]))
+        terms_one, acts_one = expert_terms(group, far_one, *slices, BF16)
+        other_one = swapped(terms_one)
+        near_terms_one, _, got[1], got[3] = lax.optimization_barrier(
+            (near_terms_one, terms_one, got[1], got[3])
+        )
         near_two = jnp.concatenate([got[1], got[3]], axis=0)
         far_two = jnp.concatenate([swapped(got[1]), swapped(got[3])], axis=0)
-        terms_one, acts_one = expert_terms(group, far_one, *slices, BF16)
-        other_one = swapped(terms_one)
-        _, far_two = lax.optimization_barrier((terms_one, far_two))
         terms_two, acts_two = expert_terms(group, far_two, *slices, BF16)
         other_two = swapped(terms_two)
-        _, near_two = lax.optimization_barrier((terms_two, near_two))
         near_terms_two, near_acts_two = expert_terms(group, near_two, *slices, F32)
     with jax.named_scope("weights"):
         rows = (far_one, far_two, near_one, near_two)

time: 82.6 us -> 83 us (level)
  starting transfers between devices: 20.7 us -> 19.6 us
    ppermute x6, starting transfers between devices: 7.75 us -> 6.31 us  [swapped(): return lax.ppermute(value, 'core', [(0, 1), (1, 0)])]
    ppermute x6, waiting for transfers between devices: 0.02 us -> 0.99 us  [swapped(): return lax.ppermute(value, 'core', [(0, 1), (1, 0)])]
  transfers between devices with their start and end apart: 15 -> 15, of which waited for: 5 -> 7; matrix products, arithmetic and copies ran while one was open for 1% -> 1% of each run, Pallas kernels for 11% -> 11%
where the time goes in v11:
time: 83 us; the launch traced here: 82.5 us
  blocking collectives  34.8 us (42%)
  starting transfers between devices  19.6 us (24%)
  waiting for transfers between devices  13.2 us (16%)
  Pallas kernels  11.2 us (13%)
  local copies, waits for them, and re-layouts  2.17 us (3%)
    all_to_all x1, blocking collectives, scattered(): lax.all_to_all(value, AXES, 0, 0, axis_index_groups=planes(), tiled=True)  18.2 us
    all_to_all x1, blocking collectives, exchanged(): return lax.all_to_all(value, axis, 0, 0, tiled=True)  16.6 us
    ppermute x6, starting transfers between devices, fetch(): return lax.ppermute(value, AXES, pairs(stage, -d))  8.75 us
    ppermute x6, waiting for transfers between devices, fetch(): return lax.ppermute(value, AXES, pairs(stage, -d))  7.74 us
    ppermute x6, starting transfers between devices, swapped(): return lax.ppermute(value, 'core', [(0, 1), (1, 0)])  6.31 us
    pallas_call x4, Pallas kernels, expert_terms(): pl.pallas_call(expert_kernel, out_shape=(jax.ShapeDtypeStruct((n, 2 * D),...  5.5 us
    ppermute x3, starting transfers between devices, give(): return lax.ppermute(value, AXES, pairs(stage, d))  4.54 us
    ppermute x3, waiting for transfers between devices, give(): return lax.ppermute(value, AXES, pairs(stage, d))  4.48 us
  transfers between devices with their start and end apart: 15, of which 7 were waited for; matrix products, arithmetic and copies ran while one was open for 1% of the time, Pallas kernels for 11%

profile of v11, /device:TPU:1, one launch (start us, length us, event | category | flops | bytes accessed | tf_op | source)
XLA Modules:
  0.0 82.5 jit_solution(7539901439445046333)
XLA Ops:
  0.6 1.5 %copies_of_row.1 = bf16[8,2,3200]{2,1,0:T(2,128)(2,1)} custom-call(bf16[1,3072]{1,0:T(2,128)(2,1)} %tokens.1, bf16[1,3072]{1,0:T(2,128)(2,1)} %cotangent.1, s32[1,2]{1,0:T(1,128)} %routes.1, bf16[1,2]{1,0:T(2,128)(2,1)} %weights.1), custom_call_target="tpu_custom_call" | custom-call | tf_op jit(solution)/shard_map/gather_z/copies_of_row/pallas_call | solution.py:81
  2.1 16.6 %all_to_all.10 = bf16[8,2,3200]{2,1,0:T(2,128)(2,1)S(1)} all-to-all(bf16[8,2,3200]{2,1,0:T(2,128)(2,1)} %copies_of_row.1), channel_id=1, replica_groups=mesh['x_hi'=2,'core'=2,'y'=4,'x_lo'=2,'z'=8] {'z'}, dimensions={0} | all-to-all | bytes 204800 | tf_op jit(solution)/shard_map/gather_z/all_to_all | solution.py:50
  19.0 1.4 %collective-permute-start.2 = (bf16[8,6272]{1,0:T(8,128)(2,1)S(1)}, bf16[8,6272]{1,0:T(8,128)(2,1)S(1)}, u32[]{:S(2)}, u32[]{:S(2)}) collective-permute-start(bf16[8,6272]{1,0:T(8,128)(2,1)S(1)} %pad_maximum_fusion.2), channel_id=1, source_target_pairs={{0,8},{1,9},{2,10},{3,11},{4,12},{5,13},{6,14},{7,15},{16,24},{17,... | collective-permute-start | bytes 301064 | tf_op jit(solution)/shard_map/gather_light/ppermute | solution.py:42
  20.3 1.5 %collective-permute-start.1 = (bf16[8,6272]{1,0:T(8,128)(2,1)S(1)}, bf16[8,6272]{1,0:T(8,128)(2,1)S(1)}, u32[]{:S(2)}, u32[]{:S(2)}) collective-permute-start(bf16[8,6272]{1,0:T(8,128)(2,1)S(1)} %pad_maximum_fusion.2), channel_id=1, source_target_pairs={{0,136},{1,137},{2,138},{3,139},{4,140},{5,141},{6,142},{7,143},{1... | collective-permute-start | bytes 301064 | tf_op jit(solution)/shard_map/gather_light/ppermute | solution.py:42
  21.9 1.6 %collective-permute-start = (bf16[8,6272]{1,0:T(8,128)(2,1)S(1)}, bf16[8,6272]{1,0:T(8,128)(2,1)S(1)}, u32[]{:S(2)}, u32[]{:S(2)}) collective-permute-start(bf16[8,6272]{1,0:T(8,128)(2,1)S(1)} %pad_maximum_fusion.2), channel_id=1, source_target_pairs={{0,128},{1,129},{2,130},{3,131},{4,132},{5,133},{6,134},{7,135},{1... | collective-permute-start | bytes 301064 | tf_op jit(solution)/shard_map/gather_light/ppermute | solution.py:42
  23.8 3.0 %collective-permute-done = bf16[8,6272]{1,0:T(8,128)(2,1)S(1)} collective-permute-done((bf16[8,6272]{1,0:T(8,128)(2,1)S(1)}, bf16[8,6272]{1,0:T(8,128)(2,1)S(1)}, u32[]{:S(2)}, u32[]{:S(2)}) %collective-permute-start) | collective-permute-done | bytes 100384 | tf_op jit(solution)/shard_map/gather_light/ppermute | solution.py:42
  26.9 2.8 %collective-permute-start.3 = (bf16[32,6272]{1,0:T(8,128)(2,1)S(1)}, bf16[32,6272]{1,0:T(8,128)(2,1)S(1)}, u32[]{:S(2)}, u32[]{:S(2)}) collective-permute-start(bf16[32,6272]{1,0:T(8,128)(2,1)S(1)} %pad_maximum_fusion.1), channel_id=1, source_target_pairs={{0,32},{1,33},{2,34},{3,35},{4,36},{5,37},{6,38},{7,39},{16,48},{1... | collective-permute-start | bytes 1204232 | tf_op jit(solution)/shard_map/gather_heavy/ppermute | solution.py:42
  29.7 0.9 %collective-permute-start.6 = (bf16[32,6272]{1,0:T(8,128)(2,1)S(1)}, bf16[32,6272]{1,0:T(8,128)(2,1)S(1)}, u32[]{:S(2)}, u32[]{:S(2)}) collective-permute-start(bf16[32,6272]{1,0:T(8,128)(2,1)S(1)} %pad_maximum_fusion.1), channel_id=1, source_target_pairs={{0,48},{1,49},{2,50},{3,51},{4,52},{5,53},{6,54},{7,55},{16,0},{17... | collective-permute-start | bytes 1204232 | tf_op jit(solution)/shard_map/gather_heavy/ppermute | solution.py:42
  30.6 0.6 collective-permute-start.7
  31.2 4.3 %collective-permute-done.3 = bf16[32,6272]{1,0:T(8,128)(2,1)S(1)} collective-permute-done((bf16[32,6272]{1,0:T(8,128)(2,1)S(1)}, bf16[32,6272]{1,0:T(8,128)(2,1)S(1)}, u32[]{:S(2)}, u32[]{:S(2)}) %collective-permute-start.3) | collective-permute-done | bytes 401440 | tf_op jit(solution)/shard_map/gather_heavy/ppermute | solution.py:42
  35.5 4.6 %collective-permute-start.4 = (bf16[32,6272]{1,0:T(8,128)(2,1)S(1)}, bf16[32,6272]{1,0:T(8,128)(2,1)S(1)}, u32[]{:S(2)}, u32[]{:S(2)}) collective-permute-start(bf16[32,6272]{1,0:T(8,128)(2,1)S(1)} %pad_maximum_fusion.1), channel_id=1, source_target_pairs={{0,64},{64,0},{1,65},{65,1},{2,66},{66,2},{3,67},{67,3},{4,68},{68... | collective-permute-start | bytes 1204232 | tf_op jit(solution)/shard_map/gather_core/ppermute | solution.py:46
  40.5 0.9 %copy-done = bf16[1,128,3072]{2,1,0:T(8,128)(2,1)S(1)} copy-done((bf16[1,128,3072]{2,1,0:T(8,128)(2,1)S(1)}, bf16[1,128,3072]{2,1,0:T(8,128)(2,1)}, u32[]{:S(2)}) %copy-start) | copy-done | bytes 786456
  41.5 1.4 %expert_terms.4 = (f32[64,6144]{1,0:T(8,128)S(1)}, bf16[64,384]{1,0:T(8,128)(2,1)S(1)}) custom-call(s32[1]{0:T(128)} %bitcast.group, bf16[64,6272]{1,0:T(8,128)(2,1)S(1)} %constant_dynamic-update-slice_fusion.rows.refs_2_, bf16[3072,256]{1,0:T(8,128)(2,1)S(1)} %pad_maximum_fusion.pair_slice, bf16[128,3072]{1,0:T(8,128)(2,1)S(1)} %bitcast.98), custom_call_target="tpu_custom_call" | custom-call | flops 301989888 | bytes 3145728 | tf_op jit(solution)/shard_map/experts/expert_terms/pallas_call | solution.py:112
  42.9 1.4 %expert_terms.5 = (bf16[64,6144]{1,0:T(8,128)(2,1)S(1)}, bf16[64,384]{1,0:T(8,128)(2,1)S(1)}) custom-call(s32[1]{0:T(128)} %bitcast.group, bf16[64,6272]{1,0:T(8,128)(2,1)S(1)} %constant_dynamic-update-slice_fusion.2.rows.refs_0_, bf16[3072,256]{1,0:T(8,128)(2,1)S(1)} %pad_maximum_fusion.pair_slice, bf16[128,3072]{1,0:T(8,128)(2,1)S(1)} %bitcast.99), custom_call_target="tpu_custom_call" | custom-call | flops 301989888 | bytes 3145728 | tf_op jit(solution)/shard_map/experts/expert_terms/pallas_call | solution.py:112
  45.5 1.4 %expert_terms.6 = (f32[64,6144]{1,0:T(8,128)S(1)}, bf16[64,384]{1,0:T(8,128)(2,1)S(1)}) custom-call(s32[1]{0:T(128)} %bitcast.group, bf16[64,6272]{1,0:T(8,128)(2,1)S(1)} %constant_dynamic-update-slice_fusion.4.rows.refs_3_, bf16[3072,256]{1,0:T(8,128)(2,1)S(1)} %pad_maximum_fusion.pair_slice, bf16[128,3072]{1,0:T(8,128)(2,1)S(1)} %bitcast.100), custom_call_target="tpu_custom_call" | custom-call | flops 301989888 | bytes 3145728 | tf_op jit(solution)/shard_map/experts/expert_terms/pallas_call | solution.py:112
  47.4 0.5 collective-permute-done.11
  47.9 1.4 %expert_terms.7 = (bf16[64,6144]{1,0:T(8,128)(2,1)S(1)}, bf16[64,384]{1,0:T(8,128)(2,1)S(1)}) custom-call(s32[1]{0:T(128)} %bitcast.group, bf16[64,6272]{1,0:T(8,128)(2,1)S(1)} %constant_dynamic-update-slice_fusion.6.rows.refs_1_, bf16[3072,256]{1,0:T(8,128)(2,1)S(1)} %pad_maximum_fusion.pair_slice, bf16[128,3072]{1,0:T(8,128)(2,1)S(1)} %bitcast.101), custom_call_target="tpu_custom_call" | custom-call | flops 301989888 | bytes 3145728 | tf_op jit(solution)/shard_map/experts/expert_terms/pallas_call | solution.py:112
  50.0 1.8 %collective-permute-start.9 = (bf16[32,6144]{1,0:T(8,128)(2,1)S(1)}, bf16[32,6144]{1,0:T(8,128)(2,1)S(1)}, u32[]{:S(2)}, u32[]{:S(2)}) collective-permute-start(bf16[32,6144]{1,0:T(8,128)(2,1)S(1)} %slice.275), channel_id=1, source_target_pairs={{0,32},{1,33},{2,34},{3,35},{4,36},{5,37},{6,38},{7,39},{16,48},{1... | collective-permute-start | bytes 1179656 | tf_op jit(solution)/shard_map/reduce_heavy/ppermute | solution.py:38
  52.3 2.4 %collective-permute-start.14 = (bf16[32,6144]{1,0:T(8,128)(2,1)S(1)}, bf16[32,6144]{1,0:T(8,128)(2,1)S(1)}, u32[]{:S(2)}, u32[]{:S(2)}) collective-permute-start(bf16[32,6144]{1,0:T(8,128)(2,1)S(1)} %get-tuple-element.51), channel_id=1, source_target_pairs={{0,48},{1,49},{2,50},{3,51},{4,52},{5,53},{6,54},{7,55},{16,0},{17... | collective-permute-start | bytes 1179656 | tf_op jit(solution)/shard_map/reduce_heavy/ppermute | solution.py:38
  54.7 3.6 %weight_grads.1 = (bf16[1,3072,128]{2,1,0:T(8,128)(2,1)}, bf16[1,3072,128]{2,1,0:T(8,128)(2,1)}, bf16[1,128,3072]{2,1,0:T(8,128)(2,1)}) custom-call(bf16[64,6272]{1,0:T(8,128)(2,1)S(1)} %constant_dynamic-update-slice_fusion.2.rows.refs_0_, bf16[64,6272]{1,0:T(8,128)(2,1)S(1)} %constant_dynamic-update-slice_fusion.6.rows.refs_1_, ...), custom_call_target="tpu_custom_call" | custom-call | flops 603979776 | bytes 5505024 | tf_op jit(solution)/shard_map/weights/weight_grads/pallas_call | solution.py:141
  58.7 4.2 %collective-permute-done.13.two = bf16[32,6144]{1,0:T(8,128)(2,1)S(1)} collective-permute-done((bf16[32,6144]{1,0:T(8,128)(2,1)S(1)}, bf16[32,6144]{1,0:T(8,128)(2,1)S(1)}, u32[]{:S(2)}, u32[]{:S(2)}) %collective-permute-start.13) | collective-permute-done | bytes 393248 | tf_op jit(solution)/shard_map/reduce_heavy/ppermute | solution.py:38
  62.9 0.6 summed_pairs.1
  63.5 18.2 %all_to_all.11 = bf16[32,2,3072]{2,1,0:T(2,128)(2,1)S(1)} all-to-all(bf16[32,2,3072]{2,1,0:T(2,128)(2,1)S(1)} %summed_pairs.1), channel_id=1, replica_groups={{0,1,2,3,4,5,6,7,8,9,10,11,12,13,14,15,128,129,130,131,132,133,134,135,..., dimensions={0} | all-to-all | bytes 786432 | tf_op jit(solution)/shard_map/reduce_plane/all_to_all | solution.py:60
  81.9 0.6 fusion.3
  (43 shorter events, 4.5 us)
Async XLA Ops:
  18.7 21.6 %copy-start.1 = (bf16[1,3072,128]{2,1,0:T(8,128)(2,1)S(1)}, bf16[1,3072,128]{2,1,0:T(8,128)(2,1)}, u32[]{:S(2)}) copy-start(bf16[1,3072,128]{2,1,0:T(8,128)(2,1)} %param.12) | copy-start | bytes 2359300
  18.7 21.6 %copy-start.2 = (bf16[1,3072,128]{2,1,0:T(8,128)(2,1)S(1)}, bf16[1,3072,128]{2,1,0:T(8,128)(2,1)}, u32[]{:S(2)}) copy-start(bf16[1,3072,128]{2,1,0:T(8,128)(2,1)} %param.11) | copy-start | bytes 2359300
  19.0 4.8 %collective-permute-start.2 = (bf16[8,6272]{1,0:T(8,128)(2,1)S(1)}, bf16[8,6272]{1,0:T(8,128)(2,1)S(1)}, u32[]{:S(2)}, u32[]{:S(2)}) collective-permute-start(bf16[8,6272]{1,0:T(8,128)(2,1)S(1)} %pad_maximum_fusion.2), channel_id=1, source_target_pairs={{0,8},{1,9},{2,10},{3,11},{4,12},{5,13},{6,14},{7,15},{16,24},{17,... | collective-permute-start | bytes 301064 | tf_op jit(solution)/shard_map/gather_light/ppermute | solution.py:42
  20.3 3.5 %collective-permute-start.1 = (bf16[8,6272]{1,0:T(8,128)(2,1)S(1)}, bf16[8,6272]{1,0:T(8,128)(2,1)S(1)}, u32[]{:S(2)}, u32[]{:S(2)}) collective-permute-start(bf16[8,6272]{1,0:T(8,128)(2,1)S(1)} %pad_maximum_fusion.2), channel_id=1, source_target_pairs={{0,136},{1,137},{2,138},{3,139},{4,140},{5,141},{6,142},{7,143},{1... | collective-permute-start | bytes 301064 | tf_op jit(solution)/shard_map/gather_light/ppermute | solution.py:42
  21.9 5.0 %collective-permute-start = (bf16[8,6272]{1,0:T(8,128)(2,1)S(1)}, bf16[8,6272]{1,0:T(8,128)(2,1)S(1)}, u32[]{:S(2)}, u32[]{:S(2)}) collective-permute-start(bf16[8,6272]{1,0:T(8,128)(2,1)S(1)} %pad_maximum_fusion.2), channel_id=1, source_target_pairs={{0,128},{1,129},{2,130},{3,131},{4,132},{5,133},{6,134},{7,135},{1... | collective-permute-start | bytes 301064 | tf_op jit(solution)/shard_map/gather_light/ppermute | solution.py:42
  26.9 8.6 %collective-permute-start.3 = (bf16[32,6272]{1,0:T(8,128)(2,1)S(1)}, bf16[32,6272]{1,0:T(8,128)(2,1)S(1)}, u32[]{:S(2)}, u32[]{:S(2)}) collective-permute-start(bf16[32,6272]{1,0:T(8,128)(2,1)S(1)} %pad_maximum_fusion.1), channel_id=1, source_target_pairs={{0,32},{1,33},{2,34},{3,35},{4,36},{5,37},{6,38},{7,39},{16,48},{1... | collective-permute-start | bytes 1204232 | tf_op jit(solution)/shard_map/gather_heavy/ppermute | solution.py:42
  29.7 15.1 %collective-permute-start.6 = (bf16[32,6272]{1,0:T(8,128)(2,1)S(1)}, bf16[32,6272]{1,0:T(8,128)(2,1)S(1)}, u32[]{:S(2)}, u32[]{:S(2)}) collective-permute-start(bf16[32,6272]{1,0:T(8,128)(2,1)S(1)} %pad_maximum_fusion.1), channel_id=1, source_target_pairs={{0,48},{1,49},{2,50},{3,51},{4,52},{5,53},{6,54},{7,55},{16,0},{17... | collective-permute-start | bytes 1204232 | tf_op jit(solution)/shard_map/gather_heavy/ppermute | solution.py:42
  30.6 14.2 %collective-permute-start.7 = (bf16[32,6272]{1,0:T(8,128)(2,1)S(1)}, bf16[32,6272]{1,0:T(8,128)(2,1)S(1)}, u32[]{:S(2)}, u32[]{:S(2)}) collective-permute-start(bf16[32,6272]{1,0:T(8,128)(2,1)S(1)} %pad_maximum_fusion.1), channel_id=1, source_target_pairs={{0,16},{1,17},{2,18},{3,19},{4,20},{5,21},{6,22},{7,23},{16,32},{1... | collective-permute-start | bytes 1204232 | tf_op jit(solution)/shard_map/gather_heavy/ppermute | solution.py:42
  35.5 7.3 %collective-permute-start.4 = (bf16[32,6272]{1,0:T(8,128)(2,1)S(1)}, bf16[32,6272]{1,0:T(8,128)(2,1)S(1)}, u32[]{:S(2)}, u32[]{:S(2)}) collective-permute-start(bf16[32,6272]{1,0:T(8,128)(2,1)S(1)} %pad_maximum_fusion.1), channel_id=1, source_target_pairs={{0,64},{64,0},{1,65},{65,1},{2,66},{66,2},{3,67},{67,3},{4,68},{68... | collective-permute-start | bytes 1204232 | tf_op jit(solution)/shard_map/gather_core/ppermute | solution.py:46
  40.2 2.7 %collective-permute-start.5 = (bf16[32,6272]{1,0:T(8,128)(2,1)S(1)}, bf16[32,6272]{1,0:T(8,128)(2,1)S(1)}, u32[]{:S(2)}, u32[]{:S(2)}) collective-permute-start(bf16[32,6272]{1,0:T(8,128)(2,1)S(1)} %collective-permute-done.3), channel_id=1, source_target_pairs={{0,64},{64,0},{1,65},{65,1},{2,66},{66,2},{3,67},{67,3},{4,68},{68... | collective-permute-start | bytes 1204232 | tf_op jit(solution)/shard_map/gather_core/ppermute | solution.py:46
  40.3 1.1 %copy-start = (bf16[1,128,3072]{2,1,0:T(8,128)(2,1)S(1)}, bf16[1,128,3072]{2,1,0:T(8,128)(2,1)}, u32[]{:S(2)}) copy-start(bf16[1,128,3072]{2,1,0:T(8,128)(2,1)} %param.13) | copy-start | bytes 2359300
  44.3 5.5 %collective-permute-start.8 = (bf16[64,6144]{1,0:T(8,128)(2,1)S(1)}, bf16[64,6144]{1,0:T(8,128)(2,1)S(1)}, u32[]{:S(2)}, u32[]{:S(2)}) collective-permute-start(bf16[64,6144]{1,0:T(8,128)(2,1)S(1)} %get-tuple-element.32), channel_id=1, source_target_pairs={{0,64},{64,0},{1,65},{65,1},{2,66},{66,2},{3,67},{67,3},{4,68},{68... | collective-permute-start | bytes 2359304 | tf_op jit(solution)/shard_map/experts/ppermute | solution.py:46
  44.9 2.4 %collective-permute-start.10 = (bf16[32,6272]{1,0:T(8,128)(2,1)S(1)}, bf16[32,6272]{1,0:T(8,128)(2,1)S(1)}, u32[]{:S(2)}, u32[]{:S(2)}) collective-permute-start(bf16[32,6272]{1,0:T(8,128)(2,1)S(1)} %collective-permute-done.6), channel_id=1, source_target_pairs={{0,64},{64,0},{1,65},{65,1},{2,66},{66,2},{3,67},{67,3},{4,68},{68... | collective-permute-start | bytes 1204232 | tf_op jit(solution)/shard_map/experts/ppermute | solution.py:46
  45.1 2.7 %collective-permute-start.11 = (bf16[32,6272]{1,0:T(8,128)(2,1)S(1)}, bf16[32,6272]{1,0:T(8,128)(2,1)S(1)}, u32[]{:S(2)}, u32[]{:S(2)}) collective-permute-start(bf16[32,6272]{1,0:T(8,128)(2,1)S(1)} %collective-permute-done.7), channel_id=1, source_target_pairs={{0,64},{64,0},{1,65},{65,1},{2,66},{66,2},{3,67},{67,3},{4,68},{68... | collective-permute-start | bytes 1204232 | tf_op jit(solution)/shard_map/experts/ppermute | solution.py:46
  49.3 2.4 %collective-permute-start.12 = (bf16[64,6144]{1,0:T(8,128)(2,1)S(1)}, bf16[64,6144]{1,0:T(8,128)(2,1)S(1)}, u32[]{:S(2)}, u32[]{:S(2)}) collective-permute-start(bf16[64,6144]{1,0:T(8,128)(2,1)S(1)} %get-tuple-element.37), channel_id=1, source_target_pairs={{0,64},{64,0},{1,65},{65,1},{2,66},{66,2},{3,67},{67,3},{4,68},{68... | collective-permute-start | bytes 2359304 | tf_op jit(solution)/shard_map/experts/ppermute | solution.py:46
  50.0 8.7 %collective-permute-start.9 = (bf16[32,6144]{1,0:T(8,128)(2,1)S(1)}, bf16[32,6144]{1,0:T(8,128)(2,1)S(1)}, u32[]{:S(2)}, u32[]{:S(2)}) collective-permute-start(bf16[32,6144]{1,0:T(8,128)(2,1)S(1)} %slice.275), channel_id=1, source_target_pairs={{0,32},{1,33},{2,34},{3,35},{4,36},{5,37},{6,38},{7,39},{16,48},{1... | collective-permute-start | bytes 1179656 | tf_op jit(solution)/shard_map/reduce_heavy/ppermute | solution.py:38
  52.0 10.9 %collective-permute-start.13 = (bf16[32,6144]{1,0:T(8,128)(2,1)S(1)}, bf16[32,6144]{1,0:T(8,128)(2,1)S(1)}, u32[]{:S(2)}, u32[]{:S(2)}) collective-permute-start(bf16[32,6144]{1,0:T(8,128)(2,1)S(1)} %get-tuple-element.52), channel_id=1, source_target_pairs={{0,16},{1,17},{2,18},{3,19},{4,20},{5,21},{6,22},{7,23},{16,32},{1... | collective-permute-start | bytes 1179656 | tf_op jit(solution)/shard_map/reduce_heavy/ppermute | solution.py:38
  52.3 10.5 %collective-permute-start.14 = (bf16[32,6144]{1,0:T(8,128)(2,1)S(1)}, bf16[32,6144]{1,0:T(8,128)(2,1)S(1)}, u32[]{:S(2)}, u32[]{:S(2)}) collective-permute-start(bf16[32,6144]{1,0:T(8,128)(2,1)S(1)} %get-tuple-element.51), channel_id=1, source_target_pairs={{0,48},{1,49},{2,50},{3,51},{4,52},{5,53},{6,54},{7,55},{16,0},{17... | collective-permute-start | bytes 1179656 | tf_op jit(solution)/shard_map/reduce_heavy/ppermute | solution.py:38

commit v12 on v10

--- a/solution.py
+++ b/solution.py
@@ -203,13 +203,13 @@
         _, far_two = lax.optimization_barrier((terms_one, far_two))
         terms_two, acts_two = expert_terms(group, far_two, *slices, BF16)
         other_two = swapped(terms_two)
-        _, near_two = lax.optimization_barrier((terms_two, near_two))
+        one = near_terms_one + other_one.astype(F32)
+        _, one, near_two = lax.optimization_barrier((terms_two, one, near_two))
         near_terms_two, near_acts_two = expert_terms(group, near_two, *slices, F32)
     with jax.named_scope("weights"):
         rows = (far_one, far_two, near_one, near_two)
         grads = weight_grads(rows, (acts_one, acts_two, near_acts_one, near_acts_two))
     with jax.named_scope("reduce_heavy"):
-        one = near_terms_one + other_one.astype(F32)
         two = near_terms_two + other_two.astype(F32)
         send = {1: two[:PLANE], 2: one[PLANE:], 3: two[PLANE:]}
         got = {d: give(send[d].astype(BF16), "heavy", d) for d in ISSUE}

time: 82.6 us -> 81.3 us (0.984)
  waiting for transfers between devices: 12.5 us -> 11.4 us
  blocking collectives: 34.1 us -> 33.2 us
    ppermute x3, waiting for transfers between devices: 4.78 us -> 3.39 us  [give(): return lax.ppermute(value, AXES, pairs(stage, d))]
    all_to_all x1, blocking collectives: 17.5 us -> 16.6 us  [scattered(): lax.all_to_all(value, AXES, 0, 0, axis_index_groups=planes(), tiled=True)]
where the time goes in v12:
time: 81.3 us; the launch traced here: 80.2 us
  blocking collectives  33.2 us (41%)
  starting transfers between devices  20.7 us (25%)
  waiting for transfers between devices  11.4 us (14%)
  Pallas kernels  11.2 us (14%)
  local copies, waits for them, and re-layouts  2.05 us (3%)
  between operations  0.86 us (1%)
  other arithmetic  0.83 us (1%)
    all_to_all x1, blocking collectives, exchanged(): return lax.all_to_all(value, axis, 0, 0, tiled=True)  16.6 us
    all_to_all x1, blocking collectives, scattered(): lax.all_to_all(value, AXES, 0, 0, axis_index_groups=planes(), tiled=True)  16.6 us
    ppermute x6, starting transfers between devices, fetch(): return lax.ppermute(value, AXES, pairs(stage, -d))  8.75 us
    ppermute x6, waiting for transfers between devices, fetch(): return lax.ppermute(value, AXES, pairs(stage, -d))  7.74 us
    ppermute x6, starting transfers between devices, swapped(): return lax.ppermute(value, 'core', [(0, 1), (1, 0)])  7.74 us
    pallas_call x4, Pallas kernels, expert_terms(): pl.pallas_call(expert_kernel, out_shape=(jax.ShapeDtypeStruct((n, 2 * D),...  5.49 us
    ppermute x3, starting transfers between devices, give(): return lax.ppermute(value, AXES, pairs(stage, d))  4.24 us
    pallas_call x1, Pallas kernels, weight_grads(): pl.pallas_call(weight_kernel, out_shape=(jax.ShapeDtypeStruct((1, D, UNIT...  3.63 us
  transfers between devices with their start and end apart: 15, of which 5 were waited for; matrix products, arithmetic and copies ran while one was open for 1% of the time, Pallas kernels for 11%

profile of v12, /device:TPU:1, one launch (start us, length us, event | category | flops | bytes accessed | tf_op | source)
XLA Modules:
  0.0 80.2 jit_solution(13355439780332518481)
XLA Ops:
  0.6 1.5 %copies_of_row.1 = bf16[8,2,3200]{2,1,0:T(2,128)(2,1)} custom-call(bf16[1,3072]{1,0:T(2,128)(2,1)} %tokens.1, bf16[1,3072]{1,0:T(2,128)(2,1)} %cotangent.1, s32[1,2]{1,0:T(1,128)} %routes.1, bf16[1,2]{1,0:T(2,128)(2,1)} %weights.1), custom_call_target="tpu_custom_call" | custom-call | tf_op jit(solution)/shard_map/gather_z/copies_of_row/pallas_call | solution.py:81
  2.1 16.6 %all_to_all.10 = bf16[8,2,3200]{2,1,0:T(2,128)(2,1)S(1)} all-to-all(bf16[8,2,3200]{2,1,0:T(2,128)(2,1)} %copies_of_row.1), channel_id=1, replica_groups=mesh['x_hi'=2,'core'=2,'y'=4,'x_lo'=2,'z'=8] {'z'}, dimensions={0} | all-to-all | bytes 204800 | tf_op jit(solution)/shard_map/gather_z/all_to_all | solution.py:50
  19.0 1.4 %collective-permute-start.2 = (bf16[8,6272]{1,0:T(8,128)(2,1)S(1)}, bf16[8,6272]{1,0:T(8,128)(2,1)S(1)}, u32[]{:S(2)}, u32[]{:S(2)}) collective-permute-start(bf16[8,6272]{1,0:T(8,128)(2,1)S(1)} %pad_maximum_fusion.4), channel_id=1, source_target_pairs={{0,8},{1,9},{2,10},{3,11},{4,12},{5,13},{6,14},{7,15},{16,24},{17,... | collective-permute-start | bytes 301064 | tf_op jit(solution)/shard_map/gather_light/ppermute | solution.py:42
  20.3 1.5 %collective-permute-start.1 = (bf16[8,6272]{1,0:T(8,128)(2,1)S(1)}, bf16[8,6272]{1,0:T(8,128)(2,1)S(1)}, u32[]{:S(2)}, u32[]{:S(2)}) collective-permute-start(bf16[8,6272]{1,0:T(8,128)(2,1)S(1)} %pad_maximum_fusion.4), channel_id=1, source_target_pairs={{0,136},{1,137},{2,138},{3,139},{4,140},{5,141},{6,142},{7,143},{1... | collective-permute-start | bytes 301064 | tf_op jit(solution)/shard_map/gather_light/ppermute | solution.py:42
  21.9 1.6 %collective-permute-start = (bf16[8,6272]{1,0:T(8,128)(2,1)S(1)}, bf16[8,6272]{1,0:T(8,128)(2,1)S(1)}, u32[]{:S(2)}, u32[]{:S(2)}) collective-permute-start(bf16[8,6272]{1,0:T(8,128)(2,1)S(1)} %pad_maximum_fusion.4), channel_id=1, source_target_pairs={{0,128},{1,129},{2,130},{3,131},{4,132},{5,133},{6,134},{7,135},{1... | collective-permute-start | bytes 301064 | tf_op jit(solution)/shard_map/gather_light/ppermute | solution.py:42
  23.8 3.0 %collective-permute-done = bf16[8,6272]{1,0:T(8,128)(2,1)S(1)} collective-permute-done((bf16[8,6272]{1,0:T(8,128)(2,1)S(1)}, bf16[8,6272]{1,0:T(8,128)(2,1)S(1)}, u32[]{:S(2)}, u32[]{:S(2)}) %collective-permute-start) | collective-permute-done | bytes 100384 | tf_op jit(solution)/shard_map/gather_light/ppermute | solution.py:42
  26.9 2.8 %collective-permute-start.3 = (bf16[32,6272]{1,0:T(8,128)(2,1)S(1)}, bf16[32,6272]{1,0:T(8,128)(2,1)S(1)}, u32[]{:S(2)}, u32[]{:S(2)}) collective-permute-start(bf16[32,6272]{1,0:T(8,128)(2,1)S(1)} %pad_maximum_fusion.3), channel_id=1, source_target_pairs={{0,32},{1,33},{2,34},{3,35},{4,36},{5,37},{6,38},{7,39},{16,48},{1... | collective-permute-start | bytes 1204232 | tf_op jit(solution)/shard_map/gather_heavy/ppermute | solution.py:42
  29.7 0.9 %collective-permute-start.6 = (bf16[32,6272]{1,0:T(8,128)(2,1)S(1)}, bf16[32,6272]{1,0:T(8,128)(2,1)S(1)}, u32[]{:S(2)}, u32[]{:S(2)}) collective-permute-start(bf16[32,6272]{1,0:T(8,128)(2,1)S(1)} %pad_maximum_fusion.3), channel_id=1, source_target_pairs={{0,48},{1,49},{2,50},{3,51},{4,52},{5,53},{6,54},{7,55},{16,0},{17... | collective-permute-start | bytes 1204232 | tf_op jit(solution)/shard_map/gather_heavy/ppermute | solution.py:42
  30.6 0.6 collective-permute-start.7
  31.2 4.3 %collective-permute-done.3 = bf16[32,6272]{1,0:T(8,128)(2,1)S(1)} collective-permute-done((bf16[32,6272]{1,0:T(8,128)(2,1)S(1)}, bf16[32,6272]{1,0:T(8,128)(2,1)S(1)}, u32[]{:S(2)}, u32[]{:S(2)}) %collective-permute-start.3) | collective-permute-done | bytes 401440 | tf_op jit(solution)/shard_map/gather_heavy/ppermute | solution.py:42
  35.5 4.6 %collective-permute-start.4 = (bf16[32,6272]{1,0:T(8,128)(2,1)S(1)}, bf16[32,6272]{1,0:T(8,128)(2,1)S(1)}, u32[]{:S(2)}, u32[]{:S(2)}) collective-permute-start(bf16[32,6272]{1,0:T(8,128)(2,1)S(1)} %pad_maximum_fusion.3), channel_id=1, source_target_pairs={{0,64},{64,0},{1,65},{65,1},{2,66},{66,2},{3,67},{67,3},{4,68},{68... | collective-permute-start | bytes 1204232 | tf_op jit(solution)/shard_map/gather_core/ppermute | solution.py:46
  40.4 0.9 %copy-done = bf16[1,128,3072]{2,1,0:T(8,128)(2,1)S(1)} copy-done((bf16[1,128,3072]{2,1,0:T(8,128)(2,1)S(1)}, bf16[1,128,3072]{2,1,0:T(8,128)(2,1)}, u32[]{:S(2)}) %copy-start) | copy-done | bytes 786456
  41.4 1.4 %expert_terms.5 = (f32[64,6144]{1,0:T(8,128)S(1)}, bf16[64,384]{1,0:T(8,128)(2,1)S(1)}) custom-call(s32[1]{0:T(128)} %bitcast.group, bf16[64,6272]{1,0:T(8,128)(2,1)S(1)} %constant_dynamic-update-slice_fusion.2.rows.refs_2_, bf16[3072,256]{1,0:T(8,128)(2,1)S(1)} %pad_maximum_fusion.pair_slice, bf16[128,3072]{1,0:T(8,128)(2,1)S(1)} %bitcast.98), custom_call_target="tpu_custom_call" | custom-call | flops 301989888 | bytes 3145728 | tf_op jit(solution)/shard_map/experts/expert_terms/pallas_call | solution.py:112
  42.8 2.2 %collective-permute-start.9 = (bf16[32,6272]{1,0:T(8,128)(2,1)S(1)}, bf16[32,6272]{1,0:T(8,128)(2,1)S(1)}, u32[]{:S(2)}, u32[]{:S(2)}) collective-permute-start(bf16[32,6272]{1,0:T(8,128)(2,1)S(1)} %collective-permute-done.7), channel_id=1, source_target_pairs={{0,64},{64,0},{1,65},{65,1},{2,66},{66,2},{3,67},{67,3},{4,68},{68... | collective-permute-start | bytes 1204232 | tf_op jit(solution)/shard_map/experts/ppermute | solution.py:46
  45.2 1.4 %expert_terms.4 = (bf16[64,6144]{1,0:T(8,128)(2,1)S(1)}, bf16[64,384]{1,0:T(8,128)(2,1)S(1)}) custom-call(s32[1]{0:T(128)} %bitcast.group, bf16[64,6272]{1,0:T(8,128)(2,1)S(1)} %constant_dynamic-update-slice_fusion.rows.refs_0_, bf16[3072,256]{1,0:T(8,128)(2,1)S(1)} %pad_maximum_fusion.pair_slice, bf16[128,3072]{1,0:T(8,128)(2,1)S(1)} %bitcast.99), custom_call_target="tpu_custom_call" | custom-call | flops 301989888 | bytes 3145728 | tf_op jit(solution)/shard_map/experts/expert_terms/pallas_call | solution.py:112
  47.2 1.4 %expert_terms.6 = (bf16[64,6144]{1,0:T(8,128)(2,1)S(1)}, bf16[64,384]{1,0:T(8,128)(2,1)S(1)}) custom-call(s32[1]{0:T(128)} %bitcast.group, bf16[64,6272]{1,0:T(8,128)(2,1)S(1)} %pad_maximum_fusion.1.rows.refs_1_, bf16[3072,256]{1,0:T(8,128)(2,1)S(1)} %pad_maximum_fusion.pair_slice, bf16[128,3072]{1,0:T(8,128)(2,1)S(1)} %bitcast.100), custom_call_target="tpu_custom_call" | custom-call | flops 301989888 | bytes 3145728 | tf_op jit(solution)/shard_map/experts/expert_terms/pallas_call | solution.py:112
  49.3 1.5 %collective-permute-start.11 = (bf16[32,6144]{1,0:T(8,128)(2,1)S(1)}, bf16[32,6144]{1,0:T(8,128)(2,1)S(1)}, u32[]{:S(2)}, u32[]{:S(2)}) collective-permute-start(bf16[32,6144]{1,0:T(8,128)(2,1)S(1)} %slice.274), channel_id=1, source_target_pairs={{0,32},{1,33},{2,34},{3,35},{4,36},{5,37},{6,38},{7,39},{16,48},{1... | collective-permute-start | bytes 1179656 | tf_op jit(solution)/shard_map/reduce_heavy/ppermute | solution.py:38
  50.8 1.4 %expert_terms.7 = (f32[64,6144]{1,0:T(8,128)S(1)}, bf16[64,384]{1,0:T(8,128)(2,1)S(1)}) custom-call(s32[1]{0:T(128)} %bitcast.group, bf16[64,6272]{1,0:T(8,128)(2,1)S(1)} %pad_maximum_fusion.2.rows.refs_3_, bf16[3072,256]{1,0:T(8,128)(2,1)S(1)} %pad_maximum_fusion.pair_slice, bf16[128,3072]{1,0:T(8,128)(2,1)S(1)} %bitcast.101), custom_call_target="tpu_custom_call" | custom-call | flops 301989888 | bytes 3145728 | tf_op jit(solution)/shard_map/experts/expert_terms/pallas_call | solution.py:112
  52.7 2.4 %collective-permute-start.14 = (bf16[32,6144]{1,0:T(8,128)(2,1)S(1)}, bf16[32,6144]{1,0:T(8,128)(2,1)S(1)}, u32[]{:S(2)}, u32[]{:S(2)}) collective-permute-start(bf16[32,6144]{1,0:T(8,128)(2,1)S(1)} %get-tuple-element.57), channel_id=1, source_target_pairs={{0,48},{1,49},{2,50},{3,51},{4,52},{5,53},{6,54},{7,55},{16,0},{17... | collective-permute-start | bytes 1179656 | tf_op jit(solution)/shard_map/reduce_heavy/ppermute | solution.py:38
  55.2 3.6 %weight_grads.1 = (bf16[1,3072,128]{2,1,0:T(8,128)(2,1)}, bf16[1,3072,128]{2,1,0:T(8,128)(2,1)}, bf16[1,128,3072]{2,1,0:T(8,128)(2,1)}) custom-call(bf16[64,6272]{1,0:T(8,128)(2,1)S(1)} %constant_dynamic-update-slice_fusion.rows.refs_0_, bf16[64,6272]{1,0:T(8,128)(2,1)S(1)} %pad_maximum_fusion.1.rows.refs_1_, ...), custom_call_target="tpu_custom_call" | custom-call | flops 603979776 | bytes 5505024 | tf_op jit(solution)/shard_map/weights/weight_grads/pallas_call | solution.py:141
  58.8 3.4 %collective-permute-done.13.two = bf16[32,6144]{1,0:T(8,128)(2,1)S(1)} collective-permute-done((bf16[32,6144]{1,0:T(8,128)(2,1)S(1)}, bf16[32,6144]{1,0:T(8,128)(2,1)S(1)}, u32[]{:S(2)}, u32[]{:S(2)}) %collective-permute-start.13) | collective-permute-done | bytes 393248 | tf_op jit(solution)/shard_map/reduce_heavy/ppermute | solution.py:38
  62.2 0.6 summed_pairs.1
  62.8 16.6 %all_to_all.11 = bf16[32,2,3072]{2,1,0:T(2,128)(2,1)S(1)} all-to-all(bf16[32,2,3072]{2,1,0:T(2,128)(2,1)S(1)} %summed_pairs.1), channel_id=1, replica_groups={{0,1,2,3,4,5,6,7,8,9,10,11,12,13,14,15,128,129,130,131,132,133,134,135,..., dimensions={0} | all-to-all | bytes 786432 | tf_op jit(solution)/shard_map/reduce_plane/all_to_all | solution.py:60
  79.6 0.6 fusion.3
  (41 shorter events, 3.3 us)
Async XLA Ops:
  18.7 21.5 %copy-start.1 = (bf16[1,3072,128]{2,1,0:T(8,128)(2,1)S(1)}, bf16[1,3072,128]{2,1,0:T(8,128)(2,1)}, u32[]{:S(2)}) copy-start(bf16[1,3072,128]{2,1,0:T(8,128)(2,1)} %param.12) | copy-start | bytes 2359300
  18.7 21.5 %copy-start.2 = (bf16[1,3072,128]{2,1,0:T(8,128)(2,1)S(1)}, bf16[1,3072,128]{2,1,0:T(8,128)(2,1)}, u32[]{:S(2)}) copy-start(bf16[1,3072,128]{2,1,0:T(8,128)(2,1)} %param.11) | copy-start | bytes 2359300
  19.0 4.8 %collective-permute-start.2 = (bf16[8,6272]{1,0:T(8,128)(2,1)S(1)}, bf16[8,6272]{1,0:T(8,128)(2,1)S(1)}, u32[]{:S(2)}, u32[]{:S(2)}) collective-permute-start(bf16[8,6272]{1,0:T(8,128)(2,1)S(1)} %pad_maximum_fusion.4), channel_id=1, source_target_pairs={{0,8},{1,9},{2,10},{3,11},{4,12},{5,13},{6,14},{7,15},{16,24},{17,... | collective-permute-start | bytes 301064 | tf_op jit(solution)/shard_map/gather_light/ppermute | solution.py:42
  20.3 3.5 %collective-permute-start.1 = (bf16[8,6272]{1,0:T(8,128)(2,1)S(1)}, bf16[8,6272]{1,0:T(8,128)(2,1)S(1)}, u32[]{:S(2)}, u32[]{:S(2)}) collective-permute-start(bf16[8,6272]{1,0:T(8,128)(2,1)S(1)} %pad_maximum_fusion.4), channel_id=1, source_target_pairs={{0,136},{1,137},{2,138},{3,139},{4,140},{5,141},{6,142},{7,143},{1... | collective-permute-start | bytes 301064 | tf_op jit(solution)/shard_map/gather_light/ppermute | solution.py:42
  21.9 5.0 %collective-permute-start = (bf16[8,6272]{1,0:T(8,128)(2,1)S(1)}, bf16[8,6272]{1,0:T(8,128)(2,1)S(1)}, u32[]{:S(2)}, u32[]{:S(2)}) collective-permute-start(bf16[8,6272]{1,0:T(8,128)(2,1)S(1)} %pad_maximum_fusion.4), channel_id=1, source_target_pairs={{0,128},{1,129},{2,130},{3,131},{4,132},{5,133},{6,134},{7,135},{1... | collective-permute-start | bytes 301064 | tf_op jit(solution)/shard_map/gather_light/ppermute | solution.py:42
  26.9 8.6 %collective-permute-start.3 = (bf16[32,6272]{1,0:T(8,128)(2,1)S(1)}, bf16[32,6272]{1,0:T(8,128)(2,1)S(1)}, u32[]{:S(2)}, u32[]{:S(2)}) collective-permute-start(bf16[32,6272]{1,0:T(8,128)(2,1)S(1)} %pad_maximum_fusion.3), channel_id=1, source_target_pairs={{0,32},{1,33},{2,34},{3,35},{4,36},{5,37},{6,38},{7,39},{16,48},{1... | collective-permute-start | bytes 1204232 | tf_op jit(solution)/shard_map/gather_heavy/ppermute | solution.py:42
  29.7 13.0 %collective-permute-start.6 = (bf16[32,6272]{1,0:T(8,128)(2,1)S(1)}, bf16[32,6272]{1,0:T(8,128)(2,1)S(1)}, u32[]{:S(2)}, u32[]{:S(2)}) collective-permute-start(bf16[32,6272]{1,0:T(8,128)(2,1)S(1)} %pad_maximum_fusion.3), channel_id=1, source_target_pairs={{0,48},{1,49},{2,50},{3,51},{4,52},{5,53},{6,54},{7,55},{16,0},{17... | collective-permute-start | bytes 1204232 | tf_op jit(solution)/shard_map/gather_heavy/ppermute | solution.py:42
  30.6 12.2 %collective-permute-start.7 = (bf16[32,6272]{1,0:T(8,128)(2,1)S(1)}, bf16[32,6272]{1,0:T(8,128)(2,1)S(1)}, u32[]{:S(2)}, u32[]{:S(2)}) collective-permute-start(bf16[32,6272]{1,0:T(8,128)(2,1)S(1)} %pad_maximum_fusion.3), channel_id=1, source_target_pairs={{0,16},{1,17},{2,18},{3,19},{4,20},{5,21},{6,22},{7,23},{16,32},{1... | collective-permute-start | bytes 1204232 | tf_op jit(solution)/shard_map/gather_heavy/ppermute | solution.py:42
  35.5 9.6 %collective-permute-start.4 = (bf16[32,6272]{1,0:T(8,128)(2,1)S(1)}, bf16[32,6272]{1,0:T(8,128)(2,1)S(1)}, u32[]{:S(2)}, u32[]{:S(2)}) collective-permute-start(bf16[32,6272]{1,0:T(8,128)(2,1)S(1)} %pad_maximum_fusion.3), channel_id=1, source_target_pairs={{0,64},{64,0},{1,65},{65,1},{2,66},{66,2},{3,67},{67,3},{4,68},{68... | collective-permute-start | bytes 1204232 | tf_op jit(solution)/shard_map/gather_core/ppermute | solution.py:46
  40.1 5.1 %collective-permute-start.5 = (bf16[32,6272]{1,0:T(8,128)(2,1)S(1)}, bf16[32,6272]{1,0:T(8,128)(2,1)S(1)}, u32[]{:S(2)}, u32[]{:S(2)}) collective-permute-start(bf16[32,6272]{1,0:T(8,128)(2,1)S(1)} %collective-permute-done.3), channel_id=1, source_target_pairs={{0,64},{64,0},{1,65},{65,1},{2,66},{66,2},{3,67},{67,3},{4,68},{68... | collective-permute-start | bytes 1204232 | tf_op jit(solution)/shard_map/gather_core/ppermute | solution.py:46
  40.2 1.1 %copy-start = (bf16[1,128,3072]{2,1,0:T(8,128)(2,1)S(1)}, bf16[1,128,3072]{2,1,0:T(8,128)(2,1)}, u32[]{:S(2)}) copy-start(bf16[1,128,3072]{2,1,0:T(8,128)(2,1)} %param.13) | copy-start | bytes 2359300
  42.8 4.4 %collective-permute-start.9 = (bf16[32,6272]{1,0:T(8,128)(2,1)S(1)}, bf16[32,6272]{1,0:T(8,128)(2,1)S(1)}, u32[]{:S(2)}, u32[]{:S(2)}) collective-permute-start(bf16[32,6272]{1,0:T(8,128)(2,1)S(1)} %collective-permute-done.7), channel_id=1, source_target_pairs={{0,64},{64,0},{1,65},{65,1},{2,66},{66,2},{3,67},{67,3},{4,68},{68... | collective-permute-start | bytes 1204232 | tf_op jit(solution)/shard_map/experts/ppermute | solution.py:46
  45.0 2.1 %collective-permute-start.8 = (bf16[32,6272]{1,0:T(8,128)(2,1)S(1)}, bf16[32,6272]{1,0:T(8,128)(2,1)S(1)}, u32[]{:S(2)}, u32[]{:S(2)}) collective-permute-start(bf16[32,6272]{1,0:T(8,128)(2,1)S(1)} %collective-permute-done.6), channel_id=1, source_target_pairs={{0,64},{64,0},{1,65},{65,1},{2,66},{66,2},{3,67},{67,3},{4,68},{68... | collective-permute-start | bytes 1204232 | tf_op jit(solution)/shard_map/experts/ppermute | solution.py:46
  46.6 2.5 %collective-permute-start.10 = (bf16[64,6144]{1,0:T(8,128)(2,1)S(1)}, bf16[64,6144]{1,0:T(8,128)(2,1)S(1)}, u32[]{:S(2)}, u32[]{:S(2)}) collective-permute-start(bf16[64,6144]{1,0:T(8,128)(2,1)S(1)} %get-tuple-element.34), channel_id=1, source_target_pairs={{0,64},{64,0},{1,65},{65,1},{2,66},{66,2},{3,67},{67,3},{4,68},{68... | collective-permute-start | bytes 2359304 | tf_op jit(solution)/shard_map/experts/ppermute | solution.py:46
  48.6 3.5 %collective-permute-start.12 = (bf16[64,6144]{1,0:T(8,128)(2,1)S(1)}, bf16[64,6144]{1,0:T(8,128)(2,1)S(1)}, u32[]{:S(2)}, u32[]{:S(2)}) collective-permute-start(bf16[64,6144]{1,0:T(8,128)(2,1)S(1)} %get-tuple-element.39), channel_id=1, source_target_pairs={{0,64},{64,0},{1,65},{65,1},{2,66},{66,2},{3,67},{67,3},{4,68},{68... | collective-permute-start | bytes 2359304 | tf_op jit(solution)/shard_map/experts/ppermute | solution.py:46
  49.3 9.5 %collective-permute-start.11 = (bf16[32,6144]{1,0:T(8,128)(2,1)S(1)}, bf16[32,6144]{1,0:T(8,128)(2,1)S(1)}, u32[]{:S(2)}, u32[]{:S(2)}) collective-permute-start(bf16[32,6144]{1,0:T(8,128)(2,1)S(1)} %slice.274), channel_id=1, source_target_pairs={{0,32},{1,33},{2,34},{3,35},{4,36},{5,37},{6,38},{7,39},{16,48},{1... | collective-permute-start | bytes 1179656 | tf_op jit(solution)/shard_map/reduce_heavy/ppermute | solution.py:38
  52.3 9.8 %collective-permute-start.13 = (bf16[32,6144]{1,0:T(8,128)(2,1)S(1)}, bf16[32,6144]{1,0:T(8,128)(2,1)S(1)}, u32[]{:S(2)}, u32[]{:S(2)}) collective-permute-start(bf16[32,6144]{1,0:T(8,128)(2,1)S(1)} %get-tuple-element.58), channel_id=1, source_target_pairs={{0,16},{1,17},{2,18},{3,19},{4,20},{5,21},{6,22},{7,23},{16,32},{1... | collective-permute-start | bytes 1179656 | tf_op jit(solution)/shard_map/reduce_heavy/ppermute | solution.py:38
  52.7 9.4 %collective-permute-start.14 = (bf16[32,6144]{1,0:T(8,128)(2,1)S(1)}, bf16[32,6144]{1,0:T(8,128)(2,1)S(1)}, u32[]{:S(2)}, u32[]{:S(2)}) collective-permute-start(bf16[32,6144]{1,0:T(8,128)(2,1)S(1)} %get-tuple-element.57), channel_id=1, source_target_pairs={{0,48},{1,49},{2,50},{3,51},{4,52},{5,53},{6,54},{7,55},{16,0},{17... | collective-permute-start | bytes 1179656 | tf_op jit(solution)/shard_map/reduce_heavy/ppermute | solution.py:38

commit v13 on v12

--- a/solution.py
+++ b/solution.py
@@ -201,14 +201,13 @@
         terms_one, acts_one = expert_terms(group, far_one, *slices, BF16)
         other_one = swapped(terms_one)
         _, far_two = lax.optimization_barrier((terms_one, far_two))
-        terms_two, acts_two = expert_terms(group, far_two, *slices, BF16)
-        other_two = swapped(terms_two)
+        last = jnp.concatenate([far_two, near_two], axis=0)
+        last_terms, last_acts = expert_terms(group, last, *slices, F32)
+        other_two = swapped(last_terms[: 2 * PLANE].astype(BF16))
+        near_terms_two = last_terms[2 * PLANE :]
         one = near_terms_one + other_one.astype(F32)
-        _, one, near_two = lax.optimization_barrier((terms_two, one, near_two))
-        near_terms_two, near_acts_two = expert_terms(group, near_two, *slices, F32)
     with jax.named_scope("weights"):
-        rows = (far_one, far_two, near_one, near_two)
-        grads = weight_grads(rows, (acts_one, acts_two, near_acts_one, near_acts_two))
+        grads = weight_grads((far_one, near_one, last), (acts_one, near_acts_one, last_acts))
     with jax.named_scope("reduce_heavy"):
         two = near_terms_two + other_two.astype(F32)
         send = {1: two[:PLANE], 2: one[PLANE:], 3: two[PLANE:]}

time: 81.3 us -> 81.4 us (level)
  Pallas kernels: 11.2 us -> 9.22 us
  waiting for transfers between devices: 11.4 us -> 13 us
    pallas_call x4 -> x3, Pallas kernels: 5.49 us -> 4.14 us  [expert_terms(): pl.pallas_call(expert_kernel, out_shape=(jax.ShapeDtypeStruct((n, 2 * D),...]
    ppermute x3, waiting for transfers between devices: 3.39 us -> 4.66 us  [give(): return lax.ppermute(value, AXES, pairs(stage, d))]
  transfers between devices with their start and end apart: 15 -> 15, of which waited for: 5 -> 6; matrix products, arithmetic and copies ran while one was open for 1% -> 1% of each run, Pallas kernels for 11% -> 9%
where the time goes in v13:
time: 81.4 us; the launch traced here: 80.3 us
  blocking collectives  33.4 us (41%)
  starting transfers between devices  20.8 us (26%)
  waiting for transfers between devices  13 us (16%)
  Pallas kernels  9.22 us (11%)
  local copies, waits for them, and re-layouts  2.23 us (3%)
  between operations  0.85 us (1%)
    all_to_all x1, blocking collectives, scattered(): lax.all_to_all(value, AXES, 0, 0, axis_index_groups=planes(), tiled=True)  16.8 us
    all_to_all x1, blocking collectives, exchanged(): return lax.all_to_all(value, axis, 0, 0, tiled=True)  16.6 us
    ppermute x6, starting transfers between devices, fetch(): return lax.ppermute(value, AXES, pairs(stage, -d))  8.75 us
    ppermute x6, starting transfers between devices, swapped(): return lax.ppermute(value, 'core', [(0, 1), (1, 0)])  7.85 us
    ppermute x6, waiting for transfers between devices, fetch(): return lax.ppermute(value, AXES, pairs(stage, -d))  7.74 us
    ppermute x3, waiting for transfers between devices, give(): return lax.ppermute(value, AXES, pairs(stage, d))  4.66 us
    ppermute x3, starting transfers between devices, give(): return lax.ppermute(value, AXES, pairs(stage, d))  4.25 us
    pallas_call x3, Pallas kernels, expert_terms(): pl.pallas_call(expert_kernel, out_shape=(jax.ShapeDtypeStruct((n, 2 * D),...  4.14 us
  transfers between devices with their start and end apart: 15, of which 6 were waited for; matrix products, arithmetic and copies ran while one was open for 1% of the time, Pallas kernels for 9%

profile of v13, /device:TPU:1, one launch (start us, length us, event | category | flops | bytes accessed | tf_op | source)
XLA Modules:
  0.0 80.3 jit_solution(7255135244409394922)
XLA Ops:
  0.6 1.5 %copies_of_row.1 = bf16[8,2,3200]{2,1,0:T(2,128)(2,1)} custom-call(bf16[1,3072]{1,0:T(2,128)(2,1)} %tokens.1, bf16[1,3072]{1,0:T(2,128)(2,1)} %cotangent.1, s32[1,2]{1,0:T(1,128)} %routes.1, bf16[1,2]{1,0:T(2,128)(2,1)} %weights.1), custom_call_target="tpu_custom_call" | custom-call | tf_op jit(solution)/shard_map/gather_z/copies_of_row/pallas_call | solution.py:81
  2.1 16.6 %all_to_all.10 = bf16[8,2,3200]{2,1,0:T(2,128)(2,1)S(1)} all-to-all(bf16[8,2,3200]{2,1,0:T(2,128)(2,1)} %copies_of_row.1), channel_id=1, replica_groups=mesh['x_hi'=2,'core'=2,'y'=4,'x_lo'=2,'z'=8] {'z'}, dimensions={0} | all-to-all | bytes 204800 | tf_op jit(solution)/shard_map/gather_z/all_to_all | solution.py:50
  19.0 1.4 %collective-permute-start.2 = (bf16[8,6272]{1,0:T(8,128)(2,1)S(1)}, bf16[8,6272]{1,0:T(8,128)(2,1)S(1)}, u32[]{:S(2)}, u32[]{:S(2)}) collective-permute-start(bf16[8,6272]{1,0:T(8,128)(2,1)S(1)} %pad_maximum_fusion.3), channel_id=1, source_target_pairs={{0,8},{1,9},{2,10},{3,11},{4,12},{5,13},{6,14},{7,15},{16,24},{17,... | collective-permute-start | bytes 301064 | tf_op jit(solution)/shard_map/gather_light/ppermute | solution.py:42
  20.3 1.5 %collective-permute-start.1 = (bf16[8,6272]{1,0:T(8,128)(2,1)S(1)}, bf16[8,6272]{1,0:T(8,128)(2,1)S(1)}, u32[]{:S(2)}, u32[]{:S(2)}) collective-permute-start(bf16[8,6272]{1,0:T(8,128)(2,1)S(1)} %pad_maximum_fusion.3), channel_id=1, source_target_pairs={{0,136},{1,137},{2,138},{3,139},{4,140},{5,141},{6,142},{7,143},{1... | collective-permute-start | bytes 301064 | tf_op jit(solution)/shard_map/gather_light/ppermute | solution.py:42
  21.9 1.6 %collective-permute-start = (bf16[8,6272]{1,0:T(8,128)(2,1)S(1)}, bf16[8,6272]{1,0:T(8,128)(2,1)S(1)}, u32[]{:S(2)}, u32[]{:S(2)}) collective-permute-start(bf16[8,6272]{1,0:T(8,128)(2,1)S(1)} %pad_maximum_fusion.3), channel_id=1, source_target_pairs={{0,128},{1,129},{2,130},{3,131},{4,132},{5,133},{6,134},{7,135},{1... | collective-permute-start | bytes 301064 | tf_op jit(solution)/shard_map/gather_light/ppermute | solution.py:42
  23.8 3.0 %collective-permute-done = bf16[8,6272]{1,0:T(8,128)(2,1)S(1)} collective-permute-done((bf16[8,6272]{1,0:T(8,128)(2,1)S(1)}, bf16[8,6272]{1,0:T(8,128)(2,1)S(1)}, u32[]{:S(2)}, u32[]{:S(2)}) %collective-permute-start) | collective-permute-done | bytes 100384 | tf_op jit(solution)/shard_map/gather_light/ppermute | solution.py:42
  26.9 2.8 %collective-permute-start.3 = (bf16[32,6272]{1,0:T(8,128)(2,1)S(1)}, bf16[32,6272]{1,0:T(8,128)(2,1)S(1)}, u32[]{:S(2)}, u32[]{:S(2)}) collective-permute-start(bf16[32,6272]{1,0:T(8,128)(2,1)S(1)} %pad_maximum_fusion.2), channel_id=1, source_target_pairs={{0,32},{1,33},{2,34},{3,35},{4,36},{5,37},{6,38},{7,39},{16,48},{1... | collective-permute-start | bytes 1204232 | tf_op jit(solution)/shard_map/gather_heavy/ppermute | solution.py:42
  29.7 0.9 %collective-permute-start.4 = (bf16[32,6272]{1,0:T(8,128)(2,1)S(1)}, bf16[32,6272]{1,0:T(8,128)(2,1)S(1)}, u32[]{:S(2)}, u32[]{:S(2)}) collective-permute-start(bf16[32,6272]{1,0:T(8,128)(2,1)S(1)} %pad_maximum_fusion.2), channel_id=1, source_target_pairs={{0,48},{1,49},{2,50},{3,51},{4,52},{5,53},{6,54},{7,55},{16,0},{17... | collective-permute-start | bytes 1204232 | tf_op jit(solution)/shard_map/gather_heavy/ppermute | solution.py:42
  30.6 0.6 collective-permute-start.5
  31.2 4.3 %collective-permute-done.3 = bf16[32,6272]{1,0:T(8,128)(2,1)S(1)} collective-permute-done((bf16[32,6272]{1,0:T(8,128)(2,1)S(1)}, bf16[32,6272]{1,0:T(8,128)(2,1)S(1)}, u32[]{:S(2)}, u32[]{:S(2)}) %collective-permute-start.3) | collective-permute-done | bytes 401440 | tf_op jit(solution)/shard_map/gather_heavy/ppermute | solution.py:42
  35.5 4.6 %collective-permute-start.6 = (bf16[32,6272]{1,0:T(8,128)(2,1)S(1)}, bf16[32,6272]{1,0:T(8,128)(2,1)S(1)}, u32[]{:S(2)}, u32[]{:S(2)}) collective-permute-start(bf16[32,6272]{1,0:T(8,128)(2,1)S(1)} %pad_maximum_fusion.2), channel_id=1, source_target_pairs={{0,64},{64,0},{1,65},{65,1},{2,66},{66,2},{3,67},{67,3},{4,68},{68... | collective-permute-start | bytes 1204232 | tf_op jit(solution)/shard_map/gather_core/ppermute | solution.py:46
  40.5 0.9 %copy-done = bf16[1,128,3072]{2,1,0:T(8,128)(2,1)S(1)} copy-done((bf16[1,128,3072]{2,1,0:T(8,128)(2,1)S(1)}, bf16[1,128,3072]{2,1,0:T(8,128)(2,1)}, u32[]{:S(2)}) %copy-start) | copy-done | bytes 786456
  41.4 1.4 %expert_terms.3 = (f32[64,6144]{1,0:T(8,128)S(1)}, bf16[64,384]{1,0:T(8,128)(2,1)S(1)}) custom-call(s32[1]{0:T(128)} %bitcast.group, bf16[64,6272]{1,0:T(8,128)(2,1)S(1)} %constant_dynamic-update-slice_fusion.rows.refs_1_, bf16[3072,256]{1,0:T(8,128)(2,1)S(1)} %pad_maximum_fusion.pair_slice, bf16[128,3072]{1,0:T(8,128)(2,1)S(1)} %bitcast.98), custom_call_target="tpu_custom_call" | custom-call | flops 301989888 | bytes 3145728 | tf_op jit(solution)/shard_map/experts/expert_terms/pallas_call | solution.py:112
  42.8 2.2 %collective-permute-start.11 = (bf16[32,6272]{1,0:T(8,128)(2,1)S(1)}, bf16[32,6272]{1,0:T(8,128)(2,1)S(1)}, u32[]{:S(2)}, u32[]{:S(2)}) collective-permute-start(bf16[32,6272]{1,0:T(8,128)(2,1)S(1)} %collective-permute-done.5), channel_id=1, source_target_pairs={{0,64},{64,0},{1,65},{65,1},{2,66},{66,2},{3,67},{67,3},{4,68},{68... | collective-permute-start | bytes 1204232 | tf_op jit(solution)/shard_map/experts/ppermute | solution.py:46
  45.1 1.4 %expert_terms.4 = (bf16[64,6144]{1,0:T(8,128)(2,1)S(1)}, bf16[64,384]{1,0:T(8,128)(2,1)S(1)}) custom-call(s32[1]{0:T(128)} %bitcast.group, bf16[64,6272]{1,0:T(8,128)(2,1)S(1)} %constant_dynamic-update-slice_fusion.2.rows.refs_0_, bf16[3072,256]{1,0:T(8,128)(2,1)S(1)} %pad_maximum_fusion.pair_slice, bf16[128,3072]{1,0:T(8,128)(2,1)S(1)} %bitcast.99), custom_call_target="tpu_custom_call" | custom-call | flops 301989888 | bytes 3145728 | tf_op jit(solution)/shard_map/experts/expert_terms/pallas_call | solution.py:112
  46.5 0.6 collective-permute-start.8
  47.3 1.4 %expert_terms.5 = (f32[128,6144]{1,0:T(8,128)S(1)}, bf16[128,384]{1,0:T(8,128)(2,1)S(1)}) custom-call(s32[1]{0:T(128)} %bitcast.group, bf16[128,6272]{1,0:T(8,128)(2,1)S(1)} %constant_dynamic-update-slice_fusion.4.rows.refs_2_, bf16[3072,256]{1,0:T(8,128)(2,1)S(1)} %pad_maximum_fusion.pair_slice, bf16[128,3072]{1,0:T(8,128)(2,1)S(1)} %bitcast.100), custom_call_target="tpu_custom_call" | custom-call | flops 603979776 | bytes 3932160 | tf_op jit(solution)/shard_map/experts/expert_terms/pallas_call | solution.py:112
  49.3 1.3 %collective-permute-start.9 = (bf16[32,6144]{1,0:T(8,128)(2,1)S(1)}, bf16[32,6144]{1,0:T(8,128)(2,1)S(1)}, u32[]{:S(2)}, u32[]{:S(2)}) collective-permute-start(bf16[32,6144]{1,0:T(8,128)(2,1)S(1)} %slice.288), channel_id=1, source_target_pairs={{0,32},{1,33},{2,34},{3,35},{4,36},{5,37},{6,38},{7,39},{16,48},{1... | collective-permute-start | bytes 1179656 | tf_op jit(solution)/shard_map/reduce_heavy/ppermute | solution.py:38
  51.6 2.7 %collective-permute-start.14 = (bf16[32,6144]{1,0:T(8,128)(2,1)S(1)}, bf16[32,6144]{1,0:T(8,128)(2,1)S(1)}, u32[]{:S(2)}, u32[]{:S(2)}) collective-permute-start(bf16[32,6144]{1,0:T(8,128)(2,1)S(1)} %get-tuple-element.49), channel_id=1, source_target_pairs={{0,48},{1,49},{2,50},{3,51},{4,52},{5,53},{6,54},{7,55},{16,0},{17... | collective-permute-start | bytes 1179656 | tf_op jit(solution)/shard_map/reduce_heavy/ppermute | solution.py:38
  54.3 3.0 %weight_grads.1 = (bf16[1,3072,128]{2,1,0:T(8,128)(2,1)}, bf16[1,3072,128]{2,1,0:T(8,128)(2,1)}, bf16[1,128,3072]{2,1,0:T(8,128)(2,1)}) custom-call(bf16[64,6272]{1,0:T(8,128)(2,1)S(1)} %constant_dynamic-update-slice_fusion.2.rows.refs_0_, bf16[64,6272]{1,0:T(8,128)(2,1)S(1)} %constant_dynamic-update-slice_fusion.rows.refs_1_, ...), custom_call_target="tpu_custom_call" | custom-call | flops 603979776 | bytes 5505024 | tf_op jit(solution)/shard_map/weights/weight_grads/pallas_call | solution.py:141
  57.9 4.2 %collective-permute-done.13.two = bf16[32,6144]{1,0:T(8,128)(2,1)S(1)} collective-permute-done((bf16[32,6144]{1,0:T(8,128)(2,1)S(1)}, bf16[32,6144]{1,0:T(8,128)(2,1)S(1)}, u32[]{:S(2)}, u32[]{:S(2)}) %collective-permute-start.13) | collective-permute-done | bytes 393248 | tf_op jit(solution)/shard_map/reduce_heavy/ppermute | solution.py:38
  62.0 0.6 summed_pairs.1
  62.6 16.8 %all_to_all.11 = bf16[32,2,3072]{2,1,0:T(2,128)(2,1)S(1)} all-to-all(bf16[32,2,3072]{2,1,0:T(2,128)(2,1)S(1)} %summed_pairs.1), channel_id=1, replica_groups={{0,1,2,3,4,5,6,7,8,9,10,11,12,13,14,15,128,129,130,131,132,133,134,135,..., dimensions={0} | all-to-all | bytes 786432 | tf_op jit(solution)/shard_map/reduce_plane/all_to_all | solution.py:60
  79.6 0.6 fusion.3
  (43 shorter events, 3.6 us)
Async XLA Ops:
  18.7 21.6 %copy-start.1 = (bf16[1,3072,128]{2,1,0:T(8,128)(2,1)S(1)}, bf16[1,3072,128]{2,1,0:T(8,128)(2,1)}, u32[]{:S(2)}) copy-start(bf16[1,3072,128]{2,1,0:T(8,128)(2,1)} %param.12) | copy-start | bytes 2359300
  18.7 21.6 %copy-start.2 = (bf16[1,3072,128]{2,1,0:T(8,128)(2,1)S(1)}, bf16[1,3072,128]{2,1,0:T(8,128)(2,1)}, u32[]{:S(2)}) copy-start(bf16[1,3072,128]{2,1,0:T(8,128)(2,1)} %param.11) | copy-start | bytes 2359300
  19.0 4.8 %collective-permute-start.2 = (bf16[8,6272]{1,0:T(8,128)(2,1)S(1)}, bf16[8,6272]{1,0:T(8,128)(2,1)S(1)}, u32[]{:S(2)}, u32[]{:S(2)}) collective-permute-start(bf16[8,6272]{1,0:T(8,128)(2,1)S(1)} %pad_maximum_fusion.3), channel_id=1, source_target_pairs={{0,8},{1,9},{2,10},{3,11},{4,12},{5,13},{6,14},{7,15},{16,24},{17,... | collective-permute-start | bytes 301064 | tf_op jit(solution)/shard_map/gather_light/ppermute | solution.py:42
  20.3 3.5 %collective-permute-start.1 = (bf16[8,6272]{1,0:T(8,128)(2,1)S(1)}, bf16[8,6272]{1,0:T(8,128)(2,1)S(1)}, u32[]{:S(2)}, u32[]{:S(2)}) collective-permute-start(bf16[8,6272]{1,0:T(8,128)(2,1)S(1)} %pad_maximum_fusion.3), channel_id=1, source_target_pairs={{0,136},{1,137},{2,138},{3,139},{4,140},{5,141},{6,142},{7,143},{1... | collective-permute-start | bytes 301064 | tf_op jit(solution)/shard_map/gather_light/ppermute | solution.py:42
  21.9 5.0 %collective-permute-start = (bf16[8,6272]{1,0:T(8,128)(2,1)S(1)}, bf16[8,6272]{1,0:T(8,128)(2,1)S(1)}, u32[]{:S(2)}, u32[]{:S(2)}) collective-permute-start(bf16[8,6272]{1,0:T(8,128)(2,1)S(1)} %pad_maximum_fusion.3), channel_id=1, source_target_pairs={{0,128},{1,129},{2,130},{3,131},{4,132},{5,133},{6,134},{7,135},{1... | collective-permute-start | bytes 301064 | tf_op jit(solution)/shard_map/gather_light/ppermute | solution.py:42
  26.9 8.6 %collective-permute-start.3 = (bf16[32,6272]{1,0:T(8,128)(2,1)S(1)}, bf16[32,6272]{1,0:T(8,128)(2,1)S(1)}, u32[]{:S(2)}, u32[]{:S(2)}) collective-permute-start(bf16[32,6272]{1,0:T(8,128)(2,1)S(1)} %pad_maximum_fusion.2), channel_id=1, source_target_pairs={{0,32},{1,33},{2,34},{3,35},{4,36},{5,37},{6,38},{7,39},{16,48},{1... | collective-permute-start | bytes 1204232 | tf_op jit(solution)/shard_map/gather_heavy/ppermute | solution.py:42
  29.7 13.1 %collective-permute-start.4 = (bf16[32,6272]{1,0:T(8,128)(2,1)S(1)}, bf16[32,6272]{1,0:T(8,128)(2,1)S(1)}, u32[]{:S(2)}, u32[]{:S(2)}) collective-permute-start(bf16[32,6272]{1,0:T(8,128)(2,1)S(1)} %pad_maximum_fusion.2), channel_id=1, source_target_pairs={{0,48},{1,49},{2,50},{3,51},{4,52},{5,53},{6,54},{7,55},{16,0},{17... | collective-permute-start | bytes 1204232 | tf_op jit(solution)/shard_map/gather_heavy/ppermute | solution.py:42
  30.6 12.2 %collective-permute-start.5 = (bf16[32,6272]{1,0:T(8,128)(2,1)S(1)}, bf16[32,6272]{1,0:T(8,128)(2,1)S(1)}, u32[]{:S(2)}, u32[]{:S(2)}) collective-permute-start(bf16[32,6272]{1,0:T(8,128)(2,1)S(1)} %pad_maximum_fusion.2), channel_id=1, source_target_pairs={{0,16},{1,17},{2,18},{3,19},{4,20},{5,21},{6,22},{7,23},{16,32},{1... | collective-permute-start | bytes 1204232 | tf_op jit(solution)/shard_map/gather_heavy/ppermute | solution.py:42
  35.5 9.5 %collective-permute-start.6 = (bf16[32,6272]{1,0:T(8,128)(2,1)S(1)}, bf16[32,6272]{1,0:T(8,128)(2,1)S(1)}, u32[]{:S(2)}, u32[]{:S(2)}) collective-permute-start(bf16[32,6272]{1,0:T(8,128)(2,1)S(1)} %pad_maximum_fusion.2), channel_id=1, source_target_pairs={{0,64},{64,0},{1,65},{65,1},{2,66},{66,2},{3,67},{67,3},{4,68},{68... | collective-permute-start | bytes 1204232 | tf_op jit(solution)/shard_map/gather_core/ppermute | solution.py:46
  40.2 4.9 %collective-permute-start.7 = (bf16[32,6272]{1,0:T(8,128)(2,1)S(1)}, bf16[32,6272]{1,0:T(8,128)(2,1)S(1)}, u32[]{:S(2)}, u32[]{:S(2)}) collective-permute-start(bf16[32,6272]{1,0:T(8,128)(2,1)S(1)} %collective-permute-done.3), channel_id=1, source_target_pairs={{0,64},{64,0},{1,65},{65,1},{2,66},{66,2},{3,67},{67,3},{4,68},{68... | collective-permute-start | bytes 1204232 | tf_op jit(solution)/shard_map/gather_core/ppermute | solution.py:46
  40.3 1.1 %copy-start = (bf16[1,128,3072]{2,1,0:T(8,128)(2,1)S(1)}, bf16[1,128,3072]{2,1,0:T(8,128)(2,1)}, u32[]{:S(2)}) copy-start(bf16[1,128,3072]{2,1,0:T(8,128)(2,1)} %param.13) | copy-start | bytes 2359300
  42.8 4.3 %collective-permute-start.11 = (bf16[32,6272]{1,0:T(8,128)(2,1)S(1)}, bf16[32,6272]{1,0:T(8,128)(2,1)S(1)}, u32[]{:S(2)}, u32[]{:S(2)}) collective-permute-start(bf16[32,6272]{1,0:T(8,128)(2,1)S(1)} %collective-permute-done.5), channel_id=1, source_target_pairs={{0,64},{64,0},{1,65},{65,1},{2,66},{66,2},{3,67},{67,3},{4,68},{68... | collective-permute-start | bytes 1204232 | tf_op jit(solution)/shard_map/experts/ppermute | solution.py:46
  45.0 2.1 %collective-permute-start.10 = (bf16[32,6272]{1,0:T(8,128)(2,1)S(1)}, bf16[32,6272]{1,0:T(8,128)(2,1)S(1)}, u32[]{:S(2)}, u32[]{:S(2)}) collective-permute-start(bf16[32,6272]{1,0:T(8,128)(2,1)S(1)} %collective-permute-done.4), channel_id=1, source_target_pairs={{0,64},{64,0},{1,65},{65,1},{2,66},{66,2},{3,67},{67,3},{4,68},{68... | collective-permute-start | bytes 1204232 | tf_op jit(solution)/shard_map/experts/ppermute | solution.py:46
  46.5 2.6 %collective-permute-start.8 = (bf16[64,6144]{1,0:T(8,128)(2,1)S(1)}, bf16[64,6144]{1,0:T(8,128)(2,1)S(1)}, u32[]{:S(2)}, u32[]{:S(2)}) collective-permute-start(bf16[64,6144]{1,0:T(8,128)(2,1)S(1)} %get-tuple-element.32), channel_id=1, source_target_pairs={{0,64},{64,0},{1,65},{65,1},{2,66},{66,2},{3,67},{67,3},{4,68},{68... | collective-permute-start | bytes 2359304 | tf_op jit(solution)/shard_map/experts/ppermute | solution.py:46
  48.8 2.4 %collective-permute-start.12 = (bf16[64,6144]{1,0:T(8,128)(2,1)S(1)}, bf16[64,6144]{1,0:T(8,128)(2,1)S(1)}, u32[]{:S(2)}, u32[]{:S(2)}) collective-permute-start(bf16[64,6144]{1,0:T(8,128)(2,1)S(1)} %slice.287), channel_id=1, source_target_pairs={{0,64},{64,0},{1,65},{65,1},{2,66},{66,2},{3,67},{67,3},{4,68},{68... | collective-permute-start | bytes 2359304 | tf_op jit(solution)/shard_map/experts/ppermute | solution.py:46
  49.3 8.6 %collective-permute-start.9 = (bf16[32,6144]{1,0:T(8,128)(2,1)S(1)}, bf16[32,6144]{1,0:T(8,128)(2,1)S(1)}, u32[]{:S(2)}, u32[]{:S(2)}) collective-permute-start(bf16[32,6144]{1,0:T(8,128)(2,1)S(1)} %slice.288), channel_id=1, source_target_pairs={{0,32},{1,33},{2,34},{3,35},{4,36},{5,37},{6,38},{7,39},{16,48},{1... | collective-permute-start | bytes 1179656 | tf_op jit(solution)/shard_map/reduce_heavy/ppermute | solution.py:38
  51.4 10.7 %collective-permute-start.13 = (bf16[32,6144]{1,0:T(8,128)(2,1)S(1)}, bf16[32,6144]{1,0:T(8,128)(2,1)S(1)}, u32[]{:S(2)}, u32[]{:S(2)}) collective-permute-start(bf16[32,6144]{1,0:T(8,128)(2,1)S(1)} %get-tuple-element.50), channel_id=1, source_target_pairs={{0,16},{1,17},{2,18},{3,19},{4,20},{5,21},{6,22},{7,23},{16,32},{1... | collective-permute-start | bytes 1179656 | tf_op jit(solution)/shard_map/reduce_heavy/ppermute | solution.py:38
  51.6 10.4 %collective-permute-start.14 = (bf16[32,6144]{1,0:T(8,128)(2,1)S(1)}, bf16[32,6144]{1,0:T(8,128)(2,1)S(1)}, u32[]{:S(2)}, u32[]{:S(2)}) collective-permute-start(bf16[32,6144]{1,0:T(8,128)(2,1)S(1)} %get-tuple-element.49), channel_id=1, source_target_pairs={{0,48},{1,49},{2,50},{3,51},{4,52},{5,53},{6,54},{7,55},{16,0},{17... | collective-permute-start | bytes 1179656 | tf_op jit(solution)/shard_map/reduce_heavy/ppermute | solution.py:38
